TPU v7x, 32 devices: a whole 2x2x4 slice. The times are simulated.
32 devices in a mesh: dp: 8 (over z, x), tensor: 4 (over y, core).
Axes of the slice: x: 2, y: 2, z: 4, core: 2. Of those that a mesh axis runs over, the one named last changes fastest.
Arguments:
- tokens: bfloat16 [8, 1024, 1024], P('dp'), may hold values from -6 to 6
- prefix: int32 [8], P('dp'), may hold values from 102 to 512, as said below
- norm_gain: float32 [1024], replicated, may hold values from 0.1 to 1.9
- in_weight: bfloat16 [1024, 2, 2048], P(None, None, 'tensor'), may hold values from -0.1875 to 0.1875
- conv_weight: float32 [4, 2048], P(None, 'tensor'), may hold values from -3 to 3
- conv_bias: float32 [2048], P('tensor'), may hold values from -0.5 to 0.5
- xproj_weight: bfloat16 [2048, 96], P('tensor'), may hold values from -0.125 to 0.125
- step_weight: bfloat16 [64, 2048], P(None, 'tensor'), may hold values from -0.75 to 0.75
- step_bias: float32 [2048], P('tensor'), may hold values from -6.5 to -2.5
- decay_log: float32 [16, 2048], P(None, 'tensor'), may hold values from -4 to 1.5
- skip_gain: float32 [2048], P('tensor'), may hold values from 0.5 to 1.5
- out_weight: bfloat16 [2048, 1024], P('tensor'), may hold values from -0.5 to 0.5
- out_cotangent: bfloat16 [8, 1024, 1024], P('dp'), may hold values from -18 to 18
Outputs:
- block_out: bfloat16 [8, 1024, 1024], P('dp')
- grad_tokens: float32 [8, 1024, 1024], P('dp')
- grad_norm_gain: float32 [1024], replicated
- grad_in_weight: float32 [1024, 2, 2048], P(None, None, 'tensor')
- grad_conv_weight: float32 [4, 2048], P(None, 'tensor')
- grad_conv_bias: float32 [2048], P('tensor')
- grad_xproj_weight: float32 [2048, 96], P('tensor')
- grad_step_weight: float32 [64, 2048], P(None, 'tensor')
- grad_step_bias: float32 [2048], P('tensor')
- grad_decay_log: float32 [16, 2048], P(None, 'tensor')
- grad_skip_gain: float32 [2048], P('tensor')
- grad_out_weight: float32 [2048, 1024], P('tensor')
Inputs may be any that keep to these rules, and one draw needn't show every extreme that they name: prefix of each sequence; both bounds are reached in every draw.
All inputs are finite; a program needn't handle non-finite values.
Results may differ from a plain program's by a relative error of at most 0.011.
Values may be sent and summed in bfloat16 or wider, within the bound.
No kernel may reach another device: no remote copies, remote signals or barrier semaphores. Data moves between devices by JAX's collectives and lax.ppermute only.
A program may use at most 128 MiB of HBM per device.

v0:
```python
import jax
import jax.numpy as jnp
from jax import lax
from jax.sharding import PartitionSpec as P

BLOCK = 64


epsilon = 1e-05


def normalize(values, gain_vec):
    return (
        values * lax.rsqrt(jnp.mean(values * values, axis=-1, keepdims=True) + epsilon) * gain_vec
    )


def convolve(signal, kernel, offset):
    kernel_width = kernel.shape[0]
    length = signal.shape[1]
    padded = jnp.pad(signal, ((0, 0), (kernel_width - 1, 0), (0, 0)))
    summed = jnp.zeros_like(signal) + offset
    for tap_index in range(kernel_width):
        summed = summed + kernel[tap_index] * padded[:, tap_index : tap_index + length]
    return summed


def conv_active(signal, kernel, offset):
    return jax.nn.silu(convolve(signal, kernel, offset))


def selective(step_size, drive_in, bmatrix, cmatrix, decay_rate):
    seq_count, length, channels = step_size.shape
    block_count = length // BLOCK

    def blocked(values):
        shaped = values.reshape((seq_count, block_count, BLOCK) + values.shape[2:])
        return jnp.swapaxes(shaped, 0, 1)

    def advance(carry_state, pieces):
        piece_step, piece_drive, piece_bmat, piece_cmat = pieces
        factor = jnp.exp(piece_step[:, :, None, :] * decay_rate)
        source = (piece_step * piece_drive)[:, :, None, :] * piece_bmat[:, :, :, None]
        state = carry_state
        outputs = []
        for position in range(BLOCK):
            state = factor[:, position] * state + source[:, position]
            outputs.append(jnp.sum(state * piece_cmat[:, position, :, None], axis=1))
        return (state, jnp.stack(outputs, axis=1))

    initial = jnp.zeros((seq_count, decay_rate.shape[0], channels), jnp.float32)
    last_state, outputs = lax.scan(
        jax.checkpoint(advance),
        initial,
        (blocked(step_size), blocked(drive_in), blocked(bmatrix), blocked(cmatrix)),
    )
    return jnp.swapaxes(outputs, 0, 1).reshape(seq_count, length, channels)


def mixer_core(
    pre_act, bmatrix, cmatrix, drive_in, gate_in, step_bias, decay_log, skip_gain, prefix_mask
):
    step_size = jax.nn.softplus(pre_act + step_bias)
    decay_rate = -jnp.exp(decay_log)
    ahead_part = selective(step_size, drive_in, bmatrix, cmatrix, decay_rate)
    masked = prefix_mask[:, :, None]
    behind = jnp.flip(
        selective(
            jnp.flip(step_size, 1),
            jnp.flip(drive_in * masked, 1),
            jnp.flip(bmatrix, 1),
            jnp.flip(cmatrix, 1),
            decay_rate,
        ),
        1,
    )
    combined = ahead_part + behind * masked + skip_gain * drive_in
    return combined * jax.nn.silu(gate_in)


def on_device(
    tokens,
    prefix,
    norm_gain,
    in_weight,
    conv_weight,
    conv_bias,
    xproj_weight,
    step_weight,
    step_bias,
    decay_log,
    skip_gain,
    out_weight,
    out_cotangent,
):
    seq_count, length, width_model = tokens.shape
    channels = in_weight.shape[2]
    rows_all = seq_count * length
    rank_step = step_weight.shape[0]
    state_count = decay_log.shape[0]
    in_flat = in_weight.reshape(width_model, 2 * channels)
    flat_tokens = tokens.astype(jnp.float32).reshape(rows_all, width_model)
    positions = lax.broadcasted_iota(jnp.int32, (seq_count, length), 1)
    prefix_mask = (positions < prefix[:, None]).astype(jnp.float32)
    normed, norm_back = jax.vjp(normalize, flat_tokens, norm_gain)
    normed_low = normed.astype(jnp.bfloat16)
    expanded = jnp.dot(normed_low, in_flat, preferred_element_type=jnp.float32)
    conv_input = expanded[:, :channels].reshape(seq_count, length, channels)
    gate_input = expanded[:, channels:].reshape(seq_count, length, channels)
    activated, conv_back = jax.vjp(conv_active, conv_input, conv_weight, conv_bias)
    drive_low = activated.astype(jnp.bfloat16).reshape(rows_all, channels)
    partial_proj = jnp.dot(drive_low, xproj_weight, preferred_element_type=jnp.float32)
    projected = lax.psum(partial_proj, "tensor").astype(jnp.bfloat16)
    raw_step = projected[:, :rank_step]
    pre_act = jnp.dot(raw_step, step_weight, preferred_element_type=jnp.float32)
    bmatrix = (
        projected[:, rank_step : rank_step + state_count]
        .astype(jnp.float32)
        .reshape(seq_count, length, state_count)
    )
    cmatrix = (
        projected[:, rank_step + state_count :]
        .astype(jnp.float32)
        .reshape(seq_count, length, state_count)
    )
    drive_in = drive_low.astype(jnp.float32).reshape(seq_count, length, channels)

    def core_fn(pre_in, bmat_in, cmat_in, drive_arg, gate_arg, bias_arg, decay_arg, skip_arg):
        return mixer_core(
            pre_in,
            bmat_in,
            cmat_in,
            drive_arg,
            gate_arg,
            bias_arg,
            decay_arg,
            skip_arg,
            prefix_mask,
        )

    gated, core_back = jax.vjp(
        core_fn,
        pre_act.reshape(seq_count, length, channels),
        bmatrix,
        cmatrix,
        drive_in,
        gate_input,
        step_bias,
        decay_log,
        skip_gain,
    )
    gated_low = gated.astype(jnp.bfloat16).reshape(rows_all, channels)
    out_partial = jnp.dot(gated_low, out_weight, preferred_element_type=jnp.float32)
    block_flat = (flat_tokens + lax.psum(out_partial, "tensor")).astype(jnp.bfloat16)
    block_out = block_flat.reshape(seq_count, length, width_model)
    cotangent = out_cotangent.reshape(rows_all, width_model)
    grad_out_weight = jnp.dot(gated_low.T, cotangent, preferred_element_type=jnp.float32)
    grad_gated = jnp.dot(cotangent, out_weight.T, preferred_element_type=jnp.float32)
    core_grads = core_back(grad_gated.reshape(seq_count, length, channels))
    (
        grad_pre,
        grad_bmat,
        grad_cmat,
        grad_drive,
        grad_gate,
        grad_step_bias,
        grad_decay_log,
        grad_skip_gain,
    ) = core_grads
    pre_low = grad_pre.reshape(rows_all, channels).astype(jnp.bfloat16)
    grad_step_weight = jnp.dot(raw_step.T, pre_low, preferred_element_type=jnp.float32)
    grad_raw = jnp.dot(pre_low, step_weight.T, preferred_element_type=jnp.float32)
    proj_partial = jnp.concatenate(
        [
            grad_raw,
            grad_bmat.reshape(rows_all, state_count),
            grad_cmat.reshape(rows_all, state_count),
        ],
        axis=1,
    )
    grad_proj = lax.psum(proj_partial, "tensor").astype(jnp.bfloat16)
    grad_xproj_weight = jnp.dot(drive_low.T, grad_proj, preferred_element_type=jnp.float32)
    drive_extra = jnp.dot(grad_proj, xproj_weight.T, preferred_element_type=jnp.float32)
    grad_drive_total = grad_drive + drive_extra.reshape(seq_count, length, channels)
    grad_conv_in, grad_conv_weight, grad_conv_bias = conv_back(grad_drive_total)
    grad_expanded = jnp.concatenate([grad_conv_in, grad_gate], axis=2).reshape(
        rows_all, 2 * channels
    )
    expanded_low = grad_expanded.astype(jnp.bfloat16)
    grad_in_weight = jnp.dot(normed_low.T, expanded_low, preferred_element_type=jnp.float32)
    grad_in_weight = grad_in_weight.reshape(width_model, 2, channels)
    normed_partial = jnp.dot(expanded_low, in_flat.T, preferred_element_type=jnp.float32)
    grad_normed = lax.psum(normed_partial, "tensor")
    grad_input, grad_norm_gain = norm_back(grad_normed)
    grad_tokens = (cotangent.astype(jnp.float32) + grad_input).reshape(
        seq_count, length, width_model
    )
    summed = lax.psum(
        (
            grad_norm_gain,
            grad_in_weight,
            grad_conv_weight,
            grad_conv_bias,
            grad_xproj_weight,
            grad_step_weight,
            grad_step_bias,
            grad_decay_log,
            grad_skip_gain,
            grad_out_weight,
        ),
        "dp",
    )
    return (
        block_out,
        grad_tokens,
        summed[0],
        summed[1],
        summed[2],
        summed[3],
        summed[4],
        summed[5],
        summed[6],
        summed[7],
        summed[8],
        summed[9],
    )


def solution(mesh):
    placed = (
        P("dp", None, None),
        P("dp"),
        P(),
        P(None, None, "tensor"),
        P(None, "tensor"),
        P("tensor"),
        P("tensor", None),
        P(None, "tensor"),
        P("tensor"),
        P(None, "tensor"),
        P("tensor"),
        P("tensor", None),
        P("dp", None, None),
    )
    return jax.shard_map(
        on_device,
        mesh=mesh,
        in_specs=placed,
        out_specs=(
            P("dp", None, None),
            P("dp", None, None),
            P(),
            P(None, None, "tensor"),
            P(None, "tensor"),
            P("tensor"),
            P("tensor", None),
            P(None, "tensor"),
            P("tensor"),
            P(None, "tensor"),
            P("tensor"),
            P("tensor", None),
        ),
        check_vma=False,
    )
```

profile of v0, /device:TPU:1, one launch (start us, length us, event | category | flops | bytes accessed | tf_op | source)
XLA Modules:
  0.0 2985.3 jit_solution(13415730608170570085)
XLA Ops:
  22.4 15.3 all-reduce.404
  48.2 16.7 reverse.12
  67.3 462.5 %while.80 = (s32[]{:T(128)}, f32[1,16,512]{2,1,0:T(8,128)S(1)}, f32[16,1,64,512]{3,2,1,0:T(8,128)}, f32[16,1,16,512]{3,2,1,0:T(8,128)}, f32[16,1,64,512]{3,2,1,0...) while((s32[]{:T(128)}, f32[1,16,512]{2,1,0:T(8,128)S(1)}, ...), condition=%wide.region_67.68_spmd.clone, body=%wide.region_2.67_spmd.clone.sunk | while | flops 3670019 | bytes 14520792 | solution.py:52
  89.7 5.9 stack.522
  118.6 5.9 stack.522
  147.5 5.9 stack.522
  176.4 5.9 stack.522
  205.3 5.9 stack.522
  234.2 5.9 stack.522
  263.1 5.9 stack.522
  292.0 5.9 stack.522
  321.0 5.9 stack.522
  349.9 5.9 stack.522
  378.8 5.9 stack.522
  407.7 5.9 stack.522
  436.6 5.9 stack.522
  465.5 5.9 stack.522
  539.9 763.1 %while.83 = (s32[]{:T(128)}, f32[16,512]{1,0:T(8,128)S(1)}, f32[1,16,512]{2,1,0:T(8,128)S(1)}, f32[16,1,64,512]{3,2,1,0:T(8,128)}, f32[16,1,64,512]{3,2,1,0:T(8,...) while((s32[]{:T(128)}, f32[16,512]{1,0:T(8,128)S(1)}, ...), condition=%wide.region_274.275_spmd.clone, body=%wide.region_205.274_spmd.clone.sunk | while | flops 76723200 | bytes 28856656 | solution.py:52
  554.7 32.0 %multiply_reduce_fusion.574 = (f32[64,512]{1,0:T(8,128)S(1)}, f32[16,512]{1,0:T(8,128)S(1)}) fusion(f32[16,512]{1,0:T(8,128)S(1)} %get-tuple-element.4352, f32[64,512]{1,0:T(8,128)S(1)} %bitcast.6488, f32[1,1,16,512]{3,2,1,0:T(8,128)S(1)} %multiply_bitcast_fusion.139, f32[1,1,16,512]{3,2,1,0:T(8,128)S(1)} %get-tuple-element.4553, ...), kind=kLoop, calls=%fused_computation.1260.clone.1 | loop fusion | flops 36134912 | bytes 2424832 | tf_op jit(solution)/shard_map/transpose(jvp())/while/body/eval_jaxpr/checkpoint/reduce_sum | solution.py:42
  602.4 32.0 %multiply_reduce_fusion.574 = (f32[64,512]{1,0:T(8,128)S(1)}, f32[16,512]{1,0:T(8,128)S(1)}) fusion(f32[16,512]{1,0:T(8,128)S(1)} %get-tuple-element.4352, f32[64,512]{1,0:T(8,128)S(1)} %bitcast.6488, f32[1,1,16,512]{3,2,1,0:T(8,128)S(1)} %multiply_bitcast_fusion.139, f32[1,1,16,512]{3,2,1,0:T(8,128)S(1)} %get-tuple-element.4553, ...), kind=kLoop, calls=%fused_computation.1260.clone.1 | loop fusion | flops 36134912 | bytes 2424832 | tf_op jit(solution)/shard_map/transpose(jvp())/while/body/eval_jaxpr/checkpoint/reduce_sum | solution.py:42
  650.1 32.0 %multiply_reduce_fusion.574 = (f32[64,512]{1,0:T(8,128)S(1)}, f32[16,512]{1,0:T(8,128)S(1)}) fusion(f32[16,512]{1,0:T(8,128)S(1)} %get-tuple-element.4352, f32[64,512]{1,0:T(8,128)S(1)} %bitcast.6488, f32[1,1,16,512]{3,2,1,0:T(8,128)S(1)} %multiply_bitcast_fusion.139, f32[1,1,16,512]{3,2,1,0:T(8,128)S(1)} %get-tuple-element.4553, ...), kind=kLoop, calls=%fused_computation.1260.clone.1 | loop fusion | flops 36134912 | bytes 2424832 | tf_op jit(solution)/shard_map/transpose(jvp())/while/body/eval_jaxpr/checkpoint/reduce_sum | solution.py:42
  697.7 32.0 %multiply_reduce_fusion.574 = (f32[64,512]{1,0:T(8,128)S(1)}, f32[16,512]{1,0:T(8,128)S(1)}) fusion(f32[16,512]{1,0:T(8,128)S(1)} %get-tuple-element.4352, f32[64,512]{1,0:T(8,128)S(1)} %bitcast.6488, f32[1,1,16,512]{3,2,1,0:T(8,128)S(1)} %multiply_bitcast_fusion.139, f32[1,1,16,512]{3,2,1,0:T(8,128)S(1)} %get-tuple-element.4553, ...), kind=kLoop, calls=%fused_computation.1260.clone.1 | loop fusion | flops 36134912 | bytes 2424832 | tf_op jit(solution)/shard_map/transpose(jvp())/while/body/eval_jaxpr/checkpoint/reduce_sum | solution.py:42
  745.4 32.0 %multiply_reduce_fusion.574 = (f32[64,512]{1,0:T(8,128)S(1)}, f32[16,512]{1,0:T(8,128)S(1)}) fusion(f32[16,512]{1,0:T(8,128)S(1)} %get-tuple-element.4352, f32[64,512]{1,0:T(8,128)S(1)} %bitcast.6488, f32[1,1,16,512]{3,2,1,0:T(8,128)S(1)} %multiply_bitcast_fusion.139, f32[1,1,16,512]{3,2,1,0:T(8,128)S(1)} %get-tuple-element.4553, ...), kind=kLoop, calls=%fused_computation.1260.clone.1 | loop fusion | flops 36134912 | bytes 2424832 | tf_op jit(solution)/shard_map/transpose(jvp())/while/body/eval_jaxpr/checkpoint/reduce_sum | solution.py:42
  793.1 32.0 %multiply_reduce_fusion.574 = (f32[64,512]{1,0:T(8,128)S(1)}, f32[16,512]{1,0:T(8,128)S(1)}) fusion(f32[16,512]{1,0:T(8,128)S(1)} %get-tuple-element.4352, f32[64,512]{1,0:T(8,128)S(1)} %bitcast.6488, f32[1,1,16,512]{3,2,1,0:T(8,128)S(1)} %multiply_bitcast_fusion.139, f32[1,1,16,512]{3,2,1,0:T(8,128)S(1)} %get-tuple-element.4553, ...), kind=kLoop, calls=%fused_computation.1260.clone.1 | loop fusion | flops 36134912 | bytes 2424832 | tf_op jit(solution)/shard_map/transpose(jvp())/while/body/eval_jaxpr/checkpoint/reduce_sum | solution.py:42
  840.7 32.0 %multiply_reduce_fusion.574 = (f32[64,512]{1,0:T(8,128)S(1)}, f32[16,512]{1,0:T(8,128)S(1)}) fusion(f32[16,512]{1,0:T(8,128)S(1)} %get-tuple-element.4352, f32[64,512]{1,0:T(8,128)S(1)} %bitcast.6488, f32[1,1,16,512]{3,2,1,0:T(8,128)S(1)} %multiply_bitcast_fusion.139, f32[1,1,16,512]{3,2,1,0:T(8,128)S(1)} %get-tuple-element.4553, ...), kind=kLoop, calls=%fused_computation.1260.clone.1 | loop fusion | flops 36134912 | bytes 2424832 | tf_op jit(solution)/shard_map/transpose(jvp())/while/body/eval_jaxpr/checkpoint/reduce_sum | solution.py:42
  888.4 32.0 %multiply_reduce_fusion.574 = (f32[64,512]{1,0:T(8,128)S(1)}, f32[16,512]{1,0:T(8,128)S(1)}) fusion(f32[16,512]{1,0:T(8,128)S(1)} %get-tuple-element.4352, f32[64,512]{1,0:T(8,128)S(1)} %bitcast.6488, f32[1,1,16,512]{3,2,1,0:T(8,128)S(1)} %multiply_bitcast_fusion.139, f32[1,1,16,512]{3,2,1,0:T(8,128)S(1)} %get-tuple-element.4553, ...), kind=kLoop, calls=%fused_computation.1260.clone.1 | loop fusion | flops 36134912 | bytes 2424832 | tf_op jit(solution)/shard_map/transpose(jvp())/while/body/eval_jaxpr/checkpoint/reduce_sum | solution.py:42
  936.1 32.0 %multiply_reduce_fusion.574 = (f32[64,512]{1,0:T(8,128)S(1)}, f32[16,512]{1,0:T(8,128)S(1)}) fusion(f32[16,512]{1,0:T(8,128)S(1)} %get-tuple-element.4352, f32[64,512]{1,0:T(8,128)S(1)} %bitcast.6488, f32[1,1,16,512]{3,2,1,0:T(8,128)S(1)} %multiply_bitcast_fusion.139, f32[1,1,16,512]{3,2,1,0:T(8,128)S(1)} %get-tuple-element.4553, ...), kind=kLoop, calls=%fused_computation.1260.clone.1 | loop fusion | flops 36134912 | bytes 2424832 | tf_op jit(solution)/shard_map/transpose(jvp())/while/body/eval_jaxpr/checkpoint/reduce_sum | solution.py:42
  983.7 32.0 %multiply_reduce_fusion.574 = (f32[64,512]{1,0:T(8,128)S(1)}, f32[16,512]{1,0:T(8,128)S(1)}) fusion(f32[16,512]{1,0:T(8,128)S(1)} %get-tuple-element.4352, f32[64,512]{1,0:T(8,128)S(1)} %bitcast.6488, f32[1,1,16,512]{3,2,1,0:T(8,128)S(1)} %multiply_bitcast_fusion.139, f32[1,1,16,512]{3,2,1,0:T(8,128)S(1)} %get-tuple-element.4553, ...), kind=kLoop, calls=%fused_computation.1260.clone.1 | loop fusion | flops 36134912 | bytes 2424832 | tf_op jit(solution)/shard_map/transpose(jvp())/while/body/eval_jaxpr/checkpoint/reduce_sum | solution.py:42
  1031.4 32.0 %multiply_reduce_fusion.574 = (f32[64,512]{1,0:T(8,128)S(1)}, f32[16,512]{1,0:T(8,128)S(1)}) fusion(f32[16,512]{1,0:T(8,128)S(1)} %get-tuple-element.4352, f32[64,512]{1,0:T(8,128)S(1)} %bitcast.6488, f32[1,1,16,512]{3,2,1,0:T(8,128)S(1)} %multiply_bitcast_fusion.139, f32[1,1,16,512]{3,2,1,0:T(8,128)S(1)} %get-tuple-element.4553, ...), kind=kLoop, calls=%fused_computation.1260.clone.1 | loop fusion | flops 36134912 | bytes 2424832 | tf_op jit(solution)/shard_map/transpose(jvp())/while/body/eval_jaxpr/checkpoint/reduce_sum | solution.py:42
  1079.1 32.0 %multiply_reduce_fusion.574 = (f32[64,512]{1,0:T(8,128)S(1)}, f32[16,512]{1,0:T(8,128)S(1)}) fusion(f32[16,512]{1,0:T(8,128)S(1)} %get-tuple-element.4352, f32[64,512]{1,0:T(8,128)S(1)} %bitcast.6488, f32[1,1,16,512]{3,2,1,0:T(8,128)S(1)} %multiply_bitcast_fusion.139, f32[1,1,16,512]{3,2,1,0:T(8,128)S(1)} %get-tuple-element.4553, ...), kind=kLoop, calls=%fused_computation.1260.clone.1 | loop fusion | flops 36134912 | bytes 2424832 | tf_op jit(solution)/shard_map/transpose(jvp())/while/body/eval_jaxpr/checkpoint/reduce_sum | solution.py:42
  1126.7 32.0 %multiply_reduce_fusion.574 = (f32[64,512]{1,0:T(8,128)S(1)}, f32[16,512]{1,0:T(8,128)S(1)}) fusion(f32[16,512]{1,0:T(8,128)S(1)} %get-tuple-element.4352, f32[64,512]{1,0:T(8,128)S(1)} %bitcast.6488, f32[1,1,16,512]{3,2,1,0:T(8,128)S(1)} %multiply_bitcast_fusion.139, f32[1,1,16,512]{3,2,1,0:T(8,128)S(1)} %get-tuple-element.4553, ...), kind=kLoop, calls=%fused_computation.1260.clone.1 | loop fusion | flops 36134912 | bytes 2424832 | tf_op jit(solution)/shard_map/transpose(jvp())/while/body/eval_jaxpr/checkpoint/reduce_sum | solution.py:42
  1174.4 32.0 %multiply_reduce_fusion.574 = (f32[64,512]{1,0:T(8,128)S(1)}, f32[16,512]{1,0:T(8,128)S(1)}) fusion(f32[16,512]{1,0:T(8,128)S(1)} %get-tuple-element.4352, f32[64,512]{1,0:T(8,128)S(1)} %bitcast.6488, f32[1,1,16,512]{3,2,1,0:T(8,128)S(1)} %multiply_bitcast_fusion.139, f32[1,1,16,512]{3,2,1,0:T(8,128)S(1)} %get-tuple-element.4553, ...), kind=kLoop, calls=%fused_computation.1260.clone.1 | loop fusion | flops 36134912 | bytes 2424832 | tf_op jit(solution)/shard_map/transpose(jvp())/while/body/eval_jaxpr/checkpoint/reduce_sum | solution.py:42
  1222.1 32.0 %multiply_reduce_fusion.574 = (f32[64,512]{1,0:T(8,128)S(1)}, f32[16,512]{1,0:T(8,128)S(1)}) fusion(f32[16,512]{1,0:T(8,128)S(1)} %get-tuple-element.4352, f32[64,512]{1,0:T(8,128)S(1)} %bitcast.6488, f32[1,1,16,512]{3,2,1,0:T(8,128)S(1)} %multiply_bitcast_fusion.139, f32[1,1,16,512]{3,2,1,0:T(8,128)S(1)} %get-tuple-element.4553, ...), kind=kLoop, calls=%fused_computation.1260.clone.1 | loop fusion | flops 36134912 | bytes 2424832 | tf_op jit(solution)/shard_map/transpose(jvp())/while/body/eval_jaxpr/checkpoint/reduce_sum | solution.py:42
  1269.8 32.0 %multiply_reduce_fusion.574 = (f32[64,512]{1,0:T(8,128)S(1)}, f32[16,512]{1,0:T(8,128)S(1)}) fusion(f32[16,512]{1,0:T(8,128)S(1)} %get-tuple-element.4352, f32[64,512]{1,0:T(8,128)S(1)} %bitcast.6488, f32[1,1,16,512]{3,2,1,0:T(8,128)S(1)} %multiply_bitcast_fusion.139, f32[1,1,16,512]{3,2,1,0:T(8,128)S(1)} %get-tuple-element.4553, ...), kind=kLoop, calls=%fused_computation.1260.clone.1 | loop fusion | flops 36134912 | bytes 2424832 | tf_op jit(solution)/shard_map/transpose(jvp())/while/body/eval_jaxpr/checkpoint/reduce_sum | solution.py:42
  1305.9 16.7 rev.26
  1325.0 397.4 %while.81 = (s32[]{:T(128)}, f32[1,16,512]{2,1,0:T(8,128)S(1)}, f32[16,1,64,512]{3,2,1,0:T(8,128)}, f32[16,1,16,512]{3,2,1,0:T(8,128)}, f32[16,1,64,512]{3,2,1,0...) while((s32[]{:T(128)}, f32[1,16,512]{2,1,0:T(8,128)S(1)}, ...), condition=%wide.region_133.134_spmd.clone, body=%wide.region_68.133_spmd.clone.sunk | while | flops 3670019 | bytes 14517384 | solution.py:52
  1722.4 16.8 reverse.15
  1742.6 742.3 %while.82 = (s32[]{:T(128)}, f32[16,512]{1,0:T(8,128)S(1)}, f32[1,16,512]{2,1,0:T(8,128)S(1)}, f32[16,1,64,512]{3,2,1,0:T(8,128)}, f32[16,1,64,512]{3,2,1,0:T(8,...) while((s32[]{:T(128)}, f32[16,512]{1,0:T(8,128)S(1)}, ...), condition=%wide.region_204.205_spmd.clone, body=%wide.region_135.204_spmd.clone.sunk | while | flops 76723200 | bytes 28914000 | solution.py:52
  1756.2 32.0 %multiply_reduce_fusion.510 = (f32[64,512]{1,0:T(8,128)S(1)}, f32[16,512]{1,0:T(8,128)S(1)}) fusion(f32[16,512]{1,0:T(8,128)S(1)} %get-tuple-element.3938, f32[64,512]{1,0:T(8,128)S(1)} %bitcast.6490, f32[1,1,16,512]{3,2,1,0:T(8,128)S(1)} %multiply_bitcast_fusion.136, f32[1,1,16,512]{3,2,1,0:T(8,128)S(1)} %get-tuple-element.4139, ...), kind=kLoop, calls=%fused_computation.785.clone.1 | loop fusion | flops 36134912 | bytes 2424832 | tf_op jit(solution)/shard_map/transpose(jvp())/while/body/eval_jaxpr/checkpoint/reduce_sum | solution.py:42
  1802.6 32.0 %multiply_reduce_fusion.510 = (f32[64,512]{1,0:T(8,128)S(1)}, f32[16,512]{1,0:T(8,128)S(1)}) fusion(f32[16,512]{1,0:T(8,128)S(1)} %get-tuple-element.3938, f32[64,512]{1,0:T(8,128)S(1)} %bitcast.6490, f32[1,1,16,512]{3,2,1,0:T(8,128)S(1)} %multiply_bitcast_fusion.136, f32[1,1,16,512]{3,2,1,0:T(8,128)S(1)} %get-tuple-element.4139, ...), kind=kLoop, calls=%fused_computation.785.clone.1 | loop fusion | flops 36134912 | bytes 2424832 | tf_op jit(solution)/shard_map/transpose(jvp())/while/body/eval_jaxpr/checkpoint/reduce_sum | solution.py:42
  1849.0 32.0 %multiply_reduce_fusion.510 = (f32[64,512]{1,0:T(8,128)S(1)}, f32[16,512]{1,0:T(8,128)S(1)}) fusion(f32[16,512]{1,0:T(8,128)S(1)} %get-tuple-element.3938, f32[64,512]{1,0:T(8,128)S(1)} %bitcast.6490, f32[1,1,16,512]{3,2,1,0:T(8,128)S(1)} %multiply_bitcast_fusion.136, f32[1,1,16,512]{3,2,1,0:T(8,128)S(1)} %get-tuple-element.4139, ...), kind=kLoop, calls=%fused_computation.785.clone.1 | loop fusion | flops 36134912 | bytes 2424832 | tf_op jit(solution)/shard_map/transpose(jvp())/while/body/eval_jaxpr/checkpoint/reduce_sum | solution.py:42
  1895.4 32.0 %multiply_reduce_fusion.510 = (f32[64,512]{1,0:T(8,128)S(1)}, f32[16,512]{1,0:T(8,128)S(1)}) fusion(f32[16,512]{1,0:T(8,128)S(1)} %get-tuple-element.3938, f32[64,512]{1,0:T(8,128)S(1)} %bitcast.6490, f32[1,1,16,512]{3,2,1,0:T(8,128)S(1)} %multiply_bitcast_fusion.136, f32[1,1,16,512]{3,2,1,0:T(8,128)S(1)} %get-tuple-element.4139, ...), kind=kLoop, calls=%fused_computation.785.clone.1 | loop fusion | flops 36134912 | bytes 2424832 | tf_op jit(solution)/shard_map/transpose(jvp())/while/body/eval_jaxpr/checkpoint/reduce_sum | solution.py:42
  1941.8 32.0 %multiply_reduce_fusion.510 = (f32[64,512]{1,0:T(8,128)S(1)}, f32[16,512]{1,0:T(8,128)S(1)}) fusion(f32[16,512]{1,0:T(8,128)S(1)} %get-tuple-element.3938, f32[64,512]{1,0:T(8,128)S(1)} %bitcast.6490, f32[1,1,16,512]{3,2,1,0:T(8,128)S(1)} %multiply_bitcast_fusion.136, f32[1,1,16,512]{3,2,1,0:T(8,128)S(1)} %get-tuple-element.4139, ...), kind=kLoop, calls=%fused_computation.785.clone.1 | loop fusion | flops 36134912 | bytes 2424832 | tf_op jit(solution)/shard_map/transpose(jvp())/while/body/eval_jaxpr/checkpoint/reduce_sum | solution.py:42
  1988.2 32.0 %multiply_reduce_fusion.510 = (f32[64,512]{1,0:T(8,128)S(1)}, f32[16,512]{1,0:T(8,128)S(1)}) fusion(f32[16,512]{1,0:T(8,128)S(1)} %get-tuple-element.3938, f32[64,512]{1,0:T(8,128)S(1)} %bitcast.6490, f32[1,1,16,512]{3,2,1,0:T(8,128)S(1)} %multiply_bitcast_fusion.136, f32[1,1,16,512]{3,2,1,0:T(8,128)S(1)} %get-tuple-element.4139, ...), kind=kLoop, calls=%fused_computation.785.clone.1 | loop fusion | flops 36134912 | bytes 2424832 | tf_op jit(solution)/shard_map/transpose(jvp())/while/body/eval_jaxpr/checkpoint/reduce_sum | solution.py:42
  2034.5 32.0 %multiply_reduce_fusion.510 = (f32[64,512]{1,0:T(8,128)S(1)}, f32[16,512]{1,0:T(8,128)S(1)}) fusion(f32[16,512]{1,0:T(8,128)S(1)} %get-tuple-element.3938, f32[64,512]{1,0:T(8,128)S(1)} %bitcast.6490, f32[1,1,16,512]{3,2,1,0:T(8,128)S(1)} %multiply_bitcast_fusion.136, f32[1,1,16,512]{3,2,1,0:T(8,128)S(1)} %get-tuple-element.4139, ...), kind=kLoop, calls=%fused_computation.785.clone.1 | loop fusion | flops 36134912 | bytes 2424832 | tf_op jit(solution)/shard_map/transpose(jvp())/while/body/eval_jaxpr/checkpoint/reduce_sum | solution.py:42
  2080.9 32.0 %multiply_reduce_fusion.510 = (f32[64,512]{1,0:T(8,128)S(1)}, f32[16,512]{1,0:T(8,128)S(1)}) fusion(f32[16,512]{1,0:T(8,128)S(1)} %get-tuple-element.3938, f32[64,512]{1,0:T(8,128)S(1)} %bitcast.6490, f32[1,1,16,512]{3,2,1,0:T(8,128)S(1)} %multiply_bitcast_fusion.136, f32[1,1,16,512]{3,2,1,0:T(8,128)S(1)} %get-tuple-element.4139, ...), kind=kLoop, calls=%fused_computation.785.clone.1 | loop fusion | flops 36134912 | bytes 2424832 | tf_op jit(solution)/shard_map/transpose(jvp())/while/body/eval_jaxpr/checkpoint/reduce_sum | solution.py:42
  2127.3 32.0 %multiply_reduce_fusion.510 = (f32[64,512]{1,0:T(8,128)S(1)}, f32[16,512]{1,0:T(8,128)S(1)}) fusion(f32[16,512]{1,0:T(8,128)S(1)} %get-tuple-element.3938, f32[64,512]{1,0:T(8,128)S(1)} %bitcast.6490, f32[1,1,16,512]{3,2,1,0:T(8,128)S(1)} %multiply_bitcast_fusion.136, f32[1,1,16,512]{3,2,1,0:T(8,128)S(1)} %get-tuple-element.4139, ...), kind=kLoop, calls=%fused_computation.785.clone.1 | loop fusion | flops 36134912 | bytes 2424832 | tf_op jit(solution)/shard_map/transpose(jvp())/while/body/eval_jaxpr/checkpoint/reduce_sum | solution.py:42
  2173.7 32.0 %multiply_reduce_fusion.510 = (f32[64,512]{1,0:T(8,128)S(1)}, f32[16,512]{1,0:T(8,128)S(1)}) fusion(f32[16,512]{1,0:T(8,128)S(1)} %get-tuple-element.3938, f32[64,512]{1,0:T(8,128)S(1)} %bitcast.6490, f32[1,1,16,512]{3,2,1,0:T(8,128)S(1)} %multiply_bitcast_fusion.136, f32[1,1,16,512]{3,2,1,0:T(8,128)S(1)} %get-tuple-element.4139, ...), kind=kLoop, calls=%fused_computation.785.clone.1 | loop fusion | flops 36134912 | bytes 2424832 | tf_op jit(solution)/shard_map/transpose(jvp())/while/body/eval_jaxpr/checkpoint/reduce_sum | solution.py:42
  2220.1 32.0 %multiply_reduce_fusion.510 = (f32[64,512]{1,0:T(8,128)S(1)}, f32[16,512]{1,0:T(8,128)S(1)}) fusion(f32[16,512]{1,0:T(8,128)S(1)} %get-tuple-element.3938, f32[64,512]{1,0:T(8,128)S(1)} %bitcast.6490, f32[1,1,16,512]{3,2,1,0:T(8,128)S(1)} %multiply_bitcast_fusion.136, f32[1,1,16,512]{3,2,1,0:T(8,128)S(1)} %get-tuple-element.4139, ...), kind=kLoop, calls=%fused_computation.785.clone.1 | loop fusion | flops 36134912 | bytes 2424832 | tf_op jit(solution)/shard_map/transpose(jvp())/while/body/eval_jaxpr/checkpoint/reduce_sum | solution.py:42
  2266.5 32.0 %multiply_reduce_fusion.510 = (f32[64,512]{1,0:T(8,128)S(1)}, f32[16,512]{1,0:T(8,128)S(1)}) fusion(f32[16,512]{1,0:T(8,128)S(1)} %get-tuple-element.3938, f32[64,512]{1,0:T(8,128)S(1)} %bitcast.6490, f32[1,1,16,512]{3,2,1,0:T(8,128)S(1)} %multiply_bitcast_fusion.136, f32[1,1,16,512]{3,2,1,0:T(8,128)S(1)} %get-tuple-element.4139, ...), kind=kLoop, calls=%fused_computation.785.clone.1 | loop fusion | flops 36134912 | bytes 2424832 | tf_op jit(solution)/shard_map/transpose(jvp())/while/body/eval_jaxpr/checkpoint/reduce_sum | solution.py:42
  2312.9 32.0 %multiply_reduce_fusion.510 = (f32[64,512]{1,0:T(8,128)S(1)}, f32[16,512]{1,0:T(8,128)S(1)}) fusion(f32[16,512]{1,0:T(8,128)S(1)} %get-tuple-element.3938, f32[64,512]{1,0:T(8,128)S(1)} %bitcast.6490, f32[1,1,16,512]{3,2,1,0:T(8,128)S(1)} %multiply_bitcast_fusion.136, f32[1,1,16,512]{3,2,1,0:T(8,128)S(1)} %get-tuple-element.4139, ...), kind=kLoop, calls=%fused_computation.785.clone.1 | loop fusion | flops 36134912 | bytes 2424832 | tf_op jit(solution)/shard_map/transpose(jvp())/while/body/eval_jaxpr/checkpoint/reduce_sum | solution.py:42
  2359.3 32.0 %multiply_reduce_fusion.510 = (f32[64,512]{1,0:T(8,128)S(1)}, f32[16,512]{1,0:T(8,128)S(1)}) fusion(f32[16,512]{1,0:T(8,128)S(1)} %get-tuple-element.3938, f32[64,512]{1,0:T(8,128)S(1)} %bitcast.6490, f32[1,1,16,512]{3,2,1,0:T(8,128)S(1)} %multiply_bitcast_fusion.136, f32[1,1,16,512]{3,2,1,0:T(8,128)S(1)} %get-tuple-element.4139, ...), kind=kLoop, calls=%fused_computation.785.clone.1 | loop fusion | flops 36134912 | bytes 2424832 | tf_op jit(solution)/shard_map/transpose(jvp())/while/body/eval_jaxpr/checkpoint/reduce_sum | solution.py:42
  2405.7 32.0 %multiply_reduce_fusion.510 = (f32[64,512]{1,0:T(8,128)S(1)}, f32[16,512]{1,0:T(8,128)S(1)}) fusion(f32[16,512]{1,0:T(8,128)S(1)} %get-tuple-element.3938, f32[64,512]{1,0:T(8,128)S(1)} %bitcast.6490, f32[1,1,16,512]{3,2,1,0:T(8,128)S(1)} %multiply_bitcast_fusion.136, f32[1,1,16,512]{3,2,1,0:T(8,128)S(1)} %get-tuple-element.4139, ...), kind=kLoop, calls=%fused_computation.785.clone.1 | loop fusion | flops 36134912 | bytes 2424832 | tf_op jit(solution)/shard_map/transpose(jvp())/while/body/eval_jaxpr/checkpoint/reduce_sum | solution.py:42
  2452.1 32.0 %multiply_reduce_fusion.510 = (f32[64,512]{1,0:T(8,128)S(1)}, f32[16,512]{1,0:T(8,128)S(1)}) fusion(f32[16,512]{1,0:T(8,128)S(1)} %get-tuple-element.3938, f32[64,512]{1,0:T(8,128)S(1)} %bitcast.6490, f32[1,1,16,512]{3,2,1,0:T(8,128)S(1)} %multiply_bitcast_fusion.136, f32[1,1,16,512]{3,2,1,0:T(8,128)S(1)} %get-tuple-element.4139, ...), kind=kLoop, calls=%fused_computation.785.clone.1 | loop fusion | flops 36134912 | bytes 2424832 | tf_op jit(solution)/shard_map/transpose(jvp())/while/body/eval_jaxpr/checkpoint/reduce_sum | solution.py:42
  2484.9 16.7 rev.29
  2512.7 15.2 all-reduce.405
  2527.9 16.7 rev.28
  2544.6 16.8 rev.27
  2561.5 10.6 multiply_reduce_fusion.265
  2602.6 134.3 %all-reduce.403.cloned.1.call-done = (f32[1024,1024]{1,0:T(8,128)}, f32[1024,1024]{1,0:T(8,128)}) async-done(((f32[1024,1024]{1,0:T(8,128)}, f32[1024,1024]{1,0:T(8,128)}), (f32[1024,1024]{1,0:T(8,128)}, f32[1024,1024]{1,0:T(8,128)})) %all-reduce.403.cloned.1.call-update) | async-done | bytes 8388624 | tf_op jit(solution)/shard_map/psum | solution.py:154
  2740.5 32.4 %all-reduce.393 = (f32[1024]{0:T(1024)}, f32[4,512]{1,0:T(4,128)}, f32[512]{0:T(512)}, f32[512]{0:T(512)}, f32[16,512]{1,0:T(8,128)}, /*index=5*/f32[512]{0:T(512)}) all-reduce(f32[1024]{0:T(1024)S(1)} %get-tuple-element.1098, f32[4,512]{1,0:T(4,128)S(1)} %pad_add_fusion.5, ...), channel_id=1, replica_groups=mesh['dp'=8,'tensor'=4] {'dp'}, use_global_device_ids=true, to_apply=%region_279.280 | all-reduce | flops 12800 | bytes 102400 | tf_op jit(solution)/shard_map/psum | solution.py:198
  2772.9 6.6 fusion.405
  2779.5 188.3 %all-reduce.401.cloned.1.call-done = (f32[1024,2,512]{2,0,1:T(8,128)}, f32[512,96]{0,1:T(8,128)}, f32[64,512]{1,0:T(8,128)}, f32[512,1024]{1,0:T(8,128)}) async-done(((f32[1024,2,512]{2,0,1:T(8,128)}, f32[512,96]{0,1:T(8,128)}, f32[64,512]{1,0:T(8,128)}, f32[512,1024]{1,0:T(8,128)}), (f32[1024,2,512]{2,0,1:T(8,128)}, f32[512,96]{0,1:T(8,128)}, f32[64,512]{1,0:T(8,128)}, ...) | async-done | bytes 6619152 | tf_op jit(solution)/shard_map/psum | solution.py:198
  2967.8 7.6 copy.76
  (4153 shorter events, 1343.4 us)
Async XLA Ops:
  7.2 8.5 copy-start
  7.2 2729.7 %all-reduce.403.cloned.1.call-start = ((), (), s32[]{:S(2)}) async-start(), calls=%async_computation.1 | async-start | bytes 16777216 | tf_op jit(solution)/shard_map/psum | solution.py:154
  14.3 7.6 copy-start.12
  14.3 7.6 copy-start.51
  14.3 7.6 copy-start.53
  14.3 7.6 copy-start.55
  14.4 7.6 copy-start.57
  16.8 5.1 copy-start.23
  21.9 22.8 copy-start.3
  37.7 7.0 copy-start.18
  38.7 6.0 copy-start.21
  38.8 6.0 copy-start.25
  38.8 6.0 copy-start.48
  73.9 5.1 copy-start.28
  73.9 5.8 copy-start.27
  102.8 5.1 copy-start.28
  102.8 5.8 copy-start.27
  131.7 5.1 copy-start.28
  131.7 5.8 copy-start.27
  160.6 5.1 copy-start.28
  160.6 5.8 copy-start.27
  189.5 5.1 copy-start.28
  189.6 5.8 copy-start.27
  218.5 5.1 copy-start.28
  218.5 5.8 copy-start.27
  247.4 5.1 copy-start.28
  247.4 5.8 copy-start.27
  276.3 5.1 copy-start.28
  276.3 5.8 copy-start.27
  305.2 5.1 copy-start.28
  305.2 5.8 copy-start.27
  334.1 5.1 copy-start.28
  334.1 5.8 copy-start.27
  363.0 5.1 copy-start.28
  363.0 5.8 copy-start.27
  391.9 5.1 copy-start.28
  391.9 5.8 copy-start.27
  420.8 5.1 copy-start.28
  420.8 5.8 copy-start.27
  449.8 5.1 copy-start.28
  449.8 5.8 copy-start.27
  478.7 5.1 copy-start.28
  478.7 5.8 copy-start.27
  507.6 5.1 copy-start.28
  507.6 5.8 copy-start.27
  530.7 4.3 copy-start.41
  2484.9 16.7 copy-start.49
  2501.6 4.8 copy-start.26
  2544.6 16.8 copy-start.4
  2544.6 16.8 copy-start.24
  2544.6 16.8 copy-start.42
  2544.6 16.8 copy-start.52
  2544.6 16.8 copy-start.54
  2544.6 16.8 copy-start.56
  2544.6 16.8 copy-start.58
  2544.6 16.8 copy-start.60
  2572.1 4.4 copy-start.17
  2581.9 385.9 %all-reduce.401.cloned.1.call-start = ((), (), s32[]{:S(2)}) async-start(), calls=%async_computation | async-start | bytes 13238272 | tf_op jit(solution)/shard_map/psum | solution.py:198
  2593.2 4.0 copy-start.14
  2593.2 4.0 copy-start.40
  2736.9 36.0 %copy-start.44 = (f32[1024]{0:T(1024)S(1)}, f32[1024]{0:T(1024)}, u32[]{:S(2)}) copy-start(f32[1024]{0:T(1024)} %copy-done.43) | copy-start | bytes 12292
  2967.8 7.6 copy-start.19
  2967.8 8.3 copy-start.20
  2967.8 8.9 copy-start.13
  (179 other events, 570.8 us)
Sparse Core Ops, SparseCore 0:
  2582.0 154.8 all-reduce.402
  2742.5 225.2 all-reduce.400
where the time goes:
time: 3040 us; the launch traced here: 2990 us
  other arithmetic  1960 us (64%)
  local copies, waits for them, and re-layouts  568 us (19%)
  waiting for transfers between devices  323 us (11%)
  blocking collectives  63 us (2%)
  matrix products  43.3 us (1%)
    reduce_sum x32, other arithmetic, advance(): factor = jnp.exp(piece_step[:, :, None, :] * decay_rate)  1020 us
    reduce_sum x2432, other arithmetic, advance(): outputs.append(jnp.sum(state * piece_cmat[:, position, :, None], axis=1))  702 us
    psum x1, waiting for transfers between devices, on_device(): lax.psum((grad_norm_gain, grad_in_weight, grad_conv_weight, grad_conv_bia...  188 us
    another operation x160, local copies, waits for them, and re-layouts, advance(): return (state, jnp.stack(outputs, axis=1))  188 us
    squeeze x160, local copies, waits for them, and re-layouts, selective(): lax.scan(jax.checkpoint(advance), initial, (blocked(step_size), blocked(d...  135 us
    psum x1, waiting for transfers between devices, on_device(): lax.psum(out_partial, 'tensor')  134 us
    exp x64, other arithmetic, advance(): factor = jnp.exp(piece_step[:, :, None, :] * decay_rate)  64.9 us

commit v1 on v0

v1 whole, which is shorter than its diff:
```python
import functools

import jax
import jax.numpy as jnp
from jax import lax
from jax.experimental import pallas as pl
from jax.experimental.pallas import tpu as pltpu
from jax.sharding import PartitionSpec as P

T = 16
LC = 128
LOG2E = 1.4426950408889634
LN2 = 0.6931471805599453
F32 = jnp.float32
BF = jnp.bfloat16
NT = (((1,), (1,)), ((), ()))
STRIDED = True
epsilon = 1e-05


def iota(shape, d):
    return lax.broadcasted_iota(jnp.int32, shape, d)


def mm(a, b):
    return jnp.dot(a, b, preferred_element_type=F32)


def mm_nt(a, b):
    return lax.dot_general(a, b, NT, preferred_element_type=F32)


def row(ref, g, t, n):
    if STRIDED:
        pair = [ref[2 * g + j, pl.ds(t, 8, stride=0), :] for j in (0, 1)]
        wide = jnp.concatenate(pair, axis=1)
        return jnp.concatenate([wide] * (n // 8), axis=0)
    pair = [jnp.broadcast_to(ref[2 * g + j, pl.ds(t, 1), :], (n, 128)) for j in (0, 1)]
    return jnp.concatenate(pair, axis=1)


def spread(base, p, n):
    return (iota((p, T * n), 0) == base + lax.rem(iota((p, T * n), 1), n)).astype(BF)


def pick(base, p, n):
    return (iota((n, p), 1) == base + iota((n, p), 0)).astype(BF)


def fold(base, p, n):
    return (iota((T * n, p), 1) == base + lax.rem(iota((T * n, p), 0), n)).astype(BF)


def blockdiag(rows, n):
    return lax.rem(iota((rows, T * n), 0), T) == lax.div(iota((rows, T * n), 1), n)


def split(ref, value):
    for g in range(value.shape[1] // 128):
        ref[g] = value[:, g * 128 : (g + 1) * 128]


def softplus(x):
    e = jnp.exp2(jnp.abs(x) * -LOG2E)
    small = e * (1.0 - e * (0.5 - e * (1.0 / 3.0 - e * 0.25)))
    return jnp.maximum(x, 0.0) + jnp.where(e < 0.03125, small, jnp.log2(1.0 + e) * LN2)


def one_minus_exp(s):
    small = s * (1.0 - s * (0.5 - s * (1.0 / 6.0 - s * (1.0 / 24.0))))
    return jnp.where(s < 0.0625, small, 1.0 - jnp.exp2(s * -LOG2E))


def front_kernel(ng, prefix_ref, proj_ref, sw_ref, bias_ref, drive_ref, z_ref, dg_ref, dlog_ref, skip_ref,
                 gated_ref, dz_ref, step_ref, dy_ref, hprev_ref, ag_ref, wg_ref, part_ref, gskip_ref,
                 step_s, sd_s, dy_s, sig_s, keep_s, bt_s, ct_s, cbd_s, rc_s, hg_s, g_s, qg_s, st_f, st_h, st_q):
    lc, c = drive_ref.shape
    p = proj_ref.shape[1]
    n = dlog_ref.shape[0]
    r = p - 2 * n
    tn = T * n
    nb = lc // T
    groups = c // 256
    i = pl.program_id(0)
    pfx = prefix_ref[0]
    rate2 = -jnp.exp(dlog_ref[...]) * LOG2E
    lanes = [slice(g * 256, (g + 1) * 256) for g in range(groups)]

    def positions(chunk):
        return iota((lc, 1), 0) + chunk * lc

    def col(ref, t0, k):
        one = jnp.broadcast_to(pltpu.roll(ref[...], lax.rem(lc - t0, lc), 1)[:, k : k + 1], (n, 128))
        return jnp.concatenate([one, one], axis=1)

    @pl.when(i == 0)
    def _():
        st_f[...] = jnp.zeros_like(st_f)
        st_h[...] = jnp.zeros_like(st_h)
        st_q[...] = jnp.zeros_like(st_q)
        gskip_ref[...] = jnp.zeros_like(gskip_ref)

    proj = proj_ref[...]
    bt_s[...] = mm_nt(pick(r, p, n), proj)

    @pl.when(i < ng)
    def _():
        chunk = ng - 1 - i
        step = softplus(mm(proj[:, :r], sw_ref[...]) + bias_ref[...])
        keep_s[chunk] = step

        @pl.when(chunk * lc < pfx)
        def _():
            mask = (positions(chunk) < pfx).astype(F32)
            split(step_s, step)
            split(sd_s, step * drive_ref[...].astype(F32) * mask)
            base = chunk * (lc * n)

            def body(ir, state):
                t0 = pl.multiple_of((nb - 1 - ir) * T, T)
                state = list(state)
                bt = pltpu.roll(bt_s[...], lax.rem(lc - t0, lc), 1)
                for k in range(T - 1, -1, -1):
                    t = t0 + k
                    bb = jnp.broadcast_to(bt[:, k : k + 1], (n, 128))
                    bb = jnp.concatenate([bb, bb], axis=1)
                    at = pl.ds(pl.multiple_of(base + t * n, n), n)
                    for g in range(groups):
                        q = jnp.exp2(row(step_s, g, t, n) * rate2[:, lanes[g]]) * state[g]
                        state[g] = q + bb * row(sd_s, g, t, n)
                        qg_s[at, lanes[g]] = q.astype(BF)
                        g_s[at, lanes[g]] = state[g].astype(BF)
                return tuple(state)

            out = lax.fori_loop(0, nb, body, tuple(st_f[g] for g in range(groups)))
            for g in range(groups):
                st_f[g] = out[g]

    @pl.when(i >= ng)
    def _():
        chunk = i - ng

        @pl.when(chunk < ng)
        def _():
            step_ref[...] = keep_s[jnp.minimum(chunk, ng - 1)]

        @pl.when(chunk >= ng)
        def _():
            step_ref[...] = softplus(mm(proj[:, :r], sw_ref[...]) + bias_ref[...])

        step = step_ref[...]
        drive = drive_ref[...].astype(F32)
        z = z_ref[...]
        sig = 1.0 / (1.0 + jnp.exp2(z * -LOG2E))
        sig_s[...] = sig
        dy = dg_ref[...] * (z * sig)
        dy_ref[...] = dy
        gskip_ref[...] += jnp.sum(dy * drive, axis=0, keepdims=True)
        split(step_s, step)
        split(sd_s, step * drive)
        ct_s[...] = mm_nt(pick(r + n, p, n), proj)
        cbd_s[...] = jnp.where(blockdiag(lc, n), mm(proj, spread(r + n, p, n)), 0.0).astype(BF)
        diag = blockdiag(T, n)

        def mxu(b, buf):
            rows = pl.ds(pl.multiple_of(b * T, T), T)
            kept = {}

            def y_part(g):
                kept[g] = mm(cbd_s[rows, :], hg_s[buf, :, lanes[g]])

            def r_part(g):
                x = mm_nt(dy_ref[rows, lanes[g]].astype(BF), hg_s[buf, :, lanes[g]])
                kept["r"] = x if g == 0 else kept["r"] + x
                if g == groups - 1:
                    rc_s[rows, :] = jnp.where(diag, kept["r"], 0.0).astype(BF)

            def end(g):
                ln = lanes[g]
                y = kept[g] + skip_ref[:, ln] * drive_ref[rows, ln].astype(F32)
                zz = z_ref[rows, ln]
                sg = sig_s[rows, ln]
                gated_ref[rows, ln] = (y * (zz * sg)).astype(BF)
                dz_ref[rows, ln] = (dg_ref[rows, ln] * y * (sg * (1.0 + zz * (1.0 - sg)))).astype(BF)

            return [functools.partial(f, g) for g in range(groups) for f in (y_part, r_part, end)]

        def vpu(with_g, b, buf, state, pieces=()):
            hs, hbs, qs = (list(s) for s in state)
            pieces = list(pieces)
            t0 = pl.multiple_of(b * T, T)
            bt = pltpu.roll(bt_s[...], lax.rem(lc - t0, lc), 1)
            ct = pltpu.roll(ct_s[...], lax.rem(lc - t0, lc), 1) if with_g else None
            base = jnp.minimum(chunk, ng - 1) * (lc * n)
            for k in range(T):
                t = t0 + k
                bb = jnp.broadcast_to(bt[:, k : k + 1], (n, 128))
                bb = jnp.concatenate([bb, bb], axis=1)
                if with_g:
                    cc = jnp.broadcast_to(ct[:, k : k + 1], (n, 128))
                    cc = jnp.concatenate([cc, cc], axis=1)
                at = pl.ds(pl.multiple_of(t * n, n), n)
                far = pl.ds(pl.multiple_of(base + t * n, n), n)
                for g in range(groups):
                    ln = lanes[g]
                    e = jnp.exp2(row(step_s, g, t, n) * rate2[:, ln])
                    hprev_ref[at, ln] = hbs[g]
                    hs[g] = e * hs[g] + bb * row(sd_s, g, t, n)
                    hbs[g] = hs[g].astype(BF)
                    if with_g:
                        hg_s[buf, pl.ds(k * n, n), ln] = hbs[g] + g_s[far, ln]
                        ag = cc * row(dy_s, g, t, n) + qs[g]
                        qs[g] = e * ag
                        agb = ag.astype(BF)
                        ag_ref[at, ln] = agb
                        wg_ref[at, ln] = agb * qg_s[far, ln]
                    else:
                        hg_s[buf, pl.ds(k * n, n), ln] = hbs[g]
                if k % 2 and pieces:
                    pieces.pop(0)()
            for f in pieces:
                f()
            return tuple(hs), tuple(hbs), tuple(qs)

        def run(with_g):
            many = range(groups)
            state = tuple(st_f[g + groups] for g in many), tuple(st_h[g] for g in many), tuple(st_q[g] for g in many)
            state = vpu(with_g, 0, 0, state)

            def body(j, state):
                state = vpu(with_g, 2 * j + 1, 1, state, mxu(2 * j, 0))
                return vpu(with_g, 2 * j + 2, 0, state, mxu(2 * j + 1, 1))

            state = lax.fori_loop(0, nb // 2 - 1, body, state)
            state = vpu(with_g, nb - 1, 1, state, mxu(nb - 2, 0))
            for f in mxu(nb - 1, 1):
                f()
            for g in many:
                st_f[g + groups] = state[0][g]
                st_h[g] = state[1][g]
                st_q[g] = state[2][g]

        live = jnp.logical_and(chunk < ng, chunk * lc < pfx)

        @pl.when(live)
        def _():
            mask = (positions(chunk) < pfx).astype(F32)
            split(dy_s, dy * mask)
            run(True)

            @pl.when(pfx < (chunk + 1) * lc)
            def _():
                keep = iota((lc * n, c), 0) + chunk * (lc * n) < pfx * n
                ag_ref[...] = jnp.where(keep, ag_ref[...].astype(F32), 0.0).astype(BF)

        @pl.when(jnp.logical_not(live))
        def _():
            run(False)

        part_ref[...] = mm(rc_s[...], fold(r + n, p, n))


def back_kernel(ng, prefix_ref, proj_ref, sw_ref, drive_ref, step_ref, dy_ref, h_ref, ag_ref, wg_ref, pin_ref, dlog_ref, skip_ref,
                part_ref, dpre_ref, ddrive_ref, gdecay_ref, gbias_ref,
                step_s, dy_s, p_s, acc_s, ct_s, bbd_s, rb_s, ds_s, v_s):
    lc, c = drive_ref.shape
    p = proj_ref.shape[1]
    n = dlog_ref.shape[0]
    r = p - 2 * n
    tn = T * n
    nb = lc // T
    groups = c // 256
    i = pl.program_id(0)
    chunk = pl.num_programs(0) - 1 - i
    rate2 = -jnp.exp(dlog_ref[...]) * LOG2E
    rate2b = rate2.astype(BF)
    lanes = [slice(g * 256, (g + 1) * 256) for g in range(groups)]

    @pl.when(i == 0)
    def _():
        p_s[...] = jnp.zeros_like(p_s)
        acc_s[...] = jnp.zeros_like(acc_s)
        gbias_ref[...] = jnp.zeros_like(gbias_ref)

    proj = proj_ref[...]
    split(step_s, step_ref[...])
    split(dy_s, dy_ref[...])
    ct_s[...] = mm_nt(pick(r + n, p, n), proj)
    bbd_s[...] = jnp.where(blockdiag(lc, n), mm(proj, spread(r, p, n)), 0.0).astype(BF)
    diag = blockdiag(T, n)
    ones = diag.astype(BF)

    def vpu(with_g, b, buf, state, pieces=()):
        ps, accs = (list(s) for s in state)
        pieces = list(pieces)
        t0 = pl.multiple_of(b * T, T)
        ct = pltpu.roll(ct_s[...], lax.rem(lc - t0, lc), 1)
        for k in range(T - 1, -1, -1):
            t = t0 + k
            cc = jnp.broadcast_to(ct[:, k : k + 1], (n, 128))
            cc = jnp.concatenate([cc, cc], axis=1)
            at = pl.ds(pl.multiple_of(t * n, n), n)
            for g in range(groups):
                ln = lanes[g]
                st = row(step_s, g, t, n)
                e = jnp.exp2(st * rate2[:, ln])
                ah = cc * row(dy_s, g, t, n) + ps[g]
                ps[g] = e * ah
                dsrc = ah.astype(BF)
                w = ps[g].astype(BF) * h_ref[at, ln]
                if with_g:
                    dsrc = dsrc + ag_ref[at, ln]
                    w = w + wg_ref[at, ln]
                ds_s[buf, pl.ds(k * n, n), ln] = dsrc
                v_s[buf, pl.ds(k * n, n), ln] = w * rate2b[:, ln]
                accs[g] = accs[g] + w.astype(F32) * st
            if k % 2 == 0 and pieces:
                pieces.pop(0)()
        for f in pieces:
            f()
        return tuple(ps), tuple(accs)

    def mxu(b, buf):
        rows = pl.ds(pl.multiple_of(b * T, T), T)
        kept = {}

        def s_part(g):
            kept["s", g] = mm(bbd_s[rows, :], ds_s[buf, :, lanes[g]])

        def v_part(g):
            kept["v", g] = mm(ones, v_s[buf, :, lanes[g]])

        def r_part(g):
            ln = lanes[g]
            sd = step_ref[rows, ln] * drive_ref[rows, ln].astype(F32)
            x = mm_nt(sd.astype(BF), ds_s[buf, :, ln])
            kept["r"] = x if g == 0 else kept["r"] + x
            if g == groups - 1:
                rb_s[rows, :] = jnp.where(diag, kept["r"], 0.0).astype(BF)

        def end(g):
            ln = lanes[g]
            step = step_ref[rows, ln]
            ssum = kept["s", g]
            drive = drive_ref[rows, ln].astype(F32)
            dpre = (kept["v", g] * LN2 + drive * ssum) * one_minus_exp(step)
            dpre_ref[rows, ln] = dpre.astype(BF)
            ddrive_ref[rows, ln] = skip_ref[:, ln] * dy_ref[rows, ln] + step * ssum
            gbias_ref[:, ln] += jnp.sum(dpre, axis=0, keepdims=True)

        return [functools.partial(f, g) for g in range(groups) for f in (s_part, v_part, r_part, end)]

    def run(with_g):
        many = range(groups)
        state = tuple(p_s[g] for g in many), tuple(acc_s[g] for g in many)
        state = vpu(with_g, nb - 1, 0, state)

        def body(j, state):
            b = nb - 1 - 2 * j
            state = vpu(with_g, b - 1, 1, state, mxu(b, 0))
            return vpu(with_g, b - 2, 0, state, mxu(b - 1, 1))

        state = lax.fori_loop(0, nb // 2 - 1, body, state)
        state = vpu(with_g, 0, 1, state, mxu(1, 0))
        for f in mxu(0, 1):
            f()
        for g in many:
            p_s[g] = state[0][g]
            acc_s[g] = state[1][g]

    live = jnp.logical_and(chunk < ng, chunk * lc < prefix_ref[0])

    @pl.when(live)
    def _():
        run(True)

    @pl.when(jnp.logical_not(live))
    def _():
        run(False)

    part_ref[...] = (pin_ref[...] + mm(rb_s[...], fold(r, p, n)) + mm_nt(dpre_ref[...], sw_ref[...])).astype(part_ref.dtype)
    gdecay_ref[...] = jnp.concatenate([acc_s[g] for g in range(groups)], axis=1) * (rate2 * LN2)


def whole(*s):
    return pl.BlockSpec(s, lambda i: (0,) * len(s))


SMEM = pl.BlockSpec(memory_space=pltpu.SMEM)


def front(prefix, proj, sw, bias, drive, z, dg, dlog, skip):
    l, c = drive.shape
    p = proj.shape[1]
    n = dlog.shape[0]
    ng = l // 2 // LC
    nc = l // LC
    s = jax.ShapeDtypeStruct
    fwd = lambda i: (jnp.maximum(i - ng, 0), 0)
    both = lambda i: (jnp.where(i < ng, ng - 1 - i, i - ng), 0)
    half = lambda i: (jnp.clip(i - ng, 0, ng - 1), 0)
    B = pl.BlockSpec
    lanes = c // 128
    v = pltpu.VMEM
    return pl.pallas_call(
        functools.partial(front_kernel, ng),
        grid=(ng + nc,),
        in_specs=[SMEM, B((LC, p), both), whole(*sw.shape), whole(1, c), B((LC, c), both), B((LC, c), fwd), B((LC, c), fwd), whole(n, c), whole(1, c)],
        out_specs=[B((LC, c), fwd), B((LC, c), fwd), B((LC, c), fwd), B((LC, c), fwd), B((LC * n, c), fwd), B((LC * n, c), half), B((LC * n, c), half), B((LC, p), fwd), whole(1, c)],
        out_shape=[s((l, c), BF), s((l, c), BF), s((l, c), F32), s((l, c), F32), s((l * n, c), BF), s((l // 2 * n, c), BF), s((l // 2 * n, c), BF), s((l, p), F32), s((1, c), F32)],
        scratch_shapes=[v((lanes, LC, 128), F32)] * 3 + [v((LC, c), F32), v((ng, LC, c), F32), v((n, LC), F32), v((n, LC), F32), v((LC, T * n), BF), v((LC, T * n), BF),
            v((2, T * n, c), BF), v((l // 2 * n, c), BF), v((l // 2 * n, c), BF), v((c // 128, n, 256), F32), v((c // 256, n, 256), BF), v((c // 256, n, 256), F32)],
        compiler_params=pltpu.CompilerParams(vmem_limit_bytes=56 << 20),
        name="front",
    )(prefix, proj, sw, bias.reshape(1, c), drive, z, dg, dlog, skip.reshape(1, c))


def back(prefix, proj, sw_wide, drive, step, dy, hprev, ag, wg, pin, dlog, skip):
    l, c = drive.shape
    p = proj.shape[1]
    n = dlog.shape[0]
    ng = l // 2 // LC
    nc = l // LC
    s = jax.ShapeDtypeStruct
    rev = lambda i: (nc - 1 - i, 0)
    half = lambda i: (jnp.minimum(nc - 1 - i, ng - 1), 0)
    B = pl.BlockSpec
    v = pltpu.VMEM
    return pl.pallas_call(
        functools.partial(back_kernel, ng),
        grid=(nc,),
        in_specs=[SMEM, B((LC, p), rev), whole(*sw_wide.shape), B((LC, c), rev), B((LC, c), rev), B((LC, c), rev), B((LC * n, c), rev), B((LC * n, c), half), B((LC * n, c), half), B((LC, p), rev), whole(n, c), whole(1, c)],
        out_specs=[B((LC, p), rev), B((LC, c), rev), B((LC, c), rev), whole(n, c), whole(1, c)],
        out_shape=[s((l, p), BF), s((l, c), BF), s((l, c), F32), s((n, c), F32), s((1, c), F32)],
        scratch_shapes=[v((c // 128, LC, 128), F32)] * 2 + [v((c // 256, n, 256), F32)] * 2 + [v((n, LC), F32), v((LC, T * n), BF), v((LC, T * n), BF), v((2, T * n, c), BF), v((2, T * n, c), BF)],
        compiler_params=pltpu.CompilerParams(vmem_limit_bytes=40 << 20),
        name="back",
    )(prefix, proj, sw_wide, drive, step, dy, hprev, ag, wg, pin, dlog, skip.reshape(1, c))


def exchange(value, name, size, bit):
    return lax.ppermute(value, name, [(j, j ^ (1 << bit)) for j in range(size)])


def bits_of(size):
    count = size.bit_length() - 1
    assert 1 << count == size
    return list(range(count))


def butterfly(value, name, size):
    total = value
    for bit in bits_of(size):
        low = total.astype(BF)
        total = low.astype(F32) + exchange(low, name, size, bit).astype(F32)
    return total


def scatter_sum(value, name, size, order):
    at = lax.axis_index(name)
    for bit in order:
        mine = (at >> bit) & 1
        half = value.shape[0] // 2
        send = lax.dynamic_slice_in_dim(value, (1 - mine) * half, half, 0).astype(BF)
        keep = lax.dynamic_slice_in_dim(value, mine * half, half, 0)
        value = keep.astype(F32) + exchange(send, name, size, bit).astype(F32)
    return value


def gather_rows(value, name, size, order):
    at = lax.axis_index(name)
    for bit in reversed(order):
        mine = (at >> bit) & 1
        other = exchange(value, name, size, bit)
        value = jnp.where(mine == 0, jnp.concatenate([value, other]), jnp.concatenate([other, value]))
    return value


def all_sum(value, name, size):
    order = bits_of(size)
    turned = order[1:] + order[:1]
    half = value.shape[0] // 2
    low = value.astype(BF)
    parts = []
    for piece, way in ((low[:half], order), (low[half:], turned)):
        mine = scatter_sum(piece, name, size, way)
        parts.append(gather_rows(mine.astype(BF), name, size, way))
    return jnp.concatenate(parts)


def shifted(values, by):
    if by == 0:
        return values
    if by > 0:
        return jnp.pad(values, ((by, 0), (0, 0)))[: values.shape[0]]
    return jnp.pad(values, ((0, -by), (0, 0)))[-by:]


def sigmoid(v):
    return 1.0 / (1.0 + jnp.exp(-v))


def on_device(sizes, tokens, prefix, norm_gain, in_weight, conv_weight, conv_bias, xproj_weight, step_weight, step_bias, decay_log, skip_gain, out_weight, out_cotangent):
    dp, tp = sizes
    seqs, length, width = tokens.shape
    assert seqs == 1
    channels = in_weight.shape[2]
    rank = step_weight.shape[0]
    taps = conv_weight.shape[0]
    n = decay_log.shape[0]
    low = tokens[0]
    xf = low.astype(F32)
    cot = out_cotangent[0]
    w_x = in_weight[:, 0, :]
    w_z = in_weight[:, 1, :]

    rs = lax.rsqrt(jnp.mean(xf * xf, axis=-1, keepdims=True) + epsilon)
    normed = (xf * rs * norm_gain).astype(BF)
    xpart = mm(normed, w_x)
    zpart = mm(normed, w_z)
    convout = conv_bias + sum(conv_weight[k] * shifted(xpart, taps - 1 - k) for k in range(taps))
    drive = (convout * sigmoid(convout)).astype(BF)
    proj = butterfly(mm(drive, xproj_weight), "tensor", tp).astype(BF)
    dgated = mm_nt(cot, out_weight)

    gated, dz, step, dy, hprev, ag, wg, pin, gskip = front(prefix, proj, step_weight, step_bias, drive, zpart, dgated, decay_log, skip_gain)

    t_order = bits_of(tp)
    rows = length // tp
    at = lax.axis_index("tensor")
    spot = 0
    part = length
    for bit in t_order:
        part //= 2
        spot = spot + ((at >> bit) & 1) * part
    mixed = scatter_sum(mm(gated, out_weight), "tensor", tp, t_order)
    mixed = (lax.dynamic_slice_in_dim(xf, spot, rows, 0) + mixed).astype(BF)
    block_out = gather_rows(mixed, "tensor", tp, t_order)

    tn = (((0,), (0,)), ((), ()))
    mm_tn = lambda a, b: lax.dot_general(a, b, tn, preferred_element_type=F32)
    g_out = mm_tn(gated, cot)
    g_in_z = mm_tn(normed, dz)
    early = all_sum(jnp.concatenate([g_in_z.astype(BF), g_out.astype(BF).reshape(-1, channels)]), "dp", dp)

    wide = jnp.pad(step_weight, ((0, 2 * n), (0, 0)))
    dpart, dpre, ddrive_scan, g_decay, g_bias = back(prefix, proj, wide, drive, step, dy, hprev, ag, wg, pin, decay_log, skip_gain)
    dproj = butterfly(dpart, "tensor", tp).astype(BF)
    g_step = mm_tn(proj[:, :rank], dpre)
    g_xproj = mm_tn(dproj, drive)
    ddrive = ddrive_scan + mm_nt(dproj, xproj_weight)
    sc = sigmoid(convout)
    dconv = ddrive * (sc * (1.0 + convout * (1.0 - sc)))
    g_conv = jnp.stack([jnp.sum(dconv * shifted(xpart, taps - 1 - k), axis=0) for k in range(taps)])
    g_convb = jnp.sum(dconv, axis=0, keepdims=True)
    dx = sum(conv_weight[k] * shifted(dconv, k - taps + 1) for k in range(taps)).astype(BF)
    g_in_x = mm_tn(normed, dx)
    dnormed = mm_nt(dx, w_x) + mm_nt(dz, w_z)
    g_norm = jnp.sum(dnormed * (xf * rs), axis=0).reshape(-1, channels)
    small = [g_conv, g_convb, g_bias, g_decay, gskip, g_step, g_xproj, g_norm]
    counts = [s.shape[0] for s in small]
    fill = -sum(counts) % (2 * dp)
    packed = jnp.concatenate([s.astype(BF) for s in small] + [jnp.zeros((fill, channels), BF), g_in_x.astype(BF)])
    late = all_sum(packed, "dp", dp).astype(F32)

    mine = scatter_sum(dnormed, "tensor", tp, t_order)
    my_x = lax.dynamic_slice_in_dim(xf, spot, rows, 0)
    my_rs = lax.dynamic_slice_in_dim(rs, spot, rows, 0)
    scaled = mine * norm_gain
    moved = my_rs * scaled - my_x * (my_rs * my_rs * my_rs) * jnp.mean(scaled * my_x, axis=-1, keepdims=True)
    moved = gather_rows(moved.astype(BF), "tensor", tp, t_order)
    grad_tokens = cot.astype(F32) + moved.astype(F32)

    out = []
    top = 0
    for count in counts:
        out.append(late[top : top + count])
        top += count
    g_conv, g_convb, g_bias, g_decay, gskip, g_step, g_xproj, g_norm = out
    g_in_x = late[top + fill :]
    early = early.astype(F32)
    g_in = jnp.stack([g_in_x, early[:width]], axis=1)
    g_out = early[width:].reshape(channels, width)
    g_norm = g_norm.reshape(-1)
    for bit in bits_of(tp):
        g_norm = g_norm + exchange(g_norm, "tensor", tp, bit)
    return (block_out[None], grad_tokens[None], g_norm, g_in, g_conv, g_convb[0], g_xproj.T, g_step, g_bias[0], g_decay, gskip[0], g_out)


def solution(mesh):
    placed = (
        P("dp", None, None),
        P("dp"),
        P(),
        P(None, None, "tensor"),
        P(None, "tensor"),
        P("tensor"),
        P("tensor", None),
        P(None, "tensor"),
        P("tensor"),
        P(None, "tensor"),
        P("tensor"),
        P("tensor", None),
        P("dp", None, None),
    )
    results = (
        P("dp", None, None),
        P("dp", None, None),
        P(),
        P(None, None, "tensor"),
        P(None, "tensor"),
        P("tensor"),
        P("tensor", None),
        P(None, "tensor"),
        P("tensor"),
        P(None, "tensor"),
        P("tensor"),
        P("tensor", None),
    )
    sizes = (mesh.shape["dp"], mesh.shape["tensor"])
    return jax.shard_map(functools.partial(on_device, sizes), mesh=mesh, in_specs=placed, out_specs=results, check_vma=False)
```

time: 3040 us -> 302 us (0.10)
  the two profiles are of different devices: /device:TPU:1 before, /device:TPU:3 now
where the time goes in v1:
time: 302 us; the launch traced here: 297 us
  starting transfers between devices  64.3 us (21%)
  Pallas kernels  64.3 us (21%)
  waiting for transfers between devices  57.1 us (19%)
  local copies, waits for them, and re-layouts  42.9 us (14%)
  other arithmetic  38.9 us (13%)
  matrix products  26.9 us (9%)
    ppermute x38, starting transfers between devices, exchange(): return lax.ppermute(value, name, [(j, j ^ 1 << bit) for j in range(size)])  64.3 us
    ppermute x38, waiting for transfers between devices, exchange(): return lax.ppermute(value, name, [(j, j ^ 1 << bit) for j in range(size)])  57.1 us
    pallas_call x1, Pallas kernels, front(): pl.pallas_call(functools.partial(front_kernel, ng), grid=(ng + nc,), in_s...  35.3 us
    pallas_call x1, Pallas kernels, back(): pl.pallas_call(functools.partial(back_kernel, ng), grid=(nc,), in_specs=[...  29.1 us
    concatenate x1, local copies, waits for them, and re-layouts, on_device(): jnp.concatenate([s.astype(BF) for s in small] + [jnp.zeros((fill, channel...  12.5 us
    dot_general x4, matrix products, mm(): return jnp.dot(a, b, preferred_element_type=F32)  9.92 us
    dot_general x4, matrix products, mm_nt(): return lax.dot_general(a, b, NT, preferred_element_type=F32)  9.3 us
    select_n x15, other arithmetic, gather_rows(): jnp.where(mine == 0, jnp.concatenate([value, other]), jnp.concatenate([ot...  8.87 us
  transfers between devices with their start and end apart: 38, of which 16 were waited for; matrix products, arithmetic and copies ran while one was open for 28% of the time, Pallas kernels for 0%

profile of v1, /device:TPU:3, one launch (start us, length us, event | category | flops | bytes accessed | tf_op | source)
XLA Modules:
  0.0 297.0 jit_solution(6894723047781191962)
XLA Ops:
  0.7 2.2 fusion
  3.0 3.8 %fusion.29 = (bf16[1024,1,512]{2,1,0:T(2,128)(2,1)}, bf16[1024,1,512]{2,1,0:T(2,128)(2,1)S(1)}) fusion(bf16[1024,2,512]{2,1,0:T(2,128)(2,1)S(1)} %copy-done.20), kind=kLoop, calls=%fused_computation.123 | loop fusion | bytes 4194304 | tf_op jit(solution)/shard_map/slice | solution.py:515
  6.8 1.3 fusion.23
  8.2 2.6 multiply_convert_fusion.2
  12.0 4.1 %convert_element_type.258 = f32[1,1024,1024]{2,1,0:T(8,128)} convert(bf16[1,1024,1024]{2,1,0:T(8,128)(2,1)} %param.13) | non-fusion elementwise | flops 1048576 | bytes 6291456 | tf_op jit(solution)/shard_map/convert_element_type | solution.py:512
  16.1 4.9 %fusion.21.z_ref = f32[1024,512]{1,0:T(8,128)} fusion(bf16[1,1024,1024]{2,1,0:T(8,128)(2,1)} %param.13, f32[1024]{0:T(1024)S(1)} %copy-done.35, f32[1024]{0:T(1024)S(1)} %add_rsqrt_fusion, bf16[1024,1,512]{2,1,0:T(2,128)(2,1)} %get-tuple-element.76), kind=kOutput, calls=%fused_computation.74 | convolution fusion | flops 1077936128 | bytes 5251072 | tf_op jit(solution)/shard_map/dot_general | solution.py:26
  21.7 4.2 %fusion.11.dg_ref = f32[1024,512]{1,0:T(8,128)} fusion(bf16[512,1024]{1,0:T(8,128)(2,1)S(1)} %copy-done, bf16[1,1024,1024]{2,1,0:T(8,128)(2,1)} %param.25), kind=kOutput, calls=%fused_computation.30 | convolution fusion | flops 1073741824 | bytes 5242880 | tf_op jit(solution)/shard_map/dot_general | solution.py:30
  26.0 1.3 collective-permute-start.1
  27.9 6.1 %collective-permute-done.1 = bf16[1024,96]{1,0:T(8,128)(2,1)S(1)} collective-permute-done((bf16[1024,96]{1,0:T(8,128)(2,1)S(1)}, bf16[1024,96]{1,0:T(8,128)(2,1)S(1)}, u32[]{:S(2)}, u32[]{:S(2)}) %collective-permute-start.1) | collective-permute-done | bytes 196640 | tf_op jit(solution)/shard_map/ppermute | solution.py:442
  34.7 35.3 %front.1 = (bf16[1024,512]{1,0:T(8,128)(2,1)}, bf16[1024,512]{1,0:T(8,128)(2,1)}, f32[1024,512]{1,0:T(8,128)}, f32[1024,512]{1,0:T(8,128)}, bf16[16384,512]{1,0:...) custom-call(s32[1]{0:T(128)S(6)} %copy.43.prefix_ref, ...), custom_call_target="tpu_custom_call" | custom-call | tf_op jit(solution)/shard_map/front/pallas_call | solution.py:405
  70.1 3.6 %fusion.13 = bf16[512,1024]{1,0:T(8,128)(2,1)} fusion(bf16[1024,512]{1,0:T(8,128)(2,1)} %get-tuple-element.26, bf16[1,1024,1024]{2,1,0:T(8,128)(2,1)S(1)} %copy-done.21), kind=kOutput, calls=%fused_computation.44 | convolution fusion | flops 1074266112 | bytes 4194304 | tf_op jit(solution)/shard_map/dot_general | solution.py:541
  73.7 3.3 %fusion.31 = f32[1024,1024]{1,0:T(8,128)} fusion(bf16[1024,512]{1,0:T(8,128)(2,1)S(1)} %copy-done.32, bf16[512,1024]{1,0:T(8,128)(2,1)S(1)} %copy-done), kind=kOutput, calls=%fused_computation.125 | convolution fusion | flops 1073741824 | bytes 6291456 | tf_op jit(solution)/shard_map/dot_general | solution.py:26
  77.5 29.1 %back.1 = (bf16[1024,96]{1,0:T(8,128)(2,1)S(1)}, bf16[1024,512]{1,0:T(8,128)(2,1)S(1)}, f32[1024,512]{1,0:T(8,128)S(1)}, f32[16,512]{1,0:T(8,128)S(1)}, f32[1,512]{1,0:T(1,128)S(1)}) custom-call(s32[1]{0:T(128)S(6)} %copy.43.prefix_ref, bf16[1024,96]{1,0:T(8,128)(2,1)S(1)} %copy-done.4, bf16[96,512]{1,0:T(8,128)(2,1)S(1)} %pad.34.sw_ref, ...), custom_call_target="tpu_custom_call" | custom-call | tf_op jit(solution)/shard_map/back/pallas_call | solution.py:429
  108.7 1.4 convolution_convert_fusion
  111.3 4.5 %collective-permute-start.26 = (bf16[512,512]{1,0:T(8,128)(2,1)}, bf16[512,512]{1,0:T(8,128)(2,1)}, u32[]{:S(2)}, u32[]{:S(2)}) collective-permute-start(bf16[512,512]{1,0:T(8,128)(2,1)} %constant_dynamic-slice_fusion.1), channel_id=1, source_target_pairs={{0,4},{4,0},{8,12},{12,8},{16,20},{20,16},{24,28},{28,24},{1,5},{5... | collective-permute-start | bytes 1572872 | tf_op jit(solution)/shard_map/ppermute | solution.py:442
  115.8 2.2 reshape.321
  118.0 1.9 constant_dynamic-slice_fusion
  119.9 1.9 collective-permute-start.32
  121.8 2.9 dynamic-slice_convert_fusion.1
  125.6 1.3 collective-permute-start.7
  127.8 5.8 %collective-permute-done.7 = bf16[1024,96]{1,0:T(8,128)(2,1)S(1)} collective-permute-done((bf16[1024,96]{1,0:T(8,128)(2,1)S(1)}, bf16[1024,96]{1,0:T(8,128)(2,1)S(1)}, u32[]{:S(2)}, u32[]{:S(2)}) %collective-permute-start.7) | collective-permute-done | bytes 196640 | tf_op jit(solution)/shard_map/ppermute | solution.py:442
  134.1 1.8 multiply_reduce_fusion.1
  137.5 1.3 fusion.25
  139.1 1.4 convolution_convert_fusion.1
  140.9 3.4 %multiply_reduce_fusion = (bf16[1024]{0:T(1024)(128)(2,1)S(1)}, f32[1024,1024]{1,0:T(8,128)}) fusion(bf16[1,1024,1024]{2,1,0:T(8,128)(2,1)S(1)} %copy-done.14, f32[1024]{0:T(1024)S(1)} %add_rsqrt_fusion, f32[1024,1024]{1,0:T(8,128)S(1)} %fusion.25, bf16[1024,512]{1,0:T(8,128)(2,1)S(1)} %copy-done.29, bf16[1024,1,512]{2,1,0:T(2,128)(2,1)S(1)} %copy-done.23), kind=kOutput, calls=%fused_computation.5 | convolution fusion | flops 1078983680 | bytes 12589056 | tf_op jit(solution)/shard_map/dot_general | solution.py:30
  148.2 12.5 %concatenate.190 = bf16[1216,512]{1,0:T(8,128)(2,1)S(1)} concatenate(bf16[1,512]{1,0:T(2,128)(2,1)} %stack.27, bf16[1,512]{1,0:T(2,128)(2,1)} %stack.28, bf16[1,512]{1,0:T(2,128)(2,1)} %stack.29, bf16[1,512]{1,0:T(2,128)(2,1)} %stack.30, bf16[1,512]{1,0:T(2,128)(2,1)} %convert_element_type.290, bf16[1,512]{1,0:T(2,128)(2,1)} %convert_element_type.291, ...), dimensions={0} | concatenate | bytes 2490368 | tf_op jit(solution)/shard_map/concatenate | solution.py:563
  160.8 1.3 collective-permute-start.12
  162.2 1.8 dynamic-slice_convert_fusion
  165.1 1.2 convert_add_fusion.4
  166.3 1.8 collective-permute-start.27
  168.1 1.2 convert_add_fusion.3
  170.6 1.5 collective-permute-start.13
  172.3 8.3 %collective-permute-done.27 = bf16[256,512]{1,0:T(8,128)(2,1)S(1)} collective-permute-done((bf16[256,512]{1,0:T(8,128)(2,1)S(1)}, bf16[256,512]{1,0:T(8,128)(2,1)S(1)}, u32[]{:S(2)}, u32[]{:S(2)}) %collective-permute-start.27) | collective-permute-done | bytes 262176 | tf_op jit(solution)/shard_map/ppermute | solution.py:442
  180.7 2.4 collective-permute-start.28
  183.3 3.5 %collective-permute-done.13 = bf16[152,512]{1,0:T(8,128)(2,1)S(1)} collective-permute-done((bf16[152,512]{1,0:T(8,128)(2,1)S(1)}, bf16[152,512]{1,0:T(8,128)(2,1)S(1)}, u32[]{:S(2)}, u32[]{:S(2)}) %collective-permute-start.13) | collective-permute-done | bytes 155680 | tf_op jit(solution)/shard_map/ppermute | solution.py:442
  186.9 2.3 collective-permute-start.14
  189.3 4.7 %collective-permute-done.28 = bf16[128,512]{1,0:T(8,128)(2,1)S(1)} collective-permute-done((bf16[128,512]{1,0:T(8,128)(2,1)S(1)}, bf16[128,512]{1,0:T(8,128)(2,1)S(1)}, u32[]{:S(2)}, u32[]{:S(2)}) %collective-permute-start.28) | collective-permute-done | bytes 131104 | tf_op jit(solution)/shard_map/ppermute | solution.py:442
  196.2 1.3 collective-permute-done.20
  198.2 5.8 %collective-permute-done.15 = bf16[76,512]{1,0:T(8,128)(2,1)S(1)} collective-permute-done((bf16[76,512]{1,0:T(8,128)(2,1)S(1)}, bf16[76,512]{1,0:T(8,128)(2,1)S(1)}, u32[]{:S(2)}, u32[]{:S(2)}) %collective-permute-start.15) | collective-permute-done | bytes 77856 | tf_op jit(solution)/shard_map/ppermute | solution.py:442
  204.0 1.3 collective-permute-start.21
  205.4 2.4 collective-permute-done.21
  207.8 2.6 collective-permute-start.16
  210.5 2.5 collective-permute-start.22
  213.3 1.6 convert_add_fusion.2
  215.0 1.3 collective-permute-start.3
  217.4 1.5 collective-permute-start.17
  219.0 5.2 %collective-permute-done.30 = bf16[256,512]{1,0:T(8,128)(2,1)S(1)} collective-permute-done((bf16[256,512]{1,0:T(8,128)(2,1)S(1)}, bf16[256,512]{1,0:T(8,128)(2,1)S(1)}, u32[]{:S(2)}, u32[]{:S(2)}) %collective-permute-start.30) | collective-permute-done | bytes 262176 | tf_op jit(solution)/shard_map/ppermute | solution.py:442
  224.5 1.3 collective-permute-start.31
  226.0 1.7 collective-permute-start.37
  228.3 1.3 collective-permute-start.9
  229.8 4.2 %collective-permute-done.23 = bf16[304,512]{1,0:T(8,128)(2,1)S(1)} collective-permute-done((bf16[304,512]{1,0:T(8,128)(2,1)S(1)}, bf16[304,512]{1,0:T(8,128)(2,1)S(1)}, u32[]{:S(2)}, u32[]{:S(2)}) %collective-permute-start.23) | collective-permute-done | bytes 311328 | tf_op jit(solution)/shard_map/ppermute | solution.py:442
  236.2 3.3 %collective-permute-done.9 = bf16[256,1024]{1,0:T(8,128)(2,1)S(1)} collective-permute-done((bf16[256,1024]{1,0:T(8,128)(2,1)S(1)}, bf16[256,1024]{1,0:T(8,128)(2,1)S(1)}, u32[]{:S(2)}, u32[]{:S(2)}) %collective-permute-start.9) | collective-permute-done | bytes 524320 | tf_op jit(solution)/shard_map/ppermute | solution.py:442
  240.3 1.3 collective-permute-start.10
  242.2 13.8 %collective-permute-start.24 = (f32[1024]{0:T(1024)S(1)}, f32[1024]{0:T(1024)S(1)}, u32[]{:S(2)}, u32[]{:S(2)}) collective-permute-start(f32[1024]{0:T(1024)S(1)} %bitcast.94), channel_id=1, source_target_pairs={{0,1},{1,0},{2,3},{3,2},{4,5},{5,4},{6,7},{7,6},{8,9},{9,8},{10,11... | collective-permute-start | bytes 12296 | tf_op jit(solution)/shard_map/ppermute | solution.py:442
  257.0 1.2 collective-permute-start.4
  261.2 6.3 %collective-permute-start.11 = (bf16[512,1024]{1,0:T(8,128)(2,1)S(1)}, bf16[512,1024]{1,0:T(8,128)(2,1)}, u32[]{:S(2)}, u32[]{:S(2)}) collective-permute-start(bf16[512,1024]{1,0:T(8,128)(2,1)S(1)} %maximum_select_fusion.3), channel_id=1, source_target_pairs={{0,1},{1,0},{2,3},{3,2},{4,5},{5,4},{6,7},{7,6},{8,9},{9,8},{10,11... | collective-permute-start | bytes 3145736 | tf_op jit(solution)/shard_map/ppermute | solution.py:442
  268.0 3.1 %collective-permute-done.4 = bf16[256,1024]{1,0:T(8,128)(2,1)S(1)} collective-permute-done((bf16[256,1024]{1,0:T(8,128)(2,1)S(1)}, bf16[256,1024]{1,0:T(8,128)(2,1)S(1)}, u32[]{:S(2)}, u32[]{:S(2)}) %collective-permute-start.4) | collective-permute-done | bytes 524320 | tf_op jit(solution)/shard_map/ppermute | solution.py:442
  271.1 1.5 maximum_select_fusion.2
  272.6 3.2 %collective-permute-start.5 = (bf16[512,1024]{1,0:T(8,128)(2,1)}, bf16[512,1024]{1,0:T(8,128)(2,1)}, u32[]{:S(2)}, u32[]{:S(2)}) collective-permute-start(bf16[512,1024]{1,0:T(8,128)(2,1)} %maximum_select_fusion.2), channel_id=1, source_target_pairs={{0,1},{1,0},{2,3},{3,2},{4,5},{5,4},{6,7},{7,6},{8,9},{9,8},{10,11... | collective-permute-start | bytes 3145736 | tf_op jit(solution)/shard_map/ppermute | solution.py:442
  276.4 1.8 fusion.28
  278.6 5.5 %copy.30 = f32[1024,2,512]{2,1,0:T(2,128)} copy(f32[1024,2,512]{2,0,1:T(8,128)S(1)} %pad_maximum_fusion) | data formatting | bytes 8388608
  284.0 3.0 %reshape.322 = f32[512,1024]{1,0:T(8,128)} reshape(f32[1024,512]{1,0:T(8,128)} %get-tuple-element.72) | data formatting | bytes 4194304 | tf_op jit(solution)/shard_map/reshape | solution.py:583
  287.1 5.0 %convert_add_fusion = f32[1,1024,1024]{2,1,0:T(8,128)} fusion(bf16[1,1024,1024]{2,1,0:T(8,128)(2,1)S(1)} %copy-done.22, bf16[1,512,1024]{2,1,0:T(8,128)(2,1)} %bitcast.17, bf16[1,512,1024]{2,1,0:T(8,128)(2,1)S(1)} %bitcast.85, pred[]{:T(512)S(6)} %eq.10), kind=kLoop, calls=%fused_computation.6 | loop fusion | flops 12582912 | bytes 8388609 | tf_op jit(solution)/shard_map/add | solution.py:572
  292.1 4.7 %maximum_select_fusion = bf16[1,1024,1024]{2,1,0:T(8,128)(2,1)} fusion(bf16[1,512,1024]{2,1,0:T(8,128)(2,1)} %bitcast.13, bf16[1,512,1024]{2,1,0:T(8,128)(2,1)} %bitcast.12, pred[]{:T(512)S(6)} %eq.10), kind=kLoop, calls=%fused_computation.25 | loop fusion | flops 9437184 | bytes 4194305 | tf_op jit(solution)/shard_map/jit(_where)/select_n | solution.py:475
  (206 shorter events, 32.5 us)
Async XLA Ops:
  0.6 21.0 %copy-start = (bf16[512,1024]{1,0:T(8,128)(2,1)S(1)}, bf16[512,1024]{1,0:T(8,128)(2,1)}, u32[]{:S(2)}) copy-start(bf16[512,1024]{1,0:T(8,128)(2,1)} %param.24) | copy-start | bytes 3145732
  3.0 3.8 %copy-start.39 = (f32[4,512]{1,0:T(4,128)S(1)}, f32[4,512]{1,0:T(4,128)}, u32[]{:S(2)}) copy-start(f32[4,512]{1,0:T(4,128)} %param.17) | copy-start | bytes 24580
  3.0 3.8 %copy-start.12 = (bf16[1,1024,1024]{2,1,0:T(8,128)(2,1)S(1)}, bf16[1,1024,1024]{2,1,0:T(8,128)(2,1)}, u32[]{:S(2)}) copy-start(bf16[1,1024,1024]{2,1,0:T(8,128)(2,1)} %param.13) | copy-start | bytes 6291460
  3.0 3.8 %copy-start.35 = (f32[1024]{0:T(1024)S(1)}, f32[1024]{0:T(1024)}, u32[]{:S(2)}) copy-start(f32[1024]{0:T(1024)} %param.15) | copy-start | bytes 12292
  10.8 5.2 %copy-start.2 = (bf16[1024,512]{1,0:T(8,128)(2,1)}, bf16[1024,512]{1,0:T(8,128)(2,1)S(1)}, u32[]{:S(2)}) copy-start(bf16[1024,512]{1,0:T(8,128)(2,1)S(1)} %get-tuple-element.70.drive_ref) | copy-start | bytes 3145732
  11.3 14.7 %collective-permute-start = (bf16[1024,96]{1,0:T(8,128)(2,1)S(1)}, bf16[1024,96]{1,0:T(8,128)(2,1)S(1)}, u32[]{:S(2)}, u32[]{:S(2)}) collective-permute-start(bf16[1024,96]{1,0:T(8,128)(2,1)S(1)} %convolution_convert_fusion.2), channel_id=1, source_target_pairs={{0,1},{1,0},{2,3},{3,2},{4,5},{5,4},{6,7},{7,6},{8,9},{9,8},{10,11... | collective-permute-start | bytes 589832 | tf_op jit(solution)/shard_map/ppermute | solution.py:442
  16.1 5.6 %copy-start.34 = (bf16[64,512]{1,0:T(8,128)(2,1)S(1)}, bf16[64,512]{1,0:T(8,128)(2,1)}, u32[]{:S(2)}) copy-start(bf16[64,512]{1,0:T(8,128)(2,1)} %sw_ref.1) | copy-start | bytes 196612
  21.7 5.6 %copy-start.37 = (f32[256]{0:T(256)}, f32[256]{0:T(256)S(1)}, u32[]{:S(2)}) copy-start(f32[256]{0:T(256)S(1)} %dynamic-slice.4) | copy-start | bytes 3076
  26.0 7.9 %collective-permute-start.1 = (bf16[1024,96]{1,0:T(8,128)(2,1)S(1)}, bf16[1024,96]{1,0:T(8,128)(2,1)S(1)}, u32[]{:S(2)}, u32[]{:S(2)}) collective-permute-start(bf16[1024,96]{1,0:T(8,128)(2,1)S(1)} %add_convert_fusion.3), channel_id=1, source_target_pairs={{0,2},{1,3},{2,0},{3,1},{4,6},{5,7},{6,4},{7,5},{8,10},{9,11},{10,... | collective-permute-start | bytes 589832 | tf_op jit(solution)/shard_map/ppermute | solution.py:442
  34.7 35.3 %copy-start.21 = (bf16[1,1024,1024]{2,1,0:T(8,128)(2,1)S(1)}, bf16[1,1024,1024]{2,1,0:T(8,128)(2,1)}, u32[]{:S(2)}) copy-start(bf16[1,1024,1024]{2,1,0:T(8,128)(2,1)} %param.25) | copy-start | bytes 6291460
  73.7 3.8 %copy-start.9 = (f32[1024,96]{1,0:T(8,128)S(1)}, f32[1024,96]{1,0:T(8,128)}, u32[]{:S(2)}) copy-start(f32[1024,96]{1,0:T(8,128)} %get-tuple-element.32.pin_ref) | copy-start | bytes 1179652
  73.7 3.8 %copy-start.10 = (f32[16,512]{1,0:T(8,128)S(1)}, f32[16,512]{1,0:T(8,128)}, u32[]{:S(2)}) copy-start(f32[16,512]{1,0:T(8,128)} %dlog_ref.3) | copy-start | bytes 98308
  73.7 3.8 %copy-start.11 = (f32[512]{0:T(512)S(1)}, f32[512]{0:T(512)}, u32[]{:S(2)}) copy-start(f32[512]{0:T(512)} %param.23) | copy-start | bytes 6148
  77.5 30.6 %copy-start.42 = (f32[1,512]{1,0:T(1,128)S(1)}, f32[1,512]{1,0:T(1,128)}, u32[]{:S(2)}) copy-start(f32[1,512]{1,0:T(1,128)} %get-tuple-element.38) | copy-start | bytes 6148
  77.5 31.2 %copy-start.13 = (bf16[1,1024,1024]{2,1,0:T(8,128)(2,1)S(1)}, bf16[1,1024,1024]{2,1,0:T(8,128)(2,1)}, u32[]{:S(2)}) copy-start(bf16[1,1024,1024]{2,1,0:T(8,128)(2,1)} %param.13) | copy-start | bytes 6291460
  77.5 31.2 %copy-start.28 = (bf16[1024,512]{1,0:T(8,128)(2,1)S(1)}, bf16[1024,512]{1,0:T(8,128)(2,1)}, u32[]{:S(2)}) copy-start(bf16[1024,512]{1,0:T(8,128)(2,1)} %get-tuple-element.35) | copy-start | bytes 3145732
  106.6 18.9 %collective-permute-start.6 = (bf16[1024,96]{1,0:T(8,128)(2,1)S(1)}, bf16[1024,96]{1,0:T(8,128)(2,1)S(1)}, u32[]{:S(2)}, u32[]{:S(2)}) collective-permute-start(bf16[1024,96]{1,0:T(8,128)(2,1)S(1)} %get-tuple-element.34), channel_id=1, source_target_pairs={{0,1},{1,0},{2,3},{3,2},{4,5},{5,4},{6,7},{7,6},{8,9},{9,8},{10,11... | collective-permute-start | bytes 589832 | tf_op jit(solution)/shard_map/ppermute | solution.py:442
  111.3 52.8 %collective-permute-start.26 = (bf16[512,512]{1,0:T(8,128)(2,1)}, bf16[512,512]{1,0:T(8,128)(2,1)}, u32[]{:S(2)}, u32[]{:S(2)}) collective-permute-start(bf16[512,512]{1,0:T(8,128)(2,1)} %constant_dynamic-slice_fusion.1), channel_id=1, source_target_pairs={{0,4},{4,0},{8,12},{12,8},{16,20},{20,16},{24,28},{28,24},{1,5},{5... | collective-permute-start | bytes 1572872 | tf_op jit(solution)/shard_map/ppermute | solution.py:442
  119.9 46.5 %collective-permute-start.32 = (bf16[512,512]{1,0:T(8,128)(2,1)}, bf16[512,512]{1,0:T(8,128)(2,1)}, u32[]{:S(2)}, u32[]{:S(2)}) collective-permute-start(bf16[512,512]{1,0:T(8,128)(2,1)} %constant_dynamic-slice_fusion), channel_id=1, source_target_pairs={{0,8},{4,12},{8,0},{12,4},{16,24},{20,28},{24,16},{28,20},{1,9},{5... | collective-permute-start | bytes 1572872 | tf_op jit(solution)/shard_map/ppermute | solution.py:442
  121.8 12.3 %copy-start.19 = (f32[1024,512]{1,0:T(8,128)S(1)}, f32[1024,512]{1,0:T(8,128)}, u32[]{:S(2)}) copy-start(f32[1024,512]{1,0:T(8,128)} %get-tuple-element.71) | copy-start | bytes 6291460
  124.8 88.5 %collective-permute-start.2 = (bf16[512,1024]{1,0:T(8,128)(2,1)}, bf16[512,1024]{1,0:T(8,128)(2,1)}, u32[]{:S(2)}, u32[]{:S(2)}) collective-permute-start(bf16[512,1024]{1,0:T(8,128)(2,1)} %dynamic-slice_convert_fusion.1), channel_id=1, source_target_pairs={{0,1},{1,0},{2,3},{3,2},{4,5},{5,4},{6,7},{7,6},{8,9},{9,8},{10,11... | collective-permute-start | bytes 3145736 | tf_op jit(solution)/shard_map/ppermute | solution.py:442
  125.5 8.6 %copy-start.18 = (f32[1024,512]{1,0:T(8,128)S(1)}, f32[1024,512]{1,0:T(8,128)}, u32[]{:S(2)}) copy-start(f32[1024,512]{1,0:T(8,128)} %copy-done.17) | copy-start | bytes 6291460
  125.5 8.5 %copy-start.6 = (f32[1024,512]{1,0:T(8,128)S(1)}, f32[1024,512]{1,0:T(8,128)}, u32[]{:S(2)}) copy-start(f32[1024,512]{1,0:T(8,128)} %copy-done.5) | copy-start | bytes 6291460
  125.6 8.1 %collective-permute-start.7 = (bf16[1024,96]{1,0:T(8,128)(2,1)S(1)}, bf16[1024,96]{1,0:T(8,128)(2,1)S(1)}, u32[]{:S(2)}, u32[]{:S(2)}) collective-permute-start(bf16[1024,96]{1,0:T(8,128)(2,1)S(1)} %add_convert_fusion.1), channel_id=1, source_target_pairs={{0,2},{1,3},{2,0},{3,1},{4,6},{5,7},{6,4},{7,5},{8,10},{9,11},{10,... | collective-permute-start | bytes 589832 | tf_op jit(solution)/shard_map/ppermute | solution.py:442
  160.7 4.4 %copy-start.31 = (bf16[1024,512]{1,0:T(8,128)(2,1)S(1)}, bf16[1024,512]{1,0:T(8,128)(2,1)}, u32[]{:S(2)}) copy-start(bf16[1024,512]{1,0:T(8,128)(2,1)} %copy-done.30) | copy-start | bytes 3145732
  160.8 8.6 %collective-permute-start.12 = (bf16[304,512]{1,0:T(8,128)(2,1)S(1)}, bf16[304,512]{1,0:T(8,128)(2,1)S(1)}, u32[]{:S(2)}, u32[]{:S(2)}) collective-permute-start(bf16[304,512]{1,0:T(8,128)(2,1)S(1)} %constant_dynamic-slice_fusion.3), channel_id=1, source_target_pairs={{0,4},{4,0},{8,12},{12,8},{16,20},{20,16},{24,28},{28,24},{1,5},{5... | collective-permute-start | bytes 933896 | tf_op jit(solution)/shard_map/ppermute | solution.py:442
  162.1 8.5 %collective-permute-start.18 = (bf16[304,512]{1,0:T(8,128)(2,1)S(1)}, bf16[304,512]{1,0:T(8,128)(2,1)S(1)}, u32[]{:S(2)}, u32[]{:S(2)}) collective-permute-start(bf16[304,512]{1,0:T(8,128)(2,1)S(1)} %constant_dynamic-slice_fusion.2), channel_id=1, source_target_pairs={{0,8},{4,12},{8,0},{12,4},{16,24},{20,28},{24,16},{28,20},{1,9},{5... | collective-permute-start | bytes 933896 | tf_op jit(solution)/shard_map/ppermute | solution.py:442
  162.2 5.9 %copy-start.24 = (bf16[1024,512]{1,0:T(8,128)(2,1)S(1)}, bf16[1024,512]{1,0:T(8,128)(2,1)}, u32[]{:S(2)}) copy-start(bf16[1024,512]{1,0:T(8,128)(2,1)} %reshape.321) | copy-start | bytes 3145732
  164.1 61.9 %collective-permute-start.8 = (bf16[512,1024]{1,0:T(8,128)(2,1)S(1)}, bf16[512,1024]{1,0:T(8,128)(2,1)S(1)}, u32[]{:S(2)}, u32[]{:S(2)}) collective-permute-start(bf16[512,1024]{1,0:T(8,128)(2,1)S(1)} %dynamic-slice_convert_fusion), channel_id=1, source_target_pairs={{0,1},{1,0},{2,3},{3,2},{4,5},{5,4},{6,7},{7,6},{8,9},{9,8},{10,11... | collective-permute-start | bytes 3145736 | tf_op jit(solution)/shard_map/ppermute | solution.py:442
  166.3 14.3 %collective-permute-start.27 = (bf16[256,512]{1,0:T(8,128)(2,1)S(1)}, bf16[256,512]{1,0:T(8,128)(2,1)S(1)}, u32[]{:S(2)}, u32[]{:S(2)}) collective-permute-start(bf16[256,512]{1,0:T(8,128)(2,1)S(1)} %dynamic-slice_convert_fusion.5), channel_id=1, source_target_pairs={{0,8},{4,12},{8,0},{12,4},{16,24},{20,28},{24,16},{28,20},{1,9},{5... | collective-permute-start | bytes 786440 | tf_op jit(solution)/shard_map/ppermute | solution.py:442
  169.4 11.3 %collective-permute-start.33 = (bf16[256,512]{1,0:T(8,128)(2,1)S(1)}, bf16[256,512]{1,0:T(8,128)(2,1)S(1)}, u32[]{:S(2)}, u32[]{:S(2)}) collective-permute-start(bf16[256,512]{1,0:T(8,128)(2,1)S(1)} %dynamic-slice_convert_fusion.4), channel_id=1, source_target_pairs={{0,16},{4,20},{8,24},{12,28},{16,0},{20,4},{24,8},{28,12},{1,17},{... | collective-permute-start | bytes 786440 | tf_op jit(solution)/shard_map/ppermute | solution.py:442
  170.6 16.1 %collective-permute-start.13 = (bf16[152,512]{1,0:T(8,128)(2,1)S(1)}, bf16[152,512]{1,0:T(8,128)(2,1)S(1)}, u32[]{:S(2)}, u32[]{:S(2)}) collective-permute-start(bf16[152,512]{1,0:T(8,128)(2,1)S(1)} %dynamic-slice_convert_fusion.7), channel_id=1, source_target_pairs={{0,8},{4,12},{8,0},{12,4},{16,24},{20,28},{24,16},{28,20},{1,9},{5... | collective-permute-start | bytes 466952 | tf_op jit(solution)/shard_map/ppermute | solution.py:442
  180.6 6.3 %collective-permute-start.19 = (bf16[152,512]{1,0:T(8,128)(2,1)S(1)}, bf16[152,512]{1,0:T(8,128)(2,1)S(1)}, u32[]{:S(2)}, u32[]{:S(2)}) collective-permute-start(bf16[152,512]{1,0:T(8,128)(2,1)S(1)} %dynamic-slice_convert_fusion.6), channel_id=1, source_target_pairs={{0,16},{4,20},{8,24},{12,28},{16,0},{20,4},{24,8},{28,12},{1,17},{... | collective-permute-start | bytes 466952 | tf_op jit(solution)/shard_map/ppermute | solution.py:442
  180.7 13.2 %collective-permute-start.28 = (bf16[128,512]{1,0:T(8,128)(2,1)S(1)}, bf16[128,512]{1,0:T(8,128)(2,1)S(1)}, u32[]{:S(2)}, u32[]{:S(2)}) collective-permute-start(bf16[128,512]{1,0:T(8,128)(2,1)S(1)} %dynamic-slice_convert_fusion.9), channel_id=1, source_target_pairs={{0,16},{4,20},{8,24},{12,28},{16,0},{20,4},{24,8},{28,12},{1,17},{... | collective-permute-start | bytes 393224 | tf_op jit(solution)/shard_map/ppermute | solution.py:442
  186.8 7.7 %collective-permute-start.34 = (bf16[128,512]{1,0:T(8,128)(2,1)S(1)}, bf16[128,512]{1,0:T(8,128)(2,1)S(1)}, u32[]{:S(2)}, u32[]{:S(2)}) collective-permute-start(bf16[128,512]{1,0:T(8,128)(2,1)S(1)} %dynamic-slice_convert_fusion.8), channel_id=1, source_target_pairs={{0,4},{4,0},{8,12},{12,8},{16,20},{20,16},{24,28},{28,24},{1,5},{5... | collective-permute-start | bytes 393224 | tf_op jit(solution)/shard_map/ppermute | solution.py:442
  186.8 26.5 %copy-start.25 = (f32[1024,1024]{1,0:T(8,128)S(1)}, f32[1024,1024]{1,0:T(8,128)}, u32[]{:S(2)}) copy-start(f32[1024,1024]{1,0:T(8,128)} %fusion.31) | copy-start | bytes 12582916
  186.9 8.9 %collective-permute-start.14 = (bf16[76,512]{1,0:T(8,128)(2,1)S(1)}, bf16[76,512]{1,0:T(8,128)(2,1)S(1)}, u32[]{:S(2)}, u32[]{:S(2)}) collective-permute-start(bf16[76,512]{1,0:T(8,128)(2,1)S(1)} %dynamic-slice_convert_fusion.11), channel_id=1, source_target_pairs={{0,16},{4,20},{8,24},{12,28},{16,0},{20,4},{24,8},{28,12},{1,17},{... | collective-permute-start | bytes 233480 | tf_op jit(solution)/shard_map/ppermute | solution.py:442
  194.0 3.6 %collective-permute-start.20 = (bf16[76,512]{1,0:T(8,128)(2,1)S(1)}, bf16[76,512]{1,0:T(8,128)(2,1)S(1)}, u32[]{:S(2)}, u32[]{:S(2)}) collective-permute-start(bf16[76,512]{1,0:T(8,128)(2,1)S(1)} %dynamic-slice_convert_fusion.10), channel_id=1, source_target_pairs={{0,4},{4,0},{8,12},{12,8},{16,20},{20,16},{24,28},{28,24},{1,5},{5... | collective-permute-start | bytes 233480 | tf_op jit(solution)/shard_map/ppermute | solution.py:442
  194.5 16.0 %collective-permute-start.29 = (bf16[128,512]{1,0:T(8,128)(2,1)S(1)}, bf16[128,512]{1,0:T(8,128)(2,1)S(1)}, u32[]{:S(2)}, u32[]{:S(2)}) collective-permute-start(bf16[128,512]{1,0:T(8,128)(2,1)S(1)} %add_convert_fusion.5), channel_id=1, source_target_pairs={{0,16},{4,20},{8,24},{12,28},{16,0},{20,4},{24,8},{28,12},{1,17},{... | collective-permute-start | bytes 393224 | tf_op jit(solution)/shard_map/ppermute | solution.py:442
  195.7 17.3 %collective-permute-start.35 = (bf16[128,512]{1,0:T(8,128)(2,1)S(1)}, bf16[128,512]{1,0:T(8,128)(2,1)S(1)}, u32[]{:S(2)}, u32[]{:S(2)}) collective-permute-start(bf16[128,512]{1,0:T(8,128)(2,1)S(1)} %add_convert_fusion.4), channel_id=1, source_target_pairs={{0,4},{4,0},{8,12},{12,8},{16,20},{20,16},{24,28},{28,24},{1,5},{5... | collective-permute-start | bytes 393224 | tf_op jit(solution)/shard_map/ppermute | solution.py:442
  197.6 6.4 %collective-permute-start.15 = (bf16[76,512]{1,0:T(8,128)(2,1)S(1)}, bf16[76,512]{1,0:T(8,128)(2,1)S(1)}, u32[]{:S(2)}, u32[]{:S(2)}) collective-permute-start(bf16[76,512]{1,0:T(8,128)(2,1)S(1)} %add_convert_fusion.7), channel_id=1, source_target_pairs={{0,16},{4,20},{8,24},{12,28},{16,0},{20,4},{24,8},{28,12},{1,17},{... | collective-permute-start | bytes 233480 | tf_op jit(solution)/shard_map/ppermute | solution.py:442
  204.0 3.8 %collective-permute-start.21 = (bf16[76,512]{1,0:T(8,128)(2,1)S(1)}, bf16[76,512]{1,0:T(8,128)(2,1)S(1)}, u32[]{:S(2)}, u32[]{:S(2)}) collective-permute-start(bf16[76,512]{1,0:T(8,128)(2,1)S(1)} %add_convert_fusion.6), channel_id=1, source_target_pairs={{0,4},{4,0},{8,12},{12,8},{16,20},{20,16},{24,28},{28,24},{1,5},{5... | collective-permute-start | bytes 233480 | tf_op jit(solution)/shard_map/ppermute | solution.py:442
  207.8 7.2 %collective-permute-start.16 = (bf16[152,512]{1,0:T(8,128)(2,1)S(1)}, bf16[152,512]{1,0:T(8,128)(2,1)S(1)}, u32[]{:S(2)}, u32[]{:S(2)}) collective-permute-start(bf16[152,512]{1,0:T(8,128)(2,1)S(1)} %maximum_select_fusion.14), channel_id=1, source_target_pairs={{0,8},{4,12},{8,0},{12,4},{16,24},{20,28},{24,16},{28,20},{1,9},{5... | collective-permute-start | bytes 466952 | tf_op jit(solution)/shard_map/ppermute | solution.py:442
  210.5 6.9 %collective-permute-start.22 = (bf16[152,512]{1,0:T(8,128)(2,1)S(1)}, bf16[152,512]{1,0:T(8,128)(2,1)S(1)}, u32[]{:S(2)}, u32[]{:S(2)}) collective-permute-start(bf16[152,512]{1,0:T(8,128)(2,1)S(1)} %maximum_select_fusion.15), channel_id=1, source_target_pairs={{0,16},{4,20},{8,24},{12,28},{16,0},{20,4},{24,8},{28,12},{1,17},{... | collective-permute-start | bytes 466952 | tf_op jit(solution)/shard_map/ppermute | solution.py:442
  213.1 11.2 %collective-permute-start.30 = (bf16[256,512]{1,0:T(8,128)(2,1)S(1)}, bf16[256,512]{1,0:T(8,128)(2,1)S(1)}, u32[]{:S(2)}, u32[]{:S(2)}) collective-permute-start(bf16[256,512]{1,0:T(8,128)(2,1)S(1)} %maximum_select_fusion.12), channel_id=1, source_target_pairs={{0,8},{4,12},{8,0},{12,4},{16,24},{20,28},{24,16},{28,20},{1,9},{5... | collective-permute-start | bytes 786440 | tf_op jit(solution)/shard_map/ppermute | solution.py:442
  213.2 11.3 %collective-permute-start.36 = (bf16[256,512]{1,0:T(8,128)(2,1)S(1)}, bf16[256,512]{1,0:T(8,128)(2,1)S(1)}, u32[]{:S(2)}, u32[]{:S(2)}) collective-permute-start(bf16[256,512]{1,0:T(8,128)(2,1)S(1)} %maximum_select_fusion.13), channel_id=1, source_target_pairs={{0,16},{4,20},{8,24},{12,28},{16,0},{20,4},{24,8},{28,12},{1,17},{... | collective-permute-start | bytes 786440 | tf_op jit(solution)/shard_map/ppermute | solution.py:442
  214.9 12.8 %copy-start.15 = (f32[1024,1024]{1,0:T(8,128)S(1)}, f32[1024,1024]{1,0:T(8,128)}, u32[]{:S(2)}) copy-start(f32[1024,1024]{1,0:T(8,128)} %get-tuple-element.86) | copy-start | bytes 12582916
  215.0 24.8 %collective-permute-start.3 = (bf16[256,1024]{1,0:T(8,128)(2,1)S(1)}, bf16[256,1024]{1,0:T(8,128)(2,1)S(1)}, u32[]{:S(2)}, u32[]{:S(2)}) collective-permute-start(bf16[256,1024]{1,0:T(8,128)(2,1)S(1)} %dynamic-slice_convert_fusion.3), channel_id=1, source_target_pairs={{0,2},{1,3},{2,0},{3,1},{4,6},{5,7},{6,4},{7,5},{8,10},{9,11},{10,... | collective-permute-start | bytes 1572872 | tf_op jit(solution)/shard_map/ppermute | solution.py:442
  217.4 10.9 %collective-permute-start.17 = (bf16[304,512]{1,0:T(8,128)(2,1)S(1)}, bf16[304,512]{1,0:T(8,128)(2,1)S(1)}, u32[]{:S(2)}, u32[]{:S(2)}) collective-permute-start(bf16[304,512]{1,0:T(8,128)(2,1)S(1)} %maximum_select_fusion.10), channel_id=1, source_target_pairs={{0,4},{4,0},{8,12},{12,8},{16,20},{20,16},{24,28},{28,24},{1,5},{5... | collective-permute-start | bytes 933896 | tf_op jit(solution)/shard_map/ppermute | solution.py:442
  224.2 9.8 %collective-permute-start.23 = (bf16[304,512]{1,0:T(8,128)(2,1)S(1)}, bf16[304,512]{1,0:T(8,128)(2,1)S(1)}, u32[]{:S(2)}, u32[]{:S(2)}) collective-permute-start(bf16[304,512]{1,0:T(8,128)(2,1)S(1)} %maximum_select_fusion.11), channel_id=1, source_target_pairs={{0,8},{4,12},{8,0},{12,4},{16,24},{20,28},{24,16},{28,20},{1,9},{5... | collective-permute-start | bytes 933896 | tf_op jit(solution)/shard_map/ppermute | solution.py:442
  224.5 35.8 %collective-permute-start.31 = (bf16[512,512]{1,0:T(8,128)(2,1)S(1)}, bf16[512,512]{1,0:T(8,128)(2,1)S(1)}, u32[]{:S(2)}, u32[]{:S(2)}) collective-permute-start(bf16[512,512]{1,0:T(8,128)(2,1)S(1)} %maximum_select_fusion.8), channel_id=1, source_target_pairs={{0,4},{4,0},{8,12},{12,8},{16,20},{20,16},{24,28},{28,24},{1,5},{5... | collective-permute-start | bytes 1572872 | tf_op jit(solution)/shard_map/ppermute | solution.py:442
  226.0 41.5 %collective-permute-start.37 = (bf16[512,512]{1,0:T(8,128)(2,1)S(1)}, bf16[512,512]{1,0:T(8,128)(2,1)S(1)}, u32[]{:S(2)}, u32[]{:S(2)}) collective-permute-start(bf16[512,512]{1,0:T(8,128)(2,1)S(1)} %maximum_select_fusion.9), channel_id=1, source_target_pairs={{0,8},{4,12},{8,0},{12,4},{16,24},{20,28},{24,16},{28,20},{1,9},{5... | collective-permute-start | bytes 1572872 | tf_op jit(solution)/shard_map/ppermute | solution.py:442
  228.3 11.2 %collective-permute-start.9 = (bf16[256,1024]{1,0:T(8,128)(2,1)S(1)}, bf16[256,1024]{1,0:T(8,128)(2,1)S(1)}, u32[]{:S(2)}, u32[]{:S(2)}) collective-permute-start(bf16[256,1024]{1,0:T(8,128)(2,1)S(1)} %dynamic-slice_convert_fusion.2), channel_id=1, source_target_pairs={{0,2},{1,3},{2,0},{3,1},{4,6},{5,7},{6,4},{7,5},{8,10},{9,11},{10,... | collective-permute-start | bytes 1572872 | tf_op jit(solution)/shard_map/ppermute | solution.py:442
  234.6 4.9 %copy-start.16 = (f32[1,1024,1024]{2,1,0:T(8,128)S(1)}, f32[1,1024,1024]{2,1,0:T(8,128)}, u32[]{:S(2)}) copy-start(f32[1,1024,1024]{2,1,0:T(8,128)} %convert_element_type.258) | copy-start | bytes 12582916
  234.8 4.7 %copy-start.36 = (f32[1024]{0:T(1024)S(1)}, f32[1024]{0:T(1024)}, u32[]{:S(2)}) copy-start(f32[1024]{0:T(1024)} %param.15) | copy-start | bytes 12292
  235.5 4.3 %copy-start.38 = (f32[256]{0:T(256)S(1)}, f32[256]{0:T(256)}, u32[]{:S(2)}) copy-start(f32[256]{0:T(256)} %copy-done.37) | copy-start | bytes 3076
  235.5 4.3 %copy-start.40 = (f32[256,1]{0,1:T(1,128)S(1)}, f32[256,1]{0,1:T(1,128)}, u32[]{:S(2)}) copy-start(f32[256,1]{0,1:T(1,128)} %multiply_multiply_fusion.1) | copy-start | bytes 3076
  240.3 20.5 %collective-permute-start.10 = (bf16[256,1024]{1,0:T(8,128)(2,1)S(1)}, bf16[256,1024]{1,0:T(8,128)(2,1)S(1)}, u32[]{:S(2)}, u32[]{:S(2)}) collective-permute-start(bf16[256,1024]{1,0:T(8,128)(2,1)S(1)} %get-tuple-element.74), channel_id=1, source_target_pairs={{0,2},{1,3},{2,0},{3,1},{4,6},{5,7},{6,4},{7,5},{8,10},{9,11},{10,... | collective-permute-start | bytes 1572872 | tf_op jit(solution)/shard_map/ppermute | solution.py:442
  242.2 14.6 %collective-permute-start.24 = (f32[1024]{0:T(1024)S(1)}, f32[1024]{0:T(1024)S(1)}, u32[]{:S(2)}, u32[]{:S(2)}) collective-permute-start(f32[1024]{0:T(1024)S(1)} %bitcast.94), channel_id=1, source_target_pairs={{0,1},{1,0},{2,3},{3,2},{4,5},{5,4},{6,7},{7,6},{8,9},{9,8},{10,11... | collective-permute-start | bytes 12296 | tf_op jit(solution)/shard_map/ppermute | solution.py:442
  256.8 2.9 collective-permute-start.25
  257.0 14.0 %collective-permute-start.4 = (bf16[256,1024]{1,0:T(8,128)(2,1)S(1)}, bf16[256,1024]{1,0:T(8,128)(2,1)S(1)}, u32[]{:S(2)}, u32[]{:S(2)}) collective-permute-start(bf16[256,1024]{1,0:T(8,128)(2,1)S(1)} %get-tuple-element.75), channel_id=1, source_target_pairs={{0,2},{1,3},{2,0},{3,1},{4,6},{5,7},{6,4},{7,5},{8,10},{9,11},{10,... | collective-permute-start | bytes 1572872 | tf_op jit(solution)/shard_map/ppermute | solution.py:442
  261.2 25.9 %collective-permute-start.11 = (bf16[512,1024]{1,0:T(8,128)(2,1)S(1)}, bf16[512,1024]{1,0:T(8,128)(2,1)}, u32[]{:S(2)}, u32[]{:S(2)}) collective-permute-start(bf16[512,1024]{1,0:T(8,128)(2,1)S(1)} %maximum_select_fusion.3), channel_id=1, source_target_pairs={{0,1},{1,0},{2,3},{3,2},{4,5},{5,4},{6,7},{7,6},{8,9},{9,8},{10,11... | collective-permute-start | bytes 3145736 | tf_op jit(solution)/shard_map/ppermute | solution.py:442
  272.6 19.5 %collective-permute-start.5 = (bf16[512,1024]{1,0:T(8,128)(2,1)}, bf16[512,1024]{1,0:T(8,128)(2,1)}, u32[]{:S(2)}, u32[]{:S(2)}) collective-permute-start(bf16[512,1024]{1,0:T(8,128)(2,1)} %maximum_select_fusion.2), channel_id=1, source_target_pairs={{0,1},{1,0},{2,3},{3,2},{4,5},{5,4},{6,7},{7,6},{8,9},{9,8},{10,11... | collective-permute-start | bytes 3145736 | tf_op jit(solution)/shard_map/ppermute | solution.py:442
  292.1 4.7 %copy-start.1 = (bf16[512,1024]{1,0:T(8,128)(2,1)S(1)}, bf16[512,1024]{1,0:T(8,128)(2,1)}, u32[]{:S(2)}) copy-start(bf16[512,1024]{1,0:T(8,128)(2,1)} %param.24) | copy-start | bytes 3145732
  (17 other events, 41.9 us)

commit v2 on v1

v2 whole, which is shorter than its diff:
```python
import functools

import jax
import jax.numpy as jnp
from jax import lax
from jax.experimental import pallas as pl
from jax.experimental.pallas import tpu as pltpu
from jax.sharding import PartitionSpec as P

T = 16
LC = 128
PIECES = (5, 2, 0)
LOG2E = 1.4426950408889634
LN2 = 0.6931471805599453
F32 = jnp.float32
BF = jnp.bfloat16
NT = (((1,), (1,)), ((), ()))
STRIDED = True
epsilon = 1e-05


def iota(shape, d):
    return lax.broadcasted_iota(jnp.int32, shape, d)


def mm(a, b):
    return jnp.dot(a, b, preferred_element_type=F32)


def mm_nt(a, b):
    return lax.dot_general(a, b, NT, preferred_element_type=F32)


def row(ref, g, t, n):
    if STRIDED:
        pair = [ref[2 * g + j, pl.ds(t, 8, stride=0), :] for j in (0, 1)]
        wide = jnp.concatenate(pair, axis=1)
        return jnp.concatenate([wide] * (n // 8), axis=0)
    pair = [jnp.broadcast_to(ref[2 * g + j, pl.ds(t, 1), :], (n, 128)) for j in (0, 1)]
    return jnp.concatenate(pair, axis=1)


def spread(base, p, n):
    return (iota((p, T * n), 0) == base + lax.rem(iota((p, T * n), 1), n)).astype(BF)


def pick(base, p, n):
    return (iota((n, p), 1) == base + iota((n, p), 0)).astype(BF)


def fold(base, p, n):
    return (iota((T * n, p), 1) == base + lax.rem(iota((T * n, p), 0), n)).astype(BF)


def blockdiag(rows, n):
    return lax.rem(iota((rows, T * n), 0), T) == lax.div(iota((rows, T * n), 1), n)


def split(ref, value):
    for g in range(value.shape[1] // 128):
        ref[g] = value[:, g * 128 : (g + 1) * 128]


def softplus(x):
    e = jnp.exp2(jnp.abs(x) * -LOG2E)
    small = e * (1.0 - e * (0.5 - e * (1.0 / 3.0 - e * 0.25)))
    return jnp.maximum(x, 0.0) + jnp.where(e < 0.03125, small, jnp.log2(1.0 + e) * LN2)


def one_minus_exp(s):
    small = s * (1.0 - s * (0.5 - s * (1.0 / 6.0 - s * (1.0 / 24.0))))
    return jnp.where(s < 0.0625, small, 1.0 - jnp.exp2(s * -LOG2E))


def front_kernel(ng, prefix_ref, proj_ref, sw_ref, bias_ref, drive_ref, z_ref, dg_ref, dlog_ref, skip_ref,
                 gated_ref, dz_ref, step_ref, dy_ref, hprev_ref, ag_ref, wg_ref, part_ref, gskip_ref,
                 step_s, sd_s, dy_s, sig_s, keep_s, bt_s, ct_s, cbd_s, rc_s, hg_s, g_s, qg_s, st_f, st_h, st_q):
    lc, c = drive_ref.shape
    p = proj_ref.shape[1]
    n = dlog_ref.shape[0]
    r = p - 2 * n
    tn = T * n
    nb = lc // T
    groups = c // 256
    i = pl.program_id(0)
    pfx = prefix_ref[0]
    rate2 = -jnp.exp(dlog_ref[...]) * LOG2E
    lanes = [slice(g * 256, (g + 1) * 256) for g in range(groups)]

    def positions(chunk):
        return iota((lc, 1), 0) + chunk * lc

    def col(ref, t0, k):
        one = jnp.broadcast_to(pltpu.roll(ref[...], lax.rem(lc - t0, lc), 1)[:, k : k + 1], (n, 128))
        return jnp.concatenate([one, one], axis=1)

    @pl.when(i == 0)
    def _():
        st_f[...] = jnp.zeros_like(st_f)
        st_h[...] = jnp.zeros_like(st_h)
        st_q[...] = jnp.zeros_like(st_q)
        gskip_ref[...] = jnp.zeros_like(gskip_ref)

    proj = proj_ref[...]
    bt_s[...] = mm_nt(pick(r, p, n), proj)

    @pl.when(i < ng)
    def _():
        chunk = ng - 1 - i
        step = softplus(mm(proj[:, :r], sw_ref[...]) + bias_ref[...])
        keep_s[chunk] = step

        @pl.when(chunk * lc < pfx)
        def _():
            mask = (positions(chunk) < pfx).astype(F32)
            split(step_s, step)
            split(sd_s, step * drive_ref[...].astype(F32) * mask)
            base = chunk * (lc * n)

            def body(ir, state):
                t0 = (nb - 1 - ir) * T
                state = list(state)
                bt = bt_s[:, t0 : t0 + T]
                for k in range(T - 1, -1, -1):
                    t = t0 + k
                    bb = jnp.broadcast_to(bt[:, k : k + 1], (n, 128))
                    bb = jnp.concatenate([bb, bb], axis=1)
                    at = pl.ds(pl.multiple_of(base + t * n, n), n)
                    for g in range(groups):
                        q = jnp.exp2(row(step_s, g, t, n) * rate2[:, lanes[g]]) * state[g]
                        state[g] = q + bb * row(sd_s, g, t, n)
                        qg_s[at, lanes[g]] = q.astype(BF)
                        g_s[at, lanes[g]] = state[g].astype(BF)
                return tuple(state)

            out = tuple(st_f[g] for g in range(groups))
            for ir in range(nb):
                out = body(ir, out)
            for g in range(groups):
                st_f[g] = out[g]

    @pl.when(i >= ng)
    def _():
        chunk = i - ng

        @pl.when(chunk < ng)
        def _():
            step_ref[...] = keep_s[jnp.minimum(chunk, ng - 1)]

        @pl.when(chunk >= ng)
        def _():
            step_ref[...] = softplus(mm(proj[:, :r], sw_ref[...]) + bias_ref[...])

        step = step_ref[...]
        drive = drive_ref[...].astype(F32)
        z = z_ref[...]
        sig = 1.0 / (1.0 + jnp.exp2(z * -LOG2E))
        sig_s[...] = sig
        dy = dg_ref[...] * (z * sig)
        dy_ref[...] = dy
        gskip_ref[...] += jnp.sum(dy * drive, axis=0, keepdims=True)
        split(step_s, step)
        split(sd_s, step * drive)
        ct_s[...] = mm_nt(pick(r + n, p, n), proj)
        cbd_s[...] = jnp.where(blockdiag(lc, n), mm(proj, spread(r + n, p, n)), 0.0).astype(BF)
        diag = blockdiag(T, n)

        def mxu(b, buf):
            rows = pl.ds(b * T, T)
            kept = {}

            def y_part(g):
                kept[g] = mm(cbd_s[rows, :], hg_s[buf, :, lanes[g]])

            def r_part(g):
                x = mm_nt(dy_ref[rows, lanes[g]].astype(BF), hg_s[buf, :, lanes[g]])
                kept["r"] = x if g == 0 else kept["r"] + x
                if g == groups - 1:
                    rc_s[rows, :] = jnp.where(diag, kept["r"], 0.0).astype(BF)

            def end(g):
                ln = lanes[g]
                y = kept[g] + skip_ref[:, ln] * drive_ref[rows, ln].astype(F32)
                zz = z_ref[rows, ln]
                sg = sig_s[rows, ln]
                gated_ref[rows, ln] = (y * (zz * sg)).astype(BF)
                dz_ref[rows, ln] = (dg_ref[rows, ln] * y * (sg * (1.0 + zz * (1.0 - sg)))).astype(BF)

            return [functools.partial(f, g) for g in range(groups) for f in (y_part, r_part, end)]

        def vpu(with_g, b, buf, state, pieces=()):
            hs, hbs, qs = (list(s) for s in state)
            pieces = list(pieces)
            t0 = b * T
            bt = bt_s[:, t0 : t0 + T]
            ct = ct_s[:, t0 : t0 + T] if with_g else None
            base = jnp.minimum(chunk, ng - 1) * (lc * n)
            for k in range(T):
                t = t0 + k
                bb = jnp.broadcast_to(bt[:, k : k + 1], (n, 128))
                bb = jnp.concatenate([bb, bb], axis=1)
                if with_g:
                    cc = jnp.broadcast_to(ct[:, k : k + 1], (n, 128))
                    cc = jnp.concatenate([cc, cc], axis=1)
                at = pl.ds(t * n, n)
                far = pl.ds(pl.multiple_of(base + t * n, n), n)
                for g in range(groups):
                    ln = lanes[g]
                    e = jnp.exp2(row(step_s, g, t, n) * rate2[:, ln])
                    hprev_ref[at, ln] = hbs[g]
                    hs[g] = e * hs[g] + bb * row(sd_s, g, t, n)
                    hbs[g] = hs[g].astype(BF)
                    if with_g:
                        hg_s[buf, pl.ds(k * n, n), ln] = hbs[g] + g_s[far, ln]
                        ag = cc * row(dy_s, g, t, n) + qs[g]
                        qs[g] = e * ag
                        agb = ag.astype(BF)
                        ag_ref[at, ln] = agb
                        wg_ref[at, ln] = agb * qg_s[far, ln]
                    else:
                        hg_s[buf, pl.ds(k * n, n), ln] = hbs[g]
                if k % 2 and pieces:
                    pieces.pop(0)()
            for f in pieces:
                f()
            return tuple(hs), tuple(hbs), tuple(qs)

        def run(with_g):
            many = range(groups)
            state = tuple(st_f[g + groups] for g in many), tuple(st_h[g] for g in many), tuple(st_q[g] for g in many)
            state = vpu(with_g, 0, 0, state)
            for b in range(1, nb):
                state = vpu(with_g, b, b, state, mxu(b - 1, b - 1))
            for f in mxu(nb - 1, nb - 1):
                f()
            for g in many:
                st_f[g + groups] = state[0][g]
                st_h[g] = state[1][g]
                st_q[g] = state[2][g]

        live = jnp.logical_and(chunk < ng, chunk * lc < pfx)

        @pl.when(live)
        def _():
            mask = (positions(chunk) < pfx).astype(F32)
            split(dy_s, dy * mask)
            run(True)

            @pl.when(pfx < (chunk + 1) * lc)
            def _():
                keep = iota((lc * n, c), 0) + chunk * (lc * n) < pfx * n
                ag_ref[...] = jnp.where(keep, ag_ref[...].astype(F32), 0.0).astype(BF)

        @pl.when(jnp.logical_not(live))
        def _():
            run(False)

        part_ref[...] = mm(rc_s[...], fold(r + n, p, n))


def back_kernel(ng, top, low, far, prefix_ref, proj_ref, sw_ref, drive_ref, step_ref, dy_ref, h_ref, ag_ref, wg_ref, pin_ref, dlog_ref, skip_ref, pc_ref, ac_ref, bc_ref, *refs):
    (part_ref, dpre_ref, ddrive_ref, po_ref, ao_ref, gbias_ref, step_s, dy_s, p_s, ct_s, bbd_s, rb_s, ds_s, v_s, w_s) = refs[far:]
    lc, c = drive_ref.shape
    p = proj_ref.shape[1]
    n = dlog_ref.shape[0]
    r = p - 2 * n
    tn = T * n
    nb = lc // T
    groups = c // 256
    i = pl.program_id(0)
    chunk = top - i
    rate2 = -jnp.exp(dlog_ref[...]) * LOG2E
    rate2b = rate2.astype(BF)
    lanes = [slice(g * 256, (g + 1) * 256) for g in range(groups)]

    @pl.when(i == 0)
    def _():
        for g in range(groups):
            p_s[g] = pc_ref[:, lanes[g]]
        ao_ref[...] = ac_ref[...]
        gbias_ref[...] = bc_ref[...]

    proj = proj_ref[...]
    split(step_s, step_ref[...])
    split(dy_s, dy_ref[...])
    ct_s[...] = mm_nt(pick(r + n, p, n), proj)
    bbd_s[...] = jnp.where(blockdiag(lc, n), mm(proj, spread(r, p, n)), 0.0).astype(BF)
    diag = blockdiag(T, n)
    ones = diag.astype(BF)
    gather = (lax.rem(iota((n, tn // 2), 1), n) == iota((n, tn // 2), 0)).astype(BF)

    never = prefix_ref[0] < 0
    done = {}

    def vpu(with_g, b, buf, state, pieces=()):
        ps = list(state)
        seen = done.get(b + 3, {})
        pieces = list(pieces)
        held = [None] * groups
        t0 = b * T
        ct = ct_s[:, t0 : t0 + T]
        for k in range(T - 1, -1, -1):
            t = t0 + k
            for g in range(groups):
                key = {T - 1: ("s", g), T // 2: ("v", g), T // 4: ("w", g)}.get(k)
                if key in seen:
                    ps[g] = jnp.where(never, seen[key], ps[g])
            cc = jnp.broadcast_to(ct[:, k : k + 1], (n, 128))
            cc = jnp.concatenate([cc, cc], axis=1)
            at = pl.ds(t * n, n)
            for g in range(groups):
                ln = lanes[g]
                st = row(step_s, g, t, n)
                e = jnp.exp2(st * rate2[:, ln])
                ah = cc * row(dy_s, g, t, n) + ps[g]
                ps[g] = e * ah
                dsrc = ah.astype(BF)
                w = ps[g].astype(BF) * h_ref[at, ln]
                if with_g:
                    dsrc = dsrc + ag_ref[at, ln]
                    w = w + wg_ref[at, ln]
                ds_s[buf, pl.ds(k * n, n), ln] = dsrc
                v_s[buf, pl.ds(k * n, n), ln] = w * rate2b[:, ln]
                ws = w * st.astype(BF)
                if k % 2:
                    held[g] = ws
                else:
                    w_s[buf, pl.ds(k // 2 * n, n), ln] = held[g] + ws
            if k % 2 == 0 and pieces:
                pieces.pop(0)()
        for f in pieces:
            f()
        return tuple(ps)

    def mxu(b, buf):
        rows = pl.ds(b * T, T)
        kept = done[b] = {}

        def s_part(g):
            kept["s", g] = mm(bbd_s[rows, :], ds_s[buf, :, lanes[g]])

        def v_part(g):
            kept["v", g] = mm(ones, v_s[buf, :, lanes[g]])
            kept["w", g] = mm(gather, w_s[buf, :, lanes[g]])
            ao_ref[:, lanes[g]] += kept["w", g]

        def r_part(g):
            ln = lanes[g]
            sd = step_ref[rows, ln] * drive_ref[rows, ln].astype(F32)
            x = mm_nt(sd.astype(BF), ds_s[buf, :, ln])
            kept["r"] = x if g == 0 else kept["r"] + x
            if g == groups - 1:
                rb_s[rows, :] = jnp.where(diag, kept["r"], 0.0).astype(BF)

        def end(g):
            ln = lanes[g]
            step = step_ref[rows, ln]
            ssum = kept["s", g]
            drive = drive_ref[rows, ln].astype(F32)
            dpre = (kept["v", g] * LN2 + drive * ssum) * one_minus_exp(step)
            dpre_ref[rows, ln] = dpre.astype(BF)
            ddrive_ref[rows, ln] = skip_ref[:, ln] * dy_ref[rows, ln] + step * ssum
            gbias_ref[:, ln] += jnp.sum(dpre, axis=0, keepdims=True)

        return [functools.partial(f, g) for g in range(groups) for f in (s_part, v_part, r_part, end)]

    def run(with_g):
        done.clear()
        many = range(groups)
        state = tuple(p_s[g] for g in many)
        state = vpu(with_g, nb - 1, nb - 1, state)
        for b in range(nb - 2, -1, -1):
            state = vpu(with_g, b, b, state, mxu(b + 1, b + 1))
        for f in mxu(0, 0):
            f()
        for g in many:
            p_s[g] = state[g]

    if low >= ng:
        run(False)
    else:
        live = jnp.logical_and(chunk < ng, chunk * lc < prefix_ref[0])

        @pl.when(live)
        def _():
            run(True)

        @pl.when(jnp.logical_not(live))
        def _():
            run(False)

    part_ref[...] = (pin_ref[...] + mm(rb_s[...], fold(r, p, n)) + mm_nt(dpre_ref[...], sw_ref[...])).astype(part_ref.dtype)
    po_ref[...] = jnp.concatenate([p_s[g] for g in range(groups)], axis=1)


def whole(*s):
    return pl.BlockSpec(s, lambda i: (0,) * len(s))


SMEM = pl.BlockSpec(memory_space=pltpu.SMEM)


def head_kernel(low_ref, gain_ref, w_ref, cw_ref, cb_ref, xw_ref, normed_ref, x_ref, drive_ref, part_ref, rs_ref, edge_s):
    taps = cw_ref.shape[0]
    lc = low_ref.shape[0]

    @pl.when(pl.program_id(0) == 0)
    def _():
        edge_s[...] = jnp.zeros_like(edge_s)

    xf = low_ref[...].astype(F32)
    rs = lax.rsqrt(jnp.mean(xf * xf, axis=-1, keepdims=True) + epsilon)
    rs_ref[...] = rs
    normed = (xf * rs * gain_ref[...]).astype(BF)
    normed_ref[...] = normed
    x = mm(normed, w_ref[...])
    x_ref[...] = x
    wide = jnp.concatenate([edge_s[...], x], axis=0)
    edge_s[...] = x[lc - 8 :]
    out = cb_ref[...] + cw_ref[taps - 1 :, :] * x
    for k in range(taps - 1):
        at = 8 - (taps - 1) + k
        out = out + cw_ref[k : k + 1, :] * wide[at : at + lc]
    drive = (out * sigmoid(out)).astype(BF)
    drive_ref[...] = drive
    part_ref[...] = mm_nt(drive, xw_ref[...]).astype(BF)


def head(low, gain, w_all, conv_weight, conv_bias, xproj_t):
    l, d = low.shape
    c = w_all.shape[1] // 2
    p = xproj_t.shape[0]
    hc = 256
    by = lambda w: pl.BlockSpec((hc, w), lambda i: (i, 0))
    s = jax.ShapeDtypeStruct
    return pl.pallas_call(
        head_kernel,
        grid=(l // hc,),
        in_specs=[by(d), whole(1, d), whole(d, c), whole(*conv_weight.shape), whole(1, c), whole(p, c)],
        out_specs=[by(d), by(c), by(c), by(p), by(1)],
        out_shape=[s((l, d), BF), s((l, c), F32), s((l, c), BF), s((l, p), BF), s((l, 1), F32)],
        scratch_shapes=[pltpu.VMEM((8, c), F32)],
        compiler_params=pltpu.CompilerParams(vmem_limit_bytes=60 << 20),
        cost_estimate=pl.CostEstimate(flops=2 * l * d * c, transcendentals=l * c, bytes_accessed=4 * l * d + 2 * d * c + 6 * l * c),
        name="head",
    )(low, gain.reshape(1, d), w_all, conv_weight, conv_bias.reshape(1, c), xproj_t)


def gates_kernel(n_ref, w_ref, c_ref, o_ref, z_ref, dg_ref):
    z_ref[...] = mm(n_ref[...], w_ref[...])
    dg_ref[...] = mm_nt(c_ref[...], o_ref[...])


def gates(normed, w_all, cot, out_weight):
    l, d = normed.shape
    c = w_all.shape[1] // 2
    by = lambda w: pl.BlockSpec((256, w), lambda i: (i, 0))
    s = jax.ShapeDtypeStruct
    return pl.pallas_call(
        gates_kernel,
        grid=(l // 256,),
        in_specs=[by(d), pl.BlockSpec((d, c), lambda i: (0, 1)), by(d), whole(c, d)],
        out_specs=[by(c), by(c)],
        out_shape=[s((l, c), F32), s((l, c), F32)],
        compiler_params=pltpu.CompilerParams(vmem_limit_bytes=60 << 20),
        cost_estimate=pl.CostEstimate(flops=4 * l * d * c, transcendentals=0, bytes_accessed=4 * (l * d + d * c + 2 * l * c)),
        name="gates",
    )(normed, w_all, cot, out_weight)


def inner_kernel(rows_a, rows_b, bits_ref, dproj_ref, ds_ref, x_ref, xb_ref, drive_ref, dz_ref, normed_ref, low_ref, rs_ref, w_ref, xw_ref, cw_ref, cb_ref,
                 gb_ref, gd_ref, dlog_ref, gk_ref, proj_ref, dpre_ref, ka_ref, sa_ref, kb_ref, sb_ref, kn_ref, sn_ref, gn_ref, edge_s, gin_s, gx_s, gs_s, gc_s, gn_s, la_s, lb_s):
    taps = cw_ref.shape[0]
    lc, c = ds_ref.shape
    d = normed_ref.shape[1]
    p = dproj_ref.shape[1]
    n = gd_ref.shape[0]
    r = p - 2 * n
    i = pl.program_id(0)
    last = pl.num_programs(0) - 1
    tn = (((0,), (0,)), ((), ()))

    @pl.when(i == 0)
    def _():
        edge_s[...] = jnp.zeros_like(edge_s)
        gin_s[...] = jnp.zeros_like(gin_s)
        gx_s[...] = jnp.zeros_like(gx_s)
        gs_s[...] = jnp.zeros_like(gs_s)
        gc_s[...] = jnp.zeros_like(gc_s)
        gn_s[...] = jnp.zeros_like(gn_s)

    x = x_ref[...]
    before = jnp.where(i == last, 0.0, xb_ref[...])
    wide = jnp.concatenate([before, x], axis=0)
    moved = [wide[8 - (taps - 1) + k : 8 - (taps - 1) + k + lc] for k in range(taps - 1)] + [x]
    out = cb_ref[...]
    for k in range(taps):
        out = out + cw_ref[k : k + 1, :] * moved[k]
    sc = sigmoid(out)
    dproj = dproj_ref[...]
    ddrive = ds_ref[...] + mm(dproj, xw_ref[...])
    dconv = ddrive * (sc * (1.0 + out * (1.0 - sc)))
    gc_s[pl.ds(taps, 1), :] += jnp.sum(dconv, axis=0, keepdims=True)
    for k in range(taps):
        gc_s[pl.ds(k, 1), :] += jnp.sum(dconv * moved[k], axis=0, keepdims=True)
    ahead = jnp.concatenate([dconv, edge_s[...]], axis=0)
    edge_s[...] = dconv[:8]
    dx = cw_ref[taps - 1 :, :] * dconv
    for k in range(taps - 1):
        by = taps - 1 - k
        dx = dx + cw_ref[k : k + 1, :] * ahead[by : by + lc]
    dx = dx.astype(BF)
    normed = normed_ref[...]
    gin_s[...] += lax.dot_general(normed, dx, tn, preferred_element_type=F32)
    gx_s[...] += lax.dot_general(dproj, drive_ref[...], tn, preferred_element_type=F32)
    gs_s[...] += lax.dot_general(proj_ref[:, :r], dpre_ref[...], tn, preferred_element_type=F32)
    dn = mm_nt(dx, w_ref[:, :c]) + mm_nt(dz_ref[...], w_ref[:, c:])
    half = pl.num_programs(0) // 2

    @pl.when(i < half)
    def _():
        sn_ref[...] = dn.astype(BF)

    @pl.when(i >= half)
    def _():
        kn_ref[...] = dn.astype(BF)

    gn_s[...] += jnp.sum(dn * (low_ref[...].astype(F32) * rs_ref[...]), axis=0, keepdims=True)

    @pl.when(i == last)
    def _():
        gn_ref[...] = gn_s[...]
        lines = [gc_s[pl.ds(0, taps + 1), :], gb_ref[...], gk_ref[...]]
        lines = jnp.concatenate(lines + [jnp.zeros((16 - taps - 3, c), F32)], axis=0)
        top = 16 + n + r + p
        la_s[pl.ds(0, 16), :] = lines.astype(BF)
        la_s[pl.ds(16, n), :] = (gd_ref[...] * -jnp.exp(dlog_ref[...])).astype(BF)
        la_s[pl.ds(16 + n, r), :] = gs_s[...].astype(BF)
        la_s[pl.ds(16 + n + r, p), :] = gx_s[...].astype(BF)
        la_s[pl.ds(top, rows_a - top), :] = gin_s[pl.ds(0, rows_a - top), :].astype(BF)
        rest = d - (rows_a - top)
        lb_s[pl.ds(0, rest), :] = gin_s[pl.ds(rows_a - top, rest), :].astype(BF)
        lb_s[pl.ds(rest, rows_b - rest), :] = jnp.zeros((rows_b - rest, c), BF)
        for bit, total, keep_ref, send_ref in ((bits_ref[0], la_s, ka_ref, sa_ref), (bits_ref[1], lb_s, kb_ref, sb_ref)):
            rows = keep_ref.shape[0]
            keep_ref[...] = total[pl.ds(pl.multiple_of(bit * rows, 16), rows), :]
            send_ref[...] = total[pl.ds(pl.multiple_of((1 - bit) * rows, 16), rows), :]


def inner(rows_a, rows_b, bits, dproj, ddrive, x, drive, dz, normed, low, rs, w_all, xproj_t, conv_weight, conv_bias, g_bias, g_decay, decay_log, g_skip, proj, dpre):
    l, c = x.shape
    d = normed.shape[1]
    p = dproj.shape[1]
    n = g_decay.shape[0]
    hc = 256
    nc = l // hc
    by = lambda w: pl.BlockSpec((hc, w), lambda i: (nc - 1 - i, 0))
    s = jax.ShapeDtypeStruct
    v = pltpu.VMEM
    edge = pl.BlockSpec((8, c), lambda i: (jnp.maximum((nc - 1 - i) * (hc // 8) - 1, 0), 0))
    upper = pl.BlockSpec((hc, d), lambda i: (jnp.maximum(nc // 2 - 1 - i, 0), 0))
    lower = pl.BlockSpec((hc, d), lambda i: (jnp.minimum(nc - 1 - i, nc // 2 - 1), 0))
    return pl.pallas_call(
        functools.partial(inner_kernel, rows_a, rows_b),
        grid=(nc,),
        in_specs=[SMEM, by(p), by(c), by(c), edge, by(c), by(c), by(d), by(d), by(1), whole(d, 2 * c), whole(p, c), whole(*conv_weight.shape), whole(1, c),
                  whole(1, c), whole(n, c), whole(n, c), whole(1, c), by(p), by(c)],
        out_specs=[whole(rows_a // 2, c)] * 2 + [whole(rows_b // 2, c)] * 2 + [lower, upper, whole(1, d)],
        out_shape=[s((rows_a // 2, c), BF)] * 2 + [s((rows_b // 2, c), BF)] * 2 + [s((l // 2, d), BF)] * 2 + [s((1, d), F32)],
        scratch_shapes=[v((8, c), F32), v((d, c), F32), v((p, c), F32), v((p - 2 * n, c), F32), v((8, c), F32), v((1, d), F32), v((rows_a, c), BF), v((rows_b, c), BF)],
        compiler_params=pltpu.CompilerParams(vmem_limit_bytes=60 << 20),
        cost_estimate=pl.CostEstimate(flops=6 * l * d * c, transcendentals=l * c, bytes_accessed=10 * l * d),
        name="inner",
    )(bits, dproj, ddrive, x, x, drive, dz, normed, low, rs, w_all, xproj_t, conv_weight, conv_bias.reshape(1, c), g_bias, g_decay, decay_log, g_skip, proj, dpre)


def outer_kernel(order_ref, normed_ref, dz_ref, gated_ref, cot_ref, w_ref, kz_ref, sz_ref, ko_ref, so_ref, km_ref, sm_ref, z_s, o_s):
    i = pl.program_id(0)
    tn = (((0,), (0,)), ((), ()))

    @pl.when(i == 0)
    def _():
        z_s[...] = jnp.zeros_like(z_s)
        o_s[...] = jnp.zeros_like(o_s)

    z_s[...] += lax.dot_general(normed_ref[...], dz_ref[...], tn, preferred_element_type=F32)
    o_s[...] += lax.dot_general(gated_ref[...], cot_ref[...], tn, preferred_element_type=F32)
    mix = mm(gated_ref[...], w_ref[...]).astype(BF)
    half = pl.num_programs(0) // 2

    @pl.when(i < half)
    def _():
        sm_ref[...] = mix

    @pl.when(i >= half)
    def _():
        km_ref[...] = mix

    @pl.when(i == pl.num_programs(0) - 1)
    def _():
        for bit, total, keep_ref, send_ref in ((order_ref[1], z_s, kz_ref, sz_ref), (order_ref[2], o_s, ko_ref, so_ref)):
            rows = keep_ref.shape[0]
            keep_ref[...] = total[pl.ds(pl.multiple_of(bit * rows, 16), rows), :].astype(BF)
            send_ref[...] = total[pl.ds(pl.multiple_of((1 - bit) * rows, 16), rows), :].astype(BF)


def outer(bits, normed, dz, gated, cot, out_weight):
    l, d = normed.shape
    c = dz.shape[1]
    hc = 256
    nc = l // hc
    by = lambda w: pl.BlockSpec((hc, w), lambda i, order: (lax.rem(i + (1 - order[0]) * (nc // 2), nc), 0))
    full = lambda *q: pl.BlockSpec(q, lambda i, order: (0,) * len(q))
    s = jax.ShapeDtypeStruct
    v = pltpu.VMEM
    return pl.pallas_call(
        outer_kernel,
        grid_spec=pltpu.PrefetchScalarGridSpec(
            num_scalar_prefetch=1,
            grid=(nc,),
            in_specs=[by(d), by(c), by(c), by(d), full(c, d)],
            out_specs=[full(d // 2, c)] * 2 + [full(c // 2, d)] * 2 + [pl.BlockSpec((hc, d), lambda i, order: (jnp.maximum(i - nc // 2, 0), 0)), pl.BlockSpec((hc, d), lambda i, order: (jnp.minimum(i, nc // 2 - 1), 0))],
            scratch_shapes=[v((d, c), F32), v((c, d), F32)],
        ),
        out_shape=[s((d // 2, c), BF)] * 2 + [s((c // 2, d), BF)] * 2 + [s((l // 2, d), BF)] * 2,
        compiler_params=pltpu.CompilerParams(vmem_limit_bytes=60 << 20),
        cost_estimate=pl.CostEstimate(flops=6 * l * d * c, transcendentals=0, bytes_accessed=10 * l * d),
        name="outer",
    )(bits, normed, dz, gated, cot, out_weight)


def merge_kernel(kinds, bits_ref, *refs):
    take = list(refs)
    ins = [[take.pop(0) for _ in range(2 + EXTRA[kind])] for kind in kinds]
    for j, (kind, (one, two, *more)) in enumerate(zip(kinds, ins)):
        rows = one.shape[0]
        if kind == "join":
            out = take.pop(0)
            out[pl.ds(pl.multiple_of(bits_ref[j] * rows, 16), rows), :] = one[...]
            out[pl.ds(pl.multiple_of((1 - bits_ref[j]) * rows, 16), rows), :] = two[...]
        elif kind == "split":
            half = rows // 2
            for out, at in ((take.pop(0), bits_ref[j]), (take.pop(0), 1 - bits_ref[j])):
                part = pl.ds(pl.multiple_of(at * half, 16), half)
                out[...] = (one[part, :].astype(F32) + two[part, :].astype(F32)).astype(BF)
        else:
            total = one[...].astype(F32) + two[...].astype(F32)
            if kind == "shift":
                total = total + more[0][...].astype(F32)
            if kind == "norm":
                x_ref, rs_ref, gain_ref = more
                x, rs = x_ref[...].astype(F32), rs_ref[...]
                scaled = total * gain_ref[...]
                total = rs * scaled - x * (rs * rs * rs) * jnp.mean(scaled * x, axis=-1, keepdims=True)
            take.pop(0)[...] = total.astype(BF)


EXTRA = dict(join=0, split=0, sum=0, shift=1, norm=3)


def merge(items):
    kinds = tuple(item[0] for item in items)
    bits = jnp.stack([jnp.asarray(item[1], jnp.int32) for item in items])
    arrays = [v for item in items for v in item[2:]]
    shapes = []
    for kind, _, one, *_ in items:
        rows, cols = one.shape
        many = {"join": [2 * rows], "split": [rows // 2] * 2}.get(kind, [rows])
        shapes.append([jax.ShapeDtypeStruct((q, cols), BF) for q in many])
    vm = pl.BlockSpec(memory_space=pltpu.VMEM)
    flat = [q for group in shapes for q in group]
    out = list(pl.pallas_call(
        functools.partial(merge_kernel, kinds),
        in_specs=[SMEM] + [vm] * len(arrays),
        out_specs=[vm] * len(flat),
        out_shape=flat,
        compiler_params=pltpu.CompilerParams(vmem_limit_bytes=24 << 20),
        name="merge",
    )(bits, *arrays))
    return [[out.pop(0) for _ in group] for group in shapes]


def ending_kernel(bits_ref, cot_ref, na_ref, nb_ref, oa_ref, ob_ref, tok_ref, go_ref):
    for bit, one, two, out, add in ((bits_ref[0], na_ref, nb_ref, tok_ref, cot_ref), (bits_ref[1], oa_ref, ob_ref, go_ref, None)):
        rows = one.shape[0]
        for at, part in ((bit, one), (1 - bit, two)):
            where = pl.ds(pl.multiple_of(at * rows, 16), rows)
            value = part[...].astype(F32)
            out[where, :] = value if add is None else value + add[where, :].astype(F32)


def ending(bits, cot, na, nb, oa, ob):
    s = jax.ShapeDtypeStruct
    vm = pl.BlockSpec(memory_space=pltpu.VMEM)
    return pl.pallas_call(
        ending_kernel,
        in_specs=[SMEM] + [vm] * 5,
        out_specs=[vm] * 2,
        out_shape=[s(cot.shape, F32), s((2 * oa.shape[0], oa.shape[1]), F32)],
        compiler_params=pltpu.CompilerParams(vmem_limit_bytes=24 << 20),
        cost_estimate=pl.CostEstimate(flops=cot.size, transcendentals=0, bytes_accessed=12 * cot.size),
        name="ending",
    )(bits, cot, na, nb, oa, ob)


def last_kernel(n, r, p, taps, bits_ref, sa_ref, oa_ref, sb_ref, ob_ref, sz_ref, oz_ref, gin_ref, gc_ref, gcb_ref, gb_ref, gk_ref, gd_ref, gs_ref, gx_ref, a_s, b_s):
    for j, mine, other, whole_s in ((0, sa_ref, oa_ref, a_s), (1, sb_ref, ob_ref, b_s)):
        half = mine.shape[0]
        whole_s[pl.ds(pl.multiple_of(bits_ref[j] * half, 16), half), :] = mine[...]
        whole_s[pl.ds(pl.multiple_of((1 - bits_ref[j]) * half, 16), half), :] = other[...]
    lines = a_s[pl.ds(0, 16), :].astype(F32)
    gc_ref[...] = lines[:taps]
    gcb_ref[...] = lines[taps : taps + 1]
    gb_ref[...] = lines[taps + 1 : taps + 2]
    gk_ref[...] = lines[taps + 2 : taps + 3]
    gd_ref[...] = a_s[pl.ds(16, n), :].astype(F32)
    gs_ref[...] = a_s[pl.ds(16 + n, r), :].astype(F32)
    gx_ref[...] = a_s[pl.ds(16 + n + r, p), :].astype(F32)
    top = 16 + n + r + p
    half = sz_ref.shape[0]
    d = 2 * half
    cut = a_s.shape[0] - top
    gin_ref[pl.ds(0, cut), 0, :] = a_s[pl.ds(top, cut), :].astype(F32)
    gin_ref[pl.ds(cut, d - cut), 0, :] = b_s[pl.ds(0, d - cut), :].astype(F32)
    gin_ref[pl.ds(pl.multiple_of(bits_ref[2] * half, 16), half), 1, :] = sz_ref[...].astype(F32)
    gin_ref[pl.ds(pl.multiple_of((1 - bits_ref[2]) * half, 16), half), 1, :] = oz_ref[...].astype(F32)


def last(bits, sa, oa, sb, ob, sz, oz, n, r, p, taps):
    half, c = sz.shape
    s = jax.ShapeDtypeStruct
    vm = pl.BlockSpec(memory_space=pltpu.VMEM)
    return pl.pallas_call(
        functools.partial(last_kernel, n, r, p, taps),
        in_specs=[SMEM] + [vm] * 6,
        out_specs=[vm] * 8,
        out_shape=[s((2 * half, 2, c), F32), s((taps, c), F32), s((1, c), F32), s((1, c), F32), s((1, c), F32), s((n, c), F32), s((r, c), F32), s((p, c), F32)],
        scratch_shapes=[pltpu.VMEM((2 * sa.shape[0], c), BF), pltpu.VMEM((2 * sb.shape[0], c), BF)],
        compiler_params=pltpu.CompilerParams(vmem_limit_bytes=24 << 20),
        name="last",
    )(bits, sa, oa, sb, ob, sz, oz)


def front(prefix, proj, sw, bias, drive, z, dg, dlog, skip):
    l, c = drive.shape
    p = proj.shape[1]
    n = dlog.shape[0]
    ng = l // 2 // LC
    nc = l // LC
    s = jax.ShapeDtypeStruct
    fwd = lambda i: (jnp.maximum(i - ng, 0), 0)
    both = lambda i: (jnp.where(i < ng, ng - 1 - i, i - ng), 0)
    half = lambda i: (jnp.clip(i - ng, 0, ng - 1), 0)
    B = pl.BlockSpec
    lanes = c // 128
    v = pltpu.VMEM
    return pl.pallas_call(
        functools.partial(front_kernel, ng),
        grid=(ng + nc,),
        in_specs=[SMEM, B((LC, p), both), whole(*sw.shape), whole(1, c), B((LC, c), both), B((LC, c), fwd), B((LC, c), fwd), whole(n, c), whole(1, c)],
        out_specs=[B((LC, c), fwd), B((LC, c), fwd), B((LC, c), fwd), B((LC, c), fwd), B((LC * n, c), fwd), B((LC * n, c), half), B((LC * n, c), half), B((LC, p), fwd), whole(1, c)],
        out_shape=[s((l, c), BF), s((l, c), BF), s((l, c), F32), s((l, c), F32), s((l * n, c), BF), s((l // 2 * n, c), BF), s((l // 2 * n, c), BF), s((l, p), F32), s((1, c), F32)],
        scratch_shapes=[v((lanes, LC, 128), F32)] * 3 + [v((LC, c), F32), v((ng, LC, c), F32), v((n, LC), F32), v((n, LC), F32), v((LC, T * n), BF), v((LC, T * n), BF),
            v((LC // T, T * n, c), BF), v((l // 2 * n, c), BF), v((l // 2 * n, c), BF), v((c // 128, n, 256), F32), v((c // 256, n, 256), BF), v((c // 256, n, 256), F32)],
        compiler_params=pltpu.CompilerParams(vmem_limit_bytes=60 << 20),
        name="front",
    )(prefix, proj, sw, bias.reshape(1, c), drive, z, dg, dlog, skip.reshape(1, c))


def back(prefix, proj, sw_wide, drive, step, dy, hprev, ag, wg, pin, dlog, skip, carry, top, low, filled=()):
    l, c = drive.shape
    p = proj.shape[1]
    n = dlog.shape[0]
    ng = l // 2 // LC
    s = jax.ShapeDtypeStruct
    rev = lambda i: (top - i, 0)
    half = lambda i: (jnp.minimum(top - i, ng - 1), 0)
    B = pl.BlockSpec
    v = pltpu.VMEM
    ins = [SMEM, B((LC, p), rev), whole(*sw_wide.shape), B((LC, c), rev), B((LC, c), rev), B((LC, c), rev), B((LC * n, c), rev), B((LC * n, c), half), B((LC * n, c), half), B((LC, p), rev), whole(n, c), whole(1, c), whole(n, c), whole(n, c), whole(1, c)]
    steps = (top - low + 1) * LC * n * c
    return pl.pallas_call(
        functools.partial(back_kernel, ng, top, low, len(filled)),
        grid=(top - low + 1,),
        in_specs=ins + [B(memory_space=pl.ANY)] * len(filled),
        out_specs=[B((LC, p), rev), B((LC, c), rev), B((LC, c), rev), whole(n, c), whole(n, c), whole(1, c)],
        out_shape=[s((l, p), BF), s((l, c), BF), s((l, c), F32), s((n, c), F32), s((n, c), F32), s((1, c), F32)],
        input_output_aliases={len(ins) + j: j for j in range(len(filled))},
        scratch_shapes=[v((c // 128, LC, 128), F32)] * 2 + [v((c // 256, n, 256), F32), v((n, LC), F32), v((LC, T * n), BF), v((LC, T * n), BF), v((LC // T, T * n, c), BF), v((LC // T, T * n, c), BF), v((LC // T, T * n // 2, c), BF)],
        compiler_params=pltpu.CompilerParams(vmem_limit_bytes=60 << 20),
        cost_estimate=pl.CostEstimate(flops=steps * 4000, transcendentals=steps, bytes_accessed=steps * 4),
        name="back",
    )(prefix, proj, sw_wide, drive, step, dy, hprev, ag, wg, pin, dlog, skip.reshape(1, c), *carry, *filled)


def sigmoid(v):
    return 1.0 / (1.0 + jnp.exp(-v))


def exchange(value, name, size, bit):
    return lax.ppermute(value, name, [(j, j ^ (1 << bit)) for j in range(size)])


def bits_of(size):
    count = size.bit_length() - 1
    assert 1 << count == size
    return list(range(count))


class Chain:
    def __init__(self, name, size, order, keep, send, swap=True, middle=("sum", ())):
        order = list(order)
        self.name, self.size, self.keep, self.send, self.middle = name, size, keep, send, middle
        turn = [("swap", order.pop())] if swap else []
        self.steps = [("halve", bit) for bit in order] + turn + [("double", bit) for bit in reversed(order)]
        self.got = None

    def mine(self, bit):
        return (lax.axis_index(self.name) >> bit) & 1

    def start(self, send):
        self.send = send
        return exchange(send, self.name, self.size, self.steps[0][1])

    def item(self):
        kind, bit = self.steps.pop(0)
        after = self.steps[0]
        if kind == "double":
            return ("join", self.mine(bit), self.send, self.got)
        one = self.keep if kind == "halve" else self.send
        if kind == "halve" and after[0] == "halve":
            return ("split", self.mine(after[1]), one, self.got)
        if kind == "swap" or after[0] == "double":
            name, more = self.middle
            return (name, 0, one, self.got, *more)
        return ("sum", 0, one, self.got)

    def accept(self, arrays):
        self.send = arrays[-1]
        self.keep = arrays[0]
        self.got = None


def ready(chains):
    live = [c for c in chains if c.got is not None and len(c.steps) > 1]
    if live:
        for c, arrays in zip(live, merge([c.item() for c in live])):
            c.accept(arrays)


def under(chains, work, *inputs):
    chains = [c for c in chains if c.steps and c.got is None]
    sends, inputs = lax.optimization_barrier(([c.send for c in chains], inputs))
    got = [c.start(v) for c, v in zip(chains, sends)]
    result = work(*inputs)
    sends, got, result = lax.optimization_barrier((sends, got, result))
    for c, v, w in zip(chains, sends, got):
        c.send, c.got = v, w
    return result


def on_device(sizes, tokens, prefix, norm_gain, in_weight, conv_weight, conv_bias, xproj_weight, step_weight, step_bias, decay_log, skip_gain, out_weight, out_cotangent):
    dp, tp = sizes
    seqs, length, width = tokens.shape
    assert seqs == 1
    channels = in_weight.shape[2]
    rank = step_weight.shape[0]
    taps = conv_weight.shape[0]
    n = decay_log.shape[0]
    p = rank + 2 * n
    low = tokens[0]
    cot = out_cotangent[0]
    w_all = lax.optimization_barrier(in_weight.reshape(width, 2 * channels))
    xproj_t = xproj_weight.T
    order = bits_of(dp)
    turned = order[1:] + order[:1]
    t_order = bits_of(tp)
    at = lax.axis_index("tensor")
    at_dp = lax.axis_index("dp")
    spot = 0
    rows = length
    for bit in t_order:
        rows //= 2
        spot = spot + ((at >> bit) & 1) * rows
    part_of = lambda v: lax.dynamic_slice_in_dim(v, spot, rows, 0)
    bit_of = lambda v, bit: (v >> bit) & 1

    normed, xpart, drive, proj, rs = head(low, norm_gain, w_all, conv_weight, conv_bias, xproj_t)
    for bit in t_order[:-1]:
        proj = (proj.astype(F32) + exchange(proj, "tensor", tp, bit).astype(F32)).astype(BF)
    proj, n_in, c_in = lax.optimization_barrier((proj, normed, cot))
    other = exchange(proj, "tensor", tp, t_order[-1])
    zpart, dgated = gates(n_in, w_all, c_in, out_weight)
    my_x, my_rs = part_of(low), part_of(rs)
    other, zpart, dgated, my_x, my_rs = lax.optimization_barrier((other, zpart, dgated, my_x, my_rs))
    proj = (proj.astype(F32) + other.astype(F32)).astype(BF)

    gated, dz, step, dy, hprev, ag, wg, pin, g_skip = front(prefix, proj, step_weight, step_bias, drive, zpart, dgated, decay_log, skip_gain)

    picks = jnp.stack([bit_of(at, t_order[0]), bit_of(at_dp, order[0]), bit_of(at_dp, turned[0])]).astype(jnp.int32)
    kz, sz, ko, so, km, sm = outer(picks, normed, dz, gated, cot, out_weight)
    gz = Chain("dp", dp, order, kz, sz)
    go = Chain("dp", dp, turned, ko, so)
    mix = Chain("tensor", tp, t_order, km, sm, swap=False, middle=("shift", (my_x,)))
    chains = [gz, go, mix]
    wide = jnp.pad(step_weight, ((0, 2 * n), (0, 0)))
    nc = length // LC
    carry = (jnp.zeros((n, channels), F32), jnp.zeros((n, channels), F32), jnp.zeros((1, channels), F32))
    filled = ()
    top = nc - 1
    for low_chunk in PIECES:
        def piece(d, carry, filled, top=top, low_chunk=low_chunk):
            return back(prefix, proj, wide, drive, step, d, hprev, ag, wg, pin, decay_log, skip_gain, carry, top, low_chunk, filled)

        *filled, p1, a1, b1 = under(chains, piece, dy, carry, tuple(filled))
        ready(chains)
        carry = (p1, a1, b1)
        top = low_chunk - 1
    dpart, dpre, ddrive_scan = filled
    _, g_decay, g_bias = carry

    for bit in t_order[:-1]:
        dpart = (dpart.astype(F32) + exchange(dpart, "tensor", tp, bit).astype(F32)).astype(BF)
    cross = Chain("tensor", tp, t_order[-1:], dpart, dpart)
    under([cross] + chains, lambda: ())
    ready(chains)
    dproj = (cross.send.astype(F32) + cross.got.astype(F32)).astype(BF)
    total = 16 + n + p + rank + width
    total += -total % 256
    rows_a = total // 2
    ka, sa, kb, sb, lower, upper, g_norm = under(chains, lambda v: inner(rows_a, total - rows_a, picks[1:], v, ddrive_scan, xpart, drive, dz, normed, low, rs, w_all, xproj_t, conv_weight, conv_bias, g_bias, g_decay, decay_log, g_skip, proj, dpre), dproj)
    ready(chains)
    up = picks[0] == 1
    la = Chain("dp", dp, order, ka, sa)
    lb = Chain("dp", dp, turned, kb, sb)
    dn = Chain("tensor", tp, t_order, jnp.where(up, upper, lower), jnp.where(up, lower, upper), swap=False, middle=("norm", (my_x, my_rs, norm_gain.reshape(1, width))))
    turns = [("tensor", tp, bit) for bit in t_order] + [("dp", dp, bit) for bit in order]

    def gains(v):
        if turns:
            name, size, bit = turns.pop(0)
            v = v + exchange(v, name, size, bit)
        return v

    while len(la.steps) > 1:
        g_norm = under([la, lb, dn] + chains, gains, g_norm)
        ready([la, lb, dn] + chains)
    while turns:
        g_norm = gains(g_norm)
    for c in [dn] + chains:
        while c.steps and c.got is None:
            under([c], lambda: ())
            ready([c])
    flags = jnp.stack([dn.mine(dn.steps[0][1]), go.mine(go.steps[0][1])]).astype(jnp.int32)
    grad_tokens, g_out = under([la, lb], lambda v: ending(flags, v, dn.send, dn.got, go.send, go.got), cot)
    block_out = merge([mix.item()] if len(mix.steps) > 1 else [("join", mix.mine(mix.steps[0][1]), mix.send, mix.got)])[0][0]
    flags = jnp.stack([c.mine(c.steps[0][1]) for c in (la, lb, gz)]).astype(jnp.int32)
    g_in, g_conv, g_convb, g_bias, g_skip, g_decay, g_step, g_xproj = last(flags, la.send, la.got, lb.send, lb.got, gz.send, gz.got, n, rank, p, taps)
    return (block_out[None], grad_tokens[None], g_norm.reshape(-1), g_in, g_conv, g_convb[0], g_xproj.T, g_step, g_bias[0], g_decay, g_skip[0], g_out)


def solution(mesh):
    placed = (
        P("dp", None, None),
        P("dp"),
        P(),
        P(None, None, "tensor"),
        P(None, "tensor"),
        P("tensor"),
        P("tensor", None),
        P(None, "tensor"),
        P("tensor"),
        P(None, "tensor"),
        P("tensor"),
        P("tensor", None),
        P("dp", None, None),
    )
    results = (
        P("dp", None, None),
        P("dp", None, None),
        P(),
        P(None, None, "tensor"),
        P(None, "tensor"),
        P("tensor"),
        P("tensor", None),
        P(None, "tensor"),
        P("tensor"),
        P(None, "tensor"),
        P("tensor"),
        P("tensor", None),
    )
    sizes = (mesh.shape["dp"], mesh.shape["tensor"])
    return jax.shard_map(functools.partial(on_device, sizes), mesh=mesh, in_specs=placed, out_specs=results, check_vma=False)
```

time: 302 us -> 226 us (0.75)
  the two profiles are of different devices: /device:TPU:3 before, /device:TPU:1 now
where the time goes in v2:
time: 226 us; the launch traced here: 223 us
  Pallas kernels  122 us (54%)
  waiting for transfers between devices  50.9 us (23%)
  starting transfers between devices  32.3 us (14%)
  local copies, waits for them, and re-layouts  9.82 us (4%)
  other arithmetic  6.36 us (3%)
    ppermute x37, waiting for transfers between devices, exchange(): return lax.ppermute(value, name, [(j, j ^ 1 << bit) for j in range(size)])  50.9 us
    pallas_call x3, Pallas kernels, back(): pl.pallas_call(functools.partial(back_kernel, ng, top, low, len(filled)),...  33.7 us
    ppermute x37, starting transfers between devices, exchange(): return lax.ppermute(value, name, [(j, j ^ 1 << bit) for j in range(size)])  32.3 us
    pallas_call x1, Pallas kernels, front(): pl.pallas_call(functools.partial(front_kernel, ng), grid=(ng + nc,), in_s...  30.9 us
    pallas_call x1, Pallas kernels, inner(): pl.pallas_call(functools.partial(inner_kernel, rows_a, rows_b), grid=(nc,...  15.8 us
    pallas_call x9, Pallas kernels, merge(): pl.pallas_call(functools.partial(merge_kernel, kinds), in_specs=[SMEM] +...  10.3 us
    pallas_call x1, Pallas kernels, outer(): pl.pallas_call(outer_kernel, grid_spec=pltpu.PrefetchScalarGridSpec(num_s...  9.57 us
    pallas_call x1, Pallas kernels, head(): pl.pallas_call(head_kernel, grid=(l // hc,), in_specs=[by(d), whole(1, d)...  6.65 us
  transfers between devices with their start and end apart: 37, of which 16 were waited for; matrix products, arithmetic and copies ran while one was open for 3% of the time, Pallas kernels for 28%

profile of v2, /device:TPU:1, one launch (start us, length us, event | category | flops | bytes accessed | tf_op | source)
XLA Modules:
  0.0 223.0 jit_solution(4343411960806992908)
XLA Ops:
  0.6 3.5 %copy.31 = bf16[128,8,2,512]{3,1,2,0:T(8,128)(2,1)} copy(bf16[128,8,2,512]{3,2,1,0:T(2,128)(2,1)} %bitcast.33) | data formatting | bytes 4194304
  4.1 6.6 %head.1 = (bf16[1024,1024]{1,0:T(8,128)(2,1)}, f32[1024,512]{1,0:T(8,128)}, bf16[1024,512]{1,0:T(8,128)(2,1)}, bf16[1024,96]{1,0:T(8,128)(2,1)}, f32[1024,1]{1,0:T(8,128)}) custom-call(bf16[1024,1024]{1,0:T(8,128)(2,1)} %bitcast.31, f32[1,1024]{1,0:T(1,128)} %bitcast.26, bf16[1024,1024]{1,0:T(8,128)(2,1)} %bitcast.28, f32[4,512]{1,0:T(4,128)} %cw_ref.3, ...), custom_call_target="tpu_custom_call" | custom-call | flops 1073741824 | bytes 8388608 | tf_op jit(solution)/shard_map/head/pallas_call | solution.py:436
  11.5 0.9 constant_dynamic-slice_fusion.refs_7_
  12.4 0.6 pad.5.sw_ref
  13.7 1.1 dynamic-slice_bitcast_fusion.refs_6_
  14.7 1.0 add_convert_fusion.3
  15.8 2.8 %collective-permute-start.1 = (bf16[1024,96]{1,0:T(8,128)(2,1)S(1)}, bf16[1024,96]{1,0:T(8,128)(2,1)S(1)}, u32[]{:S(2)}, u32[]{:S(2)}) collective-permute-start(bf16[1024,96]{1,0:T(8,128)(2,1)S(1)} %add_convert_fusion.3), channel_id=1, source_target_pairs={{0,2},{1,3},{2,0},{3,1},{4,6},{5,7},{6,4},{7,5},{8,10},{9,11},{10,... | collective-permute-start | bytes 589832 | tf_op jit(solution)/shard_map/ppermute | solution.py:801
  18.5 6.3 %gates.1 = (f32[1024,512]{1,0:T(8,128)}, f32[1024,512]{1,0:T(8,128)}) custom-call(bf16[1024,1024]{1,0:T(8,128)(2,1)} %get-tuple-element.236.n_ref.normed_ref, bf16[1024,1024]{1,0:T(8,128)(2,1)} %bitcast.29, bf16[1024,1024]{1,0:T(8,128)(2,1)} %bitcast.23, bf16[512,1024]{1,0:T(8,128)(2,1)} %w_ref.1), custom_call_target="tpu_custom_call" | custom-call | flops 2147483648 | bytes 10485760 | tf_op jit(solution)/shard_map/gates/pallas_call | solution.py:459
  25.2 0.8 add_convert_fusion.2.proj_ref
  26.0 30.9 %front.1 = (bf16[1024,512]{1,0:T(8,128)(2,1)}, bf16[1024,512]{1,0:T(8,128)(2,1)}, f32[1024,512]{1,0:T(8,128)}, f32[1024,512]{1,0:T(8,128)}, bf16[16384,512]{1,0:...) custom-call(s32[1]{0:T(128)S(6)} %copy.38.prefix_ref, ...), custom_call_target="tpu_custom_call" | custom-call | tf_op jit(solution)/shard_map/front/pallas_call | solution.py:757
  56.9 9.6 %outer.1 = (bf16[512,512]{1,0:T(8,128)(2,1)}, bf16[512,512]{1,0:T(8,128)(2,1)}, bf16[256,1024]{1,0:T(8,128)(2,1)}, bf16[256,1024]{1,0:T(8,128)(2,1)}, bf16[512,1...) custom-call(s32[3]{0:T(128)} %get-tuple-element.459.order_ref, bf16[1024,1024]{1,0:T(8,128)(2,1)} %get-tuple-element.236.n_ref.normed_ref, ...), custom_call_target="tpu_custom_call" | custom-call | flops 3221225472 | bytes 10485760 | tf_op jit(solution)/shard_map/outer/pallas_call | solution.py:616
  67.1 0.9 collective-permute-start.2
  68.0 2.3 %collective-permute-start.3 = (bf16[256,1024]{1,0:T(8,128)(2,1)}, bf16[256,1024]{1,0:T(8,128)(2,1)}, u32[]{:S(2)}, u32[]{:S(2)}) collective-permute-start(bf16[256,1024]{1,0:T(8,128)(2,1)} %get-tuple-element.253), channel_id=1, source_target_pairs={{0,8},{4,12},{8,0},{12,4},{16,24},{20,28},{24,16},{28,20},{1,9},{5... | collective-permute-start | bytes 1572872 | tf_op jit(solution)/shard_map/ppermute | solution.py:801
  70.2 0.6 broadcast.9.pc_ref.ac_ref
  71.4 11.8 %back.3 = (bf16[1024,96]{1,0:T(8,128)(2,1)}, bf16[1024,512]{1,0:T(8,128)(2,1)}, f32[1024,512]{1,0:T(8,128)}, f32[16,512]{1,0:T(8,128)}, f32[16,512]{1,0:T(8,128)}, /*index=5*/f32[1,512]{1,0:T(1,128)}) custom-call(s32[1]{0:T(128)S(6)} %copy.38.prefix_ref, bf16[1024,96]{1,0:T(8,128)(2,1)} %add_convert_fusion.2.proj_ref, bf16[96,512]{1,0:T(8,128)(2,1)} %pad.5.sw_ref, ...), custom_call_target="tpu_custom_call" | custom-call | flops 12582912000 | bytes 12582912 | tf_op jit(solution)/shard_map/back/pallas_call | solution.py:782
  83.3 2.5 %merge.9 = (bf16[256,512]{1,0:T(8,128)(2,1)S(1)}, bf16[256,512]{1,0:T(8,128)(2,1)}, bf16[128,1024]{1,0:T(8,128)(2,1)S(1)}, bf16[128,1024]{1,0:T(8,128)(2,1)}, bf...) custom-call(s32[3]{0:T(128)S(1)} %get-tuple-element.458.bits_ref, bf16[512,512]{1,0:T(8,128)(2,1)S(1)} %copy-done.2, ...), custom_call_target="tpu_custom_call" | custom-call | tf_op jit(solution)/shard_map/merge/pallas_call | solution.py:672
  85.8 0.8 copy-done.4
  86.6 0.7 copy-done.8
  87.3 1.2 collective-permute-start.7
  89.0 2.1 collective-permute-start.6
  91.0 12.0 %back.4 = (bf16[1024,96]{1,0:T(8,128)(2,1)}, bf16[1024,512]{1,0:T(8,128)(2,1)}, f32[1024,512]{1,0:T(8,128)}, f32[16,512]{1,0:T(8,128)}, f32[16,512]{1,0:T(8,128)}, /*index=5*/f32[1,512]{1,0:T(1,128)}) custom-call(s32[1]{0:T(128)S(6)} %copy.38.prefix_ref, ...), custom_call_target="tpu_custom_call", output_to_operand_aliasing={{0}: (15, {}), {1}: (16, {}), {2}: (17, {})} | custom-call | flops 12582912000 | bytes 12582912 | tf_op jit(solution)/shard_map/back/pallas_call | solution.py:782
  103.1 0.9 merge.10
  104.9 9.9 %back.5 = (bf16[1024,96]{1,0:T(8,128)(2,1)}, bf16[1024,512]{1,0:T(8,128)(2,1)}, f32[1024,512]{1,0:T(8,128)}, f32[16,512]{1,0:T(8,128)}, f32[16,512]{1,0:T(8,128)}, /*index=5*/f32[1,512]{1,0:T(1,128)}) custom-call(s32[1]{0:T(128)S(6)} %copy.38.prefix_ref, ...), custom_call_target="tpu_custom_call", output_to_operand_aliasing={{0}: (15, {}), {1}: (16, {}), {2}: (17, {})} | custom-call | flops 8388608000 | bytes 8388608 | tf_op jit(solution)/shard_map/back/pallas_call | solution.py:782
  114.8 4.1 %collective-permute-done.8.refs_1_ = bf16[256,512]{1,0:T(8,128)(2,1)S(1)} collective-permute-done((bf16[256,512]{1,0:T(8,128)(2,1)S(1)}, bf16[256,512]{1,0:T(8,128)(2,1)S(1)}, u32[]{:S(2)}, u32[]{:S(2)}) %collective-permute-start.8) | collective-permute-done | bytes 262176 | tf_op jit(solution)/shard_map/ppermute | solution.py:801
  118.9 0.6 collective-permute-start.11
  119.6 0.7 merge.11
  121.4 1.1 collective-permute-start.14
  122.5 1.2 collective-permute-start.12
  123.8 5.8 %collective-permute-done.12 = bf16[1024,96]{1,0:T(8,128)(2,1)S(1)} collective-permute-done((bf16[1024,96]{1,0:T(8,128)(2,1)S(1)}, bf16[1024,96]{1,0:T(8,128)(2,1)S(1)}, u32[]{:S(2)}, u32[]{:S(2)}) %collective-permute-start.12) | collective-permute-done | bytes 196640 | tf_op jit(solution)/shard_map/ppermute | solution.py:801
  129.6 3.7 %collective-permute-done.13.refs_1_ = bf16[256,512]{1,0:T(8,128)(2,1)S(1)} collective-permute-done((bf16[256,512]{1,0:T(8,128)(2,1)S(1)}, bf16[256,512]{1,0:T(8,128)(2,1)S(1)}, u32[]{:S(2)}, u32[]{:S(2)}) %collective-permute-start.13) | collective-permute-done | bytes 262176 | tf_op jit(solution)/shard_map/ppermute | solution.py:801
  133.3 2.4 %collective-permute-done.14.refs_3_ = bf16[128,1024]{1,0:T(8,128)(2,1)S(1)} collective-permute-done((bf16[128,1024]{1,0:T(8,128)(2,1)S(1)}, bf16[128,1024]{1,0:T(8,128)(2,1)S(1)}, u32[]{:S(2)}, u32[]{:S(2)}) %collective-permute-start.14) | collective-permute-done | bytes 262176 | tf_op jit(solution)/shard_map/ppermute | solution.py:801
  135.7 0.8 add_convert_fusion.dproj_ref
  136.5 1.4 merge.13
  139.1 15.8 %inner.1 = (bf16[320,512]{1,0:T(8,128)(2,1)}, bf16[320,512]{1,0:T(8,128)(2,1)}, bf16[320,512]{1,0:T(8,128)(2,1)}, bf16[320,512]{1,0:T(8,128)(2,1)}, bf16[512,102...) custom-call(s32[2]{0:T(128)} %get-tuple-element.456.bits_ref, ...), custom_call_target="tpu_custom_call" | custom-call | flops 3221225472 | bytes 10485760 | tf_op jit(solution)/shard_map/inner/pallas_call | solution.py:563
  154.9 1.8 broadcast_select_fusion
  156.7 1.6 collective-permute-start.20
  158.3 0.6 collective-permute-start.18
  159.0 1.7 collective-permute-start.19
  160.7 0.6 collective-permute-start.21
  161.3 0.8 collective-permute-done.21
  162.2 5.4 %collective-permute-done.18.refs_1_ = bf16[320,512]{1,0:T(8,128)(2,1)S(1)} collective-permute-done((bf16[320,512]{1,0:T(8,128)(2,1)S(1)}, bf16[320,512]{1,0:T(8,128)(2,1)S(1)}, u32[]{:S(2)}, u32[]{:S(2)}) %collective-permute-start.18) | collective-permute-done | bytes 327712 | tf_op jit(solution)/shard_map/ppermute | solution.py:801
  167.6 0.9 collective-permute-done.19.refs_3_
  168.5 0.9 merge.14
  169.5 1.3 collective-permute-start.24
  170.7 1.2 collective-permute-start.22
  172.2 10.0 %collective-permute-done.25 = f32[1,1024]{1,0:T(1,128)S(1)} collective-permute-done((f32[1,1024]{1,0:T(1,128)S(1)}, f32[1,1024]{1,0:T(1,128)S(1)}, u32[]{:S(2)}, u32[]{:S(2)}) %collective-permute-start.25) | collective-permute-done | bytes 4128 | tf_op jit(solution)/shard_map/ppermute | solution.py:801
  182.2 1.1 merge.15
  183.4 1.2 collective-permute-start.28
  184.6 0.9 collective-permute-start.26
  185.5 0.9 collective-permute-start.27
  187.0 3.0 %collective-permute-done.29 = f32[1,1024]{1,0:T(1,128)S(1)} collective-permute-done((f32[1,1024]{1,0:T(1,128)S(1)}, f32[1,1024]{1,0:T(1,128)S(1)}, u32[]{:S(2)}, u32[]{:S(2)}) %collective-permute-start.29) | collective-permute-done | bytes 4128 | tf_op jit(solution)/shard_map/ppermute | solution.py:801
  190.0 4.4 %collective-permute-done.26.refs_1_ = bf16[160,512]{1,0:T(8,128)(2,1)S(1)} collective-permute-done((bf16[160,512]{1,0:T(8,128)(2,1)S(1)}, bf16[160,512]{1,0:T(8,128)(2,1)S(1)}, u32[]{:S(2)}, u32[]{:S(2)}) %collective-permute-start.26) | collective-permute-done | bytes 163872 | tf_op jit(solution)/shard_map/ppermute | solution.py:801
  194.4 0.7 collective-permute-done.28.refs_5_
  195.1 0.7 merge.16
  195.8 2.7 %collective-permute-start.32 = (bf16[512,1024]{1,0:T(8,128)(2,1)S(1)}, bf16[512,1024]{1,0:T(8,128)(2,1)S(1)}, u32[]{:S(2)}, u32[]{:S(2)}) collective-permute-start(bf16[512,1024]{1,0:T(8,128)(2,1)S(1)} %get-tuple-element.431.na_ref), channel_id=1, source_target_pairs={{0,1},{1,0},{2,3},{3,2},{4,5},{5,4},{6,7},{7,6},{8,9},{9,8},{10,11... | collective-permute-start | bytes 3145736 | tf_op jit(solution)/shard_map/ppermute | solution.py:801
  198.5 0.8 collective-permute-start.30
  199.4 1.4 collective-permute-start.33
  200.8 6.0 %collective-permute-done.33 = f32[1,1024]{1,0:T(1,128)S(1)} collective-permute-done((f32[1,1024]{1,0:T(1,128)S(1)}, f32[1,1024]{1,0:T(1,128)S(1)}, u32[]{:S(2)}, u32[]{:S(2)}) %collective-permute-start.33) | collective-permute-done | bytes 4128 | tf_op jit(solution)/shard_map/ppermute | solution.py:801
  206.8 2.5 %collective-permute-done.31.refs_3_ = bf16[160,512]{1,0:T(8,128)(2,1)S(1)} collective-permute-done((bf16[160,512]{1,0:T(8,128)(2,1)S(1)}, bf16[160,512]{1,0:T(8,128)(2,1)S(1)}, u32[]{:S(2)}, u32[]{:S(2)}) %collective-permute-start.31) | collective-permute-done | bytes 163872 | tf_op jit(solution)/shard_map/ppermute | solution.py:801
  209.8 0.9 collective-permute-start.34
  211.2 1.5 merge.12
  212.6 0.9 copy-done
  213.5 4.4 %ending.1 = (f32[1024,1024]{1,0:T(8,128)}, f32[512,1024]{1,0:T(8,128)}) custom-call(s32[2]{0:T(128)S(1)} %get-tuple-element.457.bits_ref, bf16[1024,1024]{1,0:T(8,128)(2,1)S(1)} %bitcast.25, bf16[512,1024]{1,0:T(8,128)(2,1)S(1)} %get-tuple-element.431.na_ref, bf16[512,1024]{1,0:T(8,128)(2,1)S(1)} %collective-permute-done.32.nb_ref, ...), custom_call_target="tpu_custom_call" | custom-call | flops 1048576 | bytes 12582912 | tf_op jit(solution)/shard_map/ending/pallas_call | solution.py:695
  218.6 4.4 %last.1 = (f32[1024,2,512]{2,1,0:T(2,128)}, f32[4,512]{1,0:T(4,128)}, f32[1,512]{1,0:T(1,128)}, f32[1,512]{1,0:T(1,128)}, f32[1,512]{1,0:T(1,128)}, /*index=5*/f...) custom-call(s32[3]{0:T(128)S(1)} %pad_add_fusion.4.bits_ref, bf16[320,512]{1,0:T(8,128)(2,1)S(1)} %get-tuple-element.439.sa_ref, ...), custom_call_target="tpu_custom_call" | custom-call | tf_op jit(solution)/shard_map/last/pallas_call | solution.py:733
  (83 shorter events, 8.8 us)
Async XLA Ops:
  4.1 8.3 %copy-start.12 = (bf16[64,512]{1,0:T(8,128)(2,1)S(1)}, bf16[64,512]{1,0:T(8,128)(2,1)}, u32[]{:S(2)}) copy-start(bf16[64,512]{1,0:T(8,128)(2,1)} %sw_ref.1) | copy-start | bytes 196612
  10.8 4.0 %collective-permute-start = (bf16[1024,96]{1,0:T(8,128)(2,1)}, bf16[1024,96]{1,0:T(8,128)(2,1)S(1)}, u32[]{:S(2)}, u32[]{:S(2)}) collective-permute-start(bf16[1024,96]{1,0:T(8,128)(2,1)} %get-tuple-element.234), channel_id=1, source_target_pairs={{0,1},{1,0},{2,3},{3,2},{4,5},{5,4},{6,7},{7,6},{8,9},{9,8},{10,11... | collective-permute-start | bytes 589832 | tf_op jit(solution)/shard_map/ppermute | solution.py:801
  15.8 9.4 %collective-permute-start.1 = (bf16[1024,96]{1,0:T(8,128)(2,1)S(1)}, bf16[1024,96]{1,0:T(8,128)(2,1)S(1)}, u32[]{:S(2)}, u32[]{:S(2)}) collective-permute-start(bf16[1024,96]{1,0:T(8,128)(2,1)S(1)} %add_convert_fusion.3), channel_id=1, source_target_pairs={{0,2},{1,3},{2,0},{3,1},{4,6},{5,7},{6,4},{7,5},{8,10},{9,11},{10,... | collective-permute-start | bytes 589832 | tf_op jit(solution)/shard_map/ppermute | solution.py:801
  66.5 16.7 %collective-permute-start.4 = (bf16[512,1024]{1,0:T(8,128)(2,1)}, bf16[512,1024]{1,0:T(8,128)(2,1)S(1)}, u32[]{:S(2)}, u32[]{:S(2)}) collective-permute-start(bf16[512,1024]{1,0:T(8,128)(2,1)} %get-tuple-element.254), channel_id=1, source_target_pairs={{0,1},{1,0},{2,3},{3,2},{4,5},{5,4},{6,7},{7,6},{8,9},{9,8},{10,11... | collective-permute-start | bytes 3145736 | tf_op jit(solution)/shard_map/ppermute | solution.py:801
  67.1 16.1 %collective-permute-start.2 = (bf16[512,512]{1,0:T(8,128)(2,1)}, bf16[512,512]{1,0:T(8,128)(2,1)}, u32[]{:S(2)}, u32[]{:S(2)}) collective-permute-start(bf16[512,512]{1,0:T(8,128)(2,1)} %get-tuple-element.252), channel_id=1, source_target_pairs={{0,4},{4,0},{8,12},{12,8},{16,20},{20,16},{24,28},{28,24},{1,5},{5... | collective-permute-start | bytes 1572872 | tf_op jit(solution)/shard_map/ppermute | solution.py:801
  68.0 15.3 %collective-permute-start.3 = (bf16[256,1024]{1,0:T(8,128)(2,1)}, bf16[256,1024]{1,0:T(8,128)(2,1)}, u32[]{:S(2)}, u32[]{:S(2)}) collective-permute-start(bf16[256,1024]{1,0:T(8,128)(2,1)} %get-tuple-element.253), channel_id=1, source_target_pairs={{0,8},{4,12},{8,0},{12,4},{16,24},{20,28},{24,16},{28,20},{1,9},{5... | collective-permute-start | bytes 1572872 | tf_op jit(solution)/shard_map/ppermute | solution.py:801
  71.4 11.8 %copy-start.1 = (bf16[512,1024]{1,0:T(8,128)(2,1)S(1)}, bf16[512,1024]{1,0:T(8,128)(2,1)}, u32[]{:S(2)}) copy-start(bf16[512,1024]{1,0:T(8,128)(2,1)} %get-tuple-element.273.refs_4_) | copy-start | bytes 3145732
  71.4 11.8 %copy-start.2 = (bf16[512,512]{1,0:T(8,128)(2,1)S(1)}, bf16[512,512]{1,0:T(8,128)(2,1)}, u32[]{:S(2)}) copy-start(bf16[512,512]{1,0:T(8,128)(2,1)} %get-tuple-element.247.refs_0_) | copy-start | bytes 1572868
  71.4 11.9 %copy-start.3 = (bf16[256,1024]{1,0:T(8,128)(2,1)S(1)}, bf16[256,1024]{1,0:T(8,128)(2,1)}, u32[]{:S(2)}) copy-start(bf16[256,1024]{1,0:T(8,128)(2,1)} %get-tuple-element.271.refs_2_) | copy-start | bytes 1572868
  85.8 0.8 copy-start.4
  86.6 0.7 copy-start.8
  87.3 15.8 %copy-start.5 = (bf16[256,1024]{1,0:T(8,128)(2,1)S(1)}, bf16[256,1024]{1,0:T(8,128)(2,1)}, u32[]{:S(2)}) copy-start(bf16[256,1024]{1,0:T(8,128)(2,1)} %copy-done.4) | copy-start | bytes 1572868
  87.3 15.8 %copy-start.9 = (bf16[128,1024]{1,0:T(8,128)(2,1)S(1)}, bf16[128,1024]{1,0:T(8,128)(2,1)}, u32[]{:S(2)}) copy-start(bf16[128,1024]{1,0:T(8,128)(2,1)} %copy-done.8) | copy-start | bytes 786436
  87.3 15.8 %collective-permute-start.7 = (bf16[256,1024]{1,0:T(8,128)(2,1)}, bf16[256,1024]{1,0:T(8,128)(2,1)S(1)}, u32[]{:S(2)}, u32[]{:S(2)}) collective-permute-start(bf16[256,1024]{1,0:T(8,128)(2,1)} %get-tuple-element.287), channel_id=1, source_target_pairs={{0,2},{1,3},{2,0},{3,1},{4,6},{5,7},{6,4},{7,5},{8,10},{9,11},{10,... | collective-permute-start | bytes 1572872 | tf_op jit(solution)/shard_map/ppermute | solution.py:801
  88.5 14.5 %collective-permute-start.5 = (bf16[256,512]{1,0:T(8,128)(2,1)}, bf16[256,512]{1,0:T(8,128)(2,1)S(1)}, u32[]{:S(2)}, u32[]{:S(2)}) collective-permute-start(bf16[256,512]{1,0:T(8,128)(2,1)} %get-tuple-element.285), channel_id=1, source_target_pairs={{0,8},{4,12},{8,0},{12,4},{16,24},{20,28},{24,16},{28,20},{1,9},{5... | collective-permute-start | bytes 786440 | tf_op jit(solution)/shard_map/ppermute | solution.py:801
  89.0 14.1 %collective-permute-start.6 = (bf16[128,1024]{1,0:T(8,128)(2,1)}, bf16[128,1024]{1,0:T(8,128)(2,1)S(1)}, u32[]{:S(2)}, u32[]{:S(2)}) collective-permute-start(bf16[128,1024]{1,0:T(8,128)(2,1)} %get-tuple-element.286), channel_id=1, source_target_pairs={{0,16},{4,20},{8,24},{12,28},{16,0},{20,4},{24,8},{28,12},{1,17},{... | collective-permute-start | bytes 786440 | tf_op jit(solution)/shard_map/ppermute | solution.py:801
  104.0 14.9 %collective-permute-start.10 = (bf16[256,1024]{1,0:T(8,128)(2,1)S(1)}, bf16[256,1024]{1,0:T(8,128)(2,1)S(1)}, u32[]{:S(2)}, u32[]{:S(2)}) collective-permute-start(bf16[256,1024]{1,0:T(8,128)(2,1)S(1)} %get-tuple-element.336.refs_4_), channel_id=1, source_target_pairs={{0,2},{1,3},{2,0},{3,1},{4,6},{5,7},{6,4},{7,5},{8,10},{9,11},{10,... | collective-permute-start | bytes 1572872 | tf_op jit(solution)/shard_map/ppermute | solution.py:801
  104.3 14.6 %collective-permute-start.8 = (bf16[256,512]{1,0:T(8,128)(2,1)S(1)}, bf16[256,512]{1,0:T(8,128)(2,1)S(1)}, u32[]{:S(2)}, u32[]{:S(2)}) collective-permute-start(bf16[256,512]{1,0:T(8,128)(2,1)S(1)} %get-tuple-element.332.refs_0_), channel_id=1, source_target_pairs={{0,16},{4,20},{8,24},{12,28},{16,0},{20,4},{24,8},{28,12},{1,17},{... | collective-permute-start | bytes 786440 | tf_op jit(solution)/shard_map/ppermute | solution.py:801
  104.6 14.3 %collective-permute-start.9 = (bf16[128,1024]{1,0:T(8,128)(2,1)S(1)}, bf16[128,1024]{1,0:T(8,128)(2,1)S(1)}, u32[]{:S(2)}, u32[]{:S(2)}) collective-permute-start(bf16[128,1024]{1,0:T(8,128)(2,1)S(1)} %get-tuple-element.334.refs_2_), channel_id=1, source_target_pairs={{0,4},{4,0},{8,12},{12,8},{16,20},{20,16},{24,28},{28,24},{1,5},{5... | collective-permute-start | bytes 786440 | tf_op jit(solution)/shard_map/ppermute | solution.py:801
  114.8 6.1 %copy-start.11 = (bf16[1024,96]{1,0:T(8,128)(2,1)S(1)}, bf16[1024,96]{1,0:T(8,128)(2,1)}, u32[]{:S(2)}) copy-start(bf16[1024,96]{1,0:T(8,128)(2,1)} %get-tuple-element.331) | copy-start | bytes 589828
  118.9 2.0 collective-permute-start.11
  121.0 14.8 %collective-permute-start.15 = (bf16[512,1024]{1,0:T(8,128)(2,1)S(1)}, bf16[512,1024]{1,0:T(8,128)(2,1)S(1)}, u32[]{:S(2)}, u32[]{:S(2)}) collective-permute-start(bf16[512,1024]{1,0:T(8,128)(2,1)S(1)} %get-tuple-element.345.refs_0_), channel_id=1, source_target_pairs={{0,1},{1,0},{2,3},{3,2},{4,5},{5,4},{6,7},{7,6},{8,9},{9,8},{10,11... | collective-permute-start | bytes 3145736 | tf_op jit(solution)/shard_map/ppermute | solution.py:801
  121.4 11.9 %collective-permute-start.13 = (bf16[256,512]{1,0:T(8,128)(2,1)S(1)}, bf16[256,512]{1,0:T(8,128)(2,1)S(1)}, u32[]{:S(2)}, u32[]{:S(2)}) collective-permute-start(bf16[256,512]{1,0:T(8,128)(2,1)S(1)} %get-tuple-element.347.refs_0_), channel_id=1, source_target_pairs={{0,8},{4,12},{8,0},{12,4},{16,24},{20,28},{24,16},{28,20},{1,9},{5... | collective-permute-start | bytes 786440 | tf_op jit(solution)/shard_map/ppermute | solution.py:801
  121.4 14.3 %collective-permute-start.14 = (bf16[128,1024]{1,0:T(8,128)(2,1)S(1)}, bf16[128,1024]{1,0:T(8,128)(2,1)S(1)}, u32[]{:S(2)}, u32[]{:S(2)}) collective-permute-start(bf16[128,1024]{1,0:T(8,128)(2,1)S(1)} %get-tuple-element.349.refs_2_), channel_id=1, source_target_pairs={{0,16},{4,20},{8,24},{12,28},{16,0},{20,4},{24,8},{28,12},{1,17},{... | collective-permute-start | bytes 786440 | tf_op jit(solution)/shard_map/ppermute | solution.py:801
  122.5 7.1 %collective-permute-start.12 = (bf16[1024,96]{1,0:T(8,128)(2,1)S(1)}, bf16[1024,96]{1,0:T(8,128)(2,1)S(1)}, u32[]{:S(2)}, u32[]{:S(2)}) collective-permute-start(bf16[1024,96]{1,0:T(8,128)(2,1)S(1)} %add_convert_fusion.1), channel_id=1, source_target_pairs={{0,2},{1,3},{2,0},{3,1},{4,6},{5,7},{6,4},{7,5},{8,10},{9,11},{10,... | collective-permute-start | bytes 589832 | tf_op jit(solution)/shard_map/ppermute | solution.py:801
  137.9 16.9 %collective-permute-start.16 = (bf16[512,512]{1,0:T(8,128)(2,1)S(1)}, bf16[512,512]{1,0:T(8,128)(2,1)}, u32[]{:S(2)}, u32[]{:S(2)}) collective-permute-start(bf16[512,512]{1,0:T(8,128)(2,1)S(1)} %get-tuple-element.443.sz_ref), channel_id=1, source_target_pairs={{0,4},{4,0},{8,12},{12,8},{16,20},{20,16},{24,28},{28,24},{1,5},{5... | collective-permute-start | bytes 1572872 | tf_op jit(solution)/shard_map/ppermute | solution.py:801
  138.5 16.4 %collective-permute-start.17 = (bf16[256,1024]{1,0:T(8,128)(2,1)}, bf16[256,1024]{1,0:T(8,128)(2,1)}, u32[]{:S(2)}, u32[]{:S(2)}) collective-permute-start(bf16[256,1024]{1,0:T(8,128)(2,1)} %get-tuple-element.433.oa_ref), channel_id=1, source_target_pairs={{0,8},{4,12},{8,0},{12,4},{16,24},{20,28},{24,16},{28,20},{1,9},{5... | collective-permute-start | bytes 1572872 | tf_op jit(solution)/shard_map/ppermute | solution.py:801
  154.9 3.5 %copy-start.15 = (bf16[320,512]{1,0:T(8,128)(2,1)S(1)}, bf16[320,512]{1,0:T(8,128)(2,1)}, u32[]{:S(2)}) copy-start(bf16[320,512]{1,0:T(8,128)(2,1)} %get-tuple-element.377) | copy-start | bytes 983044
  154.9 4.1 %copy-start.14 = (bf16[320,512]{1,0:T(8,128)(2,1)S(1)}, bf16[320,512]{1,0:T(8,128)(2,1)}, u32[]{:S(2)}) copy-start(bf16[320,512]{1,0:T(8,128)(2,1)} %get-tuple-element.378) | copy-start | bytes 983044
  154.9 5.8 %copy-start.13 = (f32[1,1024]{1,0:T(1,128)S(1)}, f32[1,1024]{1,0:T(1,128)}, u32[]{:S(2)}) copy-start(f32[1,1024]{1,0:T(1,128)} %get-tuple-element.380) | copy-start | bytes 12292
  154.9 13.6 %copy-start.6 = (bf16[320,512]{1,0:T(8,128)(2,1)S(1)}, bf16[320,512]{1,0:T(8,128)(2,1)}, u32[]{:S(2)}) copy-start(bf16[320,512]{1,0:T(8,128)(2,1)} %get-tuple-element.371.refs_0_) | copy-start | bytes 983044
  154.9 13.6 %copy-start.7 = (bf16[320,512]{1,0:T(8,128)(2,1)S(1)}, bf16[320,512]{1,0:T(8,128)(2,1)}, u32[]{:S(2)}) copy-start(bf16[320,512]{1,0:T(8,128)(2,1)} %get-tuple-element.382.refs_2_) | copy-start | bytes 983044
  156.7 25.5 %copy-start.10 = (f32[1024]{0:T(1024)S(1)}, f32[1024]{0:T(1024)}, u32[]{:S(2)}) copy-start(f32[1024]{0:T(1024)} %param.15) | copy-start | bytes 12292
  156.7 11.8 %collective-permute-start.20 = (bf16[512,1024]{1,0:T(8,128)(2,1)S(1)}, bf16[512,1024]{1,0:T(8,128)(2,1)S(1)}, u32[]{:S(2)}, u32[]{:S(2)}) collective-permute-start(bf16[512,1024]{1,0:T(8,128)(2,1)S(1)} %get-tuple-element.379), channel_id=1, source_target_pairs={{0,1},{1,0},{2,3},{3,2},{4,5},{5,4},{6,7},{7,6},{8,9},{9,8},{10,11... | collective-permute-start | bytes 3145736 | tf_op jit(solution)/shard_map/ppermute | solution.py:801
  158.3 9.3 %collective-permute-start.18 = (bf16[320,512]{1,0:T(8,128)(2,1)S(1)}, bf16[320,512]{1,0:T(8,128)(2,1)S(1)}, u32[]{:S(2)}, u32[]{:S(2)}) collective-permute-start(bf16[320,512]{1,0:T(8,128)(2,1)S(1)} %copy-done.15), channel_id=1, source_target_pairs={{0,4},{4,0},{8,12},{12,8},{16,20},{20,16},{24,28},{28,24},{1,5},{5... | collective-permute-start | bytes 983048 | tf_op jit(solution)/shard_map/ppermute | solution.py:801
  159.0 9.5 %collective-permute-start.19 = (bf16[320,512]{1,0:T(8,128)(2,1)S(1)}, bf16[320,512]{1,0:T(8,128)(2,1)S(1)}, u32[]{:S(2)}, u32[]{:S(2)}) collective-permute-start(bf16[320,512]{1,0:T(8,128)(2,1)S(1)} %copy-done.14), channel_id=1, source_target_pairs={{0,8},{4,12},{8,0},{12,4},{16,24},{20,28},{24,16},{28,20},{1,9},{5... | collective-permute-start | bytes 983048 | tf_op jit(solution)/shard_map/ppermute | solution.py:801
  160.7 1.5 collective-permute-start.21
  169.5 12.8 %collective-permute-start.24 = (bf16[256,1024]{1,0:T(8,128)(2,1)S(1)}, bf16[256,1024]{1,0:T(8,128)(2,1)S(1)}, u32[]{:S(2)}, u32[]{:S(2)}) collective-permute-start(bf16[256,1024]{1,0:T(8,128)(2,1)S(1)} %get-tuple-element.392), channel_id=1, source_target_pairs={{0,2},{1,3},{2,0},{3,1},{4,6},{5,7},{6,4},{7,5},{8,10},{9,11},{10,... | collective-permute-start | bytes 1572872 | tf_op jit(solution)/shard_map/ppermute | solution.py:801
  170.7 11.5 %collective-permute-start.22 = (bf16[160,512]{1,0:T(8,128)(2,1)S(1)}, bf16[160,512]{1,0:T(8,128)(2,1)S(1)}, u32[]{:S(2)}, u32[]{:S(2)}) collective-permute-start(bf16[160,512]{1,0:T(8,128)(2,1)S(1)} %get-tuple-element.390), channel_id=1, source_target_pairs={{0,8},{4,12},{8,0},{12,4},{16,24},{20,28},{24,16},{28,20},{1,9},{5... | collective-permute-start | bytes 491528 | tf_op jit(solution)/shard_map/ppermute | solution.py:801
  171.9 10.3 %collective-permute-start.23 = (bf16[160,512]{1,0:T(8,128)(2,1)S(1)}, bf16[160,512]{1,0:T(8,128)(2,1)S(1)}, u32[]{:S(2)}, u32[]{:S(2)}) collective-permute-start(bf16[160,512]{1,0:T(8,128)(2,1)S(1)} %get-tuple-element.391), channel_id=1, source_target_pairs={{0,16},{4,20},{8,24},{12,28},{16,0},{20,4},{24,8},{28,12},{1,17},{... | collective-permute-start | bytes 491528 | tf_op jit(solution)/shard_map/ppermute | solution.py:801
  172.0 10.2 %collective-permute-start.25 = (f32[1,1024]{1,0:T(1,128)S(1)}, f32[1,1024]{1,0:T(1,128)S(1)}, u32[]{:S(2)}, u32[]{:S(2)}) collective-permute-start(f32[1,1024]{1,0:T(1,128)S(1)} %add.44), channel_id=1, source_target_pairs={{0,2},{1,3},{2,0},{3,1},{4,6},{5,7},{6,4},{7,5},{8,10},{9,11},{10,... | collective-permute-start | bytes 12296 | tf_op jit(solution)/shard_map/ppermute | solution.py:801
  183.4 11.7 %collective-permute-start.28 = (bf16[256,1024]{1,0:T(8,128)(2,1)S(1)}, bf16[256,1024]{1,0:T(8,128)(2,1)S(1)}, u32[]{:S(2)}, u32[]{:S(2)}) collective-permute-start(bf16[256,1024]{1,0:T(8,128)(2,1)S(1)} %get-tuple-element.412.refs_4_), channel_id=1, source_target_pairs={{0,2},{1,3},{2,0},{3,1},{4,6},{5,7},{6,4},{7,5},{8,10},{9,11},{10,... | collective-permute-start | bytes 1572872 | tf_op jit(solution)/shard_map/ppermute | solution.py:801
  184.6 9.8 %collective-permute-start.26 = (bf16[160,512]{1,0:T(8,128)(2,1)S(1)}, bf16[160,512]{1,0:T(8,128)(2,1)S(1)}, u32[]{:S(2)}, u32[]{:S(2)}) collective-permute-start(bf16[160,512]{1,0:T(8,128)(2,1)S(1)} %get-tuple-element.408.refs_0_), channel_id=1, source_target_pairs={{0,16},{4,20},{8,24},{12,28},{16,0},{20,4},{24,8},{28,12},{1,17},{... | collective-permute-start | bytes 491528 | tf_op jit(solution)/shard_map/ppermute | solution.py:801
  185.5 8.9 %collective-permute-start.27 = (bf16[160,512]{1,0:T(8,128)(2,1)S(1)}, bf16[160,512]{1,0:T(8,128)(2,1)S(1)}, u32[]{:S(2)}, u32[]{:S(2)}) collective-permute-start(bf16[160,512]{1,0:T(8,128)(2,1)S(1)} %get-tuple-element.410.refs_2_), channel_id=1, source_target_pairs={{0,4},{4,0},{8,12},{12,8},{16,20},{20,16},{24,28},{28,24},{1,5},{5... | collective-permute-start | bytes 491528 | tf_op jit(solution)/shard_map/ppermute | solution.py:801
  186.4 3.6 %collective-permute-start.29 = (f32[1,1024]{1,0:T(1,128)S(1)}, f32[1,1024]{1,0:T(1,128)S(1)}, u32[]{:S(2)}, u32[]{:S(2)}) collective-permute-start(f32[1,1024]{1,0:T(1,128)S(1)} %add.45), channel_id=1, source_target_pairs={{0,4},{4,0},{8,12},{12,8},{16,20},{20,16},{24,28},{28,24},{1,5},{5... | collective-permute-start | bytes 12296 | tf_op jit(solution)/shard_map/ppermute | solution.py:801
  195.8 13.5 %collective-permute-start.32 = (bf16[512,1024]{1,0:T(8,128)(2,1)S(1)}, bf16[512,1024]{1,0:T(8,128)(2,1)S(1)}, u32[]{:S(2)}, u32[]{:S(2)}) collective-permute-start(bf16[512,1024]{1,0:T(8,128)(2,1)S(1)} %get-tuple-element.431.na_ref), channel_id=1, source_target_pairs={{0,1},{1,0},{2,3},{3,2},{4,5},{5,4},{6,7},{7,6},{8,9},{9,8},{10,11... | collective-permute-start | bytes 3145736 | tf_op jit(solution)/shard_map/ppermute | solution.py:801
  198.5 8.2 %collective-permute-start.30 = (bf16[160,512]{1,0:T(8,128)(2,1)S(1)}, bf16[160,512]{1,0:T(8,128)(2,1)S(1)}, u32[]{:S(2)}, u32[]{:S(2)}) collective-permute-start(bf16[160,512]{1,0:T(8,128)(2,1)S(1)} %get-tuple-element.422.refs_0_), channel_id=1, source_target_pairs={{0,8},{4,12},{8,0},{12,4},{16,24},{20,28},{24,16},{28,20},{1,9},{5... | collective-permute-start | bytes 491528 | tf_op jit(solution)/shard_map/ppermute | solution.py:801
  199.3 9.9 %collective-permute-start.31 = (bf16[160,512]{1,0:T(8,128)(2,1)S(1)}, bf16[160,512]{1,0:T(8,128)(2,1)S(1)}, u32[]{:S(2)}, u32[]{:S(2)}) collective-permute-start(bf16[160,512]{1,0:T(8,128)(2,1)S(1)} %get-tuple-element.424.refs_2_), channel_id=1, source_target_pairs={{0,16},{4,20},{8,24},{12,28},{16,0},{20,4},{24,8},{28,12},{1,17},{... | collective-permute-start | bytes 491528 | tf_op jit(solution)/shard_map/ppermute | solution.py:801
  199.4 7.4 %collective-permute-start.33 = (f32[1,1024]{1,0:T(1,128)S(1)}, f32[1,1024]{1,0:T(1,128)S(1)}, u32[]{:S(2)}, u32[]{:S(2)}) collective-permute-start(f32[1,1024]{1,0:T(1,128)S(1)} %add.46), channel_id=1, source_target_pairs={{0,8},{4,12},{8,0},{12,4},{16,24},{20,28},{24,16},{28,20},{1,9},{5... | collective-permute-start | bytes 12296 | tf_op jit(solution)/shard_map/ppermute | solution.py:801
  209.8 8.7 %collective-permute-start.34 = (bf16[320,512]{1,0:T(8,128)(2,1)S(1)}, bf16[320,512]{1,0:T(8,128)(2,1)S(1)}, u32[]{:S(2)}, u32[]{:S(2)}) collective-permute-start(bf16[320,512]{1,0:T(8,128)(2,1)S(1)} %get-tuple-element.439.sa_ref), channel_id=1, source_target_pairs={{0,4},{4,0},{8,12},{12,8},{16,20},{20,16},{24,28},{28,24},{1,5},{5... | collective-permute-start | bytes 983048 | tf_op jit(solution)/shard_map/ppermute | solution.py:801
  210.8 7.9 %collective-permute-start.35 = (bf16[320,512]{1,0:T(8,128)(2,1)S(1)}, bf16[320,512]{1,0:T(8,128)(2,1)S(1)}, u32[]{:S(2)}, u32[]{:S(2)}) collective-permute-start(bf16[320,512]{1,0:T(8,128)(2,1)S(1)} %get-tuple-element.441.sb_ref), channel_id=1, source_target_pairs={{0,8},{4,12},{8,0},{12,4},{16,24},{20,28},{24,16},{28,20},{1,9},{5... | collective-permute-start | bytes 983048 | tf_op jit(solution)/shard_map/ppermute | solution.py:801
  210.8 7.1 %collective-permute-start.36 = (f32[1,1024]{1,0:T(1,128)S(1)}, f32[1,1024]{1,0:T(1,128)S(1)}, u32[]{:S(2)}, u32[]{:S(2)}) collective-permute-start(f32[1,1024]{1,0:T(1,128)S(1)} %add.47), channel_id=1, source_target_pairs={{0,16},{4,20},{8,24},{12,28},{16,0},{20,4},{24,8},{28,12},{1,17},{... | collective-permute-start | bytes 12296 | tf_op jit(solution)/shard_map/ppermute | solution.py:801
  211.2 2.3 %copy-start = (bf16[1,1024,1024]{2,1,0:T(8,128)(2,1)S(1)}, bf16[1,1024,1024]{2,1,0:T(8,128)(2,1)}, u32[]{:S(2)}) copy-start(bf16[1,1024,1024]{2,1,0:T(8,128)(2,1)} %param.25) | copy-start | bytes 6291460

commit v3 on v2

--- a/solution.py
+++ b/solution.py
@@ -258,8 +258,8 @@
         part_ref[...] = mm(rc_s[...], fold(r + n, p, n))
 
 
-def back_kernel(ng, top, low, far, prefix_ref, proj_ref, sw_ref, drive_ref, step_ref, dy_ref, h_ref, ag_ref, wg_ref, pin_ref, dlog_ref, skip_ref, pc_ref, ac_ref, bc_ref, *refs):
-    (part_ref, dpre_ref, ddrive_ref, po_ref, ao_ref, gbias_ref, step_s, dy_s, p_s, ct_s, bbd_s, rb_s, ds_s, v_s, w_s) = refs[far:]
+def back_kernel(ng, top, low, far, prefix_ref, proj_ref, sw_ref, drive_ref, step_ref, dy_ref, h_ref, pin_ref, dlog_ref, skip_ref, *refs):
+    (part_ref, dpre_ref, ddrive_ref, po_ref, ao_ref, gbias_ref, step_s, dy_s, p_s, ct_s, bbd_s, rb_s, ds_s, v_s, w_s, sw_s) = refs[far:]
     lc, c = drive_ref.shape
     p = proj_ref.shape[1]
     n = dlog_ref.shape[0]
@@ -275,11 +275,20 @@
 
     @pl.when(i == 0)
     def _():
-        for g in range(groups):
-            p_s[g] = pc_ref[:, lanes[g]]
-        ao_ref[...] = ac_ref[...]
-        gbias_ref[...] = bc_ref[...]
-
+        sw_s[...] = jnp.zeros_like(sw_s)
+        sw_s[pl.ds(0, r), :] = sw_ref[...]
+        if far >= 6:
+            pc_ref, ac_ref, bc_ref = refs[far - 6 : far - 3]
+            for g in range(groups):
+                p_s[g] = pc_ref[:, lanes[g]]
+            ao_ref[...] = ac_ref[...]
+            gbias_ref[...] = bc_ref[...]
+        else:
+            p_s[...] = jnp.zeros_like(p_s)
+            ao_ref[...] = jnp.zeros_like(ao_ref)
+            gbias_ref[...] = jnp.zeros_like(gbias_ref)
+
+    ag_ref, wg_ref = refs[:2] if low < ng else (None, None)
     proj = proj_ref[...]
     split(step_s, step_ref[...])
     split(dy_s, dy_ref[...])
@@ -389,7 +398,7 @@
         def _():
             run(False)
 
-    part_ref[...] = (pin_ref[...] + mm(rb_s[...], fold(r, p, n)) + mm_nt(dpre_ref[...], sw_ref[...])).astype(part_ref.dtype)
+    part_ref[...] = (pin_ref[...] + mm(rb_s[...], fold(r, p, n)) + mm_nt(dpre_ref[...], sw_s[...])).astype(part_ref.dtype)
     po_ref[...] = jnp.concatenate([p_s[g] for g in range(groups)], axis=1)
 
 
@@ -400,7 +409,7 @@
 SMEM = pl.BlockSpec(memory_space=pltpu.SMEM)
 
 
-def head_kernel(low_ref, gain_ref, w_ref, cw_ref, cb_ref, xw_ref, normed_ref, x_ref, drive_ref, part_ref, rs_ref, edge_s):
+def head_kernel(low_ref, gain_ref, w_ref, cw_ref, cb_ref, xw_ref, normed_ref, x_ref, slope_ref, drive_ref, part_ref, rs_ref, edge_s):
     taps = cw_ref.shape[0]
     lc = low_ref.shape[0]
 
@@ -414,14 +423,17 @@
     normed = (xf * rs * gain_ref[...]).astype(BF)
     normed_ref[...] = normed
     x = mm(normed, w_ref[...])
-    x_ref[...] = x
+    x_ref[...] = x.astype(BF)
     wide = jnp.concatenate([edge_s[...], x], axis=0)
     edge_s[...] = x[lc - 8 :]
     out = cb_ref[...] + cw_ref[taps - 1 :, :] * x
     for k in range(taps - 1):
         at = 8 - (taps - 1) + k
         out = out + cw_ref[k : k + 1, :] * wide[at : at + lc]
-    drive = (out * sigmoid(out)).astype(BF)
+    sc = sigmoid(out)
+    act = out * sc
+    slope_ref[...] = sc * (1.0 + out - act)
+    drive = act.astype(BF)
     drive_ref[...] = drive
     part_ref[...] = mm_nt(drive, xw_ref[...]).astype(BF)
 
@@ -437,8 +449,8 @@
         head_kernel,
         grid=(l // hc,),
         in_specs=[by(d), whole(1, d), whole(d, c), whole(*conv_weight.shape), whole(1, c), whole(p, c)],
-        out_specs=[by(d), by(c), by(c), by(p), by(1)],
-        out_shape=[s((l, d), BF), s((l, c), F32), s((l, c), BF), s((l, p), BF), s((l, 1), F32)],
+        out_specs=[by(d), by(c), by(c), by(c), by(p), by(1)],
+        out_shape=[s((l, d), BF), s((l, c), BF), s((l, c), F32), s((l, c), BF), s((l, p), BF), s((l, 1), F32)],
         scratch_shapes=[pltpu.VMEM((8, c), F32)],
         compiler_params=pltpu.CompilerParams(vmem_limit_bytes=60 << 20),
         cost_estimate=pl.CostEstimate(flops=2 * l * d * c, transcendentals=l * c, bytes_accessed=4 * l * d + 2 * d * c + 6 * l * c),
@@ -468,7 +480,7 @@
     )(normed, w_all, cot, out_weight)
 
 
-def inner_kernel(rows_a, rows_b, bits_ref, dproj_ref, ds_ref, x_ref, xb_ref, drive_ref, dz_ref, normed_ref, low_ref, rs_ref, w_ref, xw_ref, cw_ref, cb_ref,
+def inner_kernel(rows_a, rows_b, bits_ref, dproj_ref, ds_ref, x_ref, slope_ref, drive_ref, dz_ref, normed_ref, low_ref, rs_ref, w_ref, xw_ref, cw_ref,
                  gb_ref, gd_ref, dlog_ref, gk_ref, proj_ref, dpre_ref, ka_ref, sa_ref, kb_ref, sb_ref, kn_ref, sn_ref, gn_ref, edge_s, gin_s, gx_s, gs_s, gc_s, gn_s, la_s, lb_s):
     taps = cw_ref.shape[0]
     lc, c = ds_ref.shape
@@ -489,39 +501,34 @@
         gc_s[...] = jnp.zeros_like(gc_s)
         gn_s[...] = jnp.zeros_like(gn_s)
 
-    x = x_ref[...]
-    before = jnp.where(i == last, 0.0, xb_ref[...])
-    wide = jnp.concatenate([before, x], axis=0)
-    moved = [wide[8 - (taps - 1) + k : 8 - (taps - 1) + k + lc] for k in range(taps - 1)] + [x]
-    out = cb_ref[...]
-    for k in range(taps):
-        out = out + cw_ref[k : k + 1, :] * moved[k]
-    sc = sigmoid(out)
     dproj = dproj_ref[...]
-    ddrive = ds_ref[...] + mm(dproj, xw_ref[...])
-    dconv = ddrive * (sc * (1.0 + out * (1.0 - sc)))
+    x = x_ref[...].astype(F32)
+    dconv = (ds_ref[...] + mm(dproj, xw_ref[...])) * slope_ref[...]
     gc_s[pl.ds(taps, 1), :] += jnp.sum(dconv, axis=0, keepdims=True)
-    for k in range(taps):
-        gc_s[pl.ds(k, 1), :] += jnp.sum(dconv * moved[k], axis=0, keepdims=True)
     ahead = jnp.concatenate([dconv, edge_s[...]], axis=0)
     edge_s[...] = dconv[:8]
     dx = cw_ref[taps - 1 :, :] * dconv
+    gc_s[pl.ds(taps - 1, 1), :] += jnp.sum(dconv * x, axis=0, keepdims=True)
     for k in range(taps - 1):
         by = taps - 1 - k
-        dx = dx + cw_ref[k : k + 1, :] * ahead[by : by + lc]
+        moved = ahead[by : by + lc]
+        dx = dx + cw_ref[k : k + 1, :] * moved
+        gc_s[pl.ds(k, 1), :] += jnp.sum(moved * x, axis=0, keepdims=True)
     dx = dx.astype(BF)
     normed = normed_ref[...]
     gin_s[...] += lax.dot_general(normed, dx, tn, preferred_element_type=F32)
     gx_s[...] += lax.dot_general(dproj, drive_ref[...], tn, preferred_element_type=F32)
     gs_s[...] += lax.dot_general(proj_ref[:, :r], dpre_ref[...], tn, preferred_element_type=F32)
-    dn = mm_nt(dx, w_ref[:, :c]) + mm_nt(dz_ref[...], w_ref[:, c:])
+    dn = mm_nt(jnp.concatenate([dx, dz_ref[...]], axis=1), w_ref[...])
     half = pl.num_programs(0) // 2
 
-    @pl.when(i < half)
+    keeps = (i < half) == (bits_ref[2] == 1)
+
+    @pl.when(jnp.logical_not(keeps))
     def _():
         sn_ref[...] = dn.astype(BF)
 
-    @pl.when(i >= half)
+    @pl.when(keeps)
     def _():
         kn_ref[...] = dn.astype(BF)
 
@@ -540,93 +547,77 @@
         la_s[pl.ds(top, rows_a - top), :] = gin_s[pl.ds(0, rows_a - top), :].astype(BF)
         rest = d - (rows_a - top)
         lb_s[pl.ds(0, rest), :] = gin_s[pl.ds(rows_a - top, rest), :].astype(BF)
-        lb_s[pl.ds(rest, rows_b - rest), :] = jnp.zeros((rows_b - rest, c), BF)
+        if rows_b > rest:
+            lb_s[pl.ds(rest, rows_b - rest), :] = jnp.zeros((rows_b - rest, c), BF)
         for bit, total, keep_ref, send_ref in ((bits_ref[0], la_s, ka_ref, sa_ref), (bits_ref[1], lb_s, kb_ref, sb_ref)):
             rows = keep_ref.shape[0]
-            keep_ref[...] = total[pl.ds(pl.multiple_of(bit * rows, 16), rows), :]
-            send_ref[...] = total[pl.ds(pl.multiple_of((1 - bit) * rows, 16), rows), :]
-
-
-def inner(rows_a, rows_b, bits, dproj, ddrive, x, drive, dz, normed, low, rs, w_all, xproj_t, conv_weight, conv_bias, g_bias, g_decay, decay_log, g_skip, proj, dpre):
+            keep_ref[...] = total[pl.ds(pl.multiple_of(bit * rows, 8), rows), :]
+            send_ref[...] = total[pl.ds(pl.multiple_of((1 - bit) * rows, 8), rows), :]
+
+
+def inner(rows_a, rows_b, bits, dproj, ddrive, x, slope, drive, dz, normed, low, rs, w_all, xproj_t, conv_weight, g_bias, g_decay, decay_log, g_skip, proj, dpre):
     l, c = x.shape
     d = normed.shape[1]
     p = dproj.shape[1]
     n = g_decay.shape[0]
     hc = 256
     nc = l // hc
-    by = lambda w: pl.BlockSpec((hc, w), lambda i: (nc - 1 - i, 0))
+    by = lambda w: pl.BlockSpec((hc, w), lambda i, bits: (nc - 1 - i, 0))
+    full = lambda *q: pl.BlockSpec(q, lambda i, bits: (0,) * len(q))
     s = jax.ShapeDtypeStruct
     v = pltpu.VMEM
-    edge = pl.BlockSpec((8, c), lambda i: (jnp.maximum((nc - 1 - i) * (hc // 8) - 1, 0), 0))
-    upper = pl.BlockSpec((hc, d), lambda i: (jnp.maximum(nc // 2 - 1 - i, 0), 0))
-    lower = pl.BlockSpec((hc, d), lambda i: (jnp.minimum(nc - 1 - i, nc // 2 - 1), 0))
+    early = lambda i: jnp.maximum(nc // 2 - 1 - i, 0)
+    late = lambda i: jnp.minimum(nc - 1 - i, nc // 2 - 1)
+    kept = pl.BlockSpec((hc, d), lambda i, bits: (jnp.where(bits[2] == 1, early(i), late(i)), 0))
+    sent = pl.BlockSpec((hc, d), lambda i, bits: (jnp.where(bits[2] == 1, late(i), early(i)), 0))
     return pl.pallas_call(
         functools.partial(inner_kernel, rows_a, rows_b),
-        grid=(nc,),
-        in_specs=[SMEM, by(p), by(c), by(c), edge, by(c), by(c), by(d), by(d), by(1), whole(d, 2 * c), whole(p, c), whole(*conv_weight.shape), whole(1, c),
-                  whole(1, c), whole(n, c), whole(n, c), whole(1, c), by(p), by(c)],
-        out_specs=[whole(rows_a // 2, c)] * 2 + [whole(rows_b // 2, c)] * 2 + [lower, upper, whole(1, d)],
+        grid_spec=pltpu.PrefetchScalarGridSpec(
+            num_scalar_prefetch=1,
+            grid=(nc,),
+            in_specs=[by(p), by(c), by(c), by(c), by(c), by(c), by(d), by(d), by(1), full(d, 2 * c), full(p, c), full(*conv_weight.shape),
+                      full(1, c), full(n, c), full(n, c), full(1, c), by(p), by(c)],
+            out_specs=[full(rows_a // 2, c)] * 2 + [full(rows_b // 2, c)] * 2 + [kept, sent, full(1, d)],
+            scratch_shapes=[v((8, c), F32), v((d, c), F32), v((p, c), F32), v((p - 2 * n, c), F32), v((8, c), F32), v((1, d), F32), v((rows_a, c), BF), v((rows_b, c), BF)],
+        ),
         out_shape=[s((rows_a // 2, c), BF)] * 2 + [s((rows_b // 2, c), BF)] * 2 + [s((l // 2, d), BF)] * 2 + [s((1, d), F32)],
-        scratch_shapes=[v((8, c), F32), v((d, c), F32), v((p, c), F32), v((p - 2 * n, c), F32), v((8, c), F32), v((1, d), F32), v((rows_a, c), BF), v((rows_b, c), BF)],
         compiler_params=pltpu.CompilerParams(vmem_limit_bytes=60 << 20),
         cost_estimate=pl.CostEstimate(flops=6 * l * d * c, transcendentals=l * c, bytes_accessed=10 * l * d),
         name="inner",
-    )(bits, dproj, ddrive, x, x, drive, dz, normed, low, rs, w_all, xproj_t, conv_weight, conv_bias.reshape(1, c), g_bias, g_decay, decay_log, g_skip, proj, dpre)
-
-
-def outer_kernel(order_ref, normed_ref, dz_ref, gated_ref, cot_ref, w_ref, kz_ref, sz_ref, ko_ref, so_ref, km_ref, sm_ref, z_s, o_s):
-    i = pl.program_id(0)
+    )(bits, dproj, ddrive, x, slope, drive, dz, normed, low, rs, w_all, xproj_t, conv_weight, g_bias, g_decay, decay_log, g_skip, proj, dpre)
+
+
+def outer_kernel(order_ref, normed_ref, dz_ref, cols_ref, cot_ref, rows_ref, low_ref, w_ref, kz_ref, sz_ref, ko_ref, so_ref, km_ref, sm_ref):
     tn = (((0,), (0,)), ((), ()))
-
-    @pl.when(i == 0)
-    def _():
-        z_s[...] = jnp.zeros_like(z_s)
-        o_s[...] = jnp.zeros_like(o_s)
-
-    z_s[...] += lax.dot_general(normed_ref[...], dz_ref[...], tn, preferred_element_type=F32)
-    o_s[...] += lax.dot_general(gated_ref[...], cot_ref[...], tn, preferred_element_type=F32)
-    mix = mm(gated_ref[...], w_ref[...]).astype(BF)
-    half = pl.num_programs(0) // 2
-
-    @pl.when(i < half)
-    def _():
-        sm_ref[...] = mix
-
-    @pl.when(i >= half)
-    def _():
-        km_ref[...] = mix
-
-    @pl.when(i == pl.num_programs(0) - 1)
-    def _():
-        for bit, total, keep_ref, send_ref in ((order_ref[1], z_s, kz_ref, sz_ref), (order_ref[2], o_s, ko_ref, so_ref)):
-            rows = keep_ref.shape[0]
-            keep_ref[...] = total[pl.ds(pl.multiple_of(bit * rows, 16), rows), :].astype(BF)
-            send_ref[...] = total[pl.ds(pl.multiple_of((1 - bit) * rows, 16), rows), :].astype(BF)
-
-
-def outer(bits, normed, dz, gated, cot, out_weight):
+    for step, z_ref, o_ref, m_ref in ((0, sz_ref, so_ref, sm_ref), (1, kz_ref, ko_ref, km_ref)):
+        @pl.when(pl.program_id(0) == step)
+        def _(z_ref=z_ref, o_ref=o_ref, m_ref=m_ref):
+            z_ref[...] = lax.dot_general(normed_ref[...], dz_ref[...], tn, preferred_element_type=F32).astype(BF)
+            o_ref[...] = lax.dot_general(cols_ref[...], cot_ref[...], tn, preferred_element_type=F32).astype(BF)
+            mix = mm(rows_ref[...], w_ref[...])
+            m_ref[...] = (mix + jnp.where(order_ref[3] == 0, low_ref[...].astype(F32), 0.0)).astype(BF)
+
+
+def outer(bits, normed, dz, gated, cot, low, out_weight):
     l, d = normed.shape
     c = dz.shape[1]
-    hc = 256
-    nc = l // hc
-    by = lambda w: pl.BlockSpec((hc, w), lambda i, order: (lax.rem(i + (1 - order[0]) * (nc // 2), nc), 0))
     full = lambda *q: pl.BlockSpec(q, lambda i, order: (0,) * len(q))
+    half = lambda w, j: pl.BlockSpec((l, w // 2), lambda i, order: (0, lax.rem(i + 1 + order[j], 2)))
+    rows = lambda w: pl.BlockSpec((l // 2, w), lambda i, order: (lax.rem(i + 1 + order[2], 2), 0))
     s = jax.ShapeDtypeStruct
-    v = pltpu.VMEM
     return pl.pallas_call(
         outer_kernel,
         grid_spec=pltpu.PrefetchScalarGridSpec(
             num_scalar_prefetch=1,
-            grid=(nc,),
-            in_specs=[by(d), by(c), by(c), by(d), full(c, d)],
-            out_specs=[full(d // 2, c)] * 2 + [full(c // 2, d)] * 2 + [pl.BlockSpec((hc, d), lambda i, order: (jnp.maximum(i - nc // 2, 0), 0)), pl.BlockSpec((hc, d), lambda i, order: (jnp.minimum(i, nc // 2 - 1), 0))],
-            scratch_shapes=[v((d, c), F32), v((c, d), F32)],
+            grid=(2,),
+            in_specs=[half(d, 0), full(l, c), half(c, 1), full(l, d), rows(c), rows(d), full(c, d)],
+            out_specs=[full(d // 2, c)] * 2 + [full(c // 2, d)] * 2 + [full(l // 2, d)] * 2,
         ),
         out_shape=[s((d // 2, c), BF)] * 2 + [s((c // 2, d), BF)] * 2 + [s((l // 2, d), BF)] * 2,
         compiler_params=pltpu.CompilerParams(vmem_limit_bytes=60 << 20),
         cost_estimate=pl.CostEstimate(flops=6 * l * d * c, transcendentals=0, bytes_accessed=10 * l * d),
         name="outer",
-    )(bits, normed, dz, gated, cot, out_weight)
+    )(bits, normed, dz, gated, cot, gated, low, out_weight)
 
 
 def merge_kernel(kinds, bits_ref, *refs):
@@ -636,12 +627,12 @@
         rows = one.shape[0]
         if kind == "join":
             out = take.pop(0)
-            out[pl.ds(pl.multiple_of(bits_ref[j] * rows, 16), rows), :] = one[...]
-            out[pl.ds(pl.multiple_of((1 - bits_ref[j]) * rows, 16), rows), :] = two[...]
+            out[pl.ds(pl.multiple_of(bits_ref[j] * rows, 8), rows), :] = one[...]
+            out[pl.ds(pl.multiple_of((1 - bits_ref[j]) * rows, 8), rows), :] = two[...]
         elif kind == "split":
             half = rows // 2
             for out, at in ((take.pop(0), bits_ref[j]), (take.pop(0), 1 - bits_ref[j])):
-                part = pl.ds(pl.multiple_of(at * half, 16), half)
+                part = pl.ds(pl.multiple_of(at * half, 8), half)
                 out[...] = (one[part, :].astype(F32) + two[part, :].astype(F32)).astype(BF)
         else:
             total = one[...].astype(F32) + two[...].astype(F32)
@@ -658,6 +649,10 @@
 EXTRA = dict(join=0, split=0, sum=0, shift=1, norm=3)
 
 
+def once(*shape):
+    return pl.BlockSpec(shape, lambda i: (0,) * len(shape), pipeline_mode=pl.Buffered(1))
+
+
 def merge(items):
     kinds = tuple(item[0] for item in items)
     bits = jnp.stack([jnp.asarray(item[1], jnp.int32) for item in items])
@@ -667,13 +662,14 @@
         rows, cols = one.shape
         many = {"join": [2 * rows], "split": [rows // 2] * 2}.get(kind, [rows])
         shapes.append([jax.ShapeDtypeStruct((q, cols), BF) for q in many])
-    vm = pl.BlockSpec(memory_space=pltpu.VMEM)
     flat = [q for group in shapes for q in group]
+    homes = [len(group) == 2 and j == 0 for group in shapes for j in range(len(group))]
     out = list(pl.pallas_call(
         functools.partial(merge_kernel, kinds),
-        in_specs=[SMEM] + [vm] * len(arrays),
-        out_specs=[vm] * len(flat),
-        out_shape=flat,
+        grid=(1,),
+        in_specs=[SMEM] + [once(*v.shape) for v in arrays],
+        out_specs=[once(*v.shape) for v in flat],
+        out_shape=[pltpu.HBM(q.shape, q.dtype) if kept else q for q, kept in zip(flat, homes)],
         compiler_params=pltpu.CompilerParams(vmem_limit_bytes=24 << 20),
         name="merge",
     )(bits, *arrays))
@@ -684,7 +680,7 @@
     for bit, one, two, out, add in ((bits_ref[0], na_ref, nb_ref, tok_ref, cot_ref), (bits_ref[1], oa_ref, ob_ref, go_ref, None)):
         rows = one.shape[0]
         for at, part in ((bit, one), (1 - bit, two)):
-            where = pl.ds(pl.multiple_of(at * rows, 16), rows)
+            where = pl.ds(pl.multiple_of(at * rows, 8), rows)
             value = part[...].astype(F32)
             out[where, :] = value if add is None else value + add[where, :].astype(F32)
 
@@ -706,8 +702,8 @@
 def last_kernel(n, r, p, taps, bits_ref, sa_ref, oa_ref, sb_ref, ob_ref, sz_ref, oz_ref, gin_ref, gc_ref, gcb_ref, gb_ref, gk_ref, gd_ref, gs_ref, gx_ref, a_s, b_s):
     for j, mine, other, whole_s in ((0, sa_ref, oa_ref, a_s), (1, sb_ref, ob_ref, b_s)):
         half = mine.shape[0]
-        whole_s[pl.ds(pl.multiple_of(bits_ref[j] * half, 16), half), :] = mine[...]
-        whole_s[pl.ds(pl.multiple_of((1 - bits_ref[j]) * half, 16), half), :] = other[...]
+        whole_s[pl.ds(pl.multiple_of(bits_ref[j] * half, 8), half), :] = mine[...]
+        whole_s[pl.ds(pl.multiple_of((1 - bits_ref[j]) * half, 8), half), :] = other[...]
     lines = a_s[pl.ds(0, 16), :].astype(F32)
     gc_ref[...] = lines[:taps]
     gcb_ref[...] = lines[taps : taps + 1]
@@ -722,8 +718,8 @@
     cut = a_s.shape[0] - top
     gin_ref[pl.ds(0, cut), 0, :] = a_s[pl.ds(top, cut), :].astype(F32)
     gin_ref[pl.ds(cut, d - cut), 0, :] = b_s[pl.ds(0, d - cut), :].astype(F32)
-    gin_ref[pl.ds(pl.multiple_of(bits_ref[2] * half, 16), half), 1, :] = sz_ref[...].astype(F32)
-    gin_ref[pl.ds(pl.multiple_of((1 - bits_ref[2]) * half, 16), half), 1, :] = oz_ref[...].astype(F32)
+    gin_ref[pl.ds(pl.multiple_of(bits_ref[2] * half, 8), half), 1, :] = sz_ref[...].astype(F32)
+    gin_ref[pl.ds(pl.multiple_of((1 - bits_ref[2]) * half, 8), half), 1, :] = oz_ref[...].astype(F32)
 
 
 def last(bits, sa, oa, sb, ob, sz, oz, n, r, p, taps):
@@ -767,7 +763,7 @@
     )(prefix, proj, sw, bias.reshape(1, c), drive, z, dg, dlog, skip.reshape(1, c))
 
 
-def back(prefix, proj, sw_wide, drive, step, dy, hprev, ag, wg, pin, dlog, skip, carry, top, low, filled=()):
+def back(prefix, proj, sw, drive, step, dy, hprev, ag, wg, pin, dlog, skip, carry, top, low, filled=()):
     l, c = drive.shape
     p = proj.shape[1]
     n = dlog.shape[0]
@@ -777,20 +773,25 @@
     half = lambda i: (jnp.minimum(top - i, ng - 1), 0)
     B = pl.BlockSpec
     v = pltpu.VMEM
-    ins = [SMEM, B((LC, p), rev), whole(*sw_wide.shape), B((LC, c), rev), B((LC, c), rev), B((LC, c), rev), B((LC * n, c), rev), B((LC * n, c), half), B((LC * n, c), half), B((LC, p), rev), whole(n, c), whole(1, c), whole(n, c), whole(n, c), whole(1, c)]
-    steps = (top - low + 1) * LC * n * c
+    ins = [SMEM, B((LC, p), rev), whole(*sw.shape), B((LC, c), rev), B((LC, c), rev), B((LC, c), rev), B((LC * n, c), rev), B((LC, p), rev), whole(n, c), whole(1, c)]
+    extra, more = [], []
+    if low < ng:
+        extra, more = [ag, wg], [B((LC * n, c), half)] * 2
+    if filled:
+        extra, more = extra + list(carry) + list(filled), more + [whole(n, c), whole(n, c), whole(1, c)] + [B(memory_space=pl.ANY)] * 3
+    first = len(ins) + len(extra) - 3
     return pl.pallas_call(
-        functools.partial(back_kernel, ng, top, low, len(filled)),
+        functools.partial(back_kernel, ng, top, low, len(extra)),
         grid=(top - low + 1,),
-        in_specs=ins + [B(memory_space=pl.ANY)] * len(filled),
+        in_specs=ins + more,
         out_specs=[B((LC, p), rev), B((LC, c), rev), B((LC, c), rev), whole(n, c), whole(n, c), whole(1, c)],
         out_shape=[s((l, p), BF), s((l, c), BF), s((l, c), F32), s((n, c), F32), s((n, c), F32), s((1, c), F32)],
-        input_output_aliases={len(ins) + j: j for j in range(len(filled))},
-        scratch_shapes=[v((c // 128, LC, 128), F32)] * 2 + [v((c // 256, n, 256), F32), v((n, LC), F32), v((LC, T * n), BF), v((LC, T * n), BF), v((LC // T, T * n, c), BF), v((LC // T, T * n, c), BF), v((LC // T, T * n // 2, c), BF)],
+        input_output_aliases={first + j: j for j in range(3)} if filled else {},
+        scratch_shapes=[v((c // 128, LC, 128), F32)] * 2 + [v((c // 256, n, 256), F32), v((n, LC), F32), v((LC, T * n), BF), v((LC, T * n), BF), v((LC // T, T * n, c), BF), v((LC // T, T * n, c), BF), v((LC // T, T * n // 2, c), BF), v((p, c), BF)],
         compiler_params=pltpu.CompilerParams(vmem_limit_bytes=60 << 20),
-        cost_estimate=pl.CostEstimate(flops=steps * 4000, transcendentals=steps, bytes_accessed=steps * 4),
+        cost_estimate=pl.CostEstimate(flops=(top - low + 1) * LC * n * c * 4000, transcendentals=0, bytes_accessed=(top - low + 1) * LC * n * c * 4),
         name="back",
-    )(prefix, proj, sw_wide, drive, step, dy, hprev, ag, wg, pin, dlog, skip.reshape(1, c), *carry, *filled)
+    )(prefix, proj, sw, drive, step, dy, hprev, pin, dlog, skip.reshape(1, c), *extra)
 
 
 def sigmoid(v):
@@ -827,7 +828,7 @@
         after = self.steps[0]
         if kind == "double":
             return ("join", self.mine(bit), self.send, self.got)
-        one = self.keep if kind == "halve" else self.send
+        one = pltpu.with_memory_space_constraint(self.keep, pltpu.HBM) if kind == "halve" else self.send
         if kind == "halve" and after[0] == "halve":
             return ("split", self.mine(after[1]), one, self.got)
         if kind == "swap" or after[0] == "double":
@@ -835,6 +836,9 @@
             return (name, 0, one, self.got, *more)
         return ("sum", 0, one, self.got)
 
+    def ended(self):
+        return len(self.steps) == 1 and self.got is not None
+
     def accept(self, arrays):
         self.send = arrays[-1]
         self.keep = arrays[0]
@@ -842,20 +846,29 @@
 
 
 def ready(chains):
-    live = [c for c in chains if c.got is not None and len(c.steps) > 1]
+    live = [c for c in chains if c.got is not None and len(c.steps) > 1 and c not in PENDING]
     if live:
         for c, arrays in zip(live, merge([c.item() for c in live])):
             c.accept(arrays)
 
 
-def under(chains, work, *inputs):
-    chains = [c for c in chains if c.steps and c.got is None]
+PENDING = []
+
+
+def under(chains, work, *inputs, slow=()):
+    waiting = [c for c in PENDING if c.got is not None]
+    PENDING[:] = list(slow)
+    chains = [c for c in chains if c.steps and c.got is None] + list(slow)
     sends, inputs = lax.optimization_barrier(([c.send for c in chains], inputs))
     got = [c.start(v) for c, v in zip(chains, sends)]
     result = work(*inputs)
-    sends, got, result = lax.optimization_barrier((sends, got, result))
-    for c, v, w in zip(chains, sends, got):
+    hold = len(chains) - len(slow)
+    old = [c.got for c in waiting]
+    heads, firsts, old, result = lax.optimization_barrier((sends[:hold], got[:hold], old, result))
+    for c, v, w in zip(chains, list(heads) + list(sends[hold:]), list(firsts) + list(got[hold:])):
         c.send, c.got = v, w
+    for c, w in zip(waiting, old):
+        c.got = w
     return result
 
 
@@ -885,32 +898,30 @@
     part_of = lambda v: lax.dynamic_slice_in_dim(v, spot, rows, 0)
     bit_of = lambda v, bit: (v >> bit) & 1
 
-    normed, xpart, drive, proj, rs = head(low, norm_gain, w_all, conv_weight, conv_bias, xproj_t)
+    normed, xpart, slope, drive, proj, rs = head(low, norm_gain, w_all, conv_weight, conv_bias, xproj_t)
     for bit in t_order[:-1]:
         proj = (proj.astype(F32) + exchange(proj, "tensor", tp, bit).astype(F32)).astype(BF)
     proj, n_in, c_in = lax.optimization_barrier((proj, normed, cot))
     other = exchange(proj, "tensor", tp, t_order[-1])
     zpart, dgated = gates(n_in, w_all, c_in, out_weight)
-    my_x, my_rs = part_of(low), part_of(rs)
-    other, zpart, dgated, my_x, my_rs = lax.optimization_barrier((other, zpart, dgated, my_x, my_rs))
+    other, zpart, dgated = lax.optimization_barrier((other, zpart, dgated))
     proj = (proj.astype(F32) + other.astype(F32)).astype(BF)
 
     gated, dz, step, dy, hprev, ag, wg, pin, g_skip = front(prefix, proj, step_weight, step_bias, drive, zpart, dgated, decay_log, skip_gain)
 
-    picks = jnp.stack([bit_of(at, t_order[0]), bit_of(at_dp, order[0]), bit_of(at_dp, turned[0])]).astype(jnp.int32)
-    kz, sz, ko, so, km, sm = outer(picks, normed, dz, gated, cot, out_weight)
+    picks = jnp.stack([bit_of(at_dp, order[0]), bit_of(at_dp, turned[0]), bit_of(at, t_order[0]), at]).astype(jnp.int32)
+    kz, sz, ko, so, km, sm = outer(picks, normed, dz, gated, cot, low, out_weight)
     gz = Chain("dp", dp, order, kz, sz)
     go = Chain("dp", dp, turned, ko, so)
-    mix = Chain("tensor", tp, t_order, km, sm, swap=False, middle=("shift", (my_x,)))
+    mix = Chain("tensor", tp, t_order, km, sm, swap=False)
     chains = [gz, go, mix]
-    wide = jnp.pad(step_weight, ((0, 2 * n), (0, 0)))
     nc = length // LC
-    carry = (jnp.zeros((n, channels), F32), jnp.zeros((n, channels), F32), jnp.zeros((1, channels), F32))
+    carry = ()
     filled = ()
     top = nc - 1
     for low_chunk in PIECES:
         def piece(d, carry, filled, top=top, low_chunk=low_chunk):
-            return back(prefix, proj, wide, drive, step, d, hprev, ag, wg, pin, decay_log, skip_gain, carry, top, low_chunk, filled)
+            return back(prefix, proj, step_weight, drive, step, d, hprev, ag, wg, pin, decay_log, skip_gain, carry, top, low_chunk, filled)
 
         *filled, p1, a1, b1 = under(chains, piece, dy, carry, tuple(filled))
         ready(chains)
@@ -922,19 +933,16 @@
     for bit in t_order[:-1]:
         dpart = (dpart.astype(F32) + exchange(dpart, "tensor", tp, bit).astype(F32)).astype(BF)
     cross = Chain("tensor", tp, t_order[-1:], dpart, dpart)
-    under([cross] + chains, lambda: ())
-    ready(chains)
+    my_x, my_rs = under([cross, mix], lambda v, w: (part_of(v), part_of(w)), low, rs)
     dproj = (cross.send.astype(F32) + cross.got.astype(F32)).astype(BF)
     total = 16 + n + p + rank + width
-    total += -total % 256
+    total += -total % (16 << (len(order) - 1))
     rows_a = total // 2
-    ka, sa, kb, sb, lower, upper, g_norm = under(chains, lambda v: inner(rows_a, total - rows_a, picks[1:], v, ddrive_scan, xpart, drive, dz, normed, low, rs, w_all, xproj_t, conv_weight, conv_bias, g_bias, g_decay, decay_log, g_skip, proj, dpre), dproj)
-    ready(chains)
-    up = picks[0] == 1
+    ka, sa, kb, sb, kn, sn, g_norm = under([gz, go], lambda v: inner(rows_a, total - rows_a, picks, v, ddrive_scan, xpart, slope, drive, dz, normed, low, rs, w_all, xproj_t, conv_weight, g_bias, g_decay, decay_log, g_skip, proj, dpre), dproj)
     la = Chain("dp", dp, order, ka, sa)
     lb = Chain("dp", dp, turned, kb, sb)
-    dn = Chain("tensor", tp, t_order, jnp.where(up, upper, lower), jnp.where(up, lower, upper), swap=False, middle=("norm", (my_x, my_rs, norm_gain.reshape(1, width))))
-    turns = [("tensor", tp, bit) for bit in t_order] + [("dp", dp, bit) for bit in order]
+    dn = Chain("tensor", tp, t_order, kn, sn, swap=False, middle=("norm", (my_x, my_rs, norm_gain.reshape(1, width))))
+    turns = [("tensor", tp, bit) for bit in reversed(t_order)] + [("dp", dp, bit) for bit in order]
 
     def gains(v):
         if turns:
@@ -942,20 +950,25 @@
             v = v + exchange(v, name, size, bit)
         return v
 
-    while len(la.steps) > 1:
-        g_norm = under([la, lb, dn] + chains, gains, g_norm)
-        ready([la, lb, dn] + chains)
+    late = [[], [gz], [go]]
+    while not la.ended():
+        extra = late.pop(0) if late else [c for c in (gz, go) if not c.ended()]
+        ready(extra + [la, lb, dn])
+        final = len(la.steps) == 1
+        slow = [dn] if dn.got is None and len(dn.steps) > 1 and dn.steps[0][1] != t_order[0] else []
+        now = [dn] if dn.got is None and not slow and not final else []
+        g_norm = under([la, lb] + now + extra, gains, g_norm, slow=slow)
     while turns:
         g_norm = gains(g_norm)
-    for c in [dn] + chains:
-        while c.steps and c.got is None:
+    for c in (dn, gz, go):
+        while not c.ended():
+            ready([c])
             under([c], lambda: ())
-            ready([c])
-    flags = jnp.stack([dn.mine(dn.steps[0][1]), go.mine(go.steps[0][1])]).astype(jnp.int32)
-    grad_tokens, g_out = under([la, lb], lambda v: ending(flags, v, dn.send, dn.got, go.send, go.got), cot)
-    block_out = merge([mix.item()] if len(mix.steps) > 1 else [("join", mix.mine(mix.steps[0][1]), mix.send, mix.got)])[0][0]
     flags = jnp.stack([c.mine(c.steps[0][1]) for c in (la, lb, gz)]).astype(jnp.int32)
     g_in, g_conv, g_convb, g_bias, g_skip, g_decay, g_step, g_xproj = last(flags, la.send, la.got, lb.send, lb.got, gz.send, gz.got, n, rank, p, taps)
+    flags = jnp.stack([dn.mine(dn.steps[0][1]), go.mine(go.steps[0][1])]).astype(jnp.int32)
+    grad_tokens, g_out = ending(flags, cot, dn.send, dn.got, go.send, go.got)
+    block_out = merge([mix.item()] if len(mix.steps) > 1 else [("join", mix.mine(mix.steps[0][1]), mix.send, mix.got)])[0][0]
     return (block_out[None], grad_tokens[None], g_norm.reshape(-1), g_in, g_conv, g_convb[0], g_xproj.T, g_step, g_bias[0], g_decay, g_skip[0], g_out)
 
 

time: 226 us -> 217 us (0.960)
  waiting for transfers between devices: 50.9 us -> 41.2 us
  starting transfers between devices: 32.3 us -> 41.9 us
  local copies, waits for them, and re-layouts: 9.82 us -> 5.57 us
    ppermute x37, waiting for transfers between devices: 50.9 us -> 41.2 us  [exchange(): return lax.ppermute(value, name, [(j, j ^ 1 << bit) for j in range(size)])]
    ppermute x37, starting transfers between devices: 32.3 us -> 41.9 us  [exchange(): return lax.ppermute(value, name, [(j, j ^ 1 << bit) for j in range(size)])]
    unnamed x33 -> x7, local copies, waits for them, and re-layouts: 5.9 us -> 3.49 us
  transfers between devices with their start and end apart: 37 -> 37, of which waited for: 16 -> 17; matrix products, arithmetic and copies ran while one was open for 3% -> 2% of each run, Pallas kernels for 28% -> 28%
where the time goes in v3:
time: 217 us; the launch traced here: 216 us
  Pallas kernels  121 us (56%)
  starting transfers between devices  41.9 us (19%)
  waiting for transfers between devices  41.2 us (19%)
  local copies, waits for them, and re-layouts  5.57 us (3%)
  other arithmetic  4.77 us (2%)
    ppermute x37, starting transfers between devices, exchange(): return lax.ppermute(value, name, [(j, j ^ 1 << bit) for j in range(size)])  41.9 us
    ppermute x37, waiting for transfers between devices, exchange(): return lax.ppermute(value, name, [(j, j ^ 1 << bit) for j in range(size)])  41.2 us
    pallas_call x3, Pallas kernels, back(): pl.pallas_call(functools.partial(back_kernel, ng, top, low, len(extra)),...  31.6 us
    pallas_call x1, Pallas kernels, front(): pl.pallas_call(functools.partial(front_kernel, ng), grid=(ng + nc,), in_s...  31 us
    pallas_call x1, Pallas kernels, inner(): pl.pallas_call(functools.partial(inner_kernel, rows_a, rows_b), grid_spec...  15.1 us
    pallas_call x9, Pallas kernels, merge(): pl.pallas_call(functools.partial(merge_kernel, kinds), grid=(1,), in_spec...  12.4 us
    pallas_call x1, Pallas kernels, outer(): pl.pallas_call(outer_kernel, grid_spec=pltpu.PrefetchScalarGridSpec(num_s...  9.74 us
    pallas_call x1, Pallas kernels, head(): pl.pallas_call(head_kernel, grid=(l // hc,), in_specs=[by(d), whole(1, d)...  7.02 us
  transfers between devices with their start and end apart: 37, of which 17 were waited for; matrix products, arithmetic and copies ran while one was open for 2% of the time, Pallas kernels for 28%

profile of v3, /device:TPU:1, one launch (start us, length us, event | category | flops | bytes accessed | tf_op | source)
XLA Modules:
  0.0 215.7 jit_solution(1098883835203679519)
XLA Ops:
  0.6 3.5 %copy.31 = bf16[128,8,2,512]{3,1,2,0:T(8,128)(2,1)} copy(bf16[128,8,2,512]{3,2,1,0:T(2,128)(2,1)} %bitcast.34) | data formatting | bytes 4194304
  4.1 7.0 %head.1 = (bf16[1024,1024]{1,0:T(8,128)(2,1)}, bf16[1024,512]{1,0:T(8,128)(2,1)}, f32[1024,512]{1,0:T(8,128)}, bf16[1024,512]{1,0:T(8,128)(2,1)}, bf16[1024,96]{1,0:T(8,128)(2,1)}, /*index=5*/f32[1024,1]{1,0:T(8,128)}) custom-call(bf16[1024,1024]{1,0:T(8,128)(2,1)} %bitcast.30, f32[1,1024]{1,0:T(1,128)} %bitcast.25, bf16[1024,1024]{1,0:T(8,128)(2,1)} %bitcast.27, ...), custom_call_target="tpu_custom_call" | custom-call | flops 1073741824 | bytes 8388608 | tf_op jit(solution)/shard_map/head/pallas_call | solution.py:448
  12.0 0.7 pad_add_fusion
  12.9 1.0 add_convert_fusion.3
  14.0 2.5 %collective-permute-start.1 = (bf16[1024,96]{1,0:T(8,128)(2,1)S(1)}, bf16[1024,96]{1,0:T(8,128)(2,1)S(1)}, u32[]{:S(2)}, u32[]{:S(2)}) collective-permute-start(bf16[1024,96]{1,0:T(8,128)(2,1)S(1)} %add_convert_fusion.3), channel_id=1, source_target_pairs={{0,2},{1,3},{2,0},{3,1},{4,6},{5,7},{6,4},{7,5},{8,10},{9,11},{10,... | collective-permute-start | bytes 589832 | tf_op jit(solution)/shard_map/ppermute | solution.py:802
  16.4 6.3 %gates.1 = (f32[1024,512]{1,0:T(8,128)}, f32[1024,512]{1,0:T(8,128)}) custom-call(bf16[1024,1024]{1,0:T(8,128)(2,1)} %get-tuple-element.232.n_ref.normed_ref, bf16[1024,1024]{1,0:T(8,128)(2,1)} %bitcast.28, bf16[1024,1024]{1,0:T(8,128)(2,1)} %bitcast.22, bf16[512,1024]{1,0:T(8,128)(2,1)} %w_ref.1), custom_call_target="tpu_custom_call" | custom-call | flops 2147483648 | bytes 10485760 | tf_op jit(solution)/shard_map/gates/pallas_call | solution.py:471
  22.8 0.8 add_convert_fusion.2.proj_ref
  23.6 31.0 %front.1 = (bf16[1024,512]{1,0:T(8,128)(2,1)}, bf16[1024,512]{1,0:T(8,128)(2,1)}, f32[1024,512]{1,0:T(8,128)}, f32[1024,512]{1,0:T(8,128)}, bf16[16384,512]{1,0:...) custom-call(s32[1]{0:T(128)S(6)} %copy.38.prefix_ref, ...), custom_call_target="tpu_custom_call" | custom-call | tf_op jit(solution)/shard_map/front/pallas_call | solution.py:753
  54.6 9.7 %outer.1 = (bf16[512,512]{1,0:T(8,128)(2,1)}, bf16[512,512]{1,0:T(8,128)(2,1)}, bf16[256,1024]{1,0:T(8,128)(2,1)}, bf16[256,1024]{1,0:T(8,128)(2,1)}, bf16[512,1...) custom-call(s32[4]{0:T(128)} %get-tuple-element.446.order_ref.bits_ref, ...), custom_call_target="tpu_custom_call" | custom-call | flops 3221225472 | bytes 10485760 | tf_op jit(solution)/shard_map/outer/pallas_call | solution.py:608
  64.7 1.4 collective-permute-start.3
  66.1 1.6 collective-permute-start.4
  67.7 10.1 %back.3 = (bf16[1024,96]{1,0:T(8,128)(2,1)}, bf16[1024,512]{1,0:T(8,128)(2,1)}, f32[1024,512]{1,0:T(8,128)}, f32[16,512]{1,0:T(8,128)}, f32[16,512]{1,0:T(8,128)}, /*index=5*/f32[1,512]{1,0:T(1,128)}) custom-call(s32[1]{0:T(128)S(6)} %copy.38.prefix_ref, bf16[1024,96]{1,0:T(8,128)(2,1)} %add_convert_fusion.2.proj_ref, bf16[64,512]{1,0:T(8,128)(2,1)} %sw_ref.7, ...), custom_call_target="tpu_custom_call" | custom-call | flops 12582912000 | bytes 12582912 | tf_op jit(solution)/shard_map/back/pallas_call | solution.py:783
  77.8 2.9 %merge.9 = (bf16[256,512]{1,0:T(8,128)(2,1)}, bf16[256,512]{1,0:T(8,128)(2,1)S(1)}, bf16[128,1024]{1,0:T(8,128)(2,1)}, bf16[128,1024]{1,0:T(8,128)(2,1)S(1)}, bf...) custom-call(s32[3]{0:T(128)S(1)} %get-tuple-element.448.bits_ref, bf16[512,512]{1,0:T(8,128)(2,1)} %get-tuple-element.242.refs_0_, ...), custom_call_target="tpu_custom_call" | custom-call | tf_op jit(solution)/shard_map/merge/pallas_call | solution.py:667
  81.4 1.8 collective-permute-start.6
  83.2 1.2 collective-permute-start.7
  84.4 12.1 %back.4 = (bf16[1024,96]{1,0:T(8,128)(2,1)}, bf16[1024,512]{1,0:T(8,128)(2,1)}, f32[1024,512]{1,0:T(8,128)}, f32[16,512]{1,0:T(8,128)}, f32[16,512]{1,0:T(8,128)}, /*index=5*/f32[1,512]{1,0:T(1,128)}) custom-call(s32[1]{0:T(128)S(6)} %copy.38.prefix_ref, ...), custom_call_target="tpu_custom_call", output_to_operand_aliasing={{0}: (15, {}), {1}: (16, {}), {2}: (17, {})} | custom-call | flops 12582912000 | bytes 12582912 | tf_op jit(solution)/shard_map/back/pallas_call | solution.py:783
  96.5 1.5 merge.10
  98.3 1.5 collective-permute-start.9
  100.0 9.5 %back.5 = (bf16[1024,96]{1,0:T(8,128)(2,1)}, bf16[1024,512]{1,0:T(8,128)(2,1)}, f32[1024,512]{1,0:T(8,128)}, f32[16,512]{1,0:T(8,128)}, f32[16,512]{1,0:T(8,128)}, /*index=5*/f32[1,512]{1,0:T(1,128)}) custom-call(s32[1]{0:T(128)S(6)} %copy.38.prefix_ref, ...), custom_call_target="tpu_custom_call", output_to_operand_aliasing={{0}: (15, {}), {1}: (16, {}), {2}: (17, {})} | custom-call | flops 8388608000 | bytes 8388608 | tf_op jit(solution)/shard_map/back/pallas_call | solution.py:783
  109.5 3.2 %collective-permute-done.8.refs_1_ = bf16[256,512]{1,0:T(8,128)(2,1)S(1)} collective-permute-done((bf16[256,512]{1,0:T(8,128)(2,1)S(1)}, bf16[256,512]{1,0:T(8,128)(2,1)S(1)}, u32[]{:S(2)}, u32[]{:S(2)}) %collective-permute-start.8) | collective-permute-done | bytes 262176 | tf_op jit(solution)/shard_map/ppermute | solution.py:802
  112.7 1.4 collective-permute-start.11
  114.2 0.7 merge.11
  116.0 0.8 collective-permute-start.12
  116.8 0.9 constant_dynamic-slice_fusion.refs_7_
  117.7 1.1 constant_dynamic-slice_fusion.1.refs_6_
  118.8 5.0 %collective-permute-done.12 = bf16[1024,96]{1,0:T(8,128)(2,1)S(1)} collective-permute-done((bf16[1024,96]{1,0:T(8,128)(2,1)S(1)}, bf16[1024,96]{1,0:T(8,128)(2,1)S(1)}, u32[]{:S(2)}, u32[]{:S(2)}) %collective-permute-start.12) | collective-permute-done | bytes 196640 | tf_op jit(solution)/shard_map/ppermute | solution.py:802
  123.8 0.8 add_convert_fusion.dproj_ref
  124.6 0.8 collective-permute-start.14
  125.9 15.1 %inner.1 = (bf16[304,512]{1,0:T(8,128)(2,1)}, bf16[304,512]{1,0:T(8,128)(2,1)}, bf16[304,512]{1,0:T(8,128)(2,1)}, bf16[304,512]{1,0:T(8,128)(2,1)}, bf16[512,102...) custom-call(s32[4]{0:T(128)} %get-tuple-element.446.order_ref.bits_ref, ...), custom_call_target="tpu_custom_call" | custom-call | flops 3221225472 | bytes 10485760 | tf_op jit(solution)/shard_map/inner/pallas_call | solution.py:573
  141.0 1.6 collective-permute-start.18
  142.6 1.1 collective-permute-start.16
  143.7 1.1 collective-permute-start.17
  145.1 2.7 %collective-permute-done.19 = f32[1,1024]{1,0:T(1,128)S(1)} collective-permute-done((f32[1,1024]{1,0:T(1,128)}, f32[1,1024]{1,0:T(1,128)S(1)}, u32[]{:S(2)}, u32[]{:S(2)}) %collective-permute-start.19) | collective-permute-done | bytes 4128 | tf_op jit(solution)/shard_map/ppermute | solution.py:802
  147.8 0.7 add.44
  148.5 3.2 %collective-permute-done.16.refs_3_ = bf16[304,512]{1,0:T(8,128)(2,1)S(1)} collective-permute-done((bf16[304,512]{1,0:T(8,128)(2,1)}, bf16[304,512]{1,0:T(8,128)(2,1)S(1)}, u32[]{:S(2)}, u32[]{:S(2)}) %collective-permute-start.16) | collective-permute-done | bytes 311328 | tf_op jit(solution)/shard_map/ppermute | solution.py:802
  151.7 0.8 collective-permute-done.17.refs_5_
  152.5 2.5 %merge.13 = (bf16[512,512]{1,0:T(8,128)(2,1)S(1)}, bf16[152,512]{1,0:T(8,128)(2,1)}, bf16[152,512]{1,0:T(8,128)(2,1)S(1)}, bf16[152,512]{1,0:T(8,128)(2,1)}, bf1...) custom-call(s32[4]{0:T(128)S(1)} %get-tuple-element.447.bits_ref, ...), custom_call_target="tpu_custom_call" | custom-call | tf_op jit(solution)/shard_map/merge/pallas_call | solution.py:667
  155.4 1.1 collective-permute-start.20
  156.4 1.4 collective-permute-start.21
  157.9 2.0 collective-permute-start.23
  159.9 0.8 collective-permute-start.27
  160.7 2.3 %collective-permute-done.21.refs_5_ = bf16[152,512]{1,0:T(8,128)(2,1)S(1)} collective-permute-done((bf16[152,512]{1,0:T(8,128)(2,1)S(1)}, bf16[152,512]{1,0:T(8,128)(2,1)S(1)}, u32[]{:S(2)}, u32[]{:S(2)}) %collective-permute-start.21) | collective-permute-done | bytes 155680 | tf_op jit(solution)/shard_map/ppermute | solution.py:802
  163.0 4.3 %collective-permute-done.22.oz_ref = bf16[512,512]{1,0:T(8,128)(2,1)S(1)} collective-permute-done((bf16[512,512]{1,0:T(8,128)(2,1)S(1)}, bf16[512,512]{1,0:T(8,128)(2,1)S(1)}, u32[]{:S(2)}, u32[]{:S(2)}) %collective-permute-start.22) | collective-permute-done | bytes 524320 | tf_op jit(solution)/shard_map/ppermute | solution.py:802
  167.2 1.1 merge.14
  168.4 1.2 collective-permute-start.26
  169.5 0.9 collective-permute-start.24
  170.5 0.8 collective-permute-start.25
  171.3 0.7 collective-permute-start.28
  172.0 2.7 %collective-permute-done.28 = f32[1,1024]{1,0:T(1,128)S(1)} collective-permute-done((f32[1,1024]{1,0:T(1,128)S(1)}, f32[1,1024]{1,0:T(1,128)S(1)}, u32[]{:S(2)}, u32[]{:S(2)}) %collective-permute-start.28) | collective-permute-done | bytes 4128 | tf_op jit(solution)/shard_map/ppermute | solution.py:802
  174.6 7.4 %collective-permute-done.24.refs_1_ = bf16[152,512]{1,0:T(8,128)(2,1)S(1)} collective-permute-done((bf16[152,512]{1,0:T(8,128)(2,1)S(1)}, bf16[152,512]{1,0:T(8,128)(2,1)S(1)}, u32[]{:S(2)}, u32[]{:S(2)}) %collective-permute-start.24) | collective-permute-done | bytes 155680 | tf_op jit(solution)/shard_map/ppermute | solution.py:802
  182.0 1.5 collective-permute-done.26.ob_ref
  183.5 1.6 merge.15
  185.2 0.9 collective-permute-start.34
  186.5 2.4 %collective-permute-start.30 = (bf16[152,512]{1,0:T(8,128)(2,1)S(1)}, bf16[152,512]{1,0:T(8,128)(2,1)S(1)}, u32[]{:S(2)}, u32[]{:S(2)}) collective-permute-start(bf16[152,512]{1,0:T(8,128)(2,1)S(1)} %get-tuple-element.416.refs_2_), channel_id=1, source_target_pairs={{0,16},{4,20},{8,24},{12,28},{16,0},{20,4},{24,8},{28,12},{1,17},{... | collective-permute-start | bytes 466952 | tf_op jit(solution)/shard_map/ppermute | solution.py:802
  189.0 2.9 %collective-permute-done.31 = f32[1,1024]{1,0:T(1,128)S(1)} collective-permute-done((f32[1,1024]{1,0:T(1,128)S(1)}, f32[1,1024]{1,0:T(1,128)S(1)}, u32[]{:S(2)}, u32[]{:S(2)}) %collective-permute-start.31) | collective-permute-done | bytes 4128 | tf_op jit(solution)/shard_map/ppermute | solution.py:802
  191.9 1.4 collective-permute-done.30.refs_3_
  194.0 0.7 collective-permute-start.32
  195.3 1.9 collective-permute-start.35
  197.2 2.0 collective-permute-done.35
  199.8 0.8 collective-permute-done.33.ob_ref
  200.6 6.0 %collective-permute-start.36 = (bf16[512,1024]{1,0:T(8,128)(2,1)S(1)}, bf16[512,1024]{1,0:T(8,128)(2,1)S(1)}, u32[]{:S(2)}, u32[]{:S(2)}) collective-permute-start(bf16[512,1024]{1,0:T(8,128)(2,1)S(1)} %merge.17.na_ref), channel_id=1, source_target_pairs={{0,1},{1,0},{2,3},{3,2},{4,5},{5,4},{6,7},{7,6},{8,9},{9,8},{10,11... | collective-permute-start | bytes 3145736 | tf_op jit(solution)/shard_map/ppermute | solution.py:802
  206.7 1.5 merge.12
  208.1 3.8 %last.1 = (f32[1024,2,512]{2,1,0:T(2,128)}, f32[4,512]{1,0:T(4,128)}, f32[1,512]{1,0:T(1,128)}, f32[1,512]{1,0:T(1,128)}, f32[1,512]{1,0:T(1,128)}, /*index=5*/f...) custom-call(s32[3]{0:T(128)S(1)} %get-tuple-element.449.bits_ref, bf16[304,512]{1,0:T(8,128)(2,1)S(1)} %get-tuple-element.431.sa_ref, ...), custom_call_target="tpu_custom_call" | custom-call | tf_op jit(solution)/shard_map/last/pallas_call | solution.py:729
  212.0 3.7 %ending.1 = (f32[1024,1024]{1,0:T(8,128)}, f32[512,1024]{1,0:T(8,128)}) custom-call(s32[2]{0:T(128)S(1)} %get-tuple-element.450.bits_ref, bf16[1024,1024]{1,0:T(8,128)(2,1)S(1)} %bitcast.24, bf16[512,1024]{1,0:T(8,128)(2,1)S(1)} %merge.17.na_ref, bf16[512,1024]{1,0:T(8,128)(2,1)S(1)} %collective-permute-done.36.nb_ref, ...), custom_call_target="tpu_custom_call" | custom-call | flops 1048576 | bytes 12582912 | tf_op jit(solution)/shard_map/ending/pallas_call | solution.py:691
  (53 shorter events, 7.0 us)
Async XLA Ops:
  11.1 1.8 collective-permute-start
  14.0 8.9 %collective-permute-start.1 = (bf16[1024,96]{1,0:T(8,128)(2,1)S(1)}, bf16[1024,96]{1,0:T(8,128)(2,1)S(1)}, u32[]{:S(2)}, u32[]{:S(2)}) collective-permute-start(bf16[1024,96]{1,0:T(8,128)(2,1)S(1)} %add_convert_fusion.3), channel_id=1, source_target_pairs={{0,2},{1,3},{2,0},{3,1},{4,6},{5,7},{6,4},{7,5},{8,10},{9,11},{10,... | collective-permute-start | bytes 589832 | tf_op jit(solution)/shard_map/ppermute | solution.py:802
  64.4 13.4 %collective-permute-start.2 = (bf16[512,512]{1,0:T(8,128)(2,1)}, bf16[512,512]{1,0:T(8,128)(2,1)S(1)}, u32[]{:S(2)}, u32[]{:S(2)}) collective-permute-start(bf16[512,512]{1,0:T(8,128)(2,1)} %get-tuple-element.247), channel_id=1, source_target_pairs={{0,4},{4,0},{8,12},{12,8},{16,20},{20,16},{24,28},{28,24},{1,5},{5... | collective-permute-start | bytes 1572872 | tf_op jit(solution)/shard_map/ppermute | solution.py:802
  64.7 13.1 %collective-permute-start.3 = (bf16[256,1024]{1,0:T(8,128)(2,1)}, bf16[256,1024]{1,0:T(8,128)(2,1)S(1)}, u32[]{:S(2)}, u32[]{:S(2)}) collective-permute-start(bf16[256,1024]{1,0:T(8,128)(2,1)} %get-tuple-element.248), channel_id=1, source_target_pairs={{0,8},{4,12},{8,0},{12,4},{16,24},{20,28},{24,16},{28,20},{1,9},{5... | collective-permute-start | bytes 1572872 | tf_op jit(solution)/shard_map/ppermute | solution.py:802
  66.1 11.7 %collective-permute-start.4 = (bf16[512,1024]{1,0:T(8,128)(2,1)}, bf16[512,1024]{1,0:T(8,128)(2,1)S(1)}, u32[]{:S(2)}, u32[]{:S(2)}) collective-permute-start(bf16[512,1024]{1,0:T(8,128)(2,1)} %get-tuple-element.249), channel_id=1, source_target_pairs={{0,1},{1,0},{2,3},{3,2},{4,5},{5,4},{6,7},{7,6},{8,9},{9,8},{10,11... | collective-permute-start | bytes 3145736 | tf_op jit(solution)/shard_map/ppermute | solution.py:802
  80.7 15.8 %collective-permute-start.5 = (bf16[256,512]{1,0:T(8,128)(2,1)S(1)}, bf16[256,512]{1,0:T(8,128)(2,1)S(1)}, u32[]{:S(2)}, u32[]{:S(2)}) collective-permute-start(bf16[256,512]{1,0:T(8,128)(2,1)S(1)} %get-tuple-element.275), channel_id=1, source_target_pairs={{0,8},{4,12},{8,0},{12,4},{16,24},{20,28},{24,16},{28,20},{1,9},{5... | collective-permute-start | bytes 786440 | tf_op jit(solution)/shard_map/ppermute | solution.py:802
  81.4 15.1 %collective-permute-start.6 = (bf16[128,1024]{1,0:T(8,128)(2,1)S(1)}, bf16[128,1024]{1,0:T(8,128)(2,1)S(1)}, u32[]{:S(2)}, u32[]{:S(2)}) collective-permute-start(bf16[128,1024]{1,0:T(8,128)(2,1)S(1)} %get-tuple-element.276), channel_id=1, source_target_pairs={{0,16},{4,20},{8,24},{12,28},{16,0},{20,4},{24,8},{28,12},{1,17},{... | collective-permute-start | bytes 786440 | tf_op jit(solution)/shard_map/ppermute | solution.py:802
  83.2 13.3 %collective-permute-start.7 = (bf16[256,1024]{1,0:T(8,128)(2,1)S(1)}, bf16[256,1024]{1,0:T(8,128)(2,1)S(1)}, u32[]{:S(2)}, u32[]{:S(2)}) collective-permute-start(bf16[256,1024]{1,0:T(8,128)(2,1)S(1)} %get-tuple-element.277), channel_id=1, source_target_pairs={{0,2},{1,3},{2,0},{3,1},{4,6},{5,7},{6,4},{7,5},{8,10},{9,11},{10,... | collective-permute-start | bytes 1572872 | tf_op jit(solution)/shard_map/ppermute | solution.py:802
  98.0 14.7 %collective-permute-start.8 = (bf16[256,512]{1,0:T(8,128)(2,1)S(1)}, bf16[256,512]{1,0:T(8,128)(2,1)S(1)}, u32[]{:S(2)}, u32[]{:S(2)}) collective-permute-start(bf16[256,512]{1,0:T(8,128)(2,1)S(1)} %get-tuple-element.323.refs_0_), channel_id=1, source_target_pairs={{0,16},{4,20},{8,24},{12,28},{16,0},{20,4},{24,8},{28,12},{1,17},{... | collective-permute-start | bytes 786440 | tf_op jit(solution)/shard_map/ppermute | solution.py:802
  98.3 14.4 %collective-permute-start.9 = (bf16[128,1024]{1,0:T(8,128)(2,1)S(1)}, bf16[128,1024]{1,0:T(8,128)(2,1)S(1)}, u32[]{:S(2)}, u32[]{:S(2)}) collective-permute-start(bf16[128,1024]{1,0:T(8,128)(2,1)S(1)} %get-tuple-element.325.refs_2_), channel_id=1, source_target_pairs={{0,4},{4,0},{8,12},{12,8},{16,20},{20,16},{24,28},{28,24},{1,5},{5... | collective-permute-start | bytes 786440 | tf_op jit(solution)/shard_map/ppermute | solution.py:802
  99.8 12.9 %collective-permute-start.10 = (bf16[256,1024]{1,0:T(8,128)(2,1)S(1)}, bf16[256,1024]{1,0:T(8,128)(2,1)S(1)}, u32[]{:S(2)}, u32[]{:S(2)}) collective-permute-start(bf16[256,1024]{1,0:T(8,128)(2,1)S(1)} %get-tuple-element.327.refs_4_), channel_id=1, source_target_pairs={{0,2},{1,3},{2,0},{3,1},{4,6},{5,7},{6,4},{7,5},{8,10},{9,11},{10,... | collective-permute-start | bytes 1572872 | tf_op jit(solution)/shard_map/ppermute | solution.py:802
  109.5 6.0 %copy-start.2 = (bf16[1024,96]{1,0:T(8,128)(2,1)S(1)}, bf16[1024,96]{1,0:T(8,128)(2,1)}, u32[]{:S(2)}) copy-start(bf16[1024,96]{1,0:T(8,128)(2,1)} %get-tuple-element.322) | copy-start | bytes 589828
  112.7 2.8 %collective-permute-start.11 = (bf16[1024,96]{1,0:T(8,128)(2,1)}, bf16[1024,96]{1,0:T(8,128)(2,1)S(1)}, u32[]{:S(2)}, u32[]{:S(2)}) collective-permute-start(bf16[1024,96]{1,0:T(8,128)(2,1)} %get-tuple-element.322), channel_id=1, source_target_pairs={{0,1},{1,0},{2,3},{3,2},{4,5},{5,4},{6,7},{7,6},{8,9},{9,8},{10,11... | collective-permute-start | bytes 589832 | tf_op jit(solution)/shard_map/ppermute | solution.py:802
  115.6 8.2 %collective-permute-start.13 = (bf16[512,1024]{1,0:T(8,128)(2,1)S(1)}, bf16[512,1024]{1,0:T(8,128)(2,1)S(1)}, u32[]{:S(2)}, u32[]{:S(2)}) collective-permute-start(bf16[512,1024]{1,0:T(8,128)(2,1)S(1)} %get-tuple-element.335.refs_0_), channel_id=1, source_target_pairs={{0,1},{1,0},{2,3},{3,2},{4,5},{5,4},{6,7},{7,6},{8,9},{9,8},{10,11... | collective-permute-start | bytes 3145736 | tf_op jit(solution)/shard_map/ppermute | solution.py:802
  116.0 7.8 %collective-permute-start.12 = (bf16[1024,96]{1,0:T(8,128)(2,1)S(1)}, bf16[1024,96]{1,0:T(8,128)(2,1)S(1)}, u32[]{:S(2)}, u32[]{:S(2)}) collective-permute-start(bf16[1024,96]{1,0:T(8,128)(2,1)S(1)} %add_convert_fusion.1), channel_id=1, source_target_pairs={{0,2},{1,3},{2,0},{3,1},{4,6},{5,7},{6,4},{7,5},{8,10},{9,11},{10,... | collective-permute-start | bytes 589832 | tf_op jit(solution)/shard_map/ppermute | solution.py:802
  124.6 16.4 %collective-permute-start.14 = (bf16[256,512]{1,0:T(8,128)(2,1)S(1)}, bf16[256,512]{1,0:T(8,128)(2,1)S(1)}, u32[]{:S(2)}, u32[]{:S(2)}) collective-permute-start(bf16[256,512]{1,0:T(8,128)(2,1)S(1)} %get-tuple-element.360.refs_0_), channel_id=1, source_target_pairs={{0,8},{4,12},{8,0},{12,4},{16,24},{20,28},{24,16},{28,20},{1,9},{5... | collective-permute-start | bytes 786440 | tf_op jit(solution)/shard_map/ppermute | solution.py:802
  125.4 15.6 %collective-permute-start.15 = (bf16[128,1024]{1,0:T(8,128)(2,1)S(1)}, bf16[128,1024]{1,0:T(8,128)(2,1)S(1)}, u32[]{:S(2)}, u32[]{:S(2)}) collective-permute-start(bf16[128,1024]{1,0:T(8,128)(2,1)S(1)} %get-tuple-element.358.refs_0_), channel_id=1, source_target_pairs={{0,16},{4,20},{8,24},{12,28},{16,0},{20,4},{24,8},{28,12},{1,17},{... | collective-permute-start | bytes 786440 | tf_op jit(solution)/shard_map/ppermute | solution.py:802
  141.0 11.5 %collective-permute-start.18 = (bf16[512,1024]{1,0:T(8,128)(2,1)}, bf16[512,1024]{1,0:T(8,128)(2,1)S(1)}, u32[]{:S(2)}, u32[]{:S(2)}) collective-permute-start(bf16[512,1024]{1,0:T(8,128)(2,1)} %get-tuple-element.369), channel_id=1, source_target_pairs={{0,1},{1,0},{2,3},{3,2},{4,5},{5,4},{6,7},{7,6},{8,9},{9,8},{10,11... | collective-permute-start | bytes 3145736 | tf_op jit(solution)/shard_map/ppermute | solution.py:802
  142.6 9.1 %collective-permute-start.16 = (bf16[304,512]{1,0:T(8,128)(2,1)}, bf16[304,512]{1,0:T(8,128)(2,1)S(1)}, u32[]{:S(2)}, u32[]{:S(2)}) collective-permute-start(bf16[304,512]{1,0:T(8,128)(2,1)} %get-tuple-element.367), channel_id=1, source_target_pairs={{0,4},{4,0},{8,12},{12,8},{16,20},{20,16},{24,28},{28,24},{1,5},{5... | collective-permute-start | bytes 933896 | tf_op jit(solution)/shard_map/ppermute | solution.py:802
  143.7 8.8 %collective-permute-start.17 = (bf16[304,512]{1,0:T(8,128)(2,1)}, bf16[304,512]{1,0:T(8,128)(2,1)S(1)}, u32[]{:S(2)}, u32[]{:S(2)}) collective-permute-start(bf16[304,512]{1,0:T(8,128)(2,1)} %get-tuple-element.368), channel_id=1, source_target_pairs={{0,8},{4,12},{8,0},{12,4},{16,24},{20,28},{24,16},{28,20},{1,9},{5... | collective-permute-start | bytes 933896 | tf_op jit(solution)/shard_map/ppermute | solution.py:802
  144.8 3.0 %collective-permute-start.19 = (f32[1,1024]{1,0:T(1,128)}, f32[1,1024]{1,0:T(1,128)S(1)}, u32[]{:S(2)}, u32[]{:S(2)}) collective-permute-start(f32[1,1024]{1,0:T(1,128)} %get-tuple-element.370), channel_id=1, source_target_pairs={{0,2},{1,3},{2,0},{3,1},{4,6},{5,7},{6,4},{7,5},{8,10},{9,11},{10,... | collective-permute-start | bytes 12296 | tf_op jit(solution)/shard_map/ppermute | solution.py:802
  152.5 31.0 %copy-start.1 = (f32[1024]{0:T(1024)S(1)}, f32[1024]{0:T(1024)}, u32[]{:S(2)}) copy-start(f32[1024]{0:T(1024)} %param.15) | copy-start | bytes 12292
  155.0 12.2 %collective-permute-start.22 = (bf16[512,512]{1,0:T(8,128)(2,1)S(1)}, bf16[512,512]{1,0:T(8,128)(2,1)S(1)}, u32[]{:S(2)}, u32[]{:S(2)}) collective-permute-start(bf16[512,512]{1,0:T(8,128)(2,1)S(1)} %get-tuple-element.435.sz_ref), channel_id=1, source_target_pairs={{0,4},{4,0},{8,12},{12,8},{16,20},{20,16},{24,28},{28,24},{1,5},{5... | collective-permute-start | bytes 1572872 | tf_op jit(solution)/shard_map/ppermute | solution.py:802
  155.4 5.4 %collective-permute-start.20 = (bf16[152,512]{1,0:T(8,128)(2,1)S(1)}, bf16[152,512]{1,0:T(8,128)(2,1)S(1)}, u32[]{:S(2)}, u32[]{:S(2)}) collective-permute-start(bf16[152,512]{1,0:T(8,128)(2,1)S(1)} %get-tuple-element.382), channel_id=1, source_target_pairs={{0,8},{4,12},{8,0},{12,4},{16,24},{20,28},{24,16},{28,20},{1,9},{5... | collective-permute-start | bytes 466952 | tf_op jit(solution)/shard_map/ppermute | solution.py:802
  156.4 6.5 %collective-permute-start.21 = (bf16[152,512]{1,0:T(8,128)(2,1)S(1)}, bf16[152,512]{1,0:T(8,128)(2,1)S(1)}, u32[]{:S(2)}, u32[]{:S(2)}) collective-permute-start(bf16[152,512]{1,0:T(8,128)(2,1)S(1)} %get-tuple-element.383), channel_id=1, source_target_pairs={{0,16},{4,20},{8,24},{12,28},{16,0},{20,4},{24,8},{28,12},{1,17},{... | collective-permute-start | bytes 466952 | tf_op jit(solution)/shard_map/ppermute | solution.py:802
  157.9 2.8 %collective-permute-start.23 = (f32[1,1024]{1,0:T(1,128)S(1)}, f32[1,1024]{1,0:T(1,128)S(1)}, u32[]{:S(2)}, u32[]{:S(2)}) collective-permute-start(f32[1,1024]{1,0:T(1,128)S(1)} %add.44), channel_id=1, source_target_pairs={{0,1},{1,0},{2,3},{3,2},{4,5},{5,4},{6,7},{7,6},{8,9},{9,8},{10,11... | collective-permute-start | bytes 12296 | tf_op jit(solution)/shard_map/ppermute | solution.py:802
  159.9 14.7 %collective-permute-start.27 = (bf16[256,1024]{1,0:T(8,128)(2,1)S(1)}, bf16[256,1024]{1,0:T(8,128)(2,1)S(1)}, u32[]{:S(2)}, u32[]{:S(2)}) collective-permute-start(bf16[256,1024]{1,0:T(8,128)(2,1)S(1)} %get-tuple-element.396), channel_id=1, source_target_pairs={{0,2},{1,3},{2,0},{3,1},{4,6},{5,7},{6,4},{7,5},{8,10},{9,11},{10,... | collective-permute-start | bytes 1572872 | tf_op jit(solution)/shard_map/ppermute | solution.py:802
  168.4 15.2 %collective-permute-start.26 = (bf16[256,1024]{1,0:T(8,128)(2,1)S(1)}, bf16[256,1024]{1,0:T(8,128)(2,1)S(1)}, u32[]{:S(2)}, u32[]{:S(2)}) collective-permute-start(bf16[256,1024]{1,0:T(8,128)(2,1)S(1)} %get-tuple-element.427.oa_ref), channel_id=1, source_target_pairs={{0,8},{4,12},{8,0},{12,4},{16,24},{20,28},{24,16},{28,20},{1,9},{5... | collective-permute-start | bytes 1572872 | tf_op jit(solution)/shard_map/ppermute | solution.py:802
  169.5 12.5 %collective-permute-start.24 = (bf16[152,512]{1,0:T(8,128)(2,1)S(1)}, bf16[152,512]{1,0:T(8,128)(2,1)S(1)}, u32[]{:S(2)}, u32[]{:S(2)}) collective-permute-start(bf16[152,512]{1,0:T(8,128)(2,1)S(1)} %get-tuple-element.398.refs_0_), channel_id=1, source_target_pairs={{0,16},{4,20},{8,24},{12,28},{16,0},{20,4},{24,8},{28,12},{1,17},{... | collective-permute-start | bytes 466952 | tf_op jit(solution)/shard_map/ppermute | solution.py:802
  170.5 11.5 %collective-permute-start.25 = (bf16[152,512]{1,0:T(8,128)(2,1)S(1)}, bf16[152,512]{1,0:T(8,128)(2,1)S(1)}, u32[]{:S(2)}, u32[]{:S(2)}) collective-permute-start(bf16[152,512]{1,0:T(8,128)(2,1)S(1)} %get-tuple-element.400.refs_2_), channel_id=1, source_target_pairs={{0,4},{4,0},{8,12},{12,8},{16,20},{20,16},{24,28},{28,24},{1,5},{5... | collective-permute-start | bytes 466952 | tf_op jit(solution)/shard_map/ppermute | solution.py:802
  171.3 3.3 %collective-permute-start.28 = (f32[1,1024]{1,0:T(1,128)S(1)}, f32[1,1024]{1,0:T(1,128)S(1)}, u32[]{:S(2)}, u32[]{:S(2)}) collective-permute-start(f32[1,1024]{1,0:T(1,128)S(1)} %add.45), channel_id=1, source_target_pairs={{0,4},{4,0},{8,12},{12,8},{16,20},{20,16},{24,28},{28,24},{1,5},{5... | collective-permute-start | bytes 12296 | tf_op jit(solution)/shard_map/ppermute | solution.py:802
  185.2 15.4 %collective-permute-start.34 = (bf16[256,1024]{1,0:T(8,128)(2,1)S(1)}, bf16[256,1024]{1,0:T(8,128)(2,1)S(1)}, u32[]{:S(2)}, u32[]{:S(2)}) collective-permute-start(bf16[256,1024]{1,0:T(8,128)(2,1)S(1)} %get-tuple-element.410.refs_0_), channel_id=1, source_target_pairs={{0,2},{1,3},{2,0},{3,1},{4,6},{5,7},{6,4},{7,5},{8,10},{9,11},{10,... | collective-permute-start | bytes 1572872 | tf_op jit(solution)/shard_map/ppermute | solution.py:802
  186.0 5.9 %collective-permute-start.29 = (bf16[152,512]{1,0:T(8,128)(2,1)S(1)}, bf16[152,512]{1,0:T(8,128)(2,1)S(1)}, u32[]{:S(2)}, u32[]{:S(2)}) collective-permute-start(bf16[152,512]{1,0:T(8,128)(2,1)S(1)} %get-tuple-element.414.refs_0_), channel_id=1, source_target_pairs={{0,8},{4,12},{8,0},{12,4},{16,24},{20,28},{24,16},{28,20},{1,9},{5... | collective-permute-start | bytes 466952 | tf_op jit(solution)/shard_map/ppermute | solution.py:802
  186.5 6.8 %collective-permute-start.30 = (bf16[152,512]{1,0:T(8,128)(2,1)S(1)}, bf16[152,512]{1,0:T(8,128)(2,1)S(1)}, u32[]{:S(2)}, u32[]{:S(2)}) collective-permute-start(bf16[152,512]{1,0:T(8,128)(2,1)S(1)} %get-tuple-element.416.refs_2_), channel_id=1, source_target_pairs={{0,16},{4,20},{8,24},{12,28},{16,0},{20,4},{24,8},{28,12},{1,17},{... | collective-permute-start | bytes 466952 | tf_op jit(solution)/shard_map/ppermute | solution.py:802
  188.9 3.0 %collective-permute-start.31 = (f32[1,1024]{1,0:T(1,128)S(1)}, f32[1,1024]{1,0:T(1,128)S(1)}, u32[]{:S(2)}, u32[]{:S(2)}) collective-permute-start(f32[1,1024]{1,0:T(1,128)S(1)} %add.46), channel_id=1, source_target_pairs={{0,8},{4,12},{8,0},{12,4},{16,24},{20,28},{24,16},{28,20},{1,9},{5... | collective-permute-start | bytes 12296 | tf_op jit(solution)/shard_map/ppermute | solution.py:802
  194.0 5.8 %collective-permute-start.32 = (bf16[304,512]{1,0:T(8,128)(2,1)S(1)}, bf16[304,512]{1,0:T(8,128)(2,1)S(1)}, u32[]{:S(2)}, u32[]{:S(2)}) collective-permute-start(bf16[304,512]{1,0:T(8,128)(2,1)S(1)} %get-tuple-element.431.sa_ref), channel_id=1, source_target_pairs={{0,4},{4,0},{8,12},{12,8},{16,20},{20,16},{24,28},{28,24},{1,5},{5... | collective-permute-start | bytes 933896 | tf_op jit(solution)/shard_map/ppermute | solution.py:802
  194.7 5.8 %collective-permute-start.33 = (bf16[304,512]{1,0:T(8,128)(2,1)S(1)}, bf16[304,512]{1,0:T(8,128)(2,1)S(1)}, u32[]{:S(2)}, u32[]{:S(2)}) collective-permute-start(bf16[304,512]{1,0:T(8,128)(2,1)S(1)} %get-tuple-element.433.sb_ref), channel_id=1, source_target_pairs={{0,8},{4,12},{8,0},{12,4},{16,24},{20,28},{24,16},{28,20},{1,9},{5... | collective-permute-start | bytes 933896 | tf_op jit(solution)/shard_map/ppermute | solution.py:802
  195.3 3.9 %collective-permute-start.35 = (f32[1,1024]{1,0:T(1,128)S(1)}, f32[1,1024]{1,0:T(1,128)S(1)}, u32[]{:S(2)}, u32[]{:S(2)}) collective-permute-start(f32[1,1024]{1,0:T(1,128)S(1)} %add.47), channel_id=1, source_target_pairs={{0,16},{4,20},{8,24},{12,28},{16,0},{20,4},{24,8},{28,12},{1,17},{... | collective-permute-start | bytes 12296 | tf_op jit(solution)/shard_map/ppermute | solution.py:802
  200.6 11.3 %collective-permute-start.36 = (bf16[512,1024]{1,0:T(8,128)(2,1)S(1)}, bf16[512,1024]{1,0:T(8,128)(2,1)S(1)}, u32[]{:S(2)}, u32[]{:S(2)}) collective-permute-start(bf16[512,1024]{1,0:T(8,128)(2,1)S(1)} %merge.17.na_ref), channel_id=1, source_target_pairs={{0,1},{1,0},{2,3},{3,2},{4,5},{5,4},{6,7},{7,6},{8,9},{9,8},{10,11... | collective-permute-start | bytes 3145736 | tf_op jit(solution)/shard_map/ppermute | solution.py:802
  208.1 3.8 %copy-start = (bf16[1,1024,1024]{2,1,0:T(8,128)(2,1)S(1)}, bf16[1,1024,1024]{2,1,0:T(8,128)(2,1)}, u32[]{:S(2)}) copy-start(bf16[1,1024,1024]{2,1,0:T(8,128)(2,1)} %param.25) | copy-start | bytes 6291460

commit v4 on v3

--- a/solution.py
+++ b/solution.py
@@ -72,9 +72,9 @@
     return jnp.where(s < 0.0625, small, 1.0 - jnp.exp2(s * -LOG2E))
 
 
-def front_kernel(ng, prefix_ref, proj_ref, sw_ref, bias_ref, drive_ref, z_ref, dg_ref, dlog_ref, skip_ref,
-                 gated_ref, dz_ref, step_ref, dy_ref, hprev_ref, ag_ref, wg_ref, part_ref, gskip_ref,
-                 step_s, sd_s, dy_s, sig_s, keep_s, bt_s, ct_s, cbd_s, rc_s, hg_s, g_s, qg_s, st_f, st_h, st_q):
+def front_kernel(ng, nc, order_ref, proj_ref, sw_ref, bias_ref, drive_ref, z_ref, dg_ref, dlog_ref, skip_ref, normed_hbm, cot_hbm, low_hbm, w_hbm,
+                 gated_ref, dz_ref, step_ref, dy_ref, hprev_ref, ag_ref, wg_ref, part_ref, gskip_ref, kz_ref, sz_ref, ko_ref, so_ref, km_ref, sm_ref,
+                 step_s, sd_s, dy_s, sig_s, keep_s, bt_s, ct_s, cbd_s, rc_s, hg_s, g_s, qg_s, st_f, st_h, st_q, gated_s, dzs_s, normed_ref, cot_ref, low_ref, w_ref, sems):
     lc, c = drive_ref.shape
     p = proj_ref.shape[1]
     n = dlog_ref.shape[0]
@@ -83,7 +83,7 @@
     nb = lc // T
     groups = c // 256
     i = pl.program_id(0)
-    pfx = prefix_ref[0]
+    pfx = order_ref[4]
     rate2 = -jnp.exp(dlog_ref[...]) * LOG2E
     lanes = [slice(g * 256, (g + 1) * 256) for g in range(groups)]
 
@@ -139,7 +139,7 @@
             for g in range(groups):
                 st_f[g] = out[g]
 
-    @pl.when(i >= ng)
+    @pl.when(jnp.logical_and(i >= ng, i < ng + nc))
     def _():
         chunk = i - ng
 
@@ -256,6 +256,35 @@
             run(False)
 
         part_ref[...] = mm(rc_s[...], fold(r + n, p, n))
+        spot = pl.ds(pl.multiple_of(chunk * lc, lc), lc)
+        gated_s[spot, :] = gated_ref[...]
+        dzs_s[spot, :] = dz_ref[...]
+
+    tn_dims = (((0,), (0,)), ((), ()))
+    copies = [pltpu.make_async_copy(a, b, sems.at[j]) for j, (a, b) in enumerate(((normed_hbm, normed_ref), (cot_hbm, cot_ref), (low_hbm, low_ref), (w_hbm, w_ref)))]
+
+    @pl.when(i == 1)
+    def _():
+        for copy in copies:
+            copy.start()
+
+    @pl.when(i == ng + nc)
+    def _():
+        for copy in copies:
+            copy.wait()
+
+    for late, (zo_ref, oo_ref, mo_ref) in enumerate(((sz_ref, so_ref, sm_ref), (kz_ref, ko_ref, km_ref))):
+        @pl.when(i == ng + nc + late)
+        def _(late=late, zo_ref=zo_ref, oo_ref=oo_ref, mo_ref=mo_ref):
+            side = lambda j: order_ref[j] if late else 1 - order_ref[j]
+            rows = gated_s.shape[0] // 2
+            wide = normed_ref[:, pl.ds(pl.multiple_of(side(0) * (normed_ref.shape[1] // 2), 128), normed_ref.shape[1] // 2)]
+            zo_ref[...] = lax.dot_general(wide, dzs_s[...], tn_dims, preferred_element_type=F32).astype(BF)
+            cols = gated_s[:, pl.ds(pl.multiple_of(side(1) * (c // 2), 128), c // 2)]
+            oo_ref[...] = lax.dot_general(cols, cot_ref[...], tn_dims, preferred_element_type=F32).astype(BF)
+            here = pl.ds(pl.multiple_of(side(2) * rows, 8), rows)
+            mix = mm(gated_s[here, :], w_ref[...])
+            mo_ref[...] = (mix + jnp.where(order_ref[3] == 0, low_ref[here, :].astype(F32), 0.0)).astype(BF)
 
 
 def back_kernel(ng, top, low, far, prefix_ref, proj_ref, sw_ref, drive_ref, step_ref, dy_ref, h_ref, pin_ref, dlog_ref, skip_ref, *refs):
@@ -587,39 +616,6 @@
     )(bits, dproj, ddrive, x, slope, drive, dz, normed, low, rs, w_all, xproj_t, conv_weight, g_bias, g_decay, decay_log, g_skip, proj, dpre)
 
 
-def outer_kernel(order_ref, normed_ref, dz_ref, cols_ref, cot_ref, rows_ref, low_ref, w_ref, kz_ref, sz_ref, ko_ref, so_ref, km_ref, sm_ref):
-    tn = (((0,), (0,)), ((), ()))
-    for step, z_ref, o_ref, m_ref in ((0, sz_ref, so_ref, sm_ref), (1, kz_ref, ko_ref, km_ref)):
-        @pl.when(pl.program_id(0) == step)
-        def _(z_ref=z_ref, o_ref=o_ref, m_ref=m_ref):
-            z_ref[...] = lax.dot_general(normed_ref[...], dz_ref[...], tn, preferred_element_type=F32).astype(BF)
-            o_ref[...] = lax.dot_general(cols_ref[...], cot_ref[...], tn, preferred_element_type=F32).astype(BF)
-            mix = mm(rows_ref[...], w_ref[...])
-            m_ref[...] = (mix + jnp.where(order_ref[3] == 0, low_ref[...].astype(F32), 0.0)).astype(BF)
-
-
-def outer(bits, normed, dz, gated, cot, low, out_weight):
-    l, d = normed.shape
-    c = dz.shape[1]
-    full = lambda *q: pl.BlockSpec(q, lambda i, order: (0,) * len(q))
-    half = lambda w, j: pl.BlockSpec((l, w // 2), lambda i, order: (0, lax.rem(i + 1 + order[j], 2)))
-    rows = lambda w: pl.BlockSpec((l // 2, w), lambda i, order: (lax.rem(i + 1 + order[2], 2), 0))
-    s = jax.ShapeDtypeStruct
-    return pl.pallas_call(
-        outer_kernel,
-        grid_spec=pltpu.PrefetchScalarGridSpec(
-            num_scalar_prefetch=1,
-            grid=(2,),
-            in_specs=[half(d, 0), full(l, c), half(c, 1), full(l, d), rows(c), rows(d), full(c, d)],
-            out_specs=[full(d // 2, c)] * 2 + [full(c // 2, d)] * 2 + [full(l // 2, d)] * 2,
-        ),
-        out_shape=[s((d // 2, c), BF)] * 2 + [s((c // 2, d), BF)] * 2 + [s((l // 2, d), BF)] * 2,
-        compiler_params=pltpu.CompilerParams(vmem_limit_bytes=60 << 20),
-        cost_estimate=pl.CostEstimate(flops=6 * l * d * c, transcendentals=0, bytes_accessed=10 * l * d),
-        name="outer",
-    )(bits, normed, dz, gated, cot, gated, low, out_weight)
-
-
 def merge_kernel(kinds, bits_ref, *refs):
     take = list(refs)
     ins = [[take.pop(0) for _ in range(2 + EXTRA[kind])] for kind in kinds]
@@ -676,91 +672,107 @@
     return [[out.pop(0) for _ in group] for group in shapes]
 
 
-def ending_kernel(bits_ref, cot_ref, na_ref, nb_ref, oa_ref, ob_ref, tok_ref, go_ref):
-    for bit, one, two, out, add in ((bits_ref[0], na_ref, nb_ref, tok_ref, cot_ref), (bits_ref[1], oa_ref, ob_ref, go_ref, None)):
-        rows = one.shape[0]
-        for at, part in ((bit, one), (1 - bit, two)):
-            where = pl.ds(pl.multiple_of(at * rows, 8), rows)
-            value = part[...].astype(F32)
-            out[where, :] = value if add is None else value + add[where, :].astype(F32)
-
-
-def ending(bits, cot, na, nb, oa, ob):
-    s = jax.ShapeDtypeStruct
+def joined_kernel(bits_ref, one_ref, two_ref, *refs):
+    out_ref = refs[-1]
+    rows = one_ref.shape[0]
+    for at, part in ((bits_ref[0], one_ref), (1 - bits_ref[0], two_ref)):
+        where = pl.ds(pl.multiple_of(at * rows, 8), rows)
+        value = part[...].astype(F32)
+        out_ref[where, :] = value if len(refs) == 1 else value + refs[0][where, :].astype(F32)
+
+
+def joined(bit, one, two, *add):
     vm = pl.BlockSpec(memory_space=pltpu.VMEM)
+    shape = (2 * one.shape[0], one.shape[1])
     return pl.pallas_call(
-        ending_kernel,
-        in_specs=[SMEM] + [vm] * 5,
-        out_specs=[vm] * 2,
-        out_shape=[s(cot.shape, F32), s((2 * oa.shape[0], oa.shape[1]), F32)],
+        joined_kernel,
+        in_specs=[SMEM] + [vm] * (2 + len(add)),
+        out_specs=vm,
+        out_shape=jax.ShapeDtypeStruct(shape, F32),
         compiler_params=pltpu.CompilerParams(vmem_limit_bytes=24 << 20),
-        cost_estimate=pl.CostEstimate(flops=cot.size, transcendentals=0, bytes_accessed=12 * cot.size),
-        name="ending",
-    )(bits, cot, na, nb, oa, ob)
-
-
-def last_kernel(n, r, p, taps, bits_ref, sa_ref, oa_ref, sb_ref, ob_ref, sz_ref, oz_ref, gin_ref, gc_ref, gcb_ref, gb_ref, gk_ref, gd_ref, gs_ref, gx_ref, a_s, b_s):
-    for j, mine, other, whole_s in ((0, sa_ref, oa_ref, a_s), (1, sb_ref, ob_ref, b_s)):
-        half = mine.shape[0]
-        whole_s[pl.ds(pl.multiple_of(bits_ref[j] * half, 8), half), :] = mine[...]
-        whole_s[pl.ds(pl.multiple_of((1 - bits_ref[j]) * half, 8), half), :] = other[...]
-    lines = a_s[pl.ds(0, 16), :].astype(F32)
-    gc_ref[...] = lines[:taps]
-    gcb_ref[...] = lines[taps : taps + 1]
-    gb_ref[...] = lines[taps + 1 : taps + 2]
-    gk_ref[...] = lines[taps + 2 : taps + 3]
-    gd_ref[...] = a_s[pl.ds(16, n), :].astype(F32)
-    gs_ref[...] = a_s[pl.ds(16 + n, r), :].astype(F32)
-    gx_ref[...] = a_s[pl.ds(16 + n + r, p), :].astype(F32)
+        name="joined",
+    )(bit.astype(jnp.int32).reshape(1), one, two, *add)
+
+
+def last_kernel(n, r, p, taps, bits_ref, sa_ref, oa_ref, sb_ref, ob_ref, sz_ref, oz_ref, gin_ref, gc_ref, gcb_ref, gb_ref, gk_ref, gd_ref, gs_ref, gx_ref, all_s, z_s):
     top = 16 + n + r + p
-    half = sz_ref.shape[0]
-    d = 2 * half
-    cut = a_s.shape[0] - top
-    gin_ref[pl.ds(0, cut), 0, :] = a_s[pl.ds(top, cut), :].astype(F32)
-    gin_ref[pl.ds(cut, d - cut), 0, :] = b_s[pl.ds(0, d - cut), :].astype(F32)
-    gin_ref[pl.ds(pl.multiple_of(bits_ref[2] * half, 8), half), 1, :] = sz_ref[...].astype(F32)
-    gin_ref[pl.ds(pl.multiple_of((1 - bits_ref[2]) * half, 8), half), 1, :] = oz_ref[...].astype(F32)
+    hc = gin_ref.shape[0]
+
+    @pl.when(pl.program_id(0) == 0)
+    def _():
+        base = 0
+        for j, mine, other, whole_s in ((0, sa_ref, oa_ref, all_s), (1, sb_ref, ob_ref, all_s), (2, sz_ref, oz_ref, z_s)):
+            half = mine.shape[0]
+            base = 0 if j == 2 else base
+            whole_s[pl.ds(pl.multiple_of(base + bits_ref[j] * half, 8), half), :] = mine[...]
+            whole_s[pl.ds(pl.multiple_of(base + (1 - bits_ref[j]) * half, 8), half), :] = other[...]
+            base += 2 * half
+        lines = all_s[pl.ds(0, 16), :].astype(F32)
+        gc_ref[...] = lines[:taps]
+        gcb_ref[...] = lines[taps : taps + 1]
+        gb_ref[...] = lines[taps + 1 : taps + 2]
+        gk_ref[...] = lines[taps + 2 : taps + 3]
+        gd_ref[...] = all_s[pl.ds(16, n), :].astype(F32)
+        gs_ref[...] = all_s[pl.ds(16 + n, r), :].astype(F32)
+        gx_ref[...] = all_s[pl.ds(16 + n + r, p), :].astype(F32)
+
+    at = pl.program_id(0) * hc
+    gin_ref[:, 0, :] = all_s[pl.ds(pl.multiple_of(top + at, 8), hc), :].astype(F32)
+    gin_ref[:, 1, :] = z_s[pl.ds(pl.multiple_of(at, 8), hc), :].astype(F32)
 
 
 def last(bits, sa, oa, sb, ob, sz, oz, n, r, p, taps):
     half, c = sz.shape
+    hc = 256
     s = jax.ShapeDtypeStruct
-    vm = pl.BlockSpec(memory_space=pltpu.VMEM)
+    small = [s((taps, c), F32), s((1, c), F32), s((1, c), F32), s((1, c), F32), s((n, c), F32), s((r, c), F32), s((p, c), F32)]
+    arrays = [sa, oa, sb, ob, sz, oz]
     return pl.pallas_call(
         functools.partial(last_kernel, n, r, p, taps),
-        in_specs=[SMEM] + [vm] * 6,
-        out_specs=[vm] * 8,
-        out_shape=[s((2 * half, 2, c), F32), s((taps, c), F32), s((1, c), F32), s((1, c), F32), s((1, c), F32), s((n, c), F32), s((r, c), F32), s((p, c), F32)],
-        scratch_shapes=[pltpu.VMEM((2 * sa.shape[0], c), BF), pltpu.VMEM((2 * sb.shape[0], c), BF)],
+        grid=(2 * half // hc,),
+        in_specs=[SMEM] + [once(*v.shape) for v in arrays],
+        out_specs=[pl.BlockSpec((hc, 2, c), lambda i: (i, 0, 0))] + [whole(*v.shape) for v in small],
+        out_shape=[s((2 * half, 2, c), F32)] + small,
+        scratch_shapes=[pltpu.VMEM((2 * sa.shape[0] + 2 * sb.shape[0], c), BF), pltpu.VMEM((2 * half, c), BF)],
         compiler_params=pltpu.CompilerParams(vmem_limit_bytes=24 << 20),
         name="last",
-    )(bits, sa, oa, sb, ob, sz, oz)
-
-
-def front(prefix, proj, sw, bias, drive, z, dg, dlog, skip):
+    )(bits, *arrays)
+
+
+def front(order, proj, sw, bias, drive, z, dg, dlog, skip, normed, cot, low, out_weight):
     l, c = drive.shape
+    d = low.shape[1]
     p = proj.shape[1]
     n = dlog.shape[0]
     ng = l // 2 // LC
     nc = l // LC
     s = jax.ShapeDtypeStruct
-    fwd = lambda i: (jnp.maximum(i - ng, 0), 0)
-    both = lambda i: (jnp.where(i < ng, ng - 1 - i, i - ng), 0)
-    half = lambda i: (jnp.clip(i - ng, 0, ng - 1), 0)
+    fwd = lambda i, o: (jnp.clip(i - ng, 0, nc - 1), 0)
+    both = lambda i, o: (jnp.where(i < ng, ng - 1 - i, jnp.minimum(i - ng, nc - 1)), 0)
+    half = lambda i, o: (jnp.clip(i - ng, 0, ng - 1), 0)
+    full = lambda *q: pl.BlockSpec(q, lambda i, o: (0,) * len(q))
+    once = lambda *q: pl.BlockSpec(q, lambda i, o: (0,) * len(q), pipeline_mode=pl.Buffered(1))
     B = pl.BlockSpec
     lanes = c // 128
     v = pltpu.VMEM
     return pl.pallas_call(
-        functools.partial(front_kernel, ng),
-        grid=(ng + nc,),
-        in_specs=[SMEM, B((LC, p), both), whole(*sw.shape), whole(1, c), B((LC, c), both), B((LC, c), fwd), B((LC, c), fwd), whole(n, c), whole(1, c)],
-        out_specs=[B((LC, c), fwd), B((LC, c), fwd), B((LC, c), fwd), B((LC, c), fwd), B((LC * n, c), fwd), B((LC * n, c), half), B((LC * n, c), half), B((LC, p), fwd), whole(1, c)],
-        out_shape=[s((l, c), BF), s((l, c), BF), s((l, c), F32), s((l, c), F32), s((l * n, c), BF), s((l // 2 * n, c), BF), s((l // 2 * n, c), BF), s((l, p), F32), s((1, c), F32)],
-        scratch_shapes=[v((lanes, LC, 128), F32)] * 3 + [v((LC, c), F32), v((ng, LC, c), F32), v((n, LC), F32), v((n, LC), F32), v((LC, T * n), BF), v((LC, T * n), BF),
-            v((LC // T, T * n, c), BF), v((l // 2 * n, c), BF), v((l // 2 * n, c), BF), v((c // 128, n, 256), F32), v((c // 256, n, 256), BF), v((c // 256, n, 256), F32)],
+        functools.partial(front_kernel, ng, nc),
+        grid_spec=pltpu.PrefetchScalarGridSpec(
+            num_scalar_prefetch=1,
+            grid=(ng + nc + 2,),
+            in_specs=[B((LC, p), both), full(*sw.shape), full(1, c), B((LC, c), both), B((LC, c), fwd), B((LC, c), fwd), full(n, c), full(1, c),
+                      ] + [B(memory_space=pl.ANY)] * 4,
+            out_specs=[B((LC, c), fwd), B((LC, c), fwd), B((LC, c), fwd), B((LC, c), fwd), B((LC * n, c), fwd), B((LC * n, c), half), B((LC * n, c), half), B((LC, p), fwd), full(1, c)]
+                + [once(d // 2, c)] * 2 + [once(c // 2, d)] * 2 + [once(l // 2, d)] * 2,
+            scratch_shapes=[v((lanes, LC, 128), F32)] * 3 + [v((LC, c), F32), v((ng, LC, c), F32), v((n, LC), F32), v((n, LC), F32), v((LC, T * n), BF), v((LC, T * n), BF),
+                v((LC // T, T * n, c), BF), v((l // 2 * n, c), BF), v((l // 2 * n, c), BF), v((c // 128, n, 256), F32), v((c // 256, n, 256), BF), v((c // 256, n, 256), F32), v((l, c), BF), v((l, c), BF),
+                v((l, d), BF), v((l, d), BF), v((l, d), BF), v((c, d), BF), pltpu.SemaphoreType.DMA((4,))],
+        ),
+        out_shape=[s((l, c), BF), s((l, c), BF), s((l, c), F32), s((l, c), F32), s((l * n, c), BF), s((l // 2 * n, c), BF), s((l // 2 * n, c), BF), s((l, p), F32), s((1, c), F32)]
+            + [s((d // 2, c), BF)] * 2 + [s((c // 2, d), BF)] * 2 + [s((l // 2, d), BF)] * 2,
         compiler_params=pltpu.CompilerParams(vmem_limit_bytes=60 << 20),
         name="front",
-    )(prefix, proj, sw, bias.reshape(1, c), drive, z, dg, dlog, skip.reshape(1, c))
+    )(order, proj, sw, bias.reshape(1, c), drive, z, dg, dlog, skip.reshape(1, c), normed, cot, low, out_weight)
 
 
 def back(prefix, proj, sw, drive, step, dy, hprev, ag, wg, pin, dlog, skip, carry, top, low, filled=()):
@@ -907,10 +919,8 @@
     other, zpart, dgated = lax.optimization_barrier((other, zpart, dgated))
     proj = (proj.astype(F32) + other.astype(F32)).astype(BF)
 
-    gated, dz, step, dy, hprev, ag, wg, pin, g_skip = front(prefix, proj, step_weight, step_bias, drive, zpart, dgated, decay_log, skip_gain)
-
-    picks = jnp.stack([bit_of(at_dp, order[0]), bit_of(at_dp, turned[0]), bit_of(at, t_order[0]), at]).astype(jnp.int32)
-    kz, sz, ko, so, km, sm = outer(picks, normed, dz, gated, cot, low, out_weight)
+    picks = jnp.stack([bit_of(at_dp, order[0]), bit_of(at_dp, turned[0]), bit_of(at, t_order[0]), at, prefix[0]]).astype(jnp.int32)
+    gated, dz, step, dy, hprev, ag, wg, pin, g_skip, kz, sz, ko, so, km, sm = front(picks, proj, step_weight, step_bias, drive, zpart, dgated, decay_log, skip_gain, normed, cot, low, out_weight)
     gz = Chain("dp", dp, order, kz, sz)
     go = Chain("dp", dp, turned, ko, so)
     mix = Chain("tensor", tp, t_order, km, sm, swap=False)
@@ -933,7 +943,8 @@
     for bit in t_order[:-1]:
         dpart = (dpart.astype(F32) + exchange(dpart, "tensor", tp, bit).astype(F32)).astype(BF)
     cross = Chain("tensor", tp, t_order[-1:], dpart, dpart)
-    my_x, my_rs = under([cross, mix], lambda v, w: (part_of(v), part_of(w)), low, rs)
+    my_x, my_rs = under([gz, go, cross, mix], lambda v, w: (part_of(v), part_of(w)), low, rs)
+    ready([gz, go])
     dproj = (cross.send.astype(F32) + cross.got.astype(F32)).astype(BF)
     total = 16 + n + p + rank + width
     total += -total % (16 << (len(order) - 1))
@@ -950,14 +961,23 @@
             v = v + exchange(v, name, size, bit)
         return v
 
-    late = [[], [gz], [go]]
+    def closing(v, one, two, *out):
+        joint = merge([("join", mix.mine(mix.steps[0][1]), *out)])[0][0] if mix.ended() else None
+        return gains(v), joined(go.mine(go.steps[0][1]), one, two), joint
+
+    block_out = None
+    late = [[]]
+    g_out = None
     while not la.ended():
         extra = late.pop(0) if late else [c for c in (gz, go) if not c.ended()]
         ready(extra + [la, lb, dn])
         final = len(la.steps) == 1
         slow = [dn] if dn.got is None and len(dn.steps) > 1 and dn.steps[0][1] != t_order[0] else []
         now = [dn] if dn.got is None and not slow and not final else []
-        g_norm = under([la, lb] + now + extra, gains, g_norm, slow=slow)
+        if final and go.ended():
+            g_norm, g_out, block_out = under([la, lb] + now + extra, closing, g_norm, go.send, go.got, mix.send, mix.got, slow=slow)
+        else:
+            g_norm = under([la, lb] + now + extra, gains, g_norm, slow=slow)
     while turns:
         g_norm = gains(g_norm)
     for c in (dn, gz, go):
@@ -966,9 +986,14 @@
             under([c], lambda: ())
     flags = jnp.stack([c.mine(c.steps[0][1]) for c in (la, lb, gz)]).astype(jnp.int32)
     g_in, g_conv, g_convb, g_bias, g_skip, g_decay, g_step, g_xproj = last(flags, la.send, la.got, lb.send, lb.got, gz.send, gz.got, n, rank, p, taps)
-    flags = jnp.stack([dn.mine(dn.steps[0][1]), go.mine(go.steps[0][1])]).astype(jnp.int32)
-    grad_tokens, g_out = ending(flags, cot, dn.send, dn.got, go.send, go.got)
-    block_out = merge([mix.item()] if len(mix.steps) > 1 else [("join", mix.mine(mix.steps[0][1]), mix.send, mix.got)])[0][0]
+    grad_tokens = joined(dn.mine(dn.steps[0][1]), dn.send, dn.got, cot)
+    if g_out is None:
+        g_out = joined(go.mine(go.steps[0][1]), go.send, go.got)
+    if block_out is None:
+        while not mix.ended():
+            under([mix], lambda: ())
+            ready([mix])
+        block_out = merge([mix.item()] if len(mix.steps) > 1 else [("join", mix.mine(mix.steps[0][1]), mix.send, mix.got)])[0][0]
     return (block_out[None], grad_tokens[None], g_norm.reshape(-1), g_in, g_conv, g_convb[0], g_xproj.T, g_step, g_bias[0], g_decay, g_skip[0], g_out)
 
 

time: 217 us -> 211 us (0.972)
  waiting for transfers between devices: 41.2 us -> 28.2 us
  starting transfers between devices: 41.9 us -> 46.5 us
  local copies, waits for them, and re-layouts: 5.57 us -> 7.84 us
    ppermute x37, waiting for transfers between devices: 41.2 us -> 28.2 us  [exchange(): return lax.ppermute(value, name, [(j, j ^ 1 << bit) for j in range(size)])]
    ppermute x37, starting transfers between devices: 41.9 us -> 46.5 us  [exchange(): return lax.ppermute(value, name, [(j, j ^ 1 << bit) for j in range(size)])]
    unnamed x7 -> x11, local copies, waits for them, and re-layouts: 3.49 us -> 5.16 us
    pallas_call x9 -> x10, Pallas kernels: 12.4 us -> 13.9 us  [merge(): pl.pallas_call(functools.partial(merge_kernel, kinds), grid=(1,), in_spec...]
  transfers between devices with their start and end apart: 37 -> 37, of which waited for: 17 -> 14; matrix products, arithmetic and copies ran while one was open for 2% -> 2% of each run, Pallas kernels for 28% -> 30%
where the time goes in v4:
time: 211 us; the launch traced here: 210 us
  Pallas kernels  121 us (57%)
  starting transfers between devices  46.5 us (22%)
  waiting for transfers between devices  28.2 us (13%)
  local copies, waits for them, and re-layouts  7.84 us (4%)
  other arithmetic  4.11 us (2%)
    ppermute x37, starting transfers between devices, exchange(): return lax.ppermute(value, name, [(j, j ^ 1 << bit) for j in range(size)])  46.5 us
    pallas_call x1, Pallas kernels, front(): pl.pallas_call(functools.partial(front_kernel, ng, nc), grid_spec=pltpu.P...  38.9 us
    pallas_call x3, Pallas kernels, back(): pl.pallas_call(functools.partial(back_kernel, ng, top, low, len(extra)),...  31.6 us
    ppermute x37, waiting for transfers between devices, exchange(): return lax.ppermute(value, name, [(j, j ^ 1 << bit) for j in range(size)])  28.2 us
    pallas_call x1, Pallas kernels, inner(): pl.pallas_call(functools.partial(inner_kernel, rows_a, rows_b), grid_spec...  15.1 us
    pallas_call x10, Pallas kernels, merge(): pl.pallas_call(functools.partial(merge_kernel, kinds), grid=(1,), in_spec...  13.9 us
    pallas_call x1, Pallas kernels, head(): pl.pallas_call(head_kernel, grid=(l // hc,), in_specs=[by(d), whole(1, d)...  7.02 us
    pallas_call x1, Pallas kernels, gates(): pl.pallas_call(gates_kernel, grid=(l // 256,), in_specs=[by(d), pl.BlockS...  6.32 us
  transfers between devices with their start and end apart: 37, of which 14 were waited for; matrix products, arithmetic and copies ran while one was open for 2% of the time, Pallas kernels for 30%

profile of v4, /device:TPU:1, one launch (start us, length us, event | category | flops | bytes accessed | tf_op | source)
XLA Modules:
  0.0 209.7 jit_solution(5226668604947408720)
XLA Ops:
  0.6 3.5 %copy.31 = bf16[128,8,2,512]{3,1,2,0:T(8,128)(2,1)} copy(bf16[128,8,2,512]{3,2,1,0:T(2,128)(2,1)} %bitcast.35) | data formatting | bytes 4194304
  4.1 7.0 %head.1 = (bf16[1024,1024]{1,0:T(8,128)(2,1)}, bf16[1024,512]{1,0:T(8,128)(2,1)}, f32[1024,512]{1,0:T(8,128)}, bf16[1024,512]{1,0:T(8,128)(2,1)}, bf16[1024,96]{1,0:T(8,128)(2,1)}, /*index=5*/f32[1024,1]{1,0:T(8,128)}) custom-call(bf16[1024,1024]{1,0:T(8,128)(2,1)} %bitcast.27, f32[1,1024]{1,0:T(1,128)} %bitcast.25, bf16[1024,1024]{1,0:T(8,128)(2,1)} %bitcast.31, ...), custom_call_target="tpu_custom_call" | custom-call | flops 1073741824 | bytes 8388608 | tf_op jit(solution)/shard_map/head/pallas_call | solution.py:477
  11.9 0.6 stack.58.order_ref.bits_ref
  12.9 1.0 add_convert_fusion.3
  14.0 2.4 %collective-permute-start.1 = (bf16[1024,96]{1,0:T(8,128)(2,1)S(1)}, bf16[1024,96]{1,0:T(8,128)(2,1)S(1)}, u32[]{:S(2)}, u32[]{:S(2)}) collective-permute-start(bf16[1024,96]{1,0:T(8,128)(2,1)S(1)} %add_convert_fusion.3), channel_id=1, source_target_pairs={{0,2},{1,3},{2,0},{3,1},{4,6},{5,7},{6,4},{7,5},{8,10},{9,11},{10,... | collective-permute-start | bytes 589832 | tf_op jit(solution)/shard_map/ppermute | solution.py:814
  16.4 6.3 %gates.1 = (f32[1024,512]{1,0:T(8,128)}, f32[1024,512]{1,0:T(8,128)}) custom-call(bf16[1024,1024]{1,0:T(8,128)(2,1)} %get-tuple-element.235.n_ref.normed_hbm.normed_ref, bf16[1024,1024]{1,0:T(8,128)(2,1)} %bitcast.32, bf16[1024,1024]{1,0:T(8,128)(2,1)} %bitcast.22, bf16[512,1024]{1,0:T(8,128)(2,1)} %w_hbm.1), custom_call_target="tpu_custom_call" | custom-call | flops 2147483648 | bytes 10485760 | tf_op jit(solution)/shard_map/gates/pallas_call | solution.py:500
  22.8 0.8 add_convert_fusion.2.proj_ref
  23.5 38.9 %front.1 = (bf16[1024,512]{1,0:T(8,128)(2,1)}, bf16[1024,512]{1,0:T(8,128)(2,1)}, f32[1024,512]{1,0:T(8,128)}, f32[1024,512]{1,0:T(8,128)}, bf16[16384,512]{1,0:...) custom-call(s32[5]{0:T(128)} %stack.58.order_ref.bits_ref, ...), custom_call_target="tpu_custom_call" | custom-call | tf_op jit(solution)/shard_map/front/pallas_call | solution.py:758
  62.5 1.9 collective-permute-start.3
  64.4 1.7 collective-permute-start.4
  66.1 10.1 %back.3 = (bf16[1024,96]{1,0:T(8,128)(2,1)}, bf16[1024,512]{1,0:T(8,128)(2,1)}, f32[1024,512]{1,0:T(8,128)}, f32[16,512]{1,0:T(8,128)}, f32[16,512]{1,0:T(8,128)}, /*index=5*/f32[1,512]{1,0:T(1,128)}) custom-call(s32[1]{0:T(128)S(6)} %copy.38.prefix_ref, bf16[1024,96]{1,0:T(8,128)(2,1)} %add_convert_fusion.2.proj_ref, bf16[64,512]{1,0:T(8,128)(2,1)} %sw_ref.7, ...), custom_call_target="tpu_custom_call" | custom-call | flops 12582912000 | bytes 12582912 | tf_op jit(solution)/shard_map/back/pallas_call | solution.py:795
  76.2 2.9 %merge.10 = (bf16[256,512]{1,0:T(8,128)(2,1)}, bf16[256,512]{1,0:T(8,128)(2,1)S(1)}, bf16[128,1024]{1,0:T(8,128)(2,1)}, bf16[128,1024]{1,0:T(8,128)(2,1)S(1)}, b...) custom-call(s32[3]{0:T(128)S(1)} %get-tuple-element.452.bits_ref, bf16[512,512]{1,0:T(8,128)(2,1)} %get-tuple-element.243.refs_0_, ...), custom_call_target="tpu_custom_call" | custom-call | tf_op jit(solution)/shard_map/merge/pallas_call | solution.py:663
  79.4 0.7 collective-permute-start.6
  80.1 1.2 collective-permute-start.7
  81.4 12.1 %back.4 = (bf16[1024,96]{1,0:T(8,128)(2,1)}, bf16[1024,512]{1,0:T(8,128)(2,1)}, f32[1024,512]{1,0:T(8,128)}, f32[16,512]{1,0:T(8,128)}, f32[16,512]{1,0:T(8,128)}, /*index=5*/f32[1,512]{1,0:T(1,128)}) custom-call(s32[1]{0:T(128)S(6)} %copy.38.prefix_ref, ...), custom_call_target="tpu_custom_call", output_to_operand_aliasing={{0}: (15, {}), {1}: (16, {}), {2}: (17, {})} | custom-call | flops 12582912000 | bytes 12582912 | tf_op jit(solution)/shard_map/back/pallas_call | solution.py:795
  93.5 1.5 merge.11
  94.9 1.6 collective-permute-start.8
  97.0 9.5 %back.5 = (bf16[1024,96]{1,0:T(8,128)(2,1)}, bf16[1024,512]{1,0:T(8,128)(2,1)}, f32[1024,512]{1,0:T(8,128)}, f32[16,512]{1,0:T(8,128)}, f32[16,512]{1,0:T(8,128)}, /*index=5*/f32[1,512]{1,0:T(1,128)}) custom-call(s32[1]{0:T(128)S(6)} %copy.38.prefix_ref, ...), custom_call_target="tpu_custom_call", output_to_operand_aliasing={{0}: (15, {}), {1}: (16, {}), {2}: (17, {})} | custom-call | flops 8388608000 | bytes 8388608 | tf_op jit(solution)/shard_map/back/pallas_call | solution.py:795
  106.5 2.7 %collective-permute-done.8.refs_1_ = bf16[256,512]{1,0:T(8,128)(2,1)S(1)} collective-permute-done((bf16[256,512]{1,0:T(8,128)(2,1)S(1)}, bf16[256,512]{1,0:T(8,128)(2,1)S(1)}, u32[]{:S(2)}, u32[]{:S(2)}) %collective-permute-start.8) | collective-permute-done | bytes 262176 | tf_op jit(solution)/shard_map/ppermute | solution.py:814
  109.2 2.2 %collective-permute-start.11 = (bf16[1024,96]{1,0:T(8,128)(2,1)}, bf16[1024,96]{1,0:T(8,128)(2,1)S(1)}, u32[]{:S(2)}, u32[]{:S(2)}) collective-permute-start(bf16[1024,96]{1,0:T(8,128)(2,1)} %get-tuple-element.331), channel_id=1, source_target_pairs={{0,1},{1,0},{2,3},{3,2},{4,5},{5,4},{6,7},{7,6},{8,9},{9,8},{10,11... | collective-permute-start | bytes 589832 | tf_op jit(solution)/shard_map/ppermute | solution.py:814
  111.4 0.7 merge.12
  112.1 0.6 collective-permute-done.11
  113.7 1.8 collective-permute-start.13
  116.1 0.9 constant_dynamic-slice_fusion.refs_7_
  117.1 1.1 constant_dynamic-slice_fusion.1.refs_6_
  118.1 4.6 %collective-permute-done.14 = bf16[1024,96]{1,0:T(8,128)(2,1)S(1)} collective-permute-done((bf16[1024,96]{1,0:T(8,128)(2,1)S(1)}, bf16[1024,96]{1,0:T(8,128)(2,1)S(1)}, u32[]{:S(2)}, u32[]{:S(2)}) %collective-permute-start.14) | collective-permute-done | bytes 196640 | tf_op jit(solution)/shard_map/ppermute | solution.py:814
  122.8 3.9 %collective-permute-done.12.refs_1_ = bf16[256,512]{1,0:T(8,128)(2,1)S(1)} collective-permute-done((bf16[256,512]{1,0:T(8,128)(2,1)S(1)}, bf16[256,512]{1,0:T(8,128)(2,1)S(1)}, u32[]{:S(2)}, u32[]{:S(2)}) %collective-permute-start.12) | collective-permute-done | bytes 262176 | tf_op jit(solution)/shard_map/ppermute | solution.py:814
  126.6 0.7 copy-done.1
  127.4 0.8 add_convert_fusion.dproj_ref
  128.1 0.9 copy-done.2
  129.1 1.4 merge.13
  130.5 2.6 %collective-permute-start.16 = (bf16[512,512]{1,0:T(8,128)(2,1)S(1)}, bf16[512,512]{1,0:T(8,128)(2,1)S(1)}, u32[]{:S(2)}, u32[]{:S(2)}) collective-permute-start(bf16[512,512]{1,0:T(8,128)(2,1)S(1)} %get-tuple-element.441.sz_ref), channel_id=1, source_target_pairs={{0,4},{4,0},{8,12},{12,8},{16,20},{20,16},{24,28},{28,24},{1,5},{5... | collective-permute-start | bytes 1572872 | tf_op jit(solution)/shard_map/ppermute | solution.py:814
  133.1 15.1 %inner.1 = (bf16[304,512]{1,0:T(8,128)(2,1)}, bf16[304,512]{1,0:T(8,128)(2,1)}, bf16[304,512]{1,0:T(8,128)(2,1)}, bf16[304,512]{1,0:T(8,128)(2,1)}, bf16[512,102...) custom-call(s32[5]{0:T(128)} %stack.58.order_ref.bits_ref, ...), custom_call_target="tpu_custom_call" | custom-call | flops 3221225472 | bytes 10485760 | tf_op jit(solution)/shard_map/inner/pallas_call | solution.py:602
  148.2 1.6 collective-permute-start.20
  149.8 0.6 collective-permute-start.18
  150.4 1.1 collective-permute-start.19
  152.0 2.5 %collective-permute-done.21 = f32[1,1024]{1,0:T(1,128)S(1)} collective-permute-done((f32[1,1024]{1,0:T(1,128)}, f32[1,1024]{1,0:T(1,128)S(1)}, u32[]{:S(2)}, u32[]{:S(2)}) %collective-permute-start.21) | collective-permute-done | bytes 4128 | tf_op jit(solution)/shard_map/ppermute | solution.py:814
  154.5 0.7 add.42
  155.2 3.7 %collective-permute-done.18.refs_1_ = bf16[304,512]{1,0:T(8,128)(2,1)S(1)} collective-permute-done((bf16[304,512]{1,0:T(8,128)(2,1)}, bf16[304,512]{1,0:T(8,128)(2,1)S(1)}, u32[]{:S(2)}, u32[]{:S(2)}) %collective-permute-start.18) | collective-permute-done | bytes 311328 | tf_op jit(solution)/shard_map/ppermute | solution.py:814
  159.2 2.6 %merge.14 = (bf16[152,512]{1,0:T(8,128)(2,1)}, bf16[152,512]{1,0:T(8,128)(2,1)S(1)}, bf16[152,512]{1,0:T(8,128)(2,1)}, bf16[152,512]{1,0:T(8,128)(2,1)S(1)}, bf1...) custom-call(s32[3]{0:T(128)S(1)} %get-tuple-element.452.bits_ref, bf16[304,512]{1,0:T(8,128)(2,1)} %get-tuple-element.366.refs_0_, ...), custom_call_target="tpu_custom_call" | custom-call | tf_op jit(solution)/shard_map/merge/pallas_call | solution.py:663
  162.2 1.4 collective-permute-start.22
  163.6 1.3 collective-permute-start.23
  164.8 1.7 collective-permute-start.24
  166.5 0.8 collective-permute-done.24
  167.4 2.2 %collective-permute-done.23.refs_3_ = bf16[152,512]{1,0:T(8,128)(2,1)S(1)} collective-permute-done((bf16[152,512]{1,0:T(8,128)(2,1)S(1)}, bf16[152,512]{1,0:T(8,128)(2,1)S(1)}, u32[]{:S(2)}, u32[]{:S(2)}) %collective-permute-start.23) | collective-permute-done | bytes 155680 | tf_op jit(solution)/shard_map/ppermute | solution.py:814
  169.5 1.1 merge.15
  170.6 2.2 %collective-permute-start.25 = (bf16[152,512]{1,0:T(8,128)(2,1)S(1)}, bf16[152,512]{1,0:T(8,128)(2,1)S(1)}, u32[]{:S(2)}, u32[]{:S(2)}) collective-permute-start(bf16[152,512]{1,0:T(8,128)(2,1)S(1)} %get-tuple-element.398.refs_0_), channel_id=1, source_target_pairs={{0,16},{4,20},{8,24},{12,28},{16,0},{20,4},{24,8},{28,12},{1,17},{... | collective-permute-start | bytes 466952 | tf_op jit(solution)/shard_map/ppermute | solution.py:814
  172.8 1.0 collective-permute-start.26
  174.3 2.7 %collective-permute-done.28 = f32[1,1024]{1,0:T(1,128)S(1)} collective-permute-done((f32[1,1024]{1,0:T(1,128)S(1)}, f32[1,1024]{1,0:T(1,128)S(1)}, u32[]{:S(2)}, u32[]{:S(2)}) %collective-permute-start.28) | collective-permute-done | bytes 4128 | tf_op jit(solution)/shard_map/ppermute | solution.py:814
  177.0 1.6 merge.16
  178.6 2.0 collective-permute-start.34
  180.6 2.1 %collective-permute-start.29 = (bf16[152,512]{1,0:T(8,128)(2,1)S(1)}, bf16[152,512]{1,0:T(8,128)(2,1)S(1)}, u32[]{:S(2)}, u32[]{:S(2)}) collective-permute-start(bf16[152,512]{1,0:T(8,128)(2,1)S(1)} %get-tuple-element.413.refs_0_), channel_id=1, source_target_pairs={{0,8},{4,12},{8,0},{12,4},{16,24},{20,28},{24,16},{28,20},{1,9},{5... | collective-permute-start | bytes 466952 | tf_op jit(solution)/shard_map/ppermute | solution.py:814
  182.7 3.2 %collective-permute-start.30 = (bf16[152,512]{1,0:T(8,128)(2,1)S(1)}, bf16[152,512]{1,0:T(8,128)(2,1)S(1)}, u32[]{:S(2)}, u32[]{:S(2)}) collective-permute-start(bf16[152,512]{1,0:T(8,128)(2,1)S(1)} %get-tuple-element.415.refs_2_), channel_id=1, source_target_pairs={{0,16},{4,20},{8,24},{12,28},{16,0},{20,4},{24,8},{28,12},{1,17},{... | collective-permute-start | bytes 466952 | tf_op jit(solution)/shard_map/ppermute | solution.py:814
  186.0 2.9 %collective-permute-done.31 = f32[1,1024]{1,0:T(1,128)S(1)} collective-permute-done((f32[1,1024]{1,0:T(1,128)S(1)}, f32[1,1024]{1,0:T(1,128)S(1)}, u32[]{:S(2)}, u32[]{:S(2)}) %collective-permute-start.31) | collective-permute-done | bytes 4128 | tf_op jit(solution)/shard_map/ppermute | solution.py:814
  188.8 1.0 collective-permute-done.30.refs_3_
  189.8 0.6 merge.17
  190.8 1.0 collective-permute-start.33
  191.8 2.0 collective-permute-start.35
  193.8 2.7 %joined.2 = f32[512,1024]{1,0:T(8,128)} custom-call(s32[1]{0:T(128)} %bitcast.bits_ref, bf16[256,1024]{1,0:T(8,128)(2,1)} %get-tuple-element.428.one_ref, bf16[256,1024]{1,0:T(8,128)(2,1)} %collective-permute-done.17.two_ref), custom_call_target="tpu_custom_call" | custom-call | tf_op jit(solution)/shard_map/joined/pallas_call | solution.py:687
  196.5 1.5 merge.18
  197.9 0.6 add.46
  198.6 5.0 %collective-permute-start.36 = (bf16[512,1024]{1,0:T(8,128)(2,1)S(1)}, bf16[512,1024]{1,0:T(8,128)(2,1)S(1)}, u32[]{:S(2)}, u32[]{:S(2)}) collective-permute-start(bf16[512,1024]{1,0:T(8,128)(2,1)S(1)} %merge.19.one_ref), channel_id=1, source_target_pairs={{0,1},{1,0},{2,3},{3,2},{4,5},{5,4},{6,7},{7,6},{8,9},{9,8},{10,11... | collective-permute-start | bytes 3145736 | tf_op jit(solution)/shard_map/ppermute | solution.py:814
  203.6 3.6 %last.1 = (f32[1024,2,512]{2,1,0:T(2,128)}, f32[4,512]{1,0:T(4,128)}, f32[1,512]{1,0:T(1,128)}, f32[1,512]{1,0:T(1,128)}, f32[1,512]{1,0:T(1,128)}, /*index=5*/f...) custom-call(s32[3]{0:T(128)S(1)} %get-tuple-element.453.bits_ref, bf16[304,512]{1,0:T(8,128)(2,1)S(1)} %get-tuple-element.437.sa_ref, ...), custom_call_target="tpu_custom_call" | custom-call | tf_op jit(solution)/shard_map/last/pallas_call | solution.py:730
  207.2 2.4 %joined.3 = f32[1024,1024]{1,0:T(8,128)} custom-call(s32[1]{0:T(128)} %bitcast.4.bits_ref, bf16[512,1024]{1,0:T(8,128)(2,1)S(1)} %merge.19.one_ref, bf16[512,1024]{1,0:T(8,128)(2,1)S(1)} %collective-permute-done.36.two_ref, bf16[1024,1024]{1,0:T(8,128)(2,1)S(1)} %bitcast.24), custom_call_target="tpu_custom_call" | custom-call | tf_op jit(solution)/shard_map/joined/pallas_call | solution.py:687
  (58 shorter events, 5.2 us)
Async XLA Ops:
  11.1 1.8 collective-permute-start
  14.0 8.8 %collective-permute-start.1 = (bf16[1024,96]{1,0:T(8,128)(2,1)S(1)}, bf16[1024,96]{1,0:T(8,128)(2,1)S(1)}, u32[]{:S(2)}, u32[]{:S(2)}) collective-permute-start(bf16[1024,96]{1,0:T(8,128)(2,1)S(1)} %add_convert_fusion.3), channel_id=1, source_target_pairs={{0,2},{1,3},{2,0},{3,1},{4,6},{5,7},{6,4},{7,5},{8,10},{9,11},{10,... | collective-permute-start | bytes 589832 | tf_op jit(solution)/shard_map/ppermute | solution.py:814
  62.4 13.7 %collective-permute-start.2 = (bf16[512,512]{1,0:T(8,128)(2,1)}, bf16[512,512]{1,0:T(8,128)(2,1)S(1)}, u32[]{:S(2)}, u32[]{:S(2)}) collective-permute-start(bf16[512,512]{1,0:T(8,128)(2,1)} %get-tuple-element.248), channel_id=1, source_target_pairs={{0,4},{4,0},{8,12},{12,8},{16,20},{20,16},{24,28},{28,24},{1,5},{5... | collective-permute-start | bytes 1572872 | tf_op jit(solution)/shard_map/ppermute | solution.py:814
  62.5 13.7 %collective-permute-start.3 = (bf16[256,1024]{1,0:T(8,128)(2,1)}, bf16[256,1024]{1,0:T(8,128)(2,1)S(1)}, u32[]{:S(2)}, u32[]{:S(2)}) collective-permute-start(bf16[256,1024]{1,0:T(8,128)(2,1)} %get-tuple-element.249), channel_id=1, source_target_pairs={{0,8},{4,12},{8,0},{12,4},{16,24},{20,28},{24,16},{28,20},{1,9},{5... | collective-permute-start | bytes 1572872 | tf_op jit(solution)/shard_map/ppermute | solution.py:814
  64.4 11.8 %collective-permute-start.4 = (bf16[512,1024]{1,0:T(8,128)(2,1)}, bf16[512,1024]{1,0:T(8,128)(2,1)S(1)}, u32[]{:S(2)}, u32[]{:S(2)}) collective-permute-start(bf16[512,1024]{1,0:T(8,128)(2,1)} %get-tuple-element.250), channel_id=1, source_target_pairs={{0,1},{1,0},{2,3},{3,2},{4,5},{5,4},{6,7},{7,6},{8,9},{9,8},{10,11... | collective-permute-start | bytes 3145736 | tf_op jit(solution)/shard_map/ppermute | solution.py:814
  79.0 14.4 %collective-permute-start.5 = (bf16[256,512]{1,0:T(8,128)(2,1)S(1)}, bf16[256,512]{1,0:T(8,128)(2,1)S(1)}, u32[]{:S(2)}, u32[]{:S(2)}) collective-permute-start(bf16[256,512]{1,0:T(8,128)(2,1)S(1)} %get-tuple-element.276), channel_id=1, source_target_pairs={{0,8},{4,12},{8,0},{12,4},{16,24},{20,28},{24,16},{28,20},{1,9},{5... | collective-permute-start | bytes 786440 | tf_op jit(solution)/shard_map/ppermute | solution.py:814
  79.4 14.0 %collective-permute-start.6 = (bf16[128,1024]{1,0:T(8,128)(2,1)S(1)}, bf16[128,1024]{1,0:T(8,128)(2,1)S(1)}, u32[]{:S(2)}, u32[]{:S(2)}) collective-permute-start(bf16[128,1024]{1,0:T(8,128)(2,1)S(1)} %get-tuple-element.277), channel_id=1, source_target_pairs={{0,16},{4,20},{8,24},{12,28},{16,0},{20,4},{24,8},{28,12},{1,17},{... | collective-permute-start | bytes 786440 | tf_op jit(solution)/shard_map/ppermute | solution.py:814
  80.1 13.3 %collective-permute-start.7 = (bf16[256,1024]{1,0:T(8,128)(2,1)S(1)}, bf16[256,1024]{1,0:T(8,128)(2,1)S(1)}, u32[]{:S(2)}, u32[]{:S(2)}) collective-permute-start(bf16[256,1024]{1,0:T(8,128)(2,1)S(1)} %get-tuple-element.278), channel_id=1, source_target_pairs={{0,2},{1,3},{2,0},{3,1},{4,6},{5,7},{6,4},{7,5},{8,10},{9,11},{10,... | collective-permute-start | bytes 1572872 | tf_op jit(solution)/shard_map/ppermute | solution.py:814
  94.9 14.2 %collective-permute-start.8 = (bf16[256,512]{1,0:T(8,128)(2,1)S(1)}, bf16[256,512]{1,0:T(8,128)(2,1)S(1)}, u32[]{:S(2)}, u32[]{:S(2)}) collective-permute-start(bf16[256,512]{1,0:T(8,128)(2,1)S(1)} %get-tuple-element.323.refs_0_), channel_id=1, source_target_pairs={{0,16},{4,20},{8,24},{12,28},{16,0},{20,4},{24,8},{28,12},{1,17},{... | collective-permute-start | bytes 786440 | tf_op jit(solution)/shard_map/ppermute | solution.py:814
  96.6 12.6 %collective-permute-start.9 = (bf16[128,1024]{1,0:T(8,128)(2,1)S(1)}, bf16[128,1024]{1,0:T(8,128)(2,1)S(1)}, u32[]{:S(2)}, u32[]{:S(2)}) collective-permute-start(bf16[128,1024]{1,0:T(8,128)(2,1)S(1)} %get-tuple-element.325.refs_2_), channel_id=1, source_target_pairs={{0,4},{4,0},{8,12},{12,8},{16,20},{20,16},{24,28},{28,24},{1,5},{5... | collective-permute-start | bytes 786440 | tf_op jit(solution)/shard_map/ppermute | solution.py:814
  97.0 12.2 %collective-permute-start.10 = (bf16[256,1024]{1,0:T(8,128)(2,1)S(1)}, bf16[256,1024]{1,0:T(8,128)(2,1)S(1)}, u32[]{:S(2)}, u32[]{:S(2)}) collective-permute-start(bf16[256,1024]{1,0:T(8,128)(2,1)S(1)} %get-tuple-element.327.refs_4_), channel_id=1, source_target_pairs={{0,2},{1,3},{2,0},{3,1},{4,6},{5,7},{6,4},{7,5},{8,10},{9,11},{10,... | collective-permute-start | bytes 1572872 | tf_op jit(solution)/shard_map/ppermute | solution.py:814
  106.5 6.2 %copy-start.4 = (bf16[1024,96]{1,0:T(8,128)(2,1)S(1)}, bf16[1024,96]{1,0:T(8,128)(2,1)}, u32[]{:S(2)}) copy-start(bf16[1024,96]{1,0:T(8,128)(2,1)} %get-tuple-element.331) | copy-start | bytes 589828
  109.2 3.6 %collective-permute-start.11 = (bf16[1024,96]{1,0:T(8,128)(2,1)}, bf16[1024,96]{1,0:T(8,128)(2,1)S(1)}, u32[]{:S(2)}, u32[]{:S(2)}) collective-permute-start(bf16[1024,96]{1,0:T(8,128)(2,1)} %get-tuple-element.331), channel_id=1, source_target_pairs={{0,1},{1,0},{2,3},{3,2},{4,5},{5,4},{6,7},{7,6},{8,9},{9,8},{10,11... | collective-permute-start | bytes 589832 | tf_op jit(solution)/shard_map/ppermute | solution.py:814
  112.8 14.5 %collective-permute-start.15 = (bf16[512,1024]{1,0:T(8,128)(2,1)S(1)}, bf16[512,1024]{1,0:T(8,128)(2,1)S(1)}, u32[]{:S(2)}, u32[]{:S(2)}) collective-permute-start(bf16[512,1024]{1,0:T(8,128)(2,1)S(1)} %get-tuple-element.430.refs_0_), channel_id=1, source_target_pairs={{0,1},{1,0},{2,3},{3,2},{4,5},{5,4},{6,7},{7,6},{8,9},{9,8},{10,11... | collective-permute-start | bytes 3145736 | tf_op jit(solution)/shard_map/ppermute | solution.py:814
  113.2 13.4 %collective-permute-start.12 = (bf16[256,512]{1,0:T(8,128)(2,1)S(1)}, bf16[256,512]{1,0:T(8,128)(2,1)S(1)}, u32[]{:S(2)}, u32[]{:S(2)}) collective-permute-start(bf16[256,512]{1,0:T(8,128)(2,1)S(1)} %get-tuple-element.340.refs_0_), channel_id=1, source_target_pairs={{0,8},{4,12},{8,0},{12,4},{16,24},{20,28},{24,16},{28,20},{1,9},{5... | collective-permute-start | bytes 786440 | tf_op jit(solution)/shard_map/ppermute | solution.py:814
  113.7 12.9 %collective-permute-start.13 = (bf16[128,1024]{1,0:T(8,128)(2,1)S(1)}, bf16[128,1024]{1,0:T(8,128)(2,1)S(1)}, u32[]{:S(2)}, u32[]{:S(2)}) collective-permute-start(bf16[128,1024]{1,0:T(8,128)(2,1)S(1)} %get-tuple-element.342.refs_2_), channel_id=1, source_target_pairs={{0,16},{4,20},{8,24},{12,28},{16,0},{20,4},{24,8},{28,12},{1,17},{... | collective-permute-start | bytes 786440 | tf_op jit(solution)/shard_map/ppermute | solution.py:814
  115.6 7.1 %collective-permute-start.14 = (bf16[1024,96]{1,0:T(8,128)(2,1)S(1)}, bf16[1024,96]{1,0:T(8,128)(2,1)S(1)}, u32[]{:S(2)}, u32[]{:S(2)}) collective-permute-start(bf16[1024,96]{1,0:T(8,128)(2,1)S(1)} %add_convert_fusion.1), channel_id=1, source_target_pairs={{0,2},{1,3},{2,0},{3,1},{4,6},{5,7},{6,4},{7,5},{8,10},{9,11},{10,... | collective-permute-start | bytes 589832 | tf_op jit(solution)/shard_map/ppermute | solution.py:814
  126.6 0.7 copy-start.1
  128.1 0.9 copy-start.2
  130.5 17.7 %collective-permute-start.16 = (bf16[512,512]{1,0:T(8,128)(2,1)S(1)}, bf16[512,512]{1,0:T(8,128)(2,1)S(1)}, u32[]{:S(2)}, u32[]{:S(2)}) collective-permute-start(bf16[512,512]{1,0:T(8,128)(2,1)S(1)} %get-tuple-element.441.sz_ref), channel_id=1, source_target_pairs={{0,4},{4,0},{8,12},{12,8},{16,20},{20,16},{24,28},{28,24},{1,5},{5... | collective-permute-start | bytes 1572872 | tf_op jit(solution)/shard_map/ppermute | solution.py:814
  133.1 15.1 %collective-permute-start.17 = (bf16[256,1024]{1,0:T(8,128)(2,1)}, bf16[256,1024]{1,0:T(8,128)(2,1)}, u32[]{:S(2)}, u32[]{:S(2)}) collective-permute-start(bf16[256,1024]{1,0:T(8,128)(2,1)} %get-tuple-element.428.one_ref), channel_id=1, source_target_pairs={{0,8},{4,12},{8,0},{12,4},{16,24},{20,28},{24,16},{28,20},{1,9},{5... | collective-permute-start | bytes 1572872 | tf_op jit(solution)/shard_map/ppermute | solution.py:814
  148.2 28.8 %copy-start.3 = (f32[1024]{0:T(1024)S(1)}, f32[1024]{0:T(1024)}, u32[]{:S(2)}) copy-start(f32[1024]{0:T(1024)} %param.15) | copy-start | bytes 12292
  148.2 11.1 %collective-permute-start.20 = (bf16[512,1024]{1,0:T(8,128)(2,1)}, bf16[512,1024]{1,0:T(8,128)(2,1)S(1)}, u32[]{:S(2)}, u32[]{:S(2)}) collective-permute-start(bf16[512,1024]{1,0:T(8,128)(2,1)} %get-tuple-element.373), channel_id=1, source_target_pairs={{0,1},{1,0},{2,3},{3,2},{4,5},{5,4},{6,7},{7,6},{8,9},{9,8},{10,11... | collective-permute-start | bytes 3145736 | tf_op jit(solution)/shard_map/ppermute | solution.py:814
  149.8 9.1 %collective-permute-start.18 = (bf16[304,512]{1,0:T(8,128)(2,1)}, bf16[304,512]{1,0:T(8,128)(2,1)S(1)}, u32[]{:S(2)}, u32[]{:S(2)}) collective-permute-start(bf16[304,512]{1,0:T(8,128)(2,1)} %get-tuple-element.371), channel_id=1, source_target_pairs={{0,4},{4,0},{8,12},{12,8},{16,20},{20,16},{24,28},{28,24},{1,5},{5... | collective-permute-start | bytes 933896 | tf_op jit(solution)/shard_map/ppermute | solution.py:814
  150.4 8.8 %collective-permute-start.19 = (bf16[304,512]{1,0:T(8,128)(2,1)}, bf16[304,512]{1,0:T(8,128)(2,1)S(1)}, u32[]{:S(2)}, u32[]{:S(2)}) collective-permute-start(bf16[304,512]{1,0:T(8,128)(2,1)} %get-tuple-element.372), channel_id=1, source_target_pairs={{0,8},{4,12},{8,0},{12,4},{16,24},{20,28},{24,16},{28,20},{1,9},{5... | collective-permute-start | bytes 933896 | tf_op jit(solution)/shard_map/ppermute | solution.py:814
  151.5 3.0 %collective-permute-start.21 = (f32[1,1024]{1,0:T(1,128)}, f32[1,1024]{1,0:T(1,128)S(1)}, u32[]{:S(2)}, u32[]{:S(2)}) collective-permute-start(f32[1,1024]{1,0:T(1,128)} %get-tuple-element.374), channel_id=1, source_target_pairs={{0,2},{1,3},{2,0},{3,1},{4,6},{5,7},{6,4},{7,5},{8,10},{9,11},{10,... | collective-permute-start | bytes 12296 | tf_op jit(solution)/shard_map/ppermute | solution.py:814
  161.9 15.1 %collective-permute-start.27 = (bf16[256,1024]{1,0:T(8,128)(2,1)S(1)}, bf16[256,1024]{1,0:T(8,128)(2,1)S(1)}, u32[]{:S(2)}, u32[]{:S(2)}) collective-permute-start(bf16[256,1024]{1,0:T(8,128)(2,1)S(1)} %get-tuple-element.396), channel_id=1, source_target_pairs={{0,2},{1,3},{2,0},{3,1},{4,6},{5,7},{6,4},{7,5},{8,10},{9,11},{10,... | collective-permute-start | bytes 1572872 | tf_op jit(solution)/shard_map/ppermute | solution.py:814
  162.2 5.2 %collective-permute-start.22 = (bf16[152,512]{1,0:T(8,128)(2,1)S(1)}, bf16[152,512]{1,0:T(8,128)(2,1)S(1)}, u32[]{:S(2)}, u32[]{:S(2)}) collective-permute-start(bf16[152,512]{1,0:T(8,128)(2,1)S(1)} %get-tuple-element.385), channel_id=1, source_target_pairs={{0,8},{4,12},{8,0},{12,4},{16,24},{20,28},{24,16},{28,20},{1,9},{5... | collective-permute-start | bytes 466952 | tf_op jit(solution)/shard_map/ppermute | solution.py:814
  163.6 6.0 %collective-permute-start.23 = (bf16[152,512]{1,0:T(8,128)(2,1)S(1)}, bf16[152,512]{1,0:T(8,128)(2,1)S(1)}, u32[]{:S(2)}, u32[]{:S(2)}) collective-permute-start(bf16[152,512]{1,0:T(8,128)(2,1)S(1)} %get-tuple-element.386), channel_id=1, source_target_pairs={{0,16},{4,20},{8,24},{12,28},{16,0},{20,4},{24,8},{28,12},{1,17},{... | collective-permute-start | bytes 466952 | tf_op jit(solution)/shard_map/ppermute | solution.py:814
  164.8 2.5 %collective-permute-start.24 = (f32[1,1024]{1,0:T(1,128)S(1)}, f32[1,1024]{1,0:T(1,128)S(1)}, u32[]{:S(2)}, u32[]{:S(2)}) collective-permute-start(f32[1,1024]{1,0:T(1,128)S(1)} %add.42), channel_id=1, source_target_pairs={{0,1},{1,0},{2,3},{3,2},{4,5},{5,4},{6,7},{7,6},{8,9},{9,8},{10,11... | collective-permute-start | bytes 12296 | tf_op jit(solution)/shard_map/ppermute | solution.py:814
  170.6 6.3 %collective-permute-start.25 = (bf16[152,512]{1,0:T(8,128)(2,1)S(1)}, bf16[152,512]{1,0:T(8,128)(2,1)S(1)}, u32[]{:S(2)}, u32[]{:S(2)}) collective-permute-start(bf16[152,512]{1,0:T(8,128)(2,1)S(1)} %get-tuple-element.398.refs_0_), channel_id=1, source_target_pairs={{0,16},{4,20},{8,24},{12,28},{16,0},{20,4},{24,8},{28,12},{1,17},{... | collective-permute-start | bytes 466952 | tf_op jit(solution)/shard_map/ppermute | solution.py:814
  172.8 4.1 %collective-permute-start.26 = (bf16[152,512]{1,0:T(8,128)(2,1)S(1)}, bf16[152,512]{1,0:T(8,128)(2,1)S(1)}, u32[]{:S(2)}, u32[]{:S(2)}) collective-permute-start(bf16[152,512]{1,0:T(8,128)(2,1)S(1)} %get-tuple-element.400.refs_2_), channel_id=1, source_target_pairs={{0,4},{4,0},{8,12},{12,8},{16,20},{20,16},{24,28},{28,24},{1,5},{5... | collective-permute-start | bytes 466952 | tf_op jit(solution)/shard_map/ppermute | solution.py:814
  173.8 3.1 %collective-permute-start.28 = (f32[1,1024]{1,0:T(1,128)S(1)}, f32[1,1024]{1,0:T(1,128)S(1)}, u32[]{:S(2)}, u32[]{:S(2)}) collective-permute-start(f32[1,1024]{1,0:T(1,128)S(1)} %add.43), channel_id=1, source_target_pairs={{0,4},{4,0},{8,12},{12,8},{16,20},{20,16},{24,28},{28,24},{1,5},{5... | collective-permute-start | bytes 12296 | tf_op jit(solution)/shard_map/ppermute | solution.py:814
  178.6 19.9 %collective-permute-start.34 = (bf16[256,1024]{1,0:T(8,128)(2,1)S(1)}, bf16[256,1024]{1,0:T(8,128)(2,1)S(1)}, u32[]{:S(2)}, u32[]{:S(2)}) collective-permute-start(bf16[256,1024]{1,0:T(8,128)(2,1)S(1)} %get-tuple-element.426.refs_0_), channel_id=1, source_target_pairs={{0,2},{1,3},{2,0},{3,1},{4,6},{5,7},{6,4},{7,5},{8,10},{9,11},{10,... | collective-permute-start | bytes 1572872 | tf_op jit(solution)/shard_map/ppermute | solution.py:814
  180.6 8.3 %collective-permute-start.29 = (bf16[152,512]{1,0:T(8,128)(2,1)S(1)}, bf16[152,512]{1,0:T(8,128)(2,1)S(1)}, u32[]{:S(2)}, u32[]{:S(2)}) collective-permute-start(bf16[152,512]{1,0:T(8,128)(2,1)S(1)} %get-tuple-element.413.refs_0_), channel_id=1, source_target_pairs={{0,8},{4,12},{8,0},{12,4},{16,24},{20,28},{24,16},{28,20},{1,9},{5... | collective-permute-start | bytes 466952 | tf_op jit(solution)/shard_map/ppermute | solution.py:814
  182.7 7.1 %collective-permute-start.30 = (bf16[152,512]{1,0:T(8,128)(2,1)S(1)}, bf16[152,512]{1,0:T(8,128)(2,1)S(1)}, u32[]{:S(2)}, u32[]{:S(2)}) collective-permute-start(bf16[152,512]{1,0:T(8,128)(2,1)S(1)} %get-tuple-element.415.refs_2_), channel_id=1, source_target_pairs={{0,16},{4,20},{8,24},{12,28},{16,0},{20,4},{24,8},{28,12},{1,17},{... | collective-permute-start | bytes 466952 | tf_op jit(solution)/shard_map/ppermute | solution.py:814
  185.9 2.9 %collective-permute-start.31 = (f32[1,1024]{1,0:T(1,128)S(1)}, f32[1,1024]{1,0:T(1,128)S(1)}, u32[]{:S(2)}, u32[]{:S(2)}) collective-permute-start(f32[1,1024]{1,0:T(1,128)S(1)} %add.44), channel_id=1, source_target_pairs={{0,8},{4,12},{8,0},{12,4},{16,24},{20,28},{24,16},{28,20},{1,9},{5... | collective-permute-start | bytes 12296 | tf_op jit(solution)/shard_map/ppermute | solution.py:814
  190.4 8.2 %collective-permute-start.32 = (bf16[304,512]{1,0:T(8,128)(2,1)S(1)}, bf16[304,512]{1,0:T(8,128)(2,1)S(1)}, u32[]{:S(2)}, u32[]{:S(2)}) collective-permute-start(bf16[304,512]{1,0:T(8,128)(2,1)S(1)} %get-tuple-element.437.sa_ref), channel_id=1, source_target_pairs={{0,4},{4,0},{8,12},{12,8},{16,20},{20,16},{24,28},{28,24},{1,5},{5... | collective-permute-start | bytes 933896 | tf_op jit(solution)/shard_map/ppermute | solution.py:814
  190.8 7.7 %collective-permute-start.33 = (bf16[304,512]{1,0:T(8,128)(2,1)S(1)}, bf16[304,512]{1,0:T(8,128)(2,1)S(1)}, u32[]{:S(2)}, u32[]{:S(2)}) collective-permute-start(bf16[304,512]{1,0:T(8,128)(2,1)S(1)} %get-tuple-element.439.sb_ref), channel_id=1, source_target_pairs={{0,8},{4,12},{8,0},{12,4},{16,24},{20,28},{24,16},{28,20},{1,9},{5... | collective-permute-start | bytes 933896 | tf_op jit(solution)/shard_map/ppermute | solution.py:814
  191.8 6.2 %collective-permute-start.35 = (f32[1,1024]{1,0:T(1,128)S(1)}, f32[1,1024]{1,0:T(1,128)S(1)}, u32[]{:S(2)}, u32[]{:S(2)}) collective-permute-start(f32[1,1024]{1,0:T(1,128)S(1)} %add.45), channel_id=1, source_target_pairs={{0,16},{4,20},{8,24},{12,28},{16,0},{20,4},{24,8},{28,12},{1,17},{... | collective-permute-start | bytes 12296 | tf_op jit(solution)/shard_map/ppermute | solution.py:814
  198.5 8.7 %copy-start = (bf16[1,1024,1024]{2,1,0:T(8,128)(2,1)S(1)}, bf16[1,1024,1024]{2,1,0:T(8,128)(2,1)}, u32[]{:S(2)}) copy-start(bf16[1,1024,1024]{2,1,0:T(8,128)(2,1)} %param.25) | copy-start | bytes 6291460
  198.6 8.6 %collective-permute-start.36 = (bf16[512,1024]{1,0:T(8,128)(2,1)S(1)}, bf16[512,1024]{1,0:T(8,128)(2,1)S(1)}, u32[]{:S(2)}, u32[]{:S(2)}) collective-permute-start(bf16[512,1024]{1,0:T(8,128)(2,1)S(1)} %merge.19.one_ref), channel_id=1, source_target_pairs={{0,1},{1,0},{2,3},{3,2},{4,5},{5,4},{6,7},{7,6},{8,9},{9,8},{10,11... | collective-permute-start | bytes 3145736 | tf_op jit(solution)/shard_map/ppermute | solution.py:814

commit v5 on v4

--- a/solution.py
+++ b/solution.py
@@ -827,6 +827,7 @@
         turn = [("swap", order.pop())] if swap else []
         self.steps = [("halve", bit) for bit in order] + turn + [("double", bit) for bit in reversed(order)]
         self.got = None
+        self.far = False
 
     def mine(self, bit):
         return (lax.axis_index(self.name) >> bit) & 1
@@ -839,7 +840,8 @@
         kind, bit = self.steps.pop(0)
         after = self.steps[0]
         if kind == "double":
-            return ("join", self.mine(bit), self.send, self.got)
+            got = pltpu.with_memory_space_constraint(self.got, pltpu.HBM) if self.far else self.got
+            return ("join", self.mine(bit), self.send, got)
         one = pltpu.with_memory_space_constraint(self.keep, pltpu.HBM) if kind == "halve" else self.send
         if kind == "halve" and after[0] == "halve":
             return ("split", self.mine(after[1]), one, self.got)
@@ -924,6 +926,7 @@
     gz = Chain("dp", dp, order, kz, sz)
     go = Chain("dp", dp, turned, ko, so)
     mix = Chain("tensor", tp, t_order, km, sm, swap=False)
+    gz.far = go.far = True
     chains = [gz, go, mix]
     nc = length // LC
     carry = ()

time: 211 us -> 211 us (level)
    unnamed x11 -> x9, local copies, waits for them, and re-layouts: 5.16 us -> 3.5 us
  transfers between devices with their start and end apart: 37 -> 37, of which waited for: 14 -> 16; matrix products, arithmetic and copies ran while one was open for 2% -> 2% of each run, Pallas kernels for 30% -> 30%
where the time goes in v5:
time: 211 us; the launch traced here: 210 us
  Pallas kernels  122 us (58%)
  starting transfers between devices  46.6 us (22%)
  waiting for transfers between devices  29.8 us (14%)
  local copies, waits for them, and re-layouts  6.14 us (3%)
  other arithmetic  4.12 us (2%)
    ppermute x37, starting transfers between devices, exchange(): return lax.ppermute(value, name, [(j, j ^ 1 << bit) for j in range(size)])  46.6 us
    pallas_call x1, Pallas kernels, front(): pl.pallas_call(functools.partial(front_kernel, ng, nc), grid_spec=pltpu.P...  38.9 us
    pallas_call x3, Pallas kernels, back(): pl.pallas_call(functools.partial(back_kernel, ng, top, low, len(extra)),...  31.6 us
    ppermute x37, waiting for transfers between devices, exchange(): return lax.ppermute(value, name, [(j, j ^ 1 << bit) for j in range(size)])  29.8 us
    pallas_call x1, Pallas kernels, inner(): pl.pallas_call(functools.partial(inner_kernel, rows_a, rows_b), grid_spec...  15 us
    pallas_call x10, Pallas kernels, merge(): pl.pallas_call(functools.partial(merge_kernel, kinds), grid=(1,), in_spec...  14.3 us
    pallas_call x1, Pallas kernels, head(): pl.pallas_call(head_kernel, grid=(l // hc,), in_specs=[by(d), whole(1, d)...  7.03 us
    pallas_call x1, Pallas kernels, gates(): pl.pallas_call(gates_kernel, grid=(l // 256,), in_specs=[by(d), pl.BlockS...  6.3 us
  transfers between devices with their start and end apart: 37, of which 16 were waited for; matrix products, arithmetic and copies ran while one was open for 2% of the time, Pallas kernels for 30%

profile of v5, /device:TPU:1, one launch (start us, length us, event | category | flops | bytes accessed | tf_op | source)
XLA Modules:
  0.0 210.1 jit_solution(10083811803447459355)
XLA Ops:
  0.6 3.5 %copy.31 = bf16[128,8,2,512]{3,1,2,0:T(8,128)(2,1)} copy(bf16[128,8,2,512]{3,2,1,0:T(2,128)(2,1)} %bitcast.35) | data formatting | bytes 4194304
  4.1 7.0 %head.1 = (bf16[1024,1024]{1,0:T(8,128)(2,1)}, bf16[1024,512]{1,0:T(8,128)(2,1)}, f32[1024,512]{1,0:T(8,128)}, bf16[1024,512]{1,0:T(8,128)(2,1)}, bf16[1024,96]{1,0:T(8,128)(2,1)}, /*index=5*/f32[1024,1]{1,0:T(8,128)}) custom-call(bf16[1024,1024]{1,0:T(8,128)(2,1)} %bitcast.27, f32[1,1024]{1,0:T(1,128)} %bitcast.25, bf16[1024,1024]{1,0:T(8,128)(2,1)} %bitcast.31, ...), custom_call_target="tpu_custom_call" | custom-call | flops 1073741824 | bytes 8388608 | tf_op jit(solution)/shard_map/head/pallas_call | solution.py:477
  12.9 1.0 add_convert_fusion.3
  14.0 2.4 %collective-permute-start.1 = (bf16[1024,96]{1,0:T(8,128)(2,1)S(1)}, bf16[1024,96]{1,0:T(8,128)(2,1)S(1)}, u32[]{:S(2)}, u32[]{:S(2)}) collective-permute-start(bf16[1024,96]{1,0:T(8,128)(2,1)S(1)} %add_convert_fusion.3), channel_id=1, source_target_pairs={{0,2},{1,3},{2,0},{3,1},{4,6},{5,7},{6,4},{7,5},{8,10},{9,11},{10,... | collective-permute-start | bytes 589832 | tf_op jit(solution)/shard_map/ppermute | solution.py:814
  16.4 6.3 %gates.1 = (f32[1024,512]{1,0:T(8,128)}, f32[1024,512]{1,0:T(8,128)}) custom-call(bf16[1024,1024]{1,0:T(8,128)(2,1)} %get-tuple-element.235.n_ref.normed_hbm.normed_ref, bf16[1024,1024]{1,0:T(8,128)(2,1)} %bitcast.32, bf16[1024,1024]{1,0:T(8,128)(2,1)} %bitcast.22, bf16[512,1024]{1,0:T(8,128)(2,1)} %w_hbm.1), custom_call_target="tpu_custom_call" | custom-call | flops 2147483648 | bytes 10485760 | tf_op jit(solution)/shard_map/gates/pallas_call | solution.py:500
  22.8 0.8 add_convert_fusion.2.proj_ref
  23.5 38.9 %front.1 = (bf16[1024,512]{1,0:T(8,128)(2,1)}, bf16[1024,512]{1,0:T(8,128)(2,1)}, f32[1024,512]{1,0:T(8,128)}, f32[1024,512]{1,0:T(8,128)}, bf16[16384,512]{1,0:...) custom-call(s32[5]{0:T(128)} %stack.58.order_ref.bits_ref, ...), custom_call_target="tpu_custom_call" | custom-call | tf_op jit(solution)/shard_map/front/pallas_call | solution.py:758
  62.4 0.7 collective-permute-start.2
  63.1 1.4 collective-permute-start.4
  64.5 10.1 %back.3 = (bf16[1024,96]{1,0:T(8,128)(2,1)}, bf16[1024,512]{1,0:T(8,128)(2,1)}, f32[1024,512]{1,0:T(8,128)}, f32[16,512]{1,0:T(8,128)}, f32[16,512]{1,0:T(8,128)}, /*index=5*/f32[1,512]{1,0:T(1,128)}) custom-call(s32[1]{0:T(128)S(6)} %copy.38.prefix_ref, bf16[1024,96]{1,0:T(8,128)(2,1)} %add_convert_fusion.2.proj_ref, bf16[64,512]{1,0:T(8,128)(2,1)} %sw_ref.7, ...), custom_call_target="tpu_custom_call" | custom-call | flops 12582912000 | bytes 12582912 | tf_op jit(solution)/shard_map/back/pallas_call | solution.py:795
  74.6 0.7 collective-permute-done.2.refs_1_
  75.3 2.8 %merge.10 = (bf16[256,512]{1,0:T(8,128)(2,1)}, bf16[256,512]{1,0:T(8,128)(2,1)S(1)}, bf16[128,1024]{1,0:T(8,128)(2,1)}, bf16[128,1024]{1,0:T(8,128)(2,1)S(1)}, b...) custom-call(s32[3]{0:T(128)S(1)} %get-tuple-element.452.bits_ref, bf16[512,512]{1,0:T(8,128)(2,1)} %get-tuple-element.243.refs_0_, ...), custom_call_target="tpu_custom_call" | custom-call | tf_op jit(solution)/shard_map/merge/pallas_call | solution.py:663
  78.2 1.0 collective-permute-start.5
  79.2 2.6 %collective-permute-start.6 = (bf16[128,1024]{1,0:T(8,128)(2,1)S(1)}, bf16[128,1024]{1,0:T(8,128)(2,1)S(1)}, u32[]{:S(2)}, u32[]{:S(2)}) collective-permute-start(bf16[128,1024]{1,0:T(8,128)(2,1)S(1)} %get-tuple-element.277), channel_id=1, source_target_pairs={{0,16},{4,20},{8,24},{12,28},{16,0},{20,4},{24,8},{28,12},{1,17},{... | collective-permute-start | bytes 786440 | tf_op jit(solution)/shard_map/ppermute | solution.py:814
  81.8 1.2 collective-permute-start.7
  83.0 12.1 %back.4 = (bf16[1024,96]{1,0:T(8,128)(2,1)}, bf16[1024,512]{1,0:T(8,128)(2,1)}, f32[1024,512]{1,0:T(8,128)}, f32[16,512]{1,0:T(8,128)}, f32[16,512]{1,0:T(8,128)}, /*index=5*/f32[1,512]{1,0:T(1,128)}) custom-call(s32[1]{0:T(128)S(6)} %copy.38.prefix_ref, ...), custom_call_target="tpu_custom_call", output_to_operand_aliasing={{0}: (15, {}), {1}: (16, {}), {2}: (17, {})} | custom-call | flops 12582912000 | bytes 12582912 | tf_op jit(solution)/shard_map/back/pallas_call | solution.py:795
  95.1 1.5 merge.11
  96.7 1.2 collective-permute-start.9
  98.1 9.5 %back.5 = (bf16[1024,96]{1,0:T(8,128)(2,1)}, bf16[1024,512]{1,0:T(8,128)(2,1)}, f32[1024,512]{1,0:T(8,128)}, f32[16,512]{1,0:T(8,128)}, f32[16,512]{1,0:T(8,128)}, /*index=5*/f32[1,512]{1,0:T(1,128)}) custom-call(s32[1]{0:T(128)S(6)} %copy.38.prefix_ref, ...), custom_call_target="tpu_custom_call", output_to_operand_aliasing={{0}: (15, {}), {1}: (16, {}), {2}: (17, {})} | custom-call | flops 8388608000 | bytes 8388608 | tf_op jit(solution)/shard_map/back/pallas_call | solution.py:795
  107.6 3.5 %collective-permute-done.8.refs_1_ = bf16[256,512]{1,0:T(8,128)(2,1)S(1)} collective-permute-done((bf16[256,512]{1,0:T(8,128)(2,1)S(1)}, bf16[256,512]{1,0:T(8,128)(2,1)S(1)}, u32[]{:S(2)}, u32[]{:S(2)}) %collective-permute-start.8) | collective-permute-done | bytes 262176 | tf_op jit(solution)/shard_map/ppermute | solution.py:814
  111.1 1.1 collective-permute-start.11
  112.3 0.7 merge.12
  114.1 1.3 collective-permute-start.12
  115.4 1.9 collective-permute-start.13
  117.6 0.9 constant_dynamic-slice_fusion.refs_7_
  118.5 1.1 constant_dynamic-slice_fusion.1.refs_6_
  119.6 5.0 %collective-permute-done.14 = bf16[1024,96]{1,0:T(8,128)(2,1)S(1)} collective-permute-done((bf16[1024,96]{1,0:T(8,128)(2,1)S(1)}, bf16[1024,96]{1,0:T(8,128)(2,1)S(1)}, u32[]{:S(2)}, u32[]{:S(2)}) %collective-permute-start.14) | collective-permute-done | bytes 196640 | tf_op jit(solution)/shard_map/ppermute | solution.py:814
  124.6 2.9 %collective-permute-done.12.refs_1_ = bf16[256,512]{1,0:T(8,128)(2,1)S(1)} collective-permute-done((bf16[256,512]{1,0:T(8,128)(2,1)S(1)}, bf16[256,512]{1,0:T(8,128)(2,1)S(1)}, u32[]{:S(2)}, u32[]{:S(2)}) %collective-permute-start.12) | collective-permute-done | bytes 262176 | tf_op jit(solution)/shard_map/ppermute | solution.py:814
  127.4 0.8 add_convert_fusion.dproj_ref
  128.2 1.9 merge.13
  130.1 0.9 collective-permute-start.16
  131.0 1.9 collective-permute-start.17
  132.9 15.0 %inner.1 = (bf16[304,512]{1,0:T(8,128)(2,1)}, bf16[304,512]{1,0:T(8,128)(2,1)}, bf16[304,512]{1,0:T(8,128)(2,1)}, bf16[304,512]{1,0:T(8,128)(2,1)}, bf16[512,102...) custom-call(s32[5]{0:T(128)} %stack.58.order_ref.bits_ref, ...), custom_call_target="tpu_custom_call" | custom-call | flops 3221225472 | bytes 10485760 | tf_op jit(solution)/shard_map/inner/pallas_call | solution.py:602
  148.0 1.6 collective-permute-start.20
  149.5 1.2 collective-permute-start.18
  150.8 1.3 collective-permute-start.19
  152.1 1.1 collective-permute-start.21
  153.2 1.9 collective-permute-done.21
  155.0 0.7 add.42
  155.7 3.0 %collective-permute-done.18.refs_1_ = bf16[304,512]{1,0:T(8,128)(2,1)S(1)} collective-permute-done((bf16[304,512]{1,0:T(8,128)(2,1)}, bf16[304,512]{1,0:T(8,128)(2,1)S(1)}, u32[]{:S(2)}, u32[]{:S(2)}) %collective-permute-start.18) | collective-permute-done | bytes 311328 | tf_op jit(solution)/shard_map/ppermute | solution.py:814
  158.7 0.9 collective-permute-done.19.refs_3_
  159.6 2.6 %merge.14 = (bf16[152,512]{1,0:T(8,128)(2,1)}, bf16[152,512]{1,0:T(8,128)(2,1)S(1)}, bf16[152,512]{1,0:T(8,128)(2,1)}, bf16[152,512]{1,0:T(8,128)(2,1)S(1)}, bf1...) custom-call(s32[3]{0:T(128)S(1)} %get-tuple-element.452.bits_ref, bf16[304,512]{1,0:T(8,128)(2,1)} %get-tuple-element.366.refs_0_, ...), custom_call_target="tpu_custom_call" | custom-call | tf_op jit(solution)/shard_map/merge/pallas_call | solution.py:663
  162.2 1.1 collective-permute-start.27
  163.3 1.3 collective-permute-start.22
  164.6 1.0 collective-permute-start.23
  165.6 1.7 collective-permute-start.24
  167.3 0.8 collective-permute-done.24
  168.2 2.8 %collective-permute-done.23.refs_3_ = bf16[152,512]{1,0:T(8,128)(2,1)S(1)} collective-permute-done((bf16[152,512]{1,0:T(8,128)(2,1)S(1)}, bf16[152,512]{1,0:T(8,128)(2,1)S(1)}, u32[]{:S(2)}, u32[]{:S(2)}) %collective-permute-start.23) | collective-permute-done | bytes 155680 | tf_op jit(solution)/shard_map/ppermute | solution.py:814
  171.0 1.1 merge.15
  172.1 1.7 collective-permute-start.25
  173.8 0.9 collective-permute-start.26
  175.2 2.7 %collective-permute-done.28 = f32[1,1024]{1,0:T(1,128)S(1)} collective-permute-done((f32[1,1024]{1,0:T(1,128)S(1)}, f32[1,1024]{1,0:T(1,128)S(1)}, u32[]{:S(2)}, u32[]{:S(2)}) %collective-permute-start.28) | collective-permute-done | bytes 4128 | tf_op jit(solution)/shard_map/ppermute | solution.py:814
  177.9 0.9 collective-permute-done.25.refs_1_
  178.8 1.6 merge.16
  180.5 3.5 %collective-permute-start.29 = (bf16[152,512]{1,0:T(8,128)(2,1)S(1)}, bf16[152,512]{1,0:T(8,128)(2,1)S(1)}, u32[]{:S(2)}, u32[]{:S(2)}) collective-permute-start(bf16[152,512]{1,0:T(8,128)(2,1)S(1)} %get-tuple-element.413.refs_0_), channel_id=1, source_target_pairs={{0,8},{4,12},{8,0},{12,4},{16,24},{20,28},{24,16},{28,20},{1,9},{5... | collective-permute-start | bytes 466952 | tf_op jit(solution)/shard_map/ppermute | solution.py:814
  184.0 3.1 %collective-permute-start.30 = (bf16[152,512]{1,0:T(8,128)(2,1)S(1)}, bf16[152,512]{1,0:T(8,128)(2,1)S(1)}, u32[]{:S(2)}, u32[]{:S(2)}) collective-permute-start(bf16[152,512]{1,0:T(8,128)(2,1)S(1)} %get-tuple-element.415.refs_2_), channel_id=1, source_target_pairs={{0,16},{4,20},{8,24},{12,28},{16,0},{20,4},{24,8},{28,12},{1,17},{... | collective-permute-start | bytes 466952 | tf_op jit(solution)/shard_map/ppermute | solution.py:814
  187.1 3.7 %collective-permute-done.31 = f32[1,1024]{1,0:T(1,128)S(1)} collective-permute-done((f32[1,1024]{1,0:T(1,128)S(1)}, f32[1,1024]{1,0:T(1,128)S(1)}, u32[]{:S(2)}, u32[]{:S(2)}) %collective-permute-start.31) | collective-permute-done | bytes 4128 | tf_op jit(solution)/shard_map/ppermute | solution.py:814
  191.4 2.3 %collective-permute-start.33 = (bf16[304,512]{1,0:T(8,128)(2,1)S(1)}, bf16[304,512]{1,0:T(8,128)(2,1)S(1)}, u32[]{:S(2)}, u32[]{:S(2)}) collective-permute-start(bf16[304,512]{1,0:T(8,128)(2,1)S(1)} %get-tuple-element.439.sb_ref), channel_id=1, source_target_pairs={{0,8},{4,12},{8,0},{12,4},{16,24},{20,28},{24,16},{28,20},{1,9},{5... | collective-permute-start | bytes 933896 | tf_op jit(solution)/shard_map/ppermute | solution.py:814
  193.7 1.5 collective-permute-start.35
  195.2 2.7 %joined.2 = f32[512,1024]{1,0:T(8,128)} custom-call(s32[1]{0:T(128)} %bitcast.bits_ref, bf16[256,1024]{1,0:T(8,128)(2,1)} %get-tuple-element.428.one_ref, bf16[256,1024]{1,0:T(8,128)(2,1)} %collective-permute-done.17.two_ref), custom_call_target="tpu_custom_call" | custom-call | tf_op jit(solution)/shard_map/joined/pallas_call | solution.py:687
  197.8 1.5 merge.18
  200.0 4.1 %collective-permute-start.36 = (bf16[512,1024]{1,0:T(8,128)(2,1)S(1)}, bf16[512,1024]{1,0:T(8,128)(2,1)S(1)}, u32[]{:S(2)}, u32[]{:S(2)}) collective-permute-start(bf16[512,1024]{1,0:T(8,128)(2,1)S(1)} %merge.19.one_ref), channel_id=1, source_target_pairs={{0,1},{1,0},{2,3},{3,2},{4,5},{5,4},{6,7},{7,6},{8,9},{9,8},{10,11... | collective-permute-start | bytes 3145736 | tf_op jit(solution)/shard_map/ppermute | solution.py:814
  204.1 3.6 %last.1 = (f32[1024,2,512]{2,1,0:T(2,128)}, f32[4,512]{1,0:T(4,128)}, f32[1,512]{1,0:T(1,128)}, f32[1,512]{1,0:T(1,128)}, f32[1,512]{1,0:T(1,128)}, /*index=5*/f...) custom-call(s32[3]{0:T(128)S(1)} %get-tuple-element.453.bits_ref, bf16[304,512]{1,0:T(8,128)(2,1)S(1)} %get-tuple-element.437.sa_ref, ...), custom_call_target="tpu_custom_call" | custom-call | tf_op jit(solution)/shard_map/last/pallas_call | solution.py:730
  207.7 2.4 %joined.3 = f32[1024,1024]{1,0:T(8,128)} custom-call(s32[1]{0:T(128)} %bitcast.4.bits_ref, bf16[512,1024]{1,0:T(8,128)(2,1)S(1)} %merge.19.one_ref, bf16[512,1024]{1,0:T(8,128)(2,1)S(1)} %collective-permute-done.36.two_ref, bf16[1024,1024]{1,0:T(8,128)(2,1)S(1)} %bitcast.24), custom_call_target="tpu_custom_call" | custom-call | tf_op jit(solution)/shard_map/joined/pallas_call | solution.py:687
  (56 shorter events, 5.1 us)
Async XLA Ops:
  11.1 1.8 collective-permute-start
  14.0 8.8 %collective-permute-start.1 = (bf16[1024,96]{1,0:T(8,128)(2,1)S(1)}, bf16[1024,96]{1,0:T(8,128)(2,1)S(1)}, u32[]{:S(2)}, u32[]{:S(2)}) collective-permute-start(bf16[1024,96]{1,0:T(8,128)(2,1)S(1)} %add_convert_fusion.3), channel_id=1, source_target_pairs={{0,2},{1,3},{2,0},{3,1},{4,6},{5,7},{6,4},{7,5},{8,10},{9,11},{10,... | collective-permute-start | bytes 589832 | tf_op jit(solution)/shard_map/ppermute | solution.py:814
  62.4 12.8 %collective-permute-start.2 = (bf16[512,512]{1,0:T(8,128)(2,1)}, bf16[512,512]{1,0:T(8,128)(2,1)S(1)}, u32[]{:S(2)}, u32[]{:S(2)}) collective-permute-start(bf16[512,512]{1,0:T(8,128)(2,1)} %get-tuple-element.248), channel_id=1, source_target_pairs={{0,4},{4,0},{8,12},{12,8},{16,20},{20,16},{24,28},{28,24},{1,5},{5... | collective-permute-start | bytes 1572872 | tf_op jit(solution)/shard_map/ppermute | solution.py:814
  63.1 12.2 %collective-permute-start.3 = (bf16[256,1024]{1,0:T(8,128)(2,1)}, bf16[256,1024]{1,0:T(8,128)(2,1)S(1)}, u32[]{:S(2)}, u32[]{:S(2)}) collective-permute-start(bf16[256,1024]{1,0:T(8,128)(2,1)} %get-tuple-element.249), channel_id=1, source_target_pairs={{0,8},{4,12},{8,0},{12,4},{16,24},{20,28},{24,16},{28,20},{1,9},{5... | collective-permute-start | bytes 1572872 | tf_op jit(solution)/shard_map/ppermute | solution.py:814
  63.1 12.2 %collective-permute-start.4 = (bf16[512,1024]{1,0:T(8,128)(2,1)}, bf16[512,1024]{1,0:T(8,128)(2,1)S(1)}, u32[]{:S(2)}, u32[]{:S(2)}) collective-permute-start(bf16[512,1024]{1,0:T(8,128)(2,1)} %get-tuple-element.250), channel_id=1, source_target_pairs={{0,1},{1,0},{2,3},{3,2},{4,5},{5,4},{6,7},{7,6},{8,9},{9,8},{10,11... | collective-permute-start | bytes 3145736 | tf_op jit(solution)/shard_map/ppermute | solution.py:814
  78.2 16.9 %collective-permute-start.5 = (bf16[256,512]{1,0:T(8,128)(2,1)S(1)}, bf16[256,512]{1,0:T(8,128)(2,1)S(1)}, u32[]{:S(2)}, u32[]{:S(2)}) collective-permute-start(bf16[256,512]{1,0:T(8,128)(2,1)S(1)} %get-tuple-element.276), channel_id=1, source_target_pairs={{0,8},{4,12},{8,0},{12,4},{16,24},{20,28},{24,16},{28,20},{1,9},{5... | collective-permute-start | bytes 786440 | tf_op jit(solution)/shard_map/ppermute | solution.py:814
  79.2 15.9 %collective-permute-start.6 = (bf16[128,1024]{1,0:T(8,128)(2,1)S(1)}, bf16[128,1024]{1,0:T(8,128)(2,1)S(1)}, u32[]{:S(2)}, u32[]{:S(2)}) collective-permute-start(bf16[128,1024]{1,0:T(8,128)(2,1)S(1)} %get-tuple-element.277), channel_id=1, source_target_pairs={{0,16},{4,20},{8,24},{12,28},{16,0},{20,4},{24,8},{28,12},{1,17},{... | collective-permute-start | bytes 786440 | tf_op jit(solution)/shard_map/ppermute | solution.py:814
  81.8 13.3 %collective-permute-start.7 = (bf16[256,1024]{1,0:T(8,128)(2,1)S(1)}, bf16[256,1024]{1,0:T(8,128)(2,1)S(1)}, u32[]{:S(2)}, u32[]{:S(2)}) collective-permute-start(bf16[256,1024]{1,0:T(8,128)(2,1)S(1)} %get-tuple-element.278), channel_id=1, source_target_pairs={{0,2},{1,3},{2,0},{3,1},{4,6},{5,7},{6,4},{7,5},{8,10},{9,11},{10,... | collective-permute-start | bytes 1572872 | tf_op jit(solution)/shard_map/ppermute | solution.py:814
  96.6 14.5 %collective-permute-start.8 = (bf16[256,512]{1,0:T(8,128)(2,1)S(1)}, bf16[256,512]{1,0:T(8,128)(2,1)S(1)}, u32[]{:S(2)}, u32[]{:S(2)}) collective-permute-start(bf16[256,512]{1,0:T(8,128)(2,1)S(1)} %get-tuple-element.323.refs_0_), channel_id=1, source_target_pairs={{0,16},{4,20},{8,24},{12,28},{16,0},{20,4},{24,8},{28,12},{1,17},{... | collective-permute-start | bytes 786440 | tf_op jit(solution)/shard_map/ppermute | solution.py:814
  96.7 14.4 %collective-permute-start.9 = (bf16[128,1024]{1,0:T(8,128)(2,1)S(1)}, bf16[128,1024]{1,0:T(8,128)(2,1)S(1)}, u32[]{:S(2)}, u32[]{:S(2)}) collective-permute-start(bf16[128,1024]{1,0:T(8,128)(2,1)S(1)} %get-tuple-element.325.refs_2_), channel_id=1, source_target_pairs={{0,4},{4,0},{8,12},{12,8},{16,20},{20,16},{24,28},{28,24},{1,5},{5... | collective-permute-start | bytes 786440 | tf_op jit(solution)/shard_map/ppermute | solution.py:814
  97.8 13.2 %collective-permute-start.10 = (bf16[256,1024]{1,0:T(8,128)(2,1)S(1)}, bf16[256,1024]{1,0:T(8,128)(2,1)S(1)}, u32[]{:S(2)}, u32[]{:S(2)}) collective-permute-start(bf16[256,1024]{1,0:T(8,128)(2,1)S(1)} %get-tuple-element.327.refs_4_), channel_id=1, source_target_pairs={{0,2},{1,3},{2,0},{3,1},{4,6},{5,7},{6,4},{7,5},{8,10},{9,11},{10,... | collective-permute-start | bytes 1572872 | tf_op jit(solution)/shard_map/ppermute | solution.py:814
  107.6 6.0 %copy-start.2 = (bf16[1024,96]{1,0:T(8,128)(2,1)S(1)}, bf16[1024,96]{1,0:T(8,128)(2,1)}, u32[]{:S(2)}) copy-start(bf16[1024,96]{1,0:T(8,128)(2,1)} %get-tuple-element.331) | copy-start | bytes 589828
  111.1 2.5 %collective-permute-start.11 = (bf16[1024,96]{1,0:T(8,128)(2,1)}, bf16[1024,96]{1,0:T(8,128)(2,1)S(1)}, u32[]{:S(2)}, u32[]{:S(2)}) collective-permute-start(bf16[1024,96]{1,0:T(8,128)(2,1)} %get-tuple-element.331), channel_id=1, source_target_pairs={{0,1},{1,0},{2,3},{3,2},{4,5},{5,4},{6,7},{7,6},{8,9},{9,8},{10,11... | collective-permute-start | bytes 589832 | tf_op jit(solution)/shard_map/ppermute | solution.py:814
  113.6 13.8 %collective-permute-start.15 = (bf16[512,1024]{1,0:T(8,128)(2,1)S(1)}, bf16[512,1024]{1,0:T(8,128)(2,1)S(1)}, u32[]{:S(2)}, u32[]{:S(2)}) collective-permute-start(bf16[512,1024]{1,0:T(8,128)(2,1)S(1)} %get-tuple-element.430.refs_0_), channel_id=1, source_target_pairs={{0,1},{1,0},{2,3},{3,2},{4,5},{5,4},{6,7},{7,6},{8,9},{9,8},{10,11... | collective-permute-start | bytes 3145736 | tf_op jit(solution)/shard_map/ppermute | solution.py:814
  114.1 13.4 %collective-permute-start.12 = (bf16[256,512]{1,0:T(8,128)(2,1)S(1)}, bf16[256,512]{1,0:T(8,128)(2,1)S(1)}, u32[]{:S(2)}, u32[]{:S(2)}) collective-permute-start(bf16[256,512]{1,0:T(8,128)(2,1)S(1)} %get-tuple-element.340.refs_0_), channel_id=1, source_target_pairs={{0,8},{4,12},{8,0},{12,4},{16,24},{20,28},{24,16},{28,20},{1,9},{5... | collective-permute-start | bytes 786440 | tf_op jit(solution)/shard_map/ppermute | solution.py:814
  115.4 12.1 %collective-permute-start.13 = (bf16[128,1024]{1,0:T(8,128)(2,1)S(1)}, bf16[128,1024]{1,0:T(8,128)(2,1)}, u32[]{:S(2)}, u32[]{:S(2)}) collective-permute-start(bf16[128,1024]{1,0:T(8,128)(2,1)S(1)} %get-tuple-element.342.refs_2_), channel_id=1, source_target_pairs={{0,16},{4,20},{8,24},{12,28},{16,0},{20,4},{24,8},{28,12},{1,17},{... | collective-permute-start | bytes 786440 | tf_op jit(solution)/shard_map/ppermute | solution.py:814
  117.3 7.2 %collective-permute-start.14 = (bf16[1024,96]{1,0:T(8,128)(2,1)S(1)}, bf16[1024,96]{1,0:T(8,128)(2,1)S(1)}, u32[]{:S(2)}, u32[]{:S(2)}) collective-permute-start(bf16[1024,96]{1,0:T(8,128)(2,1)S(1)} %add_convert_fusion.1), channel_id=1, source_target_pairs={{0,2},{1,3},{2,0},{3,1},{4,6},{5,7},{6,4},{7,5},{8,10},{9,11},{10,... | collective-permute-start | bytes 589832 | tf_op jit(solution)/shard_map/ppermute | solution.py:814
  127.4 0.8 copy-start.3
  130.1 17.8 %collective-permute-start.16 = (bf16[512,512]{1,0:T(8,128)(2,1)S(1)}, bf16[512,512]{1,0:T(8,128)(2,1)S(1)}, u32[]{:S(2)}, u32[]{:S(2)}) collective-permute-start(bf16[512,512]{1,0:T(8,128)(2,1)S(1)} %get-tuple-element.441.sz_ref), channel_id=1, source_target_pairs={{0,4},{4,0},{8,12},{12,8},{16,20},{20,16},{24,28},{28,24},{1,5},{5... | collective-permute-start | bytes 1572872 | tf_op jit(solution)/shard_map/ppermute | solution.py:814
  131.0 17.0 %collective-permute-start.17 = (bf16[256,1024]{1,0:T(8,128)(2,1)}, bf16[256,1024]{1,0:T(8,128)(2,1)}, u32[]{:S(2)}, u32[]{:S(2)}) collective-permute-start(bf16[256,1024]{1,0:T(8,128)(2,1)} %get-tuple-element.428.one_ref), channel_id=1, source_target_pairs={{0,8},{4,12},{8,0},{12,4},{16,24},{20,28},{24,16},{28,20},{1,9},{5... | collective-permute-start | bytes 1572872 | tf_op jit(solution)/shard_map/ppermute | solution.py:814
  147.9 30.9 %copy-start.1 = (f32[1024]{0:T(1024)S(1)}, f32[1024]{0:T(1024)}, u32[]{:S(2)}) copy-start(f32[1024]{0:T(1024)} %param.15) | copy-start | bytes 12292
  148.0 11.6 %collective-permute-start.20 = (bf16[512,1024]{1,0:T(8,128)(2,1)}, bf16[512,1024]{1,0:T(8,128)(2,1)S(1)}, u32[]{:S(2)}, u32[]{:S(2)}) collective-permute-start(bf16[512,1024]{1,0:T(8,128)(2,1)} %get-tuple-element.373), channel_id=1, source_target_pairs={{0,1},{1,0},{2,3},{3,2},{4,5},{5,4},{6,7},{7,6},{8,9},{9,8},{10,11... | collective-permute-start | bytes 3145736 | tf_op jit(solution)/shard_map/ppermute | solution.py:814
  149.5 9.1 %collective-permute-start.18 = (bf16[304,512]{1,0:T(8,128)(2,1)}, bf16[304,512]{1,0:T(8,128)(2,1)S(1)}, u32[]{:S(2)}, u32[]{:S(2)}) collective-permute-start(bf16[304,512]{1,0:T(8,128)(2,1)} %get-tuple-element.371), channel_id=1, source_target_pairs={{0,4},{4,0},{8,12},{12,8},{16,20},{20,16},{24,28},{28,24},{1,5},{5... | collective-permute-start | bytes 933896 | tf_op jit(solution)/shard_map/ppermute | solution.py:814
  150.8 8.8 %collective-permute-start.19 = (bf16[304,512]{1,0:T(8,128)(2,1)}, bf16[304,512]{1,0:T(8,128)(2,1)S(1)}, u32[]{:S(2)}, u32[]{:S(2)}) collective-permute-start(bf16[304,512]{1,0:T(8,128)(2,1)} %get-tuple-element.372), channel_id=1, source_target_pairs={{0,8},{4,12},{8,0},{12,4},{16,24},{20,28},{24,16},{28,20},{1,9},{5... | collective-permute-start | bytes 933896 | tf_op jit(solution)/shard_map/ppermute | solution.py:814
  152.1 3.0 %collective-permute-start.21 = (f32[1,1024]{1,0:T(1,128)}, f32[1,1024]{1,0:T(1,128)S(1)}, u32[]{:S(2)}, u32[]{:S(2)}) collective-permute-start(f32[1,1024]{1,0:T(1,128)} %get-tuple-element.374), channel_id=1, source_target_pairs={{0,2},{1,3},{2,0},{3,1},{4,6},{5,7},{6,4},{7,5},{8,10},{9,11},{10,... | collective-permute-start | bytes 12296 | tf_op jit(solution)/shard_map/ppermute | solution.py:814
  162.2 16.6 %collective-permute-start.27 = (bf16[256,1024]{1,0:T(8,128)(2,1)S(1)}, bf16[256,1024]{1,0:T(8,128)(2,1)S(1)}, u32[]{:S(2)}, u32[]{:S(2)}) collective-permute-start(bf16[256,1024]{1,0:T(8,128)(2,1)S(1)} %get-tuple-element.396), channel_id=1, source_target_pairs={{0,2},{1,3},{2,0},{3,1},{4,6},{5,7},{6,4},{7,5},{8,10},{9,11},{10,... | collective-permute-start | bytes 1572872 | tf_op jit(solution)/shard_map/ppermute | solution.py:814
  163.3 4.9 %collective-permute-start.22 = (bf16[152,512]{1,0:T(8,128)(2,1)S(1)}, bf16[152,512]{1,0:T(8,128)(2,1)S(1)}, u32[]{:S(2)}, u32[]{:S(2)}) collective-permute-start(bf16[152,512]{1,0:T(8,128)(2,1)S(1)} %get-tuple-element.385), channel_id=1, source_target_pairs={{0,8},{4,12},{8,0},{12,4},{16,24},{20,28},{24,16},{28,20},{1,9},{5... | collective-permute-start | bytes 466952 | tf_op jit(solution)/shard_map/ppermute | solution.py:814
  164.6 6.4 %collective-permute-start.23 = (bf16[152,512]{1,0:T(8,128)(2,1)S(1)}, bf16[152,512]{1,0:T(8,128)(2,1)S(1)}, u32[]{:S(2)}, u32[]{:S(2)}) collective-permute-start(bf16[152,512]{1,0:T(8,128)(2,1)S(1)} %get-tuple-element.386), channel_id=1, source_target_pairs={{0,16},{4,20},{8,24},{12,28},{16,0},{20,4},{24,8},{28,12},{1,17},{... | collective-permute-start | bytes 466952 | tf_op jit(solution)/shard_map/ppermute | solution.py:814
  165.6 2.5 %collective-permute-start.24 = (f32[1,1024]{1,0:T(1,128)S(1)}, f32[1,1024]{1,0:T(1,128)S(1)}, u32[]{:S(2)}, u32[]{:S(2)}) collective-permute-start(f32[1,1024]{1,0:T(1,128)S(1)} %add.42), channel_id=1, source_target_pairs={{0,1},{1,0},{2,3},{3,2},{4,5},{5,4},{6,7},{7,6},{8,9},{9,8},{10,11... | collective-permute-start | bytes 12296 | tf_op jit(solution)/shard_map/ppermute | solution.py:814
  172.1 6.7 %collective-permute-start.25 = (bf16[152,512]{1,0:T(8,128)(2,1)S(1)}, bf16[152,512]{1,0:T(8,128)(2,1)S(1)}, u32[]{:S(2)}, u32[]{:S(2)}) collective-permute-start(bf16[152,512]{1,0:T(8,128)(2,1)S(1)} %get-tuple-element.398.refs_0_), channel_id=1, source_target_pairs={{0,16},{4,20},{8,24},{12,28},{16,0},{20,4},{24,8},{28,12},{1,17},{... | collective-permute-start | bytes 466952 | tf_op jit(solution)/shard_map/ppermute | solution.py:814
  173.8 5.0 %collective-permute-start.26 = (bf16[152,512]{1,0:T(8,128)(2,1)S(1)}, bf16[152,512]{1,0:T(8,128)(2,1)S(1)}, u32[]{:S(2)}, u32[]{:S(2)}) collective-permute-start(bf16[152,512]{1,0:T(8,128)(2,1)S(1)} %get-tuple-element.400.refs_2_), channel_id=1, source_target_pairs={{0,4},{4,0},{8,12},{12,8},{16,20},{20,16},{24,28},{28,24},{1,5},{5... | collective-permute-start | bytes 466952 | tf_op jit(solution)/shard_map/ppermute | solution.py:814
  174.7 3.2 %collective-permute-start.28 = (f32[1,1024]{1,0:T(1,128)S(1)}, f32[1,1024]{1,0:T(1,128)S(1)}, u32[]{:S(2)}, u32[]{:S(2)}) collective-permute-start(f32[1,1024]{1,0:T(1,128)S(1)} %add.43), channel_id=1, source_target_pairs={{0,4},{4,0},{8,12},{12,8},{16,20},{20,16},{24,28},{28,24},{1,5},{5... | collective-permute-start | bytes 12296 | tf_op jit(solution)/shard_map/ppermute | solution.py:814
  180.4 19.5 %collective-permute-start.34 = (bf16[256,1024]{1,0:T(8,128)(2,1)S(1)}, bf16[256,1024]{1,0:T(8,128)(2,1)S(1)}, u32[]{:S(2)}, u32[]{:S(2)}) collective-permute-start(bf16[256,1024]{1,0:T(8,128)(2,1)S(1)} %get-tuple-element.426.refs_0_), channel_id=1, source_target_pairs={{0,2},{1,3},{2,0},{3,1},{4,6},{5,7},{6,4},{7,5},{8,10},{9,11},{10,... | collective-permute-start | bytes 1572872 | tf_op jit(solution)/shard_map/ppermute | solution.py:814
  180.5 10.2 %collective-permute-start.29 = (bf16[152,512]{1,0:T(8,128)(2,1)S(1)}, bf16[152,512]{1,0:T(8,128)(2,1)S(1)}, u32[]{:S(2)}, u32[]{:S(2)}) collective-permute-start(bf16[152,512]{1,0:T(8,128)(2,1)S(1)} %get-tuple-element.413.refs_0_), channel_id=1, source_target_pairs={{0,8},{4,12},{8,0},{12,4},{16,24},{20,28},{24,16},{28,20},{1,9},{5... | collective-permute-start | bytes 466952 | tf_op jit(solution)/shard_map/ppermute | solution.py:814
  184.0 6.8 %collective-permute-start.30 = (bf16[152,512]{1,0:T(8,128)(2,1)S(1)}, bf16[152,512]{1,0:T(8,128)(2,1)S(1)}, u32[]{:S(2)}, u32[]{:S(2)}) collective-permute-start(bf16[152,512]{1,0:T(8,128)(2,1)S(1)} %get-tuple-element.415.refs_2_), channel_id=1, source_target_pairs={{0,16},{4,20},{8,24},{12,28},{16,0},{20,4},{24,8},{28,12},{1,17},{... | collective-permute-start | bytes 466952 | tf_op jit(solution)/shard_map/ppermute | solution.py:814
  187.1 3.7 %collective-permute-start.31 = (f32[1,1024]{1,0:T(1,128)S(1)}, f32[1,1024]{1,0:T(1,128)S(1)}, u32[]{:S(2)}, u32[]{:S(2)}) collective-permute-start(f32[1,1024]{1,0:T(1,128)S(1)} %add.44), channel_id=1, source_target_pairs={{0,8},{4,12},{8,0},{12,4},{16,24},{20,28},{24,16},{28,20},{1,9},{5... | collective-permute-start | bytes 12296 | tf_op jit(solution)/shard_map/ppermute | solution.py:814
  191.4 8.5 %collective-permute-start.32 = (bf16[304,512]{1,0:T(8,128)(2,1)S(1)}, bf16[304,512]{1,0:T(8,128)(2,1)S(1)}, u32[]{:S(2)}, u32[]{:S(2)}) collective-permute-start(bf16[304,512]{1,0:T(8,128)(2,1)S(1)} %get-tuple-element.437.sa_ref), channel_id=1, source_target_pairs={{0,4},{4,0},{8,12},{12,8},{16,20},{20,16},{24,28},{28,24},{1,5},{5... | collective-permute-start | bytes 933896 | tf_op jit(solution)/shard_map/ppermute | solution.py:814
  191.4 8.5 %collective-permute-start.33 = (bf16[304,512]{1,0:T(8,128)(2,1)S(1)}, bf16[304,512]{1,0:T(8,128)(2,1)S(1)}, u32[]{:S(2)}, u32[]{:S(2)}) collective-permute-start(bf16[304,512]{1,0:T(8,128)(2,1)S(1)} %get-tuple-element.439.sb_ref), channel_id=1, source_target_pairs={{0,8},{4,12},{8,0},{12,4},{16,24},{20,28},{24,16},{28,20},{1,9},{5... | collective-permute-start | bytes 933896 | tf_op jit(solution)/shard_map/ppermute | solution.py:814
  193.7 5.6 %collective-permute-start.35 = (f32[1,1024]{1,0:T(1,128)S(1)}, f32[1,1024]{1,0:T(1,128)S(1)}, u32[]{:S(2)}, u32[]{:S(2)}) collective-permute-start(f32[1,1024]{1,0:T(1,128)S(1)} %add.45), channel_id=1, source_target_pairs={{0,16},{4,20},{8,24},{12,28},{16,0},{20,4},{24,8},{28,12},{1,17},{... | collective-permute-start | bytes 12296 | tf_op jit(solution)/shard_map/ppermute | solution.py:814
  199.9 7.8 %copy-start = (bf16[1,1024,1024]{2,1,0:T(8,128)(2,1)S(1)}, bf16[1,1024,1024]{2,1,0:T(8,128)(2,1)}, u32[]{:S(2)}) copy-start(bf16[1,1024,1024]{2,1,0:T(8,128)(2,1)} %param.25) | copy-start | bytes 6291460
  200.0 7.7 %collective-permute-start.36 = (bf16[512,1024]{1,0:T(8,128)(2,1)S(1)}, bf16[512,1024]{1,0:T(8,128)(2,1)S(1)}, u32[]{:S(2)}, u32[]{:S(2)}) collective-permute-start(bf16[512,1024]{1,0:T(8,128)(2,1)S(1)} %merge.19.one_ref), channel_id=1, source_target_pairs={{0,1},{1,0},{2,3},{3,2},{4,5},{5,4},{6,7},{7,6},{8,9},{9,8},{10,11... | collective-permute-start | bytes 3145736 | tf_op jit(solution)/shard_map/ppermute | solution.py:814
